TPU v7x, 256 devices: a whole 4x4x8 slice. The times are simulated.
256 devices in a mesh: rows: 32 (over z, x_lo, core), cols: 8 (over x_hi, y).
Axes of the slice: x: 4 (x_hi: 2, x_lo: 2; x = x_hi * 2 + x_lo), y: 4, z: 8, core: 2. Of those that a mesh axis runs over, the one named last changes fastest.
Arguments:
- frames_in: bfloat16 [3, 192, 64, 256], P(None, 'rows', 'cols'), may hold values from -6 to 6
- cotangent: bfloat16 [3, 192, 64, 256], P(None, 'rows', 'cols'), may hold values from -6 to 6
- core: float32 [110592], P(('rows', 'cols')), may hold values from -0.3 to 0.3
- moment_one: float32 [110592], P(('rows', 'cols')), may hold values from -0.6 to 0.6
- moment_two: float32 [110592], P(('rows', 'cols')), may hold values from 0.01 to 0.16
- u_in: bfloat16 [256, 64], replicated, may hold values from -0.375 to 0.375
- u_out: bfloat16 [256, 64], replicated, may hold values from -0.375 to 0.375
Outputs:
- frames_grad: bfloat16 [3, 192, 64, 256], P(None, 'rows', 'cols')
- core_next: float32 [110592], P(('rows', 'cols'))
- moment_one_next: float32 [110592], P(('rows', 'cols'))
- moment_two_next: float32 [110592], P(('rows', 'cols'))
- kernel_next: bfloat16 [27, 256, 256], replicated
All inputs are finite; a program needn't handle non-finite values.
Results may differ from a plain program's by a relative error of at most 0.014.
Values may be sent and summed in bfloat16 or wider, within the bound.
No kernel may reach another device: no remote copies, remote signals or barrier semaphores. Data moves between devices by JAX's collectives and lax.ppermute only.
A program may use at most 64 MiB of HBM per device.

v0:
```python
import math

import jax
import jax.numpy as jnp
from jax import lax
from jax.sharding import PartitionSpec as P

beta_one = 0.9
beta_two = 0.999
learn_rate = 0.06
epsilon = 1e-08
fix_one = 1.0 - 0.9**10
fix_two = 1.0 - 0.999**10


def extended(block, sides, width):
    for axis, dim in sides:
        count = lax.axis_size(axis)
        forward = [(i, i + 1) for i in range(count - 1)]
        backward = [(target, source) for source, target in forward]
        low = lax.ppermute(
            lax.slice_in_dim(block, block.shape[dim] - width, None, axis=dim), axis, forward
        )
        high = lax.ppermute(lax.slice_in_dim(block, 0, width, axis=dim), axis, backward)
        block = jnp.concatenate([low, block, high], axis=dim)
    return block


def split_up(x, dim, devices):
    before, after = (x.shape[:dim], x.shape[dim + 1 :])
    return jnp.moveaxis(x.reshape(*before, devices, -1, *after), dim, 0)


def sum_at_owner(x, axis, dim):
    tiles = split_up(x, dim, lax.axis_size(axis))
    arrived = lax.all_to_all(tiles, axis, split_axis=0, concat_axis=0, tiled=True)
    return arrived.astype(jnp.float32).sum(axis=0)


def sum_at_owner_2(x, axis, dim):
    devices = lax.axis_size(axis)
    tiles = lax.all_to_all(split_up(x, dim, devices), axis, 0, 0, tiled=True)
    return jnp.sum(tiles, axis=0)


def build(flat_core, u_in, u_out):
    rank = u_in.shape[1]
    cube = flat_core.reshape(-1, rank).astype(jnp.bfloat16)
    halfway = lax.dot_general(
        cube, u_out, (((1,), (1,)), ((), ())), preferred_element_type=jnp.float32
    ).astype(jnp.bfloat16)
    halfway = halfway.reshape(-1, rank, u_out.shape[0])
    kernel = jnp.einsum("ip,tpo->tio", u_in, halfway, preferred_element_type=jnp.float32)
    return kernel.astype(jnp.bfloat16)


def offsets():
    return [(a, b, c) for a in range(3) for b in range(3) for c in range(3)]


def forward_sum(padded, kernel, frames, rows, cols):
    chans = padded.shape[3]
    total = jnp.zeros((frames * rows * cols, kernel.shape[2]), jnp.float32)
    for tap, (a, b, c) in enumerate(offsets()):
        piece = padded[a : a + frames, b : b + rows, c : c + cols, :].reshape(-1, chans)
        total = total + jnp.dot(piece, kernel[tap], preferred_element_type=jnp.float32)
    return total.reshape(frames, rows, cols, -1)


def backward_sum(padded, kernel, frames, rows, cols):
    chans = padded.shape[3]
    total = jnp.zeros((frames * rows * cols, kernel.shape[1]), jnp.float32)
    for tap, (a, b, c) in enumerate(offsets()):
        piece = padded[
            2 - a : 2 - a + frames, 2 - b : 2 - b + rows, 2 - c : 2 - c + cols, :
        ].reshape(-1, chans)
        total = total + lax.dot_general(
            piece, kernel[tap], (((1,), (1,)), ((), ())), preferred_element_type=jnp.float32
        )
    return total.reshape(frames, rows, cols, -1)


def core_terms(padded, slope, u_in, u_out, frames, rows, cols):
    chans = padded.shape[3]
    shape_pad = padded.shape
    in_proj = jnp.dot(padded.reshape(-1, chans), u_in, preferred_element_type=jnp.float32).astype(
        jnp.bfloat16
    )
    in_proj = in_proj.reshape(shape_pad[0], shape_pad[1], shape_pad[2], -1)
    out_proj = jnp.dot(slope.reshape(-1, chans), u_out, preferred_element_type=jnp.float32).astype(
        jnp.bfloat16
    )
    grads = []
    for tap, (a, b, c) in enumerate(offsets()):
        piece = in_proj[a : a + frames, b : b + rows, c : c + cols, :].reshape(-1, in_proj.shape[3])
        grads.append(
            lax.dot_general(
                piece, out_proj, (((0,), (0,)), ((), ())), preferred_element_type=jnp.float32
            )
        )
    return jnp.stack(grads).reshape(-1)


def time_pad(tile):
    return jnp.pad(tile, ((1, 1), (0, 0), (0, 0), (0, 0)))


def slope_of(cotangent, pre):
    sig = jax.nn.sigmoid(pre)
    return (cotangent.astype(jnp.float32) * sig * (1.0 + pre * (1.0 - sig))).astype(jnp.bfloat16)


def body(frames_in, cotangent, core, moment_one, moment_two, u_in, u_out):
    frames, rows, cols = (frames_in.shape[0], frames_in.shape[1], frames_in.shape[2])
    whole_core = lax.all_gather(core, ("rows", "cols"), axis=0, tiled=True)
    kernel = build(whole_core, u_in, u_out)
    rimmed = extended(frames_in, (("rows", 1), ("cols", 2)), 1)
    padded = time_pad(rimmed)
    pre = forward_sum(padded, kernel, frames, rows, cols)
    slope = slope_of(cotangent, pre)
    slope_rimmed = extended(slope, (("rows", 1), ("cols", 2)), 1)
    slope_pad = time_pad(slope_rimmed)
    frames_grad = backward_sum(slope_pad, kernel, frames, rows, cols).astype(jnp.bfloat16)
    local_grad = core_terms(padded, slope, u_in, u_out, frames, rows, cols)
    partial_grad = sum_at_owner(local_grad.astype(jnp.bfloat16), "rows", 0)
    core_grad = sum_at_owner_2(partial_grad, "cols", 0)
    cells = frames * rows * lax.axis_size("rows") * cols * lax.axis_size("cols")
    core_grad = core_grad / math.sqrt(cells)
    moment_one_next = beta_one * moment_one + (1.0 - beta_one) * core_grad
    moment_two_next = beta_two * moment_two + (1.0 - beta_two) * core_grad * core_grad
    core_next = core - learn_rate * (moment_one_next / fix_one) / (
        jnp.sqrt(moment_two_next / fix_two) + epsilon
    )
    new_whole = lax.all_gather(core_next, ("rows", "cols"), axis=0, tiled=True)
    kernel_next = build(new_whole, u_in, u_out)
    return (frames_grad, core_next, moment_one_next, moment_two_next, kernel_next)


def solution(mesh):
    in_specs = (
        P(None, "rows", "cols", None),
        P(None, "rows", "cols", None),
        P(("rows", "cols")),
        P(("rows", "cols")),
        P(("rows", "cols")),
        P(),
        P(),
    )
    out_specs = (
        P(None, "rows", "cols", None),
        P(("rows", "cols")),
        P(("rows", "cols")),
        P(("rows", "cols")),
        P(),
    )
    return jax.shard_map(body, mesh=mesh, in_specs=in_specs, out_specs=out_specs, check_vma=False)
```

profile of v0, /device:TPU:1, one launch (start us, length us, event | category | flops | bytes accessed | tf_op | source)
XLA Modules:
  0.0 256.4 jit_solution(16659377730110197114)
XLA Ops:
  0.6 0.7 fusion.96
  1.4 4.5 %collective-permute-start = (bf16[3,1,8,256]{3,2,1,0:T(8,128)(2,1)S(1)}, bf16[3,1,8,256]{3,2,1,0:T(8,128)(2,1)S(1)}, u32[]{:S(2)}, u32[]{:S(2)}) collective-permute-start(bf16[3,1,8,256]{3,2,1,0:T(8,128)(2,1)S(1)} %get-tuple-element.126), channel_id=1, source_target_pairs={{0,8},{8,16},{16,24},{24,32},{32,40},{40,48},{48,56},{56,64},{64,7... | collective-permute-start | bytes 36872 | tf_op jit(solution)/shard_map/ppermute | solution.py:21
  5.9 1.9 collective-permute-start.1
  7.9 0.9 dynamic-update-slice
  8.8 82.9 %all-reduce.6 = bf16[110592]{0:T(1024)(128)(2,1)S(1)} all-reduce(f32[110592]{0:T(1024)S(1)} %dynamic-update-slice), channel_id=1, replica_groups=mesh['rows'=32,'cols'=8] {'rows','cols'}, use_global_device_ids=true, to_apply=%add.2 | all-reduce | flops 110592 | bytes 663552
  91.9 1.1 convolution_convert_fusion.1
  93.0 1.1 convert_bitcast_fusion.1
  94.3 1.3 collective-permute-start.3
  95.6 4.0 %collective-permute-start.2 = (bf16[3,8,1,256]{3,2,1,0:T(2,128)(2,1)S(1)}, bf16[3,8,1,256]{3,2,1,0:T(2,128)(2,1)S(1)}, u32[]{:S(2)}, u32[]{:S(2)}) collective-permute-start(bf16[3,8,1,256]{3,2,1,0:T(2,128)(2,1)S(1)} %get-tuple-element.116), channel_id=1, source_target_pairs={{0,1},{1,2},{2,3},{3,4},{4,5},{5,6},{6,7},{8,9},{9,10},{10,11},{11... | collective-permute-start | bytes 36872 | tf_op jit(solution)/shard_map/ppermute | solution.py:21
  99.8 0.7 collective-permute-done.2
  101.4 1.3 fusion.80
  102.9 1.1 fusion.79
  104.0 1.1 fusion.76
  110.1 3.6 %collective-permute-start.5 = (bf16[3,1,8,256]{3,2,1,0:T(8,128)(2,1)S(1)}, bf16[3,1,8,256]{3,2,1,0:T(8,128)(2,1)S(1)}, u32[]{:S(2)}, u32[]{:S(2)}) collective-permute-start(bf16[3,1,8,256]{3,2,1,0:T(8,128)(2,1)S(1)} %get-tuple-element.121), channel_id=1, source_target_pairs={{8,0},{16,8},{24,16},{32,24},{40,32},{48,40},{56,48},{64,56},{72,6... | collective-permute-start | bytes 36872 | tf_op jit(solution)/shard_map/ppermute | solution.py:24
  113.7 1.9 collective-permute-start.4
  121.5 0.5 broadcast.109
  122.0 2.0 reduce.2
  124.0 0.9 reshape.387
  124.9 7.6 %all-to-all-start = ((bf16[32,2,1728]{2,1,0:T(2,128)(2,1)}), bf16[32,2,1728]{2,1,0:T(2,128)(2,1)S(1)}, u32[]{:S(2)}, u32[]{:S(2)}) async-start(bf16[32,2,1728]{2,1,0:T(2,128)(2,1)} %reshape.387), calls=%async_computation | async-start | bytes 458752 | tf_op jit(solution)/shard_map/all_to_all | solution.py:36
  132.6 1.6 collective-permute-start.7
  134.1 4.6 %collective-permute-start.6 = (bf16[3,8,1,256]{3,2,1,0:T(2,128)(2,1)S(1)}, bf16[3,8,1,256]{3,2,1,0:T(2,128)(2,1)S(1)}, u32[]{:S(2)}, u32[]{:S(2)}) collective-permute-start(bf16[3,8,1,256]{3,2,1,0:T(2,128)(2,1)S(1)} %get-tuple-element.112), channel_id=1, source_target_pairs={{0,1},{1,2},{2,3},{3,4},{4,5},{5,6},{6,7},{8,9},{9,10},{10,11},{11... | collective-permute-start | bytes 36872 | tf_op jit(solution)/shard_map/ppermute | solution.py:21
  138.7 0.9 collective-permute-done.6
  139.8 1.1 fusion.78
  140.8 1.1 fusion.75
  147.2 0.7 all_to_all.11
  147.9 12.6 %all-to-all-start.1 = ((f32[8,1,432]{2,1,0:T(1,128)}), f32[8,1,432]{2,1,0:T(1,128)S(1)}, u32[]{:S(2)}, u32[]{:S(2)}) async-start(f32[8,1,432]{2,1,0:T(1,128)} %all_to_all.11), calls=%async_computation.1 | async-start | bytes 32768 | tf_op jit(solution)/shard_map/all_to_all | solution.py:42
  160.6 1.7 fusion.7
  162.3 4.9 %all-to-all-done.1 = f32[8,1,432]{2,1,0:T(1,128)S(1)} async-done(((f32[8,1,432]{2,1,0:T(1,128)}), f32[8,1,432]{2,1,0:T(1,128)S(1)}, u32[]{:S(2)}, u32[]{:S(2)}) %all-to-all-start.1) | async-done | bytes 13856 | tf_op jit(solution)/shard_map/all_to_all | solution.py:42
  167.2 0.6 fusion.87
  167.9 79.3 %all-reduce.7 = bf16[110592]{0:T(1024)(128)(2,1)S(1)} all-reduce(f32[110592]{0:T(1024)S(1)} %get-tuple-element.30), channel_id=1, replica_groups=mesh['rows'=32,'cols'=8] {'rows','cols'}, use_global_device_ids=true, to_apply=%add.3 | all-reduce | flops 110592 | bytes 663552
  247.8 2.9 %convert_bitcast_fusion = bf16[27,256,256]{1,2,0:T(8,128)(2,1)} fusion(bf16[27,64,256]{2,1,0:T(8,128)(2,1)S(1)} %bitcast.435, bf16[256,64]{0,1:T(8,128)(2,1)S(1)} %copy-done), kind=kOutput, calls=%fused_computation | convolution fusion | flops 228261888 | bytes 4456448 | tf_op jit(solution)/shard_map/ip,tpo->tio/dot_general | solution.py:53
  250.7 5.7 %copy.24 = bf16[27,256,256]{2,1,0:T(8,128)(2,1)} copy(bf16[27,256,256]{1,2,0:T(8,128)(2,1)} %convert_bitcast_fusion) | data formatting | bytes 7077888
  (133 shorter events, 18.1 us)
Async XLA Ops:
  0.6 92.4 %copy-start = (bf16[256,64]{0,1:T(8,128)(2,1)S(1)}, bf16[256,64]{0,1:T(8,128)(2,1)}, u32[]{:S(2)}) copy-start(bf16[256,64]{0,1:T(8,128)(2,1)} %param.12) | copy-start | bytes 98308
  1.4 92.8 %collective-permute-start = (bf16[3,1,8,256]{3,2,1,0:T(8,128)(2,1)S(1)}, bf16[3,1,8,256]{3,2,1,0:T(8,128)(2,1)S(1)}, u32[]{:S(2)}, u32[]{:S(2)}) collective-permute-start(bf16[3,1,8,256]{3,2,1,0:T(8,128)(2,1)S(1)} %get-tuple-element.126), channel_id=1, source_target_pairs={{0,8},{8,16},{16,24},{24,32},{32,40},{40,48},{48,56},{56,64},{64,7... | collective-permute-start | bytes 36872 | tf_op jit(solution)/shard_map/ppermute | solution.py:21
  5.9 88.3 %collective-permute-start.1 = (bf16[3,1,8,256]{3,2,1,0:T(8,128)(2,1)S(1)}, bf16[3,1,8,256]{3,2,1,0:T(8,128)(2,1)S(1)}, u32[]{:S(2)}, u32[]{:S(2)}) collective-permute-start(bf16[3,1,8,256]{3,2,1,0:T(8,128)(2,1)S(1)} %get-tuple-element.125), channel_id=1, source_target_pairs={{8,0},{16,8},{24,16},{32,24},{40,32},{48,40},{56,48},{64,56},{72,6... | collective-permute-start | bytes 36872 | tf_op jit(solution)/shard_map/ppermute | solution.py:24
  8.8 85.4 %copy-start.4 = (bf16[3,6,8,256]{3,2,1,0:T(8,128)(2,1)S(1)}, bf16[3,6,8,256]{3,2,1,0:T(8,128)(2,1)}, u32[]{:S(2)}) copy-start(bf16[3,6,8,256]{3,2,1,0:T(8,128)(2,1)} %param.7) | copy-start | bytes 221188
  94.2 5.4 %copy-start.1 = (bf16[27,256,256]{1,2,0:T(8,128)(2,1)}, bf16[27,256,256]{1,2,0:T(8,128)(2,1)S(1)}, u32[]{:S(2)}) copy-start(bf16[27,256,256]{1,2,0:T(8,128)(2,1)S(1)} %convert_bitcast_fusion.1) | copy-start | bytes 10616836
  94.3 5.5 %collective-permute-start.3 = (bf16[3,8,1,256]{3,2,1,0:T(2,128)(2,1)S(1)}, bf16[3,8,1,256]{3,2,1,0:T(2,128)(2,1)S(1)}, u32[]{:S(2)}, u32[]{:S(2)}) collective-permute-start(bf16[3,8,1,256]{3,2,1,0:T(2,128)(2,1)S(1)} %get-tuple-element.117), channel_id=1, source_target_pairs={{1,0},{2,1},{3,2},{4,3},{5,4},{6,5},{7,6},{9,8},{10,9},{11,10},{12... | collective-permute-start | bytes 36872 | tf_op jit(solution)/shard_map/ppermute | solution.py:24
  95.6 4.9 %collective-permute-start.2 = (bf16[3,8,1,256]{3,2,1,0:T(2,128)(2,1)S(1)}, bf16[3,8,1,256]{3,2,1,0:T(2,128)(2,1)S(1)}, u32[]{:S(2)}, u32[]{:S(2)}) collective-permute-start(bf16[3,8,1,256]{3,2,1,0:T(2,128)(2,1)S(1)} %get-tuple-element.116), channel_id=1, source_target_pairs={{0,1},{1,2},{2,3},{3,4},{4,5},{5,6},{6,7},{8,9},{9,10},{10,11},{11... | collective-permute-start | bytes 36872 | tf_op jit(solution)/shard_map/ppermute | solution.py:21
  101.2 3.8 %copy-start.2 = (bf16[27,256,256]{1,2,0:T(8,128)(2,1)S(1)}, bf16[27,256,256]{1,2,0:T(8,128)(2,1)}, u32[]{:S(2)}) copy-start(bf16[27,256,256]{1,2,0:T(8,128)(2,1)} %copy-done.1) | copy-start | bytes 10616836
  107.2 2.8 %copy-start.6 = (bf16[3,6,8,256]{3,2,1,0:T(8,128)(2,1)S(1)}, bf16[3,6,8,256]{3,2,1,0:T(8,128)(2,1)}, u32[]{:S(2)}) copy-start(bf16[3,6,8,256]{3,2,1,0:T(8,128)(2,1)} %param.8) | copy-start | bytes 221188
  107.4 8.2 %copy-start.5 = (bf16[256,64]{0,1:T(8,128)(2,1)S(1)}, bf16[256,64]{0,1:T(8,128)(2,1)}, u32[]{:S(2)}) copy-start(bf16[256,64]{0,1:T(8,128)(2,1)} %param.13) | copy-start | bytes 98308
  110.1 22.4 %collective-permute-start.5 = (bf16[3,1,8,256]{3,2,1,0:T(8,128)(2,1)S(1)}, bf16[3,1,8,256]{3,2,1,0:T(8,128)(2,1)S(1)}, u32[]{:S(2)}, u32[]{:S(2)}) collective-permute-start(bf16[3,1,8,256]{3,2,1,0:T(8,128)(2,1)S(1)} %get-tuple-element.121), channel_id=1, source_target_pairs={{8,0},{16,8},{24,16},{32,24},{40,32},{48,40},{56,48},{64,56},{72,6... | collective-permute-start | bytes 36872 | tf_op jit(solution)/shard_map/ppermute | solution.py:24
  113.7 18.8 %collective-permute-start.4 = (bf16[3,1,8,256]{3,2,1,0:T(8,128)(2,1)S(1)}, bf16[3,1,8,256]{3,2,1,0:T(8,128)(2,1)S(1)}, u32[]{:S(2)}, u32[]{:S(2)}) collective-permute-start(bf16[3,1,8,256]{3,2,1,0:T(8,128)(2,1)S(1)} %get-tuple-element.120), channel_id=1, source_target_pairs={{0,8},{8,16},{16,24},{24,32},{32,40},{40,48},{48,56},{56,64},{64,7... | collective-permute-start | bytes 36872 | tf_op jit(solution)/shard_map/ppermute | solution.py:21
  124.9 21.6 %all-to-all-start = ((bf16[32,2,1728]{2,1,0:T(2,128)(2,1)}), bf16[32,2,1728]{2,1,0:T(2,128)(2,1)S(1)}, u32[]{:S(2)}, u32[]{:S(2)}) async-start(bf16[32,2,1728]{2,1,0:T(2,128)(2,1)} %reshape.387), calls=%async_computation | async-start | bytes 458752 | tf_op jit(solution)/shard_map/all_to_all | solution.py:36
  132.5 9.7 %copy-start.3 = (bf16[27,256,256]{1,2,0:T(8,128)(2,1)S(1)}, bf16[27,256,256]{1,2,0:T(8,128)(2,1)}, u32[]{:S(2)}) copy-start(bf16[27,256,256]{1,2,0:T(8,128)(2,1)} %copy-done.1) | copy-start | bytes 10616836
  132.6 6.2 %collective-permute-start.7 = (bf16[3,8,1,256]{3,2,1,0:T(2,128)(2,1)S(1)}, bf16[3,8,1,256]{3,2,1,0:T(2,128)(2,1)S(1)}, u32[]{:S(2)}, u32[]{:S(2)}) collective-permute-start(bf16[3,8,1,256]{3,2,1,0:T(2,128)(2,1)S(1)} %get-tuple-element.111), channel_id=1, source_target_pairs={{1,0},{2,1},{3,2},{4,3},{5,4},{6,5},{7,6},{9,8},{10,9},{11,10},{12... | collective-permute-start | bytes 36872 | tf_op jit(solution)/shard_map/ppermute | solution.py:24
  134.1 5.5 %collective-permute-start.6 = (bf16[3,8,1,256]{3,2,1,0:T(2,128)(2,1)S(1)}, bf16[3,8,1,256]{3,2,1,0:T(2,128)(2,1)S(1)}, u32[]{:S(2)}, u32[]{:S(2)}) collective-permute-start(bf16[3,8,1,256]{3,2,1,0:T(2,128)(2,1)S(1)} %get-tuple-element.112), channel_id=1, source_target_pairs={{0,1},{1,2},{2,3},{3,4},{4,5},{5,6},{6,7},{8,9},{9,10},{10,11},{11... | collective-permute-start | bytes 36872 | tf_op jit(solution)/shard_map/ppermute | solution.py:21
  144.7 22.5 %copy-start.7 = (f32[432]{0:T(512)S(1)}, f32[432]{0:T(512)}, u32[]{:S(2)}) copy-start(f32[432]{0:T(512)} %param.9) | copy-start | bytes 5188
  144.7 22.5 %copy-start.8 = (f32[432]{0:T(512)S(1)}, f32[432]{0:T(512)}, u32[]{:S(2)}) copy-start(f32[432]{0:T(512)} %param.10) | copy-start | bytes 5188
  144.7 22.5 %copy-start.9 = (f32[432]{0:T(512)S(1)}, f32[432]{0:T(512)}, u32[]{:S(2)}) copy-start(f32[432]{0:T(512)} %param.11) | copy-start | bytes 5188
  147.9 19.2 %all-to-all-start.1 = ((f32[8,1,432]{2,1,0:T(1,128)}), f32[8,1,432]{2,1,0:T(1,128)S(1)}, u32[]{:S(2)}, u32[]{:S(2)}) async-start(f32[8,1,432]{2,1,0:T(1,128)} %all_to_all.11), calls=%async_computation.1 | async-start | bytes 32768 | tf_op jit(solution)/shard_map/all_to_all | solution.py:42
where the time goes:
time: 257 us; the launch traced here: 256 us
  blocking collectives  162 us (63%)
  starting transfers between devices  43.6 us (17%)
  matrix products  27.6 us (11%)
  local copies, waits for them, and re-layouts  11.4 us (4%)
  waiting for transfers between devices  6.48 us (3%)
  other arithmetic  3.75 us (1%)
    unnamed x2, blocking collectives  162 us
    ppermute x4, starting transfers between devices, extended(): lax.ppermute(lax.slice_in_dim(block, block.shape[dim] - width, None, axis...  15 us
    all_to_all x1, starting transfers between devices, sum_at_owner_2(): tiles = lax.all_to_all(split_up(x, dim, devices), axis, 0, 0, tiled=True)  12.6 us
    dot_general x27, matrix products, forward_sum(): jnp.dot(piece, kernel[tap], preferred_element_type=jnp.float32)  8.49 us
    ppermute x4, starting transfers between devices, extended(): lax.ppermute(lax.slice_in_dim(block, 0, width, axis=dim), axis, backward)  8.4 us
    dot_general x27, matrix products, backward_sum(): lax.dot_general(piece, kernel[tap], (((1,), (1,)), ((), ())), preferred_e...  8.1 us
    unnamed x27, local copies, waits for them, and re-layouts  7.96 us
    all_to_all x1, starting transfers between devices, sum_at_owner(): lax.all_to_all(tiles, axis, split_axis=0, concat_axis=0, tiled=True)  7.56 us
  transfers between devices with their start and end apart: 10, of which 3 were waited for; matrix products, arithmetic and copies ran while one was open for 8% of the time, Pallas kernels for 0%

commit v1 on v0

v1 whole, which is shorter than its diff:
```python
import jax
import jax.numpy as jnp
import numpy as np
from jax import lax
from jax.experimental import pallas as pl
from jax.experimental.pallas import tpu as pltpu
from jax.sharding import PartitionSpec as P

beta_one = 0.9
beta_two = 0.999
learn_rate = 0.06
epsilon = 1e-08
fix_one = 1.0 - 0.9**10
fix_two = 1.0 - 0.999**10

BF = jnp.bfloat16
F32 = jnp.float32
AXES = ("rows", "cols")

OWN = 432
FRAMES, ROWS, COLS = 3, 6, 8
CELLS = FRAMES * ROWS * COLS
SIDE = FRAMES * 8
TABLE = 864


def ring_tables():
    take = np.zeros((216, 512), np.float32)
    wrap = np.zeros((256, 128), np.float32)
    for r in range(8):
        for c in range(8):
            first = 27 * c // 8
            col = 32 * r + 4 * c
            for j in range(4):
                take[27 * r + first + j, col + j] = 1
            over = 48 * c % 128 + OWN - 512
            if over > 0:
                take[27 * r + first + 4, 256 + col] = 1
                wrap[col, :over] = 1
    return take, wrap


def dot(a, b):
    return jnp.dot(a, b, preferred_element_type=F32)


def dot_nt(a, b):
    return lax.dot_general(a, b, (((1,), (1,)), ((), ())), preferred_element_type=F32)


def dot_tn(a, b):
    return lax.dot_general(a, b, (((0,), (0,)), ((), ())), preferred_element_type=F32)


def lane(shape):
    return lax.broadcasted_iota(jnp.int32, shape, 1)


def sublane(shape):
    return lax.broadcasted_iota(jnp.int32, shape, 0)


def ring_shift():
    return lax.rem(lax.axis_index("cols") * 48, 128)


def to_ring(v, shift):
    turned = pltpu.roll(v, shift, axis=1)
    above = jnp.concatenate([turned[3:4], turned[0:3]], axis=0)
    return jnp.where(lane(v.shape) >= shift, turned, above)


def from_ring(v, shift):
    turned = pltpu.roll(v, lax.rem(128 - shift, 128), axis=1)
    below = jnp.concatenate([turned[1:4], turned[0:1]], axis=0)
    return jnp.where(lane(v.shape) < 128 - shift, turned, below)


def in_ring(shift):
    place = sublane((4, 128)) * 128 + lane((4, 128)) - shift
    place = jnp.where(place < 0, place + 512, place)
    return place < OWN


def load_flat(ref, scratch):
    scratch[...] = jnp.zeros_like(scratch)
    for k in range(3):
        scratch[k, :] = ref[pl.ds(128 * k, 128)]
    scratch[3, 0 : OWN - 384] = ref[pl.ds(384, OWN - 384)]
    return scratch[0:4, :]


def store_flat(ref, v):
    for k in range(3):
        ref[pl.ds(128 * k, 128)] = v[k]
    ref[pl.ds(384, OWN - 384)] = v[3, 0 : OWN - 384]


def spread(ref, v):
    block = jnp.concatenate([v, v, v, v], axis=0).astype(BF)
    for k in range(64):
        ref[16 * k : 16 * k + 16, :] = block


def start_kernel(core_ref, x_ref, send_ref, first_ref, last_ref, flat):
    spread(send_ref, to_ring(load_flat(core_ref, flat), ring_shift()))
    for f in range(FRAMES):
        first_ref[f] = x_ref[f, 0]
        last_ref[f] = x_ref[f, ROWS - 1]


def sides_kernel(own_ref, above_ref, below_ref, low_ref, high_ref, low, high):
    for f in range(FRAMES):
        for y in range(8):
            if y == 0:
                tile = above_ref[f]
            elif y == 7:
                tile = below_ref[f]
            else:
                tile = own_ref[f, y - 1]
            tile = tile.astype(F32)
            low[8 * f + y : 8 * f + y + 1, :] = tile[0:1, :]
            high[8 * f + y : 8 * f + y + 1, :] = tile[7:8, :]
    low_ref[...] = low[...].astype(BF)
    high_ref[...] = high[...].astype(BF)


def shifted(tile, left, right, bounds, period):
    at = lane(tile.shape) % period
    row = sublane(tile.shape)
    back = jnp.where(row == 0, left, pltpu.roll(tile, 1, axis=0))
    ahead = jnp.where(row == 7, right, pltpu.roll(tile, 7, axis=0))
    return jnp.where(at < bounds[0], back, jnp.where(at < bounds[1], tile, ahead))


def rank_kernel(
    x_ref, above_ref, below_ref, left_ref, right_ref, ut_ref, core_ref, one_ref, two_ref,
    q_ref, ring_ref, proj, edge, flat,
):
    pick_row = sublane((256, 64))
    pick_at = pick_row % 128
    pick = (lane((256, 64)) == (pick_at % 32) * 2 + pick_row // 128) & (pick_at < 96)
    wide = dot(pick.astype(BF), ut_ref[...]).astype(BF)

    def project(v):
        return dot_nt(v, wide).astype(BF).astype(F32)

    own = project(x_ref[...])
    above = project(above_ref[...])
    below = project(below_ref[...])
    for f in range(FRAMES):
        proj[f, 0] = above[8 * f : 8 * f + 8]
        proj[f, 7] = below[8 * f : 8 * f + 8]
        for y in range(ROWS):
            at = 48 * f + 8 * y
            proj[f, y + 1] = own[at : at + 8]
    edge[0] = project(left_ref[...])
    edge[1] = project(right_ref[...])
    for f in range(FRAMES):
        for y in range(8):
            k = 8 * f + y
            left = jnp.broadcast_to(edge[0, k : k + 1, :], (8, 256))
            right = jnp.broadcast_to(edge[1, k : k + 1, :], (8, 256))
            proj[f, y] = shifted(proj[f, y], left, right, (32, 64), 128)
    for b in range(3):
        q_ref[b, 0:48, :] = jnp.zeros((48, 256), BF)
        q_ref[b, 192:240, :] = jnp.zeros((48, 256), BF)
        for f in range(FRAMES):
            rows = proj[f, b : b + ROWS].reshape(48, 256)
            q_ref[b, 48 * f + 48 : 48 * f + 96, :] = rows.astype(BF)
    shift = ring_shift()
    for k, ref in enumerate((core_ref, one_ref, two_ref)):
        ring_ref[k] = to_ring(load_flat(ref, flat), shift)


def gather_table(got_ref, take_ref, wrap_ref, table_ref):
    over = wrap_ref[...] > 0
    take = take_ref[...]
    for g in range(4):
        block = got_ref[256 * g : 256 * g + 256, :]
        none = jnp.zeros_like(block)
        both = jnp.concatenate(
            [jnp.where(over, none, block), jnp.where(over, block, none)], axis=0
        )
        table_ref[216 * g : 216 * g + 216, :] = dot(take, both)


def forward_kernel(
    got_ref, q_ref, cot_ref, ot_ref, take_ref, give_ref, wrap_ref,
    send_ref, table_out, outp_ref, first_ref, last_ref, table, grads,
):
    gather_table(got_ref, take_ref, wrap_ref, table)
    table_out[...] = table[...].astype(BF)
    even = jnp.zeros((CELLS, 128), F32)
    odd = jnp.zeros((CELLS, 128), F32)
    for a in range(3):
        for b in range(3):
            k = 3 * a + b
            weights = table_out[96 * k : 96 * k + 96, :]
            rows = q_ref[b, 48 * a : 48 * a + CELLS, :]
            even = even + dot(rows[:, 0:96], weights)
            odd = odd + dot(rows[:, 128:224], weights)
    mid = (even[:, 0:64] + odd[:, 64:128]).astype(BF)
    pre = dot(mid, ot_ref[...])
    sig = jax.nn.sigmoid(pre)
    slope = (cot_ref[...].astype(F32) * sig * (1.0 + pre * (1.0 - sig))).astype(BF)
    ot = ot_ref[...]
    out_t = dot_nt(ot, slope).astype(BF)
    wide = jnp.concatenate([ot, ot, ot, ot], axis=0)
    outp = dot_nt(slope, wide)
    outp_ref[...] = outp.astype(BF)
    for f in range(FRAMES):
        first_ref[8 * f : 8 * f + 8, :] = outp[48 * f : 48 * f + 8].astype(BF)
        last_ref[8 * f : 8 * f + 8, :] = outp[48 * f + 40 : 48 * f + 48].astype(BF)
    for a in range(3):
        for b in range(3):
            k = 3 * a + b
            part = dot(out_t, q_ref[b, 48 * a : 48 * a + CELLS, :])
            stack = jnp.concatenate([part[:, 0:128], part[:, 128:256]], axis=0)
            grads[96 * k : 96 * k + 96, :] = stack.T[0:96, :]
    over = wrap_ref[...] > 0
    give = give_ref[...]
    for g in range(4):
        part = dot(give, grads[216 * g : 216 * g + 216, :].astype(BF))
        send_ref[256 * g : 256 * g + 256, :] = jnp.where(over, part[256:512], part[0:256]).astype(BF)


def backward_kernel(
    outp_ref, above_ref, below_ref, left_ref, right_ref, table_ref, ut_ref, grad_ref, tiles, edge, qs
):
    own = outp_ref[...].astype(F32)
    above = above_ref[...].astype(F32)
    below = below_ref[...].astype(F32)
    for f in range(FRAMES):
        tiles[f, 0] = above[8 * f : 8 * f + 8]
        tiles[f, 7] = below[8 * f : 8 * f + 8]
        for y in range(ROWS):
            at = 48 * f + 8 * y
            tiles[f, y + 1] = own[at : at + 8]
    edge[0] = left_ref[...].astype(F32)
    edge[1] = right_ref[...].astype(F32)
    for f in range(FRAMES):
        for y in range(8):
            k = 8 * f + y
            left = jnp.broadcast_to(edge[0, k : k + 1, :], (8, 256))
            right = jnp.broadcast_to(edge[1, k : k + 1, :], (8, 256))
            tiles[f, y] = shifted(tiles[f, y], left, right, (64, 128), 256)
    for b in range(3):
        qs[b, 0:48, :] = jnp.zeros((48, 256), BF)
        qs[b, 192:240, :] = jnp.zeros((48, 256), BF)
        for f in range(FRAMES):
            rows = tiles[f, b : b + ROWS].reshape(48, 256)
            qs[b, 48 * f + 48 : 48 * f + 96, :] = rows.astype(BF)
    total = jnp.zeros((CELLS, 64), F32)
    for a in range(3):
        for b in range(3):
            rows = qs[2 - b, 48 * (2 - a) : 48 * (2 - a) + CELLS, :]
            for c in range(3):
                t = 9 * a + 3 * b + c
                part = table_ref[32 * t : 32 * t + 32, :]
                cube = jnp.concatenate([part[:, 0:64], part[:, 64:128]], axis=0)
                piece = rows[:, 64 * (2 - c) : 64 * (2 - c) + 64]
                total = total + dot_nt(piece, cube)
    pick_row = sublane((64, 64))
    pick = lane((64, 64)) == (pick_row % 32) * 2 + pick_row // 32
    ut = dot(pick.astype(BF), ut_ref[...]).astype(BF)
    grad_ref[...] = dot(total.astype(BF), ut).astype(BF)


def adam_kernel(got_ref, ring_ref, send_ref, next_ref):
    total = jnp.zeros((8, 128), F32)
    for g in range(8):
        part = got_ref[128 * g : 128 * g + 128, :].astype(F32)
        total = total + part.reshape(16, 8, 128).sum(axis=0)
    grad = (total[0:4] + total[4:8]) * (1.0 / 192.0)
    core, one, two = ring_ref[0], ring_ref[1], ring_ref[2]
    one = beta_one * one + (1.0 - beta_one) * grad
    two = beta_two * two + (1.0 - beta_two) * grad * grad
    core = core - learn_rate * (one / fix_one) / (jnp.sqrt(two / fix_two) + epsilon)
    next_ref[0] = core
    next_ref[1] = one
    next_ref[2] = two
    spread(send_ref, jnp.where(in_ring(ring_shift()), core, 0.0))


def flat_kernel(next_ref, core_ref, one_ref, two_ref):
    shift = ring_shift()
    for k, ref in enumerate((core_ref, one_ref, two_ref)):
        store_flat(ref, from_ring(next_ref[k], shift))


def build_kernel(got_ref, ut_ref, ot_ref, take_ref, wrap_ref, out_ref, table, half, result, sems):
    gather_table(got_ref, take_ref, wrap_ref, table)
    cube = table[...].astype(BF)
    even = dot(cube[:, 0:64], ot_ref[...]).astype(BF)
    odd = dot(cube[:, 64:128], ot_ref[...]).astype(BF)
    for t in range(27):
        half[t, 0:32, :] = even[32 * t : 32 * t + 32]
        half[t, 32:64, :] = odd[32 * t : 32 * t + 32]
    pick_row = sublane((64, 64))
    pick = lane((64, 64)) == (pick_row % 32) * 2 + pick_row // 32
    ut = dot(pick.astype(BF), ut_ref[...]).astype(BF)
    u = ut.astype(F32).T.astype(BF)
    for a in range(9):
        for t in range(3 * a, 3 * a + 3):
            result[t] = dot(u, half[t]).astype(BF)
        pltpu.make_async_copy(
            result.at[pl.ds(3 * a, 3)], out_ref.at[pl.ds(3 * a, 3)], sems.at[a]
        ).start()
    for a in range(9):
        pltpu.make_async_copy(
            result.at[pl.ds(3 * a, 3)], out_ref.at[pl.ds(3 * a, 3)], sems.at[a]
        ).wait()


def call(kernel, outs, scratch, args, out_specs=None, flops=10**7, nbytes=10**6):
    whole = pl.BlockSpec(memory_space=pltpu.VMEM)
    return pl.pallas_call(
        kernel,
        out_shape=[jax.ShapeDtypeStruct(shape, dtype) for shape, dtype in outs],
        in_specs=[whole] * len(args),
        out_specs=out_specs or [whole] * len(outs),
        scratch_shapes=scratch,
        compiler_params=pltpu.CompilerParams(vmem_limit_bytes=32 << 20),
        cost_estimate=pl.CostEstimate(flops=flops, bytes_accessed=nbytes, transcendentals=0),
    )(*args)


def both_ways(high, low, axis):
    count = lax.axis_size(axis)
    forward = [(i, i + 1) for i in range(count - 1)]
    backward = [(i + 1, i) for i in range(count - 1)]
    return lax.ppermute(high, axis, forward), lax.ppermute(low, axis, backward)


def exchange(x):
    return lax.all_to_all(x, AXES, 0, 0, tiled=True)


def body(frames_in, cotangent, core, moment_one, moment_two, u_in, u_out):
    take_np, wrap_np = ring_tables()
    take = jnp.asarray(take_np, BF)
    give = jnp.asarray(take_np.T.copy(), BF)
    wrap = jnp.asarray(wrap_np, F32)
    ut, ot = u_in.T, u_out.T
    vm = pltpu.VMEM

    send, first, last = call(
        start_kernel,
        [((1024, 128), BF), ((FRAMES, 8, 256), BF), ((FRAMES, 8, 256), BF)],
        [vm((8, 128), F32)],
        [core, frames_in],
    )
    got = exchange(send)
    above, below = both_ways(last, first, "rows")
    low, high = call(
        sides_kernel, [((SIDE, 256), BF)] * 2, [vm((SIDE, 256), F32)] * 2, [frames_in, above, below]
    )
    left, right = both_ways(high, low, "cols")
    q, ring = call(
        rank_kernel,
        [((3, 240, 256), BF), ((3, 4, 128), F32)],
        [vm((FRAMES, 8, 8, 256), F32), vm((2, SIDE, 256), F32), vm((8, 128), F32)],
        [
            frames_in.reshape(CELLS, 256), above.reshape(SIDE, 256), below.reshape(SIDE, 256),
            left, right, ut, core, moment_one, moment_two,
        ],
    )
    send, table, outp, first, last = call(
        forward_kernel,
        [
            ((1024, 128), BF), ((TABLE, 128), BF), ((CELLS, 256), BF), ((SIDE, 256), BF), ((SIDE, 256), BF),
        ],
        [vm((TABLE, 128), F32), vm((TABLE, 128), F32)],
        [got, q, cotangent.reshape(CELLS, 256), ot, take, give, wrap],
    )
    got = exchange(send)
    above, below = both_ways(last, first, "rows")
    low, high = call(
        sides_kernel,
        [((SIDE, 256), BF)] * 2,
        [vm((SIDE, 256), F32)] * 2,
        [
            outp.reshape(FRAMES, ROWS, COLS, 256), above.reshape(FRAMES, 8, 256), below.reshape(FRAMES, 8, 256),
        ],
    )
    left, right = both_ways(high, low, "cols")
    (frames_grad,) = call(
        backward_kernel,
        [((CELLS, 256), BF)],
        [vm((FRAMES, 8, 8, 256), F32), vm((2, SIDE, 256), F32), vm((3, 240, 256), BF)],
        [outp, above, below, left, right, table, ut],
    )
    send, latest = call(adam_kernel, [((1024, 128), BF), ((3, 4, 128), F32)], [], [got, ring])
    got = exchange(send)
    core_next, one_next, two_next = call(flat_kernel, [((OWN,), F32)] * 3, [], [latest])
    (kernel_next,) = call(
        build_kernel,
        [((27, 256, 256), BF)],
        [
            vm((TABLE, 128), F32), vm((27, 64, 256), BF), vm((27, 256, 256), BF),
            pltpu.SemaphoreType.DMA((9,)),
        ],
        [got, ut, ot, take, wrap],
        out_specs=[pl.BlockSpec(memory_space=pl.ANY)],
    )
    frames_grad = frames_grad.reshape(FRAMES, ROWS, COLS, 256)
    return frames_grad, core_next, one_next, two_next, kernel_next


def solution(mesh):
    in_specs = (
        P(None, "rows", "cols", None),
        P(None, "rows", "cols", None),
        P(AXES),
        P(AXES),
        P(AXES),
        P(),
        P(),
    )
    out_specs = (
        P(None, "rows", "cols", None),
        P(AXES),
        P(AXES),
        P(AXES),
        P(),
    )
    return jax.shard_map(body, mesh=mesh, in_specs=in_specs, out_specs=out_specs, check_vma=False)
```

time: 257 us -> 115 us (0.45)
  the two profiles are of different devices: /device:TPU:1 before, /device:TPU:123 now
where the time goes in v1:
time: 115 us; the launch traced here: 114 us
  starting transfers between devices  51.1 us (44%)
  waiting for transfers between devices  22.6 us (20%)
  blocking collectives  19.7 us (17%)
  local copies, waits for them, and re-layouts  10.6 us (9%)
  Pallas kernels  9.07 us (8%)
    all_to_all x2, starting transfers between devices, exchange(): return lax.all_to_all(x, AXES, 0, 0, tiled=True)  26.2 us
    ppermute x4, waiting for transfers between devices, both_ways(): lax.ppermute(low, axis, backward)  22.6 us
    all_to_all x1, blocking collectives, exchange(): return lax.all_to_all(x, AXES, 0, 0, tiled=True)  19.7 us
    ppermute x4, starting transfers between devices, both_ways(): lax.ppermute(high, axis, forward)  17.2 us
    unnamed x34, local copies, waits for them, and re-layouts  10.6 us
    pallas_call x9, Pallas kernels, call(): pl.pallas_call(kernel, out_shape=[jax.ShapeDtypeStruct(shape, dtype) for...  9.07 us
    ppermute x4, starting transfers between devices, both_ways(): lax.ppermute(low, axis, backward)  7.68 us
  transfers between devices with their start and end apart: 10, of which 4 were waited for; matrix products, arithmetic and copies ran while one was open for 0% of the time, Pallas kernels for 2%

profile of v1, /device:TPU:123, one launch (start us, length us, event | category | flops | bytes accessed | tf_op | source)
XLA Modules:
  0.0 113.9 jit_solution(6932369355311343127)
XLA Ops:
  0.7 0.9 copy-done.2
  1.6 0.7 copy-done.13
  2.3 0.8 shard_map.137
  3.1 14.2 %all-to-all-start = ((bf16[256,4,128]{2,1,0:T(4,128)(2,1)}), bf16[256,4,128]{2,1,0:T(4,128)(2,1)S(1)}, u32[]{:S(2)}, u32[]{:S(2)}) async-start(bf16[256,4,128]{2,1,0:T(4,128)(2,1)} %bitcast), calls=%async_computation | async-start | bytes 524288 | tf_op jit(solution)/shard_map/all_to_all | solution.py:337
  17.2 4.8 %collective-permute-start = (bf16[3,8,256]{2,1,0:T(8,128)(2,1)S(1)}, bf16[3,8,256]{2,1,0:T(8,128)(2,1)S(1)}, u32[]{:S(2)}, u32[]{:S(2)}) collective-permute-start(bf16[3,8,256]{2,1,0:T(8,128)(2,1)S(1)} %get-tuple-element.25), channel_id=1, source_target_pairs={{0,8},{8,16},{16,24},{24,32},{32,40},{40,48},{48,56},{56,64},{64,7... | collective-permute-start | bytes 36872 | tf_op jit(solution)/shard_map/ppermute | solution.py:333
  22.1 1.9 %collective-permute-start.1 = (bf16[3,8,256]{2,1,0:T(8,128)(2,1)S(1)}, bf16[3,8,256]{2,1,0:T(8,128)(2,1)S(1)}, u32[]{:S(2)}, u32[]{:S(2)}) collective-permute-start(bf16[3,8,256]{2,1,0:T(8,128)(2,1)S(1)} %get-tuple-element.26), channel_id=1, source_target_pairs={{8,0},{16,8},{24,16},{32,24},{40,32},{48,40},{56,48},{64,56},{72,6... | collective-permute-start | bytes 36872 | tf_op jit(solution)/shard_map/ppermute | solution.py:333
  24.0 5.2 %collective-permute-done.1.below_ref = bf16[3,8,256]{2,1,0:T(8,128)(2,1)S(1)} collective-permute-done((bf16[3,8,256]{2,1,0:T(8,128)(2,1)S(1)}, bf16[3,8,256]{2,1,0:T(8,128)(2,1)S(1)}, u32[]{:S(2)}, u32[]{:S(2)}) %collective-permute-start.1) | collective-permute-done | bytes 12320 | tf_op jit(solution)/shard_map/ppermute | solution.py:333
  29.2 0.9 copy-done.3
  30.1 3.8 %collective-permute-start.2 = (bf16[24,256]{1,0:T(8,128)(2,1)S(1)}, bf16[24,256]{1,0:T(8,128)(2,1)S(1)}, u32[]{:S(2)}, u32[]{:S(2)}) collective-permute-start(bf16[24,256]{1,0:T(8,128)(2,1)S(1)} %get-tuple-element.27), channel_id=1, source_target_pairs={{0,1},{1,2},{2,3},{3,4},{4,5},{5,6},{6,7},{8,9},{9,10},{10,11},{11... | collective-permute-start | bytes 36872 | tf_op jit(solution)/shard_map/ppermute | solution.py:333
  33.9 1.9 %collective-permute-start.3 = (bf16[24,256]{1,0:T(8,128)(2,1)S(1)}, bf16[24,256]{1,0:T(8,128)(2,1)S(1)}, u32[]{:S(2)}, u32[]{:S(2)}) collective-permute-start(bf16[24,256]{1,0:T(8,128)(2,1)S(1)} %get-tuple-element.28), channel_id=1, source_target_pairs={{1,0},{2,1},{3,2},{4,3},{5,4},{6,5},{7,6},{9,8},{10,9},{11,10},{12... | collective-permute-start | bytes 36872 | tf_op jit(solution)/shard_map/ppermute | solution.py:333
  35.9 6.1 %collective-permute-done.3.right_ref = bf16[24,256]{1,0:T(8,128)(2,1)S(1)} collective-permute-done((bf16[24,256]{1,0:T(8,128)(2,1)S(1)}, bf16[24,256]{1,0:T(8,128)(2,1)S(1)}, u32[]{:S(2)}, u32[]{:S(2)}) %collective-permute-start.3) | collective-permute-done | bytes 12320 | tf_op jit(solution)/shard_map/ppermute | solution.py:333
  42.0 0.9 copy-done.4
  42.9 0.8 copy-done.7
  43.6 0.7 copy-done.14
  45.0 0.7 copy-done.16
  46.2 0.9 copy-done
  47.2 0.9 copy-done.5
  48.1 0.9 copy-done.9
  49.0 0.8 copy-done.10
  49.8 0.9 copy-done.12
  50.6 1.8 %shard_map.140 = (bf16[1024,128]{1,0:T(8,128)(2,1)S(1)}, bf16[864,128]{1,0:T(8,128)(2,1)S(1)}, bf16[144,256]{1,0:T(8,128)(2,1)S(1)}, bf16[24,256]{1,0:T(8,128)(2,1)S(1)}, bf16[24,256]{1,0:T(8,128)(2,1)S(1)}) custom-call(bf16[1024,128]{1,0:T(8,128)(2,1)S(1)} %bitcast.18, bf16[3,240,256]{2,1,0:T(8,128)(2,1)S(1)} %get-tuple-element.29.q_ref, ...), custom_call_target="tpu_custom_call" | custom-call | flops 10000000 | bytes 1000000 | tf_op jit(solution)/shard_map/pallas_call | solution.py:318
  52.5 19.7 %all_to_all.33 = bf16[256,4,128]{2,1,0:T(4,128)(2,1)S(1)} all-to-all(bf16[256,4,128]{2,1,0:T(4,128)(2,1)S(1)} %bitcast.24), channel_id=1, replica_groups=mesh['rows'=32,'cols'=8] {'rows','cols'}, dimensions={0} | all-to-all | bytes 524288 | tf_op jit(solution)/shard_map/all_to_all | solution.py:337
  72.2 0.8 shard_map.143
  73.0 12.0 %all-to-all-start.2 = ((bf16[256,4,128]{2,1,0:T(4,128)(2,1)}), bf16[256,4,128]{2,1,0:T(4,128)(2,1)S(1)}, u32[]{:S(2)}, u32[]{:S(2)}) async-start(bf16[256,4,128]{2,1,0:T(4,128)(2,1)} %bitcast.14), calls=%async_computation.2 | async-start | bytes 524288 | tf_op jit(solution)/shard_map/all_to_all | solution.py:337
  85.0 4.8 %collective-permute-start.4 = (bf16[24,256]{1,0:T(8,128)(2,1)S(1)}, bf16[24,256]{1,0:T(8,128)(2,1)S(1)}, u32[]{:S(2)}, u32[]{:S(2)}) collective-permute-start(bf16[24,256]{1,0:T(8,128)(2,1)S(1)} %get-tuple-element.31), channel_id=1, source_target_pairs={{0,8},{8,16},{16,24},{24,32},{32,40},{40,48},{48,56},{56,64},{64,7... | collective-permute-start | bytes 36872 | tf_op jit(solution)/shard_map/ppermute | solution.py:333
  89.8 1.9 %collective-permute-start.5 = (bf16[24,256]{1,0:T(8,128)(2,1)S(1)}, bf16[24,256]{1,0:T(8,128)(2,1)S(1)}, u32[]{:S(2)}, u32[]{:S(2)}) collective-permute-start(bf16[24,256]{1,0:T(8,128)(2,1)S(1)} %get-tuple-element.32), channel_id=1, source_target_pairs={{8,0},{16,8},{24,16},{32,24},{40,32},{48,40},{56,48},{64,56},{72,6... | collective-permute-start | bytes 36872 | tf_op jit(solution)/shard_map/ppermute | solution.py:333
  91.7 5.2 %collective-permute-done.5.below_ref = bf16[24,256]{1,0:T(8,128)(2,1)S(1)} collective-permute-done((bf16[24,256]{1,0:T(8,128)(2,1)S(1)}, bf16[24,256]{1,0:T(8,128)(2,1)S(1)}, u32[]{:S(2)}, u32[]{:S(2)}) %collective-permute-start.5) | collective-permute-done | bytes 12320 | tf_op jit(solution)/shard_map/ppermute | solution.py:333
  97.0 3.8 %collective-permute-start.6 = (bf16[24,256]{1,0:T(8,128)(2,1)S(1)}, bf16[24,256]{1,0:T(8,128)(2,1)S(1)}, u32[]{:S(2)}, u32[]{:S(2)}) collective-permute-start(bf16[24,256]{1,0:T(8,128)(2,1)S(1)} %get-tuple-element.33), channel_id=1, source_target_pairs={{0,1},{1,2},{2,3},{3,4},{4,5},{5,6},{6,7},{8,9},{9,10},{10,11},{11... | collective-permute-start | bytes 36872 | tf_op jit(solution)/shard_map/ppermute | solution.py:333
  100.8 1.9 %collective-permute-start.7 = (bf16[24,256]{1,0:T(8,128)(2,1)S(1)}, bf16[24,256]{1,0:T(8,128)(2,1)S(1)}, u32[]{:S(2)}, u32[]{:S(2)}) collective-permute-start(bf16[24,256]{1,0:T(8,128)(2,1)S(1)} %get-tuple-element.34), channel_id=1, source_target_pairs={{1,0},{2,1},{3,2},{4,3},{5,4},{6,5},{7,6},{9,8},{10,9},{11,10},{12... | collective-permute-start | bytes 36872 | tf_op jit(solution)/shard_map/ppermute | solution.py:333
  102.7 6.1 %collective-permute-done.7.right_ref = bf16[24,256]{1,0:T(8,128)(2,1)S(1)} collective-permute-done((bf16[24,256]{1,0:T(8,128)(2,1)S(1)}, bf16[24,256]{1,0:T(8,128)(2,1)S(1)}, u32[]{:S(2)}, u32[]{:S(2)}) %collective-permute-start.7) | collective-permute-done | bytes 12320 | tf_op jit(solution)/shard_map/ppermute | solution.py:333
  108.9 1.5 %shard_map.142 = bf16[144,256]{1,0:T(8,128)(2,1)} custom-call(bf16[144,256]{1,0:T(8,128)(2,1)S(1)} %get-tuple-element.30.outp_ref, bf16[24,256]{1,0:T(8,128)(2,1)S(1)} %collective-permute-done.4.above_ref, bf16[24,256]{1,0:T(8,128)(2,1)S(1)} %collective-permute-done.5.below_ref, bf16[24,256]{1,0:T(8,128)(2,1)S(1)} %collective-permute-done.6.left_ref, ...), custom_call_target="tpu_custom_call" | custom-call | flops 10000000 | bytes 1000000 | tf_op jit(solution)/shard_map/pallas_call | solution.py:318
  111.1 2.9 %shard_map.145 = bf16[27,256,256]{2,1,0:T(8,128)(2,1)} custom-call(bf16[1024,128]{1,0:T(8,128)(2,1)S(1)} %bitcast.16, bf16[64,256]{1,0:T(8,128)(2,1)S(1)} %bitcast.22, bf16[64,256]{1,0:T(8,128)(2,1)S(1)} %bitcast.26, bf16[216,512]{1,0:T(8,128)(2,1)S(1)} %copy-done.1, f32[256,128]{1,0:T(8,128)S(1)} %copy-done.6), custom_call_target="tpu_custom_call" | custom-call | flops 10000000 | bytes 1000000 | tf_op jit(solution)/shard_map/pallas_call | solution.py:318
  (32 shorter events, 2.0 us)
Async XLA Ops:
  0.6 110.4 %copy-start.1 = (bf16[216,512]{1,0:T(8,128)(2,1)S(1)}, bf16[216,512]{1,0:T(8,128)(2,1)}, u32[]{:S(2)}) copy-start(bf16[216,512]{1,0:T(8,128)(2,1)} %constant.6.clone.take_ref) | copy-start | bytes 663556
  0.6 0.9 copy-start.2
  1.6 0.7 copy-start.13
  2.3 106.6 %copy-start.8 = (bf16[256,64]{0,1:T(8,128)(2,1)S(1)}, bf16[256,64]{0,1:T(8,128)(2,1)}, u32[]{:S(2)}) copy-start(bf16[256,64]{0,1:T(8,128)(2,1)} %param.15) | copy-start | bytes 98308
  2.3 108.8 %copy-start.6 = (f32[256,128]{1,0:T(8,128)S(1)}, f32[256,128]{1,0:T(8,128)}, u32[]{:S(2)}) copy-start(f32[256,128]{1,0:T(8,128)} %constant.8.clone.wrap_ref) | copy-start | bytes 393220
  2.3 108.8 %copy-start.11 = (bf16[256,64]{0,1:T(8,128)(2,1)S(1)}, bf16[256,64]{0,1:T(8,128)(2,1)}, u32[]{:S(2)}) copy-start(bf16[256,64]{0,1:T(8,128)(2,1)} %param.16) | copy-start | bytes 98308
  3.1 43.1 %all-to-all-start = ((bf16[256,4,128]{2,1,0:T(4,128)(2,1)}), bf16[256,4,128]{2,1,0:T(4,128)(2,1)S(1)}, u32[]{:S(2)}, u32[]{:S(2)}) async-start(bf16[256,4,128]{2,1,0:T(4,128)(2,1)} %bitcast), calls=%async_computation | async-start | bytes 524288 | tf_op jit(solution)/shard_map/all_to_all | solution.py:337
  17.2 6.7 %collective-permute-start = (bf16[3,8,256]{2,1,0:T(8,128)(2,1)S(1)}, bf16[3,8,256]{2,1,0:T(8,128)(2,1)S(1)}, u32[]{:S(2)}, u32[]{:S(2)}) collective-permute-start(bf16[3,8,256]{2,1,0:T(8,128)(2,1)S(1)} %get-tuple-element.25), channel_id=1, source_target_pairs={{0,8},{8,16},{16,24},{24,32},{32,40},{40,48},{48,56},{56,64},{64,7... | collective-permute-start | bytes 36872 | tf_op jit(solution)/shard_map/ppermute | solution.py:333
  22.1 7.1 %collective-permute-start.1 = (bf16[3,8,256]{2,1,0:T(8,128)(2,1)S(1)}, bf16[3,8,256]{2,1,0:T(8,128)(2,1)S(1)}, u32[]{:S(2)}, u32[]{:S(2)}) collective-permute-start(bf16[3,8,256]{2,1,0:T(8,128)(2,1)S(1)} %get-tuple-element.26), channel_id=1, source_target_pairs={{8,0},{16,8},{24,16},{32,24},{40,32},{48,40},{56,48},{64,56},{72,6... | collective-permute-start | bytes 36872 | tf_op jit(solution)/shard_map/ppermute | solution.py:333
  29.2 0.9 copy-start.3
  30.1 5.8 %collective-permute-start.2 = (bf16[24,256]{1,0:T(8,128)(2,1)S(1)}, bf16[24,256]{1,0:T(8,128)(2,1)S(1)}, u32[]{:S(2)}, u32[]{:S(2)}) collective-permute-start(bf16[24,256]{1,0:T(8,128)(2,1)S(1)} %get-tuple-element.27), channel_id=1, source_target_pairs={{0,1},{1,2},{2,3},{3,4},{4,5},{5,6},{6,7},{8,9},{9,10},{10,11},{11... | collective-permute-start | bytes 36872 | tf_op jit(solution)/shard_map/ppermute | solution.py:333
  33.9 8.1 %collective-permute-start.3 = (bf16[24,256]{1,0:T(8,128)(2,1)S(1)}, bf16[24,256]{1,0:T(8,128)(2,1)S(1)}, u32[]{:S(2)}, u32[]{:S(2)}) collective-permute-start(bf16[24,256]{1,0:T(8,128)(2,1)S(1)} %get-tuple-element.28), channel_id=1, source_target_pairs={{1,0},{2,1},{3,2},{4,3},{5,4},{6,5},{7,6},{9,8},{10,9},{11,10},{12... | collective-permute-start | bytes 36872 | tf_op jit(solution)/shard_map/ppermute | solution.py:333
  42.0 0.9 copy-start.4
  42.9 0.8 copy-start.7
  43.6 0.7 copy-start.14
  44.3 0.7 copy-start.15
  45.0 0.7 copy-start.16
  46.2 0.9 copy-start
  47.1 0.9 copy-start.5
  48.1 0.9 copy-start.9
  49.0 0.8 copy-start.10
  49.8 0.9 copy-start.12
  73.0 38.1 %all-to-all-start.2 = ((bf16[256,4,128]{2,1,0:T(4,128)(2,1)}), bf16[256,4,128]{2,1,0:T(4,128)(2,1)S(1)}, u32[]{:S(2)}, u32[]{:S(2)}) async-start(bf16[256,4,128]{2,1,0:T(4,128)(2,1)} %bitcast.14), calls=%async_computation.2 | async-start | bytes 524288 | tf_op jit(solution)/shard_map/all_to_all | solution.py:337
  85.0 6.7 %collective-permute-start.4 = (bf16[24,256]{1,0:T(8,128)(2,1)S(1)}, bf16[24,256]{1,0:T(8,128)(2,1)S(1)}, u32[]{:S(2)}, u32[]{:S(2)}) collective-permute-start(bf16[24,256]{1,0:T(8,128)(2,1)S(1)} %get-tuple-element.31), channel_id=1, source_target_pairs={{0,8},{8,16},{16,24},{24,32},{32,40},{40,48},{48,56},{56,64},{64,7... | collective-permute-start | bytes 36872 | tf_op jit(solution)/shard_map/ppermute | solution.py:333
  89.8 7.1 %collective-permute-start.5 = (bf16[24,256]{1,0:T(8,128)(2,1)S(1)}, bf16[24,256]{1,0:T(8,128)(2,1)S(1)}, u32[]{:S(2)}, u32[]{:S(2)}) collective-permute-start(bf16[24,256]{1,0:T(8,128)(2,1)S(1)} %get-tuple-element.32), channel_id=1, source_target_pairs={{8,0},{16,8},{24,16},{32,24},{40,32},{48,40},{56,48},{64,56},{72,6... | collective-permute-start | bytes 36872 | tf_op jit(solution)/shard_map/ppermute | solution.py:333
  97.0 5.8 %collective-permute-start.6 = (bf16[24,256]{1,0:T(8,128)(2,1)S(1)}, bf16[24,256]{1,0:T(8,128)(2,1)S(1)}, u32[]{:S(2)}, u32[]{:S(2)}) collective-permute-start(bf16[24,256]{1,0:T(8,128)(2,1)S(1)} %get-tuple-element.33), channel_id=1, source_target_pairs={{0,1},{1,2},{2,3},{3,4},{4,5},{5,6},{6,7},{8,9},{9,10},{10,11},{11... | collective-permute-start | bytes 36872 | tf_op jit(solution)/shard_map/ppermute | solution.py:333
  100.8 8.1 %collective-permute-start.7 = (bf16[24,256]{1,0:T(8,128)(2,1)S(1)}, bf16[24,256]{1,0:T(8,128)(2,1)S(1)}, u32[]{:S(2)}, u32[]{:S(2)}) collective-permute-start(bf16[24,256]{1,0:T(8,128)(2,1)S(1)} %get-tuple-element.34), channel_id=1, source_target_pairs={{1,0},{2,1},{3,2},{4,3},{5,4},{6,5},{7,6},{9,8},{10,9},{11,10},{12... | collective-permute-start | bytes 36872 | tf_op jit(solution)/shard_map/ppermute | solution.py:333

commit v2 on v1

v2 whole, which is shorter than its diff:
```python
import jax
import jax.numpy as jnp
import numpy as np
from jax import lax
from jax.experimental import pallas as pl
from jax.experimental.pallas import tpu as pltpu
from jax.sharding import PartitionSpec as P

beta_one = 0.9
beta_two = 0.999
learn_rate = 0.06
epsilon = 1e-08
fix_one = 1.0 - 0.9**10
fix_two = 1.0 - 0.999**10

BF = jnp.bfloat16
F32 = jnp.float32
AXES = ("rows", "cols")

OWN = 432
FRAMES, ROWS, COLS = 3, 6, 8
CELLS = FRAMES * ROWS * COLS
SIDE = FRAMES * 8
TABLE = 864


RELAYS = ((7, 0, 0), (4, 0, 0), (3, 3, 64))
SLOTS = ((0, 24, -8), (24, 24, 8), (48, 18, -1), (66, 18, 1), (84, 3, -9), (87, 3, -7), (90, 3, 7), (93, 3, 9))


def ring_tables():
    take = np.zeros((216, 512), np.float32)
    give = np.zeros((512, 240), np.float32)
    over = np.zeros((256, 128), np.float32)
    for r in range(8):
        for c in range(8):
            first = 27 * r + 27 * c // 8
            col = 32 * r + 4 * c
            for j in range(4):
                take[first + j, col + j] = 1
                give[col + j, first + j] = 1
            wrapped = 48 * c % 128 + OWN - 512
            if wrapped > 0:
                take[first + 4, 256 + col] = 1
                give[256 + col, first + 4] = 1
                over[col, :wrapped] = 1
        for k, (c, j, at) in enumerate(RELAYS):
            col = 32 * r + 4 * c + j
            give[256 + col, 216 + 8 * k + r] = 1
            over[col, at : at + 64] = 1
    return take, give, over


def dot(a, b):
    return jnp.dot(a, b, preferred_element_type=F32)


def dot_nt(a, b):
    return lax.dot_general(a, b, (((1,), (1,)), ((), ())), preferred_element_type=F32)


def dot_tn(a, b):
    return lax.dot_general(a, b, (((0,), (0,)), ((), ())), preferred_element_type=F32)


def lane(shape):
    return lax.broadcasted_iota(jnp.int32, shape, 1)


def sublane(shape):
    return lax.broadcasted_iota(jnp.int32, shape, 0)


def ring_shift():
    return lax.rem(lax.axis_index("cols") * 48, 128)


def to_ring(v, shift):
    turned = pltpu.roll(v, shift, axis=1)
    above = jnp.concatenate([turned[3:4], turned[0:3]], axis=0)
    return jnp.where(lane(v.shape) >= shift, turned, above)


def from_ring(v, shift):
    turned = pltpu.roll(v, lax.rem(128 - shift, 128), axis=1)
    below = jnp.concatenate([turned[1:4], turned[0:1]], axis=0)
    return jnp.where(lane(v.shape) < 128 - shift, turned, below)


def in_ring(shift):
    place = sublane((4, 128)) * 128 + lane((4, 128)) - shift
    place = jnp.where(place < 0, place + 512, place)
    return place < OWN


def load_flat(ref, scratch):
    scratch[...] = jnp.zeros_like(scratch)
    for k in range(3):
        scratch[k, :] = ref[pl.ds(128 * k, 128)]
    scratch[3, 0 : OWN - 384] = ref[pl.ds(384, OWN - 384)]
    return scratch[0:4, :]


def store_flat(ref, v):
    for k in range(3):
        ref[pl.ds(128 * k, 128)] = v[k]
    ref[pl.ds(384, OWN - 384)] = v[3, 0 : OWN - 384]


def fetch(pairs, sems):
    copies = [pltpu.make_async_copy(src, dst, sems.at[k]) for k, (src, dst) in enumerate(pairs)]
    for copy in copies:
        copy.start()
    return copies


def start_kernel(core_ref, x_ref, send_ref, first_ref, last_ref, own, flat, sems):
    copies = fetch(
        ((core_ref, own), (x_ref.at[:, 0], first_ref), (x_ref.at[:, ROWS - 1], last_ref)), sems
    )
    copies[0].wait()
    v = to_ring(load_flat(own, flat), ring_shift())
    block = jnp.concatenate([v, v, v, v], axis=0).astype(BF)
    for k in range(64):
        send_ref[16 * k : 16 * k + 16, :] = block
    copies[1].wait()
    copies[2].wait()


def sides_kernel(own_ref, above_ref, below_ref, low_ref, high_ref, low, high):
    for f in range(FRAMES):
        for y in range(8):
            if y == 0:
                tile = above_ref[f]
            elif y == 7:
                tile = below_ref[f]
            else:
                tile = own_ref[f, y - 1]
            tile = tile.astype(F32)
            low[8 * f + y : 8 * f + y + 1, :] = tile[0:1, :]
            high[8 * f + y : 8 * f + y + 1, :] = tile[7:8, :]
    low_ref[...] = low[...].astype(BF)
    high_ref[...] = high[...].astype(BF)


def shifted(tile, left, right, bounds, period):
    at = lane(tile.shape) % period
    row = sublane(tile.shape)
    back = jnp.where(row == 0, left, pltpu.roll(tile, 1, axis=0))
    ahead = jnp.where(row == 7, right, pltpu.roll(tile, 7, axis=0))
    return jnp.where(at < bounds[0], back, jnp.where(at < bounds[1], tile, ahead))


def fetch_kernel(
    x_ref, ut_ref, ot_ref, cot_ref, core_ref, one_ref, two_ref, take_ref, give_ref, over_ref,
    own_ref, wide_ref, utp_ref, u_ref, ring_ref, ot_out, cot_out, take_out, give_out, over_out,
    x, ut, owns, flat, sems,
):
    copies = fetch(
        (
            (ut_ref, ut), (x_ref, x), (core_ref, owns[0]), (one_ref, owns[1]), (two_ref, owns[2]),
            (take_ref, take_out), (give_ref, give_out), (over_ref, over_out), (ot_ref, ot_out), (cot_ref, cot_out),
        ),
        sems,
    )
    row = sublane((256, 64))
    at = row % 128
    pick = (lane((256, 64)) == (at % 32) * 2 + row // 128) & (at < 96)
    half_row = sublane((64, 64))
    half_pick = lane((64, 64)) == (half_row % 32) * 2 + half_row // 32
    copies[0].wait()
    wide = dot(pick.astype(BF), ut[...]).astype(BF)
    wide_ref[...] = wide
    utp = dot(half_pick.astype(BF), ut[...])
    utp_ref[...] = utp.astype(BF)
    u_ref[...] = utp.T.astype(BF)
    copies[1].wait()
    own_ref[...] = dot_nt(x[...], wide).astype(BF).astype(F32)
    shift = ring_shift()
    for k in range(3):
        copies[2 + k].wait()
        ring_ref[k] = to_ring(load_flat(owns[k], flat), shift)
    for k in range(5, 10):
        copies[k].wait()


def stack_rows(tiles, out_ref):
    for b in range(3):
        out_ref[b, 0:48, :] = jnp.zeros((48, 256), BF)
        out_ref[b, 192:240, :] = jnp.zeros((48, 256), BF)
        for f in range(FRAMES):
            rows = tiles[f, b : b + ROWS].reshape(48, 256)
            out_ref[b, 48 * f + 48 : 48 * f + 96, :] = rows.astype(BF)


def rank_kernel(own_ref, wide_ref, above_ref, below_ref, left_ref, right_ref, q_ref, tiles, edge):
    wide = wide_ref[...]

    def project(v):
        return dot_nt(v, wide).astype(BF).astype(F32)

    above = project(above_ref[...])
    below = project(below_ref[...])
    for f in range(FRAMES):
        tiles[f, 0] = above[8 * f : 8 * f + 8]
        tiles[f, 7] = below[8 * f : 8 * f + 8]
        for y in range(ROWS):
            at = 48 * f + 8 * y
            tiles[f, y + 1] = own_ref[at : at + 8, :]
    edge[0] = project(left_ref[...])
    edge[1] = project(right_ref[...])
    for f in range(FRAMES):
        for y in range(8):
            k = 8 * f + y
            left = jnp.broadcast_to(edge[0, k : k + 1, :], (8, 256))
            right = jnp.broadcast_to(edge[1, k : k + 1, :], (8, 256))
            tiles[f, y] = shifted(tiles[f, y], left, right, (32, 64), 128)
    stack_rows(tiles, q_ref)


def gather_table(got_ref, take_ref, over_ref, table_ref):
    over = over_ref[...] > 0
    take = take_ref[...]
    for g in range(4):
        block = got_ref[256 * g : 256 * g + 256, :]
        none = jnp.zeros_like(block)
        both = jnp.concatenate(
            [jnp.where(over, none, block), jnp.where(over, block, none)], axis=0
        )
        table_ref[216 * g : 216 * g + 216, :] = dot(take, both)


def forward_kernel(
    got_ref, q_ref, cot_ref, ot_ref, take_ref, give_ref, over_ref,
    send_ref, table_out, outp_ref, table, grads, border, pixels,
):
    gather_table(got_ref, take_ref, over_ref, table)
    table_out[...] = table[...].astype(BF)
    even = jnp.zeros((CELLS, 128), F32)
    odd = jnp.zeros((CELLS, 128), F32)
    for a in range(3):
        for b in range(3):
            k = 3 * a + b
            weights = table_out[96 * k : 96 * k + 96, :]
            rows = q_ref[b, 48 * a : 48 * a + CELLS, :]
            even = even + dot(rows[:, 0:96], weights)
            odd = odd + dot(rows[:, 128:224], weights)
    mid = (even[:, 0:64] + odd[:, 64:128]).astype(BF)
    pre = dot(mid, ot_ref[...])
    sig = jax.nn.sigmoid(pre)
    slope = (cot_ref[...].astype(F32) * sig * (1.0 + pre * (1.0 - sig))).astype(BF)
    ot = ot_ref[...]
    out_t = dot_nt(ot, slope).astype(BF)
    wide = jnp.concatenate([ot, ot, ot, ot], axis=0)
    outp = dot_nt(slope, wide).astype(BF).astype(F32)
    outp_ref[...] = outp
    border[...] = outp[:, 0:128]
    for f in range(FRAMES):
        pixels[8 * f : 8 * f + 8, :] = border[48 * f : 48 * f + 8, :]
        pixels[24 + 8 * f : 32 + 8 * f, :] = border[48 * f + 40 : 48 * f + 48, :]
    pixels[48:66, :] = border[pl.ds(0, 18, stride=8), :]
    pixels[66:84, :] = border[pl.ds(7, 18, stride=8), :]
    for k, cell in enumerate((0, 7, 40, 47)):
        pixels[84 + 3 * k : 87 + 3 * k, :] = border[pl.ds(cell, 3, stride=48), :]
    for a in range(3):
        for b in range(3):
            k = 3 * a + b
            part = dot(out_t, q_ref[b, 48 * a : 48 * a + CELLS, :])
            stack = jnp.concatenate([part[:, 0:128], part[:, 128:256]], axis=0)
            grads[96 * k : 96 * k + 96, :] = stack.T[0:96, :]
    over = over_ref[...] > 0
    give = give_ref[...]
    for g in range(4):
        source = [grads[216 * g : 216 * g + 216, :]]
        for k in range(3):
            source.append(pixels[32 * k + 8 * g : 32 * k + 8 * g + 8, :])
        part = dot(give, jnp.concatenate(source, axis=0).astype(BF))
        send_ref[256 * g : 256 * g + 256, :] = jnp.where(over, part[256:512], part[0:256]).astype(BF)


def adam_kernel(got_ref, ring_ref, send_ref, next_ref, passed):
    total = jnp.zeros((8, 128), F32)
    passed[0:40, :] = jnp.zeros((40, 128), F32)
    passed[1064:1104, :] = jnp.zeros((40, 128), F32)
    for g in range(8):
        part = got_ref[128 * g : 128 * g + 128, :].astype(F32)
        passed[128 * g + 40 : 128 * g + 168, :] = part
        total = total + part.reshape(16, 8, 128).sum(axis=0)
    grad = (total[0:4] + total[4:8]) * (1.0 / 192.0)
    core, one, two = ring_ref[0], ring_ref[1], ring_ref[2]
    one = beta_one * one + (1.0 - beta_one) * grad
    two = beta_two * two + (1.0 - beta_two) * grad * grad
    core = core - learn_rate * (one / fix_one) / (jnp.sqrt(two / fix_two) + epsilon)
    next_ref[0] = core
    next_ref[1] = one
    next_ref[2] = two
    own = jnp.where(in_ring(ring_shift()), core, 0.0)
    own = jnp.concatenate([own, own], axis=0)
    row, col = lax.axis_index("rows"), lax.axis_index("cols")
    slot, mask = row, jnp.zeros((8, 128), jnp.bool_)
    for k, (c, j, at) in enumerate(RELAYS):
        slot = slot + jnp.where(col == c, 32 * k, 0)
        spot = (sublane((8, 128)) % 4 == j) & (lane((8, 128)) // 64 == at // 64)
        mask = mask | (spot & (jnp.full((8, 128), col, jnp.int32) == c))
    move = 0
    for first, count, offset in SLOTS:
        move = move + jnp.where((slot >= first) & (slot < first + count), 4 * offset, 0)
    for k in range(64):
        upper = passed[pl.ds(40 + 16 * k - move, 8), :]
        lower = passed[pl.ds(48 + 16 * k - move, 8), :]
        block = jnp.concatenate([jnp.where(mask, upper, own), jnp.where(mask, lower, own)], axis=0)
        send_ref[16 * k : 16 * k + 16, :] = block.astype(BF)


def flat_kernel(next_ref, core_ref, one_ref, two_ref):
    shift = ring_shift()
    for k, ref in enumerate((core_ref, one_ref, two_ref)):
        store_flat(ref, from_ring(next_ref[k], shift))


def finish_kernel(
    got_ref, outp_ref, old_ref, utp_ref, u_ref, ot_ref, take_ref, over_ref,
    out_ref, grad_ref, table, half, result, got, pixels, tiles, qs, sems,
):
    gather_table(got_ref, take_ref, over_ref, table)
    cube = table[...].astype(BF)
    even = dot(cube[:, 0:64], ot_ref[...]).astype(BF)
    odd = dot(cube[:, 64:128], ot_ref[...]).astype(BF)
    for t in range(27):
        half[t, 0:32, :] = even[32 * t : 32 * t + 32]
        half[t, 32:64, :] = odd[32 * t : 32 * t + 32]
    u = u_ref[...]

    def store(a):
        part = pl.ds(3 * a, 3)
        return pltpu.make_async_copy(result.at[part], out_ref.at[part], sems.at[a])

    for a in range(9):
        for t in range(3 * a, 3 * a + 3):
            result[t] = dot(u, half[t]).astype(BF)
        store(a).start()

    for g in range(4):
        got[256 * g : 256 * g + 256, :] = got_ref[256 * g : 256 * g + 256, :].astype(F32)
    for k, (c, j, at) in enumerate(RELAYS):
        rows = got[pl.ds(4 * c + j, 32, stride=32), :]
        pixels[32 * k : 32 * k + 32, 0:128] = jnp.where(lane((32, 128)) // 64 == at // 64, rows, 0.0)
    spread = (sublane((128, 256)) % 64 == lane((128, 256)) % 64).astype(BF)
    pixels[...] = dot(pixels[:, 0:128].astype(BF), spread)
    row, col = lax.axis_index("rows"), lax.axis_index("cols")
    zero = jnp.zeros((8, 256), F32)

    def inside(flag, v):
        return jnp.where(jnp.full((8, 256), flag.astype(jnp.int32), jnp.int32) > 0, v, zero)

    def spot(k):
        return jnp.broadcast_to(pixels[k : k + 1, :], (8, 256))

    for f in range(FRAMES):
        for y in range(8):
            if y == 0:
                tile, left, right = pixels[24 + 8 * f : 32 + 8 * f, :], spot(93 + f), spot(90 + f)
            elif y == 7:
                tile, left, right = pixels[8 * f : 8 * f + 8, :], spot(87 + f), spot(84 + f)
            else:
                at = 48 * f + 8 * (y - 1)
                tile = outp_ref[at : at + 8, :]
                left, right = spot(66 + 6 * f + y - 1), spot(48 + 6 * f + y - 1)
            tile = shifted(tile, inside(col > 0, left), inside(col < 7, right), (64, 128), 256)
            if y == 0:
                tile = inside(row > 0, tile)
            elif y == 7:
                tile = inside(row < 31, tile)
            tiles[f, y] = tile
    stack_rows(tiles, qs)
    total = jnp.zeros((CELLS, 64), F32)
    for a in range(3):
        for b in range(3):
            rows = qs[2 - b, 48 * (2 - a) : 48 * (2 - a) + CELLS, :]
            for c in range(3):
                t = 9 * a + 3 * b + c
                part = old_ref[32 * t : 32 * t + 32, :]
                cube = jnp.concatenate([part[:, 0:64], part[:, 64:128]], axis=0)
                piece = rows[:, 64 * (2 - c) : 64 * (2 - c) + 64]
                total = total + dot_nt(piece, cube)
    grad_ref[...] = dot(total.astype(BF), utp_ref[...]).astype(BF)
    for a in range(9):
        store(a).wait()


def call(kernel, args, outs, scratch, flops=10**7):
    def spec(far):
        return pl.BlockSpec(memory_space=pl.ANY if far else pltpu.VMEM)

    return pl.pallas_call(
        kernel,
        out_shape=[jax.ShapeDtypeStruct(shape, dtype) for shape, dtype, _ in outs],
        in_specs=[spec(far) for _, far in args],
        out_specs=[spec(far) for _, _, far in outs],
        scratch_shapes=scratch,
        compiler_params=pltpu.CompilerParams(vmem_limit_bytes=32 << 20),
        cost_estimate=pl.CostEstimate(flops=flops, bytes_accessed=10**5, transcendentals=0),
    )(*[arg for arg, _ in args])


def near(*args):
    return [(arg, False) for arg in args]


def far(*args):
    return [(arg, True) for arg in args]


def both_ways(high, low, axis):
    count = lax.axis_size(axis)
    forward = [(i, i + 1) for i in range(count - 1)]
    backward = [(i + 1, i) for i in range(count - 1)]
    return lax.ppermute(high, axis, forward), lax.ppermute(low, axis, backward)


def exchange(x):
    return lax.all_to_all(x, AXES, 0, 0, tiled=True)


def body(frames_in, cotangent, core, moment_one, moment_two, u_in, u_out):
    take, give, over = ring_tables()
    take, give, over = jnp.asarray(take, BF), jnp.asarray(give, BF), jnp.asarray(over, F32)
    vm, dma = pltpu.VMEM, pltpu.SemaphoreType.DMA
    edge = (FRAMES, 8, 256)

    send, first, last = call(
        start_kernel,
        far(core, frames_in),
        [((1024, 128), BF, False), (edge, BF, False), (edge, BF, False)],
        [vm((OWN,), F32), vm((8, 128), F32), dma((3,))],
    )
    above, below = both_ways(last, first, "rows")
    got = exchange(send)
    own, wide, utp, u, ring, ot, cot, take, give, over = call(
        fetch_kernel,
        far(
            frames_in.reshape(CELLS, 256), u_in.T, u_out.T, cotangent.reshape(CELLS, 256),
            core, moment_one, moment_two, take, give, over,
        ),
        [
            ((CELLS, 256), F32, False), ((256, 256), BF, False), ((64, 256), BF, False), ((256, 64), BF, False),
            ((3, 4, 128), F32, False), ((64, 256), BF, False), ((CELLS, 256), BF, False),
            ((216, 512), BF, False), ((512, 240), BF, False), ((256, 128), F32, False),
        ],
        [
            vm((CELLS, 256), BF), vm((64, 256), BF), [vm((OWN,), F32) for _ in range(3)], vm((8, 128), F32),
            dma((10,)),
        ],
    )
    low, high = call(
        sides_kernel,
        near(frames_in, above, below),
        [((SIDE, 256), BF, False)] * 2,
        [vm((SIDE, 256), F32)] * 2,
    )
    left, right = both_ways(high, low, "cols")
    (q,) = call(
        rank_kernel,
        near(own, wide, above.reshape(SIDE, 256), below.reshape(SIDE, 256), left, right),
        [((3, 240, 256), BF, False)],
        [vm((FRAMES, 8, 8, 256), F32), vm((2, SIDE, 256), F32)],
    )
    send, table, outp = call(
        forward_kernel,
        near(got, q, cot, ot, take, give, over),
        [((1024, 128), BF, False), ((TABLE, 128), BF, False), ((CELLS, 256), F32, False)],
        [vm((TABLE, 128), F32), vm((TABLE, 128), F32), vm((CELLS, 128), F32), vm((96, 128), F32)],
    )
    got = exchange(send)
    send, latest = call(
        adam_kernel,
        near(got, ring),
        [((1024, 128), BF, False), ((3, 4, 128), F32, False)],
        [vm((1104, 128), F32)],
    )
    got = exchange(send)
    core_next, one_next, two_next = call(flat_kernel, near(latest), [((OWN,), F32, False)] * 3, [])
    got, core_next, one_next, two_next = lax.optimization_barrier((got, core_next, one_next, two_next))
    kernel_next, frames_grad = call(
        finish_kernel,
        near(got, outp, table, utp, u, ot, take, over),
        [((27, 256, 256), BF, True), ((CELLS, 256), BF, False)],
        [
            vm((TABLE, 128), F32), vm((27, 64, 256), BF), vm((27, 256, 256), BF), vm((1024, 128), F32),
            vm((96, 256), F32), vm((FRAMES, 8, 8, 256), F32), vm((3, 240, 256), BF), dma((9,)),
        ],
    )
    frames_grad = frames_grad.reshape(FRAMES, ROWS, COLS, 256)
    return frames_grad, core_next, one_next, two_next, kernel_next


def solution(mesh):
    in_specs = (
        P(None, "rows", "cols", None),
        P(None, "rows", "cols", None),
        P(AXES),
        P(AXES),
        P(AXES),
        P(),
        P(),
    )
    out_specs = (
        P(None, "rows", "cols", None),
        P(AXES),
        P(AXES),
        P(AXES),
        P(),
    )
    return jax.shard_map(body, mesh=mesh, in_specs=in_specs, out_specs=out_specs, check_vma=False)
```

time: 115 us -> 104 us (0.904)
  the two profiles are of different devices: /device:TPU:123 before, /device:TPU:1 now
where the time goes in v2:
time: 104 us; the launch traced here: 103 us
  starting transfers between devices  31.6 us (30%)
  blocking collectives  31.6 us (30%)
  waiting for transfers between devices  18.3 us (18%)
  local copies, waits for them, and re-layouts  10.6 us (10%)
  Pallas kernels  10.4 us (10%)
    all_to_all x1, blocking collectives, exchange(): return lax.all_to_all(x, AXES, 0, 0, tiled=True)  31.6 us
    all_to_all x2, starting transfers between devices, exchange(): return lax.all_to_all(x, AXES, 0, 0, tiled=True)  21.8 us
    all_to_all x2, waiting for transfers between devices, exchange(): return lax.all_to_all(x, AXES, 0, 0, tiled=True)  14.9 us
    unnamed x26, local copies, waits for them, and re-layouts  10.6 us
    pallas_call x8, Pallas kernels, call(): pl.pallas_call(kernel, out_shape=[jax.ShapeDtypeStruct(shape, dtype) for...  10.4 us
    ppermute x2, starting transfers between devices, both_ways(): lax.ppermute(high, axis, forward)  6.66 us
    ppermute x2, waiting for transfers between devices, both_ways(): lax.ppermute(low, axis, backward)  3.42 us
    ppermute x2, starting transfers between devices, both_ways(): lax.ppermute(low, axis, backward)  3.21 us
  transfers between devices with their start and end apart: 6, of which 2 were waited for; matrix products, arithmetic and copies ran while one was open for 0% of the time, Pallas kernels for 3%

profile of v2, /device:TPU:1, one launch (start us, length us, event | category | flops | bytes accessed | tf_op | source)
XLA Modules:
  0.0 103.3 jit_solution(694819481992620163)
XLA Ops:
  0.6 0.0 copy-start
  0.6 0.9 copy-done
  1.5 0.7 copy-done.9
  2.2 0.8 shard_map.137
  3.0 15.7 %all-to-all-start = ((bf16[256,4,128]{2,1,0:T(4,128)(2,1)}), bf16[256,4,128]{2,1,0:T(4,128)(2,1)S(1)}, u32[]{:S(2)}, u32[]{:S(2)}) async-start(bf16[256,4,128]{2,1,0:T(4,128)(2,1)} %bitcast), calls=%async_computation | async-start | bytes 524288 | tf_op jit(solution)/shard_map/all_to_all | solution.py:422
  18.7 3.5 %collective-permute-start = (bf16[3,8,256]{2,1,0:T(8,128)(2,1)S(1)}, bf16[3,8,256]{2,1,0:T(8,128)(2,1)S(1)}, u32[]{:S(2)}, u32[]{:S(2)}) collective-permute-start(bf16[3,8,256]{2,1,0:T(8,128)(2,1)S(1)} %get-tuple-element.37), channel_id=1, source_target_pairs={{0,8},{8,16},{16,24},{24,32},{32,40},{40,48},{48,56},{56,64},{64,7... | collective-permute-start | bytes 36872 | tf_op jit(solution)/shard_map/ppermute | solution.py:418
  22.3 1.9 %collective-permute-start.1 = (bf16[3,8,256]{2,1,0:T(8,128)(2,1)S(1)}, bf16[3,8,256]{2,1,0:T(8,128)(2,1)S(1)}, u32[]{:S(2)}, u32[]{:S(2)}) collective-permute-start(bf16[3,8,256]{2,1,0:T(8,128)(2,1)S(1)} %get-tuple-element.38), channel_id=1, source_target_pairs={{8,0},{16,8},{24,16},{32,24},{40,32},{48,40},{56,48},{64,56},{72,6... | collective-permute-start | bytes 36872 | tf_op jit(solution)/shard_map/ppermute | solution.py:418
  24.2 0.0 collective-permute-done.above_ref
  24.2 3.4 %collective-permute-done.1.below_ref = bf16[3,8,256]{2,1,0:T(8,128)(2,1)S(1)} collective-permute-done((bf16[3,8,256]{2,1,0:T(8,128)(2,1)S(1)}, bf16[3,8,256]{2,1,0:T(8,128)(2,1)S(1)}, u32[]{:S(2)}, u32[]{:S(2)}) %collective-permute-start.1) | collective-permute-done | bytes 12320 | tf_op jit(solution)/shard_map/ppermute | solution.py:418
  27.6 0.9 copy-done.1
  28.6 3.1 %collective-permute-start.2 = (bf16[24,256]{1,0:T(8,128)(2,1)S(1)}, bf16[24,256]{1,0:T(8,128)(2,1)S(1)}, u32[]{:S(2)}, u32[]{:S(2)}) collective-permute-start(bf16[24,256]{1,0:T(8,128)(2,1)S(1)} %get-tuple-element.39), channel_id=1, source_target_pairs={{0,1},{1,2},{2,3},{3,4},{4,5},{5,6},{6,7},{8,9},{9,10},{10,11},{11... | collective-permute-start | bytes 36872 | tf_op jit(solution)/shard_map/ppermute | solution.py:418
  31.7 1.3 %collective-permute-start.3 = (bf16[24,256]{1,0:T(8,128)(2,1)S(1)}, bf16[24,256]{1,0:T(8,128)(2,1)S(1)}, u32[]{:S(2)}, u32[]{:S(2)}) collective-permute-start(bf16[24,256]{1,0:T(8,128)(2,1)S(1)} %get-tuple-element.40), channel_id=1, source_target_pairs={{1,0},{2,1},{3,2},{4,3},{5,4},{6,5},{7,6},{9,8},{10,9},{11,10},{12... | collective-permute-start | bytes 36872 | tf_op jit(solution)/shard_map/ppermute | solution.py:418
  33.0 0.0 copy-start.2
  33.0 0.9 copy-done.2
  33.9 0.9 copy-done.3
  34.8 0.9 copy-done.4
  35.8 0.9 copy-done.5
  36.7 0.9 copy-done.6
  37.6 0.8 copy-done.7
  38.3 0.8 copy-done.8
  39.1 0.7 copy-done.10
  39.7 0.7 copy-done.11
  40.4 0.7 copy-done.12
  41.1 1.6 %shard_map.138 = (f32[144,256]{1,0:T(8,128)S(1)}, bf16[256,256]{1,0:T(8,128)(2,1)S(1)}, bf16[64,256]{1,0:T(8,128)(2,1)S(1)}, bf16[256,64]{1,0:T(8,128)(2,1)S(1)}...) custom-call(bf16[144,256]{1,0:T(8,128)(2,1)S(1)} %bitcast.16, ...), custom_call_target="tpu_custom_call" | custom-call | flops 10000000 | bytes 100000 | tf_op jit(solution)/shard_map/pallas_call | solution.py:395
  42.7 0.3 shard_map.140.q_ref
  43.1 1.8 %shard_map.141 = (bf16[1024,128]{1,0:T(8,128)(2,1)S(1)}, bf16[864,128]{1,0:T(8,128)(2,1)S(1)}, f32[144,256]{1,0:T(8,128)S(1)}) custom-call(bf16[1024,128]{1,0:T(8,128)(2,1)S(1)} %bitcast.15, bf16[3,240,256]{2,1,0:T(8,128)(2,1)S(1)} %shard_map.140.q_ref, bf16[144,256]{1,0:T(8,128)(2,1)S(1)} %get-tuple-element.41.cot_ref, ...), custom_call_target="tpu_custom_call" | custom-call | flops 10000000 | bytes 100000 | tf_op jit(solution)/shard_map/pallas_call | solution.py:395
  44.9 31.6 %all_to_all.34 = bf16[256,4,128]{2,1,0:T(4,128)(2,1)S(1)} all-to-all(bf16[256,4,128]{2,1,0:T(4,128)(2,1)S(1)} %bitcast.17), channel_id=1, replica_groups=mesh['rows'=32,'cols'=8] {'rows','cols'}, dimensions={0} | all-to-all | bytes 524288 | tf_op jit(solution)/shard_map/all_to_all | solution.py:422
  76.5 0.8 shard_map.142
  77.4 6.1 %all-to-all-start.2 = ((bf16[256,4,128]{2,1,0:T(4,128)(2,1)}), bf16[256,4,128]{2,1,0:T(4,128)(2,1)S(1)}, u32[]{:S(2)}, u32[]{:S(2)}) async-start(bf16[256,4,128]{2,1,0:T(4,128)(2,1)} %bitcast.10), calls=%async_computation.2 | async-start | bytes 524288 | tf_op jit(solution)/shard_map/all_to_all | solution.py:422
  83.5 0.7 shard_map.143
  84.1 14.9 %all-to-all-done.2 = bf16[256,4,128]{2,1,0:T(4,128)(2,1)S(1)} async-done(((bf16[256,4,128]{2,1,0:T(4,128)(2,1)}), bf16[256,4,128]{2,1,0:T(4,128)(2,1)S(1)}, u32[]{:S(2)}, u32[]{:S(2)}) %all-to-all-start.2) | async-done | bytes 262176 | tf_op jit(solution)/shard_map/all_to_all | solution.py:422
  99.0 4.3 %shard_map.144 = (bf16[27,256,256]{2,1,0:T(8,128)(2,1)}, bf16[144,256]{1,0:T(8,128)(2,1)}) custom-call(bf16[1024,128]{1,0:T(8,128)(2,1)S(1)} %bitcast.13, f32[144,256]{1,0:T(8,128)S(1)} %get-tuple-element.54.outp_ref, bf16[864,128]{1,0:T(8,128)(2,1)S(1)} %get-tuple-element.55.old_ref, bf16[64,256]{1,0:T(8,128)(2,1)S(1)} %get-tuple-element.56.utp_ref, ...), custom_call_target="tpu_custom_call" | custom-call | flops 10000000 | bytes 100000 | tf_op jit(solution)/shard_map/pallas_call | solution.py:395
  (15 shorter events, 0.1 us)
Async XLA Ops:
  0.6 0.9 copy-start
  1.5 0.7 copy-start.9
  3.0 40.0 %all-to-all-start = ((bf16[256,4,128]{2,1,0:T(4,128)(2,1)}), bf16[256,4,128]{2,1,0:T(4,128)(2,1)S(1)}, u32[]{:S(2)}, u32[]{:S(2)}) async-start(bf16[256,4,128]{2,1,0:T(4,128)(2,1)} %bitcast), calls=%async_computation | async-start | bytes 524288 | tf_op jit(solution)/shard_map/all_to_all | solution.py:422
  18.7 5.5 %collective-permute-start = (bf16[3,8,256]{2,1,0:T(8,128)(2,1)S(1)}, bf16[3,8,256]{2,1,0:T(8,128)(2,1)S(1)}, u32[]{:S(2)}, u32[]{:S(2)}) collective-permute-start(bf16[3,8,256]{2,1,0:T(8,128)(2,1)S(1)} %get-tuple-element.37), channel_id=1, source_target_pairs={{0,8},{8,16},{16,24},{24,32},{32,40},{40,48},{48,56},{56,64},{64,7... | collective-permute-start | bytes 36872 | tf_op jit(solution)/shard_map/ppermute | solution.py:418
  22.3 5.4 %collective-permute-start.1 = (bf16[3,8,256]{2,1,0:T(8,128)(2,1)S(1)}, bf16[3,8,256]{2,1,0:T(8,128)(2,1)S(1)}, u32[]{:S(2)}, u32[]{:S(2)}) collective-permute-start(bf16[3,8,256]{2,1,0:T(8,128)(2,1)S(1)} %get-tuple-element.38), channel_id=1, source_target_pairs={{8,0},{16,8},{24,16},{32,24},{40,32},{48,40},{56,48},{64,56},{72,6... | collective-permute-start | bytes 36872 | tf_op jit(solution)/shard_map/ppermute | solution.py:418
  27.6 0.9 copy-start.1
  28.6 14.1 %collective-permute-start.2 = (bf16[24,256]{1,0:T(8,128)(2,1)S(1)}, bf16[24,256]{1,0:T(8,128)(2,1)S(1)}, u32[]{:S(2)}, u32[]{:S(2)}) collective-permute-start(bf16[24,256]{1,0:T(8,128)(2,1)S(1)} %get-tuple-element.39), channel_id=1, source_target_pairs={{0,1},{1,2},{2,3},{3,4},{4,5},{5,6},{6,7},{8,9},{9,10},{10,11},{11... | collective-permute-start | bytes 36872 | tf_op jit(solution)/shard_map/ppermute | solution.py:418
  31.7 11.0 %collective-permute-start.3 = (bf16[24,256]{1,0:T(8,128)(2,1)S(1)}, bf16[24,256]{1,0:T(8,128)(2,1)S(1)}, u32[]{:S(2)}, u32[]{:S(2)}) collective-permute-start(bf16[24,256]{1,0:T(8,128)(2,1)S(1)} %get-tuple-element.40), channel_id=1, source_target_pairs={{1,0},{2,1},{3,2},{4,3},{5,4},{6,5},{7,6},{9,8},{10,9},{11,10},{12... | collective-permute-start | bytes 36872 | tf_op jit(solution)/shard_map/ppermute | solution.py:418
  33.0 0.9 copy-start.2
  33.9 0.9 copy-start.3
  34.8 0.9 copy-start.4
  35.8 0.9 copy-start.5
  36.7 0.9 copy-start.6
  37.5 0.8 copy-start.7
  38.3 0.8 copy-start.8
  39.1 0.7 copy-start.10
  39.7 0.7 copy-start.11
  40.4 0.7 copy-start.12
  77.4 21.7 %all-to-all-start.2 = ((bf16[256,4,128]{2,1,0:T(4,128)(2,1)}), bf16[256,4,128]{2,1,0:T(4,128)(2,1)S(1)}, u32[]{:S(2)}, u32[]{:S(2)}) async-start(bf16[256,4,128]{2,1,0:T(4,128)(2,1)} %bitcast.10), calls=%async_computation.2 | async-start | bytes 524288 | tf_op jit(solution)/shard_map/all_to_all | solution.py:422

commit v3 on v2

--- a/solution.py
+++ b/solution.py
@@ -114,17 +114,20 @@
     return copies
 
 
-def start_kernel(core_ref, x_ref, send_ref, first_ref, last_ref, own, flat, sems):
+def start_kernel(core_ref, x_ref, send_ref, first_ref, last_ref, inner_ref, own, flat, sems):
     copies = fetch(
-        ((core_ref, own), (x_ref.at[:, 0], first_ref), (x_ref.at[:, ROWS - 1], last_ref)), sems
+        (
+            (core_ref, own), (x_ref.at[:, 0], first_ref), (x_ref.at[:, ROWS - 1], last_ref), (x_ref, inner_ref),
+        ),
+        sems,
     )
     copies[0].wait()
     v = to_ring(load_flat(own, flat), ring_shift())
     block = jnp.concatenate([v, v, v, v], axis=0).astype(BF)
     for k in range(64):
         send_ref[16 * k : 16 * k + 16, :] = block
-    copies[1].wait()
-    copies[2].wait()
+    for k in range(1, 4):
+        copies[k].wait()
 
 
 def sides_kernel(own_ref, above_ref, below_ref, low_ref, high_ref, low, high):
@@ -154,11 +157,11 @@
 def fetch_kernel(
     x_ref, ut_ref, ot_ref, cot_ref, core_ref, one_ref, two_ref, take_ref, give_ref, over_ref,
     own_ref, wide_ref, utp_ref, u_ref, ring_ref, ot_out, cot_out, take_out, give_out, over_out,
-    x, ut, owns, flat, sems,
+    ut, owns, flat, sems,
 ):
     copies = fetch(
         (
-            (ut_ref, ut), (x_ref, x), (core_ref, owns[0]), (one_ref, owns[1]), (two_ref, owns[2]),
+            (ut_ref, ut), (core_ref, owns[0]), (one_ref, owns[1]), (two_ref, owns[2]),
             (take_ref, take_out), (give_ref, give_out), (over_ref, over_out), (ot_ref, ot_out), (cot_ref, cot_out),
         ),
         sems,
@@ -174,13 +177,12 @@
     utp = dot(half_pick.astype(BF), ut[...])
     utp_ref[...] = utp.astype(BF)
     u_ref[...] = utp.T.astype(BF)
-    copies[1].wait()
-    own_ref[...] = dot_nt(x[...], wide).astype(BF).astype(F32)
+    own_ref[...] = dot_nt(x_ref[...], wide).astype(BF).astype(F32)
     shift = ring_shift()
     for k in range(3):
-        copies[2 + k].wait()
+        copies[1 + k].wait()
         ring_ref[k] = to_ring(load_flat(owns[k], flat), shift)
-    for k in range(5, 10):
+    for k in range(4, 9):
         copies[k].wait()
 
 
@@ -390,7 +392,7 @@
 
 def call(kernel, args, outs, scratch, flops=10**7):
     def spec(far):
-        return pl.BlockSpec(memory_space=pl.ANY if far else pltpu.VMEM)
+        return pl.BlockSpec(memory_space=pltpu.HBM if far else pltpu.VMEM)
 
     return pl.pallas_call(
         kernel,
@@ -400,7 +402,7 @@
         scratch_shapes=scratch,
         compiler_params=pltpu.CompilerParams(vmem_limit_bytes=32 << 20),
         cost_estimate=pl.CostEstimate(flops=flops, bytes_accessed=10**5, transcendentals=0),
-    )(*[arg for arg, _ in args])
+    )(*[pltpu.with_memory_space_constraint(arg, pltpu.HBM) if far else arg for arg, far in args])
 
 
 def near(*args):
@@ -428,19 +430,18 @@
     vm, dma = pltpu.VMEM, pltpu.SemaphoreType.DMA
     edge = (FRAMES, 8, 256)
 
-    send, first, last = call(
+    send, first, last, inner = call(
         start_kernel,
         far(core, frames_in),
-        [((1024, 128), BF, False), (edge, BF, False), (edge, BF, False)],
-        [vm((OWN,), F32), vm((8, 128), F32), dma((3,))],
+        [((1024, 128), BF, False), (edge, BF, False), (edge, BF, False), ((FRAMES, ROWS, COLS, 256), BF, False)],
+        [vm((OWN,), F32), vm((8, 128), F32), dma((4,))],
     )
     above, below = both_ways(last, first, "rows")
     got = exchange(send)
     own, wide, utp, u, ring, ot, cot, take, give, over = call(
         fetch_kernel,
-        far(
-            frames_in.reshape(CELLS, 256), u_in.T, u_out.T, cotangent.reshape(CELLS, 256),
-            core, moment_one, moment_two, take, give, over,
+        near(inner.reshape(CELLS, 256)) + far(
+            u_in.T, u_out.T, cotangent.reshape(CELLS, 256), core, moment_one, moment_two, take, give, over,
         ),
         [
             ((CELLS, 256), F32, False), ((256, 256), BF, False), ((64, 256), BF, False), ((256, 64), BF, False),
@@ -448,13 +449,13 @@
             ((216, 512), BF, False), ((512, 240), BF, False), ((256, 128), F32, False),
         ],
         [
-            vm((CELLS, 256), BF), vm((64, 256), BF), [vm((OWN,), F32) for _ in range(3)], vm((8, 128), F32),
-            dma((10,)),
+            vm((64, 256), BF), [vm((OWN,), F32) for _ in range(3)], vm((8, 128), F32),
+            dma((9,)),
         ],
     )
     low, high = call(
         sides_kernel,
-        near(frames_in, above, below),
+        near(inner, above, below),
         [((SIDE, 256), BF, False)] * 2,
         [vm((SIDE, 256), F32)] * 2,
     )

time: 104 us -> 96.7 us (0.930)
  local copies, waits for them, and re-layouts: 10.6 us -> 0 us
  waiting for transfers between devices: 18.3 us -> 20 us
  blocking collectives: 31.6 us -> 32.8 us
    unnamed x26 -> x0, local copies, waits for them, and re-layouts: 10.6 us -> none
    ppermute x2, waiting for transfers between devices: 3.42 us -> 5.1 us  [both_ways(): lax.ppermute(low, axis, backward)]
    all_to_all x1, blocking collectives: 31.6 us -> 32.8 us  [exchange(): return lax.all_to_all(x, AXES, 0, 0, tiled=True)]
  transfers between devices with their start and end apart: 6 -> 6, of which waited for: 2 -> 3; matrix products, arithmetic and copies ran while one was open for 0% -> 0% of each run, Pallas kernels for 3% -> 3%
where the time goes in v3:
time: 96.7 us; the launch traced here: 96.3 us
  blocking collectives  32.8 us (34%)
  starting transfers between devices  31.6 us (33%)
  waiting for transfers between devices  20 us (21%)
  Pallas kernels  11.2 us (12%)
    all_to_all x1, blocking collectives, exchange(): return lax.all_to_all(x, AXES, 0, 0, tiled=True)  32.8 us
    all_to_all x2, starting transfers between devices, exchange(): return lax.all_to_all(x, AXES, 0, 0, tiled=True)  21.8 us
    all_to_all x2, waiting for transfers between devices, exchange(): return lax.all_to_all(x, AXES, 0, 0, tiled=True)  14.9 us
    pallas_call x8, Pallas kernels, call(): pl.pallas_call(kernel, out_shape=[jax.ShapeDtypeStruct(shape, dtype) for...  11.2 us
    ppermute x2, starting transfers between devices, both_ways(): lax.ppermute(high, axis, forward)  6.66 us
    ppermute x2, waiting for transfers between devices, both_ways(): lax.ppermute(low, axis, backward)  5.1 us
    ppermute x2, starting transfers between devices, both_ways(): lax.ppermute(low, axis, backward)  3.21 us
  transfers between devices with their start and end apart: 6, of which 3 were waited for; matrix products, arithmetic and copies ran while one was open for 0% of the time, Pallas kernels for 3%

profile of v3, /device:TPU:1, one launch (start us, length us, event | category | flops | bytes accessed | tf_op | source)
XLA Modules:
  0.0 96.3 jit_solution(10899610444660611333)
XLA Ops:
  0.6 1.7 %shard_map.137 = (bf16[1024,128]{1,0:T(8,128)(2,1)}, bf16[3,8,256]{2,1,0:T(8,128)(2,1)S(1)}, bf16[3,8,256]{2,1,0:T(8,128)(2,1)S(1)}, bf16[3,6,8,256]{3,2,1,0:T(8,128)(2,1)S(1)}) custom-call(f32[432]{0:T(512)} %core_ref.3, bf16[3,6,8,256]{3,2,1,0:T(8,128)(2,1)} %x_ref.1), custom_call_target="tpu_custom_call" | custom-call | flops 10000000 | bytes 100000 | tf_op jit(solution)/shard_map/pallas_call | solution.py:397
  2.3 15.7 %all-to-all-start = ((bf16[256,4,128]{2,1,0:T(4,128)(2,1)}), bf16[256,4,128]{2,1,0:T(4,128)(2,1)S(1)}, u32[]{:S(2)}, u32[]{:S(2)}) async-start(bf16[256,4,128]{2,1,0:T(4,128)(2,1)} %bitcast), calls=%async_computation | async-start | bytes 524288 | tf_op jit(solution)/shard_map/all_to_all | solution.py:424
  18.0 3.5 %collective-permute-start = (bf16[3,8,256]{2,1,0:T(8,128)(2,1)S(1)}, bf16[3,8,256]{2,1,0:T(8,128)(2,1)S(1)}, u32[]{:S(2)}, u32[]{:S(2)}) collective-permute-start(bf16[3,8,256]{2,1,0:T(8,128)(2,1)S(1)} %get-tuple-element.39), channel_id=1, source_target_pairs={{0,8},{8,16},{16,24},{24,32},{32,40},{40,48},{48,56},{56,64},{64,7... | collective-permute-start | bytes 36872 | tf_op jit(solution)/shard_map/ppermute | solution.py:420
  21.6 1.9 %collective-permute-start.1 = (bf16[3,8,256]{2,1,0:T(8,128)(2,1)S(1)}, bf16[3,8,256]{2,1,0:T(8,128)(2,1)S(1)}, u32[]{:S(2)}, u32[]{:S(2)}) collective-permute-start(bf16[3,8,256]{2,1,0:T(8,128)(2,1)S(1)} %get-tuple-element.40), channel_id=1, source_target_pairs={{8,0},{16,8},{24,16},{32,24},{40,32},{48,40},{56,48},{64,56},{72,6... | collective-permute-start | bytes 36872 | tf_op jit(solution)/shard_map/ppermute | solution.py:420
  23.5 0.0 collective-permute-done.above_ref
  23.5 3.4 %collective-permute-done.1.below_ref = bf16[3,8,256]{2,1,0:T(8,128)(2,1)S(1)} collective-permute-done((bf16[3,8,256]{2,1,0:T(8,128)(2,1)S(1)}, bf16[3,8,256]{2,1,0:T(8,128)(2,1)S(1)}, u32[]{:S(2)}, u32[]{:S(2)}) %collective-permute-start.1) | collective-permute-done | bytes 12320 | tf_op jit(solution)/shard_map/ppermute | solution.py:420
  27.0 3.1 %collective-permute-start.2 = (bf16[24,256]{1,0:T(8,128)(2,1)S(1)}, bf16[24,256]{1,0:T(8,128)(2,1)S(1)}, u32[]{:S(2)}, u32[]{:S(2)}) collective-permute-start(bf16[24,256]{1,0:T(8,128)(2,1)S(1)} %get-tuple-element.41), channel_id=1, source_target_pairs={{0,1},{1,2},{2,3},{3,4},{4,5},{5,6},{6,7},{8,9},{9,10},{10,11},{11... | collective-permute-start | bytes 36872 | tf_op jit(solution)/shard_map/ppermute | solution.py:420
  30.1 1.3 %collective-permute-start.3 = (bf16[24,256]{1,0:T(8,128)(2,1)S(1)}, bf16[24,256]{1,0:T(8,128)(2,1)S(1)}, u32[]{:S(2)}, u32[]{:S(2)}) collective-permute-start(bf16[24,256]{1,0:T(8,128)(2,1)S(1)} %get-tuple-element.42), channel_id=1, source_target_pairs={{1,0},{2,1},{3,2},{4,3},{5,4},{6,5},{7,6},{9,8},{10,9},{11,10},{12... | collective-permute-start | bytes 36872 | tf_op jit(solution)/shard_map/ppermute | solution.py:420
  31.4 1.4 %shard_map.138 = (f32[144,256]{1,0:T(8,128)S(1)}, bf16[256,256]{1,0:T(8,128)(2,1)S(1)}, bf16[64,256]{1,0:T(8,128)(2,1)S(1)}, bf16[256,64]{1,0:T(8,128)(2,1)S(1)}...) custom-call(bf16[144,256]{1,0:T(8,128)(2,1)S(1)} %bitcast.16, ...), custom_call_target="tpu_custom_call" | custom-call | flops 10000000 | bytes 100000 | tf_op jit(solution)/shard_map/pallas_call | solution.py:397
  32.8 0.0 collective-permute-done.2.left_ref
  32.9 1.7 %collective-permute-done.3.right_ref = bf16[24,256]{1,0:T(8,128)(2,1)S(1)} collective-permute-done((bf16[24,256]{1,0:T(8,128)(2,1)S(1)}, bf16[24,256]{1,0:T(8,128)(2,1)S(1)}, u32[]{:S(2)}, u32[]{:S(2)}) %collective-permute-start.3) | collective-permute-done | bytes 12320 | tf_op jit(solution)/shard_map/ppermute | solution.py:420
  34.5 0.3 shard_map.140.q_ref
  34.9 0.0 all-to-all-done
  34.9 1.8 %shard_map.141 = (bf16[1024,128]{1,0:T(8,128)(2,1)S(1)}, bf16[864,128]{1,0:T(8,128)(2,1)S(1)}, f32[144,256]{1,0:T(8,128)S(1)}) custom-call(bf16[1024,128]{1,0:T(8,128)(2,1)S(1)} %bitcast.15, bf16[3,240,256]{2,1,0:T(8,128)(2,1)S(1)} %shard_map.140.q_ref, bf16[144,256]{1,0:T(8,128)(2,1)S(1)} %get-tuple-element.43.cot_ref, ...), custom_call_target="tpu_custom_call" | custom-call | flops 10000000 | bytes 100000 | tf_op jit(solution)/shard_map/pallas_call | solution.py:397
  36.7 32.8 %all_to_all.34 = bf16[256,4,128]{2,1,0:T(4,128)(2,1)S(1)} all-to-all(bf16[256,4,128]{2,1,0:T(4,128)(2,1)S(1)} %bitcast.17), channel_id=1, replica_groups=mesh['rows'=32,'cols'=8] {'rows','cols'}, dimensions={0} | all-to-all | bytes 524288 | tf_op jit(solution)/shard_map/all_to_all | solution.py:424
  69.5 0.8 shard_map.142
  70.4 6.1 %all-to-all-start.2 = ((bf16[256,4,128]{2,1,0:T(4,128)(2,1)}), bf16[256,4,128]{2,1,0:T(4,128)(2,1)S(1)}, u32[]{:S(2)}, u32[]{:S(2)}) async-start(bf16[256,4,128]{2,1,0:T(4,128)(2,1)} %bitcast.10), calls=%async_computation.2 | async-start | bytes 524288 | tf_op jit(solution)/shard_map/all_to_all | solution.py:424
  76.5 0.7 shard_map.143
  77.1 14.9 %all-to-all-done.2 = bf16[256,4,128]{2,1,0:T(4,128)(2,1)S(1)} async-done(((bf16[256,4,128]{2,1,0:T(4,128)(2,1)}), bf16[256,4,128]{2,1,0:T(4,128)(2,1)S(1)}, u32[]{:S(2)}, u32[]{:S(2)}) %all-to-all-start.2) | async-done | bytes 262176 | tf_op jit(solution)/shard_map/all_to_all | solution.py:424
  92.0 4.3 %shard_map.144 = (bf16[27,256,256]{2,1,0:T(8,128)(2,1)}, bf16[144,256]{1,0:T(8,128)(2,1)}) custom-call(bf16[1024,128]{1,0:T(8,128)(2,1)S(1)} %bitcast.13, f32[144,256]{1,0:T(8,128)S(1)} %get-tuple-element.56.outp_ref, bf16[864,128]{1,0:T(8,128)(2,1)S(1)} %get-tuple-element.57.old_ref, bf16[64,256]{1,0:T(8,128)(2,1)S(1)} %get-tuple-element.58.utp_ref, ...), custom_call_target="tpu_custom_call" | custom-call | flops 10000000 | bytes 100000 | tf_op jit(solution)/shard_map/pallas_call | solution.py:397
  (1 shorter events, 0.0 us)
Async XLA Ops:
  2.3 32.5 %all-to-all-start = ((bf16[256,4,128]{2,1,0:T(4,128)(2,1)}), bf16[256,4,128]{2,1,0:T(4,128)(2,1)S(1)}, u32[]{:S(2)}, u32[]{:S(2)}) async-start(bf16[256,4,128]{2,1,0:T(4,128)(2,1)} %bitcast), calls=%async_computation | async-start | bytes 524288 | tf_op jit(solution)/shard_map/all_to_all | solution.py:424
  18.0 5.5 %collective-permute-start = (bf16[3,8,256]{2,1,0:T(8,128)(2,1)S(1)}, bf16[3,8,256]{2,1,0:T(8,128)(2,1)S(1)}, u32[]{:S(2)}, u32[]{:S(2)}) collective-permute-start(bf16[3,8,256]{2,1,0:T(8,128)(2,1)S(1)} %get-tuple-element.39), channel_id=1, source_target_pairs={{0,8},{8,16},{16,24},{24,32},{32,40},{40,48},{48,56},{56,64},{64,7... | collective-permute-start | bytes 36872 | tf_op jit(solution)/shard_map/ppermute | solution.py:420
  21.6 5.4 %collective-permute-start.1 = (bf16[3,8,256]{2,1,0:T(8,128)(2,1)S(1)}, bf16[3,8,256]{2,1,0:T(8,128)(2,1)S(1)}, u32[]{:S(2)}, u32[]{:S(2)}) collective-permute-start(bf16[3,8,256]{2,1,0:T(8,128)(2,1)S(1)} %get-tuple-element.40), channel_id=1, source_target_pairs={{8,0},{16,8},{24,16},{32,24},{40,32},{48,40},{56,48},{64,56},{72,6... | collective-permute-start | bytes 36872 | tf_op jit(solution)/shard_map/ppermute | solution.py:420
  27.0 5.9 %collective-permute-start.2 = (bf16[24,256]{1,0:T(8,128)(2,1)S(1)}, bf16[24,256]{1,0:T(8,128)(2,1)S(1)}, u32[]{:S(2)}, u32[]{:S(2)}) collective-permute-start(bf16[24,256]{1,0:T(8,128)(2,1)S(1)} %get-tuple-element.41), channel_id=1, source_target_pairs={{0,1},{1,2},{2,3},{3,4},{4,5},{5,6},{6,7},{8,9},{9,10},{10,11},{11... | collective-permute-start | bytes 36872 | tf_op jit(solution)/shard_map/ppermute | solution.py:420
  30.1 4.4 %collective-permute-start.3 = (bf16[24,256]{1,0:T(8,128)(2,1)S(1)}, bf16[24,256]{1,0:T(8,128)(2,1)S(1)}, u32[]{:S(2)}, u32[]{:S(2)}) collective-permute-start(bf16[24,256]{1,0:T(8,128)(2,1)S(1)} %get-tuple-element.42), channel_id=1, source_target_pairs={{1,0},{2,1},{3,2},{4,3},{5,4},{6,5},{7,6},{9,8},{10,9},{11,10},{12... | collective-permute-start | bytes 36872 | tf_op jit(solution)/shard_map/ppermute | solution.py:420
  70.4 21.7 %all-to-all-start.2 = ((bf16[256,4,128]{2,1,0:T(4,128)(2,1)}), bf16[256,4,128]{2,1,0:T(4,128)(2,1)S(1)}, u32[]{:S(2)}, u32[]{:S(2)}) async-start(bf16[256,4,128]{2,1,0:T(4,128)(2,1)} %bitcast.10), calls=%async_computation.2 | async-start | bytes 524288 | tf_op jit(solution)/shard_map/all_to_all | solution.py:424

commit v4 on v3

--- a/solution.py
+++ b/solution.py
@@ -114,36 +114,47 @@
     return copies
 
 
-def start_kernel(core_ref, x_ref, send_ref, first_ref, last_ref, inner_ref, own, flat, sems):
-    copies = fetch(
-        (
-            (core_ref, own), (x_ref.at[:, 0], first_ref), (x_ref.at[:, ROWS - 1], last_ref), (x_ref, inner_ref),
-        ),
-        sems,
-    )
-    copies[0].wait()
+def even_first(axis, first, last):
+    even = jnp.full(first.shape, lax.rem(lax.axis_index(axis), 2), jnp.int32) == 0
+    return jnp.where(even, last, first), jnp.where(even, first, last)
+
+
+def columns_kernel(x_ref, inner_ref, one_ref, two_ref, low, high, sems):
+    fetch(((x_ref, inner_ref),), sems)[0].wait()
+    for f in range(FRAMES):
+        for y in range(ROWS):
+            tile = inner_ref[f, y].astype(F32)
+            k = ROWS * f + y
+            low[k : k + 1, :] = tile[0:1, :]
+            high[k : k + 1, :] = tile[7:8, :]
+    one, two = even_first("cols", low[...], high[...])
+    one_ref[...] = one.astype(BF)
+    two_ref[...] = two.astype(BF)
+
+
+def start_kernel(core_ref, send_ref, own, flat, sems):
+    fetch(((core_ref, own),), sems)[0].wait()
     v = to_ring(load_flat(own, flat), ring_shift())
     block = jnp.concatenate([v, v, v, v], axis=0).astype(BF)
     for k in range(64):
         send_ref[16 * k : 16 * k + 16, :] = block
-    for k in range(1, 4):
-        copies[k].wait()
-
-
-def sides_kernel(own_ref, above_ref, below_ref, low_ref, high_ref, low, high):
+
+
+def rows_kernel(inner_ref, one_ref, two_ref, left_ref, right_ref, up_ref, down_ref, first, last):
+    right, left = even_first("cols", two_ref[...].astype(F32), one_ref[...].astype(F32))
+    left_ref[...] = left
+    right_ref[...] = right
+    first[...] = jnp.zeros_like(first)
+    last[...] = jnp.zeros_like(last)
     for f in range(FRAMES):
-        for y in range(8):
-            if y == 0:
-                tile = above_ref[f]
-            elif y == 7:
-                tile = below_ref[f]
-            else:
-                tile = own_ref[f, y - 1]
-            tile = tile.astype(F32)
-            low[8 * f + y : 8 * f + y + 1, :] = tile[0:1, :]
-            high[8 * f + y : 8 * f + y + 1, :] = tile[7:8, :]
-    low_ref[...] = low[...].astype(BF)
-    high_ref[...] = high[...].astype(BF)
+        for y, rows in ((0, first), (ROWS - 1, last)):
+            k = ROWS * f + y
+            rows[16 * f : 16 * f + 8, :] = inner_ref[f, y].astype(F32)
+            rows[16 * f + 8 : 16 * f + 9, :] = left_ref[k : k + 1, :]
+            rows[16 * f + 9 : 16 * f + 10, :] = right_ref[k : k + 1, :]
+    one, two = even_first("rows", first[...], last[...])
+    up_ref[...] = one.astype(BF)
+    down_ref[...] = two.astype(BF)
 
 
 def shifted(tile, left, right, bounds, period):
@@ -195,28 +206,30 @@
             out_ref[b, 48 * f + 48 : 48 * f + 96, :] = rows.astype(BF)
 
 
-def rank_kernel(own_ref, wide_ref, above_ref, below_ref, left_ref, right_ref, q_ref, tiles, edge):
+def rank_kernel(own_ref, wide_ref, one_ref, two_ref, left_ref, right_ref, q_ref, tiles, edge, rims):
     wide = wide_ref[...]
 
     def project(v):
-        return dot_nt(v, wide).astype(BF).astype(F32)
-
-    above = project(above_ref[...])
-    below = project(below_ref[...])
-    for f in range(FRAMES):
-        tiles[f, 0] = above[8 * f : 8 * f + 8]
-        tiles[f, 7] = below[8 * f : 8 * f + 8]
-        for y in range(ROWS):
-            at = 48 * f + 8 * y
-            tiles[f, y + 1] = own_ref[at : at + 8, :]
+        return dot_nt(v.astype(BF), wide).astype(BF).astype(F32)
+
+    below, above = even_first("rows", project(two_ref[...]), project(one_ref[...]))
+    rims[0] = above
+    rims[1] = below
     edge[0] = project(left_ref[...])
     edge[1] = project(right_ref[...])
     for f in range(FRAMES):
         for y in range(8):
-            k = 8 * f + y
-            left = jnp.broadcast_to(edge[0, k : k + 1, :], (8, 256))
-            right = jnp.broadcast_to(edge[1, k : k + 1, :], (8, 256))
-            tiles[f, y] = shifted(tiles[f, y], left, right, (32, 64), 128)
+            if y in (0, 7):
+                rim = rims.at[y // 7]
+                at = 16 * f
+                tile, left, right = rim[at : at + 8, :], rim[at + 8 : at + 9, :], rim[at + 9 : at + 10, :]
+            else:
+                k = ROWS * f + y - 1
+                tile = own_ref[8 * k : 8 * k + 8, :]
+                left, right = edge[0, k : k + 1, :], edge[1, k : k + 1, :]
+            left = jnp.broadcast_to(left, (8, 256))
+            right = jnp.broadcast_to(right, (8, 256))
+            tiles[f, y] = shifted(tile, left, right, (32, 64), 128)
     stack_rows(tiles, q_ref)
 
 
@@ -413,11 +426,12 @@
     return [(arg, True) for arg in args]
 
 
-def both_ways(high, low, axis):
+def swap(one, two, axis):
     count = lax.axis_size(axis)
-    forward = [(i, i + 1) for i in range(count - 1)]
-    backward = [(i + 1, i) for i in range(count - 1)]
-    return lax.ppermute(high, axis, forward), lax.ppermute(low, axis, backward)
+    pairs = [[(i, i + 1) for i in range(k, count - 1, 2)] for k in range(2)]
+    return tuple(
+        lax.ppermute(x, axis, forward + [(b, a) for a, b in forward]) for x, forward in zip((one, two), pairs)
+    )
 
 
 def exchange(x):
@@ -428,15 +442,23 @@
     take, give, over = ring_tables()
     take, give, over = jnp.asarray(take, BF), jnp.asarray(give, BF), jnp.asarray(over, F32)
     vm, dma = pltpu.VMEM, pltpu.SemaphoreType.DMA
-    edge = (FRAMES, 8, 256)
-
-    send, first, last, inner = call(
+    side = (FRAMES * ROWS, 256)
+    rim = (FRAMES * 16, 256)
+
+    inner, one, two = call(
+        columns_kernel,
+        far(frames_in),
+        [((FRAMES, ROWS, COLS, 256), BF, False), (side, BF, False), (side, BF, False)],
+        [vm(side, F32), vm(side, F32), dma((1,))],
+    )
+    one, two = swap(one, two, "cols")
+    (send,) = call(
         start_kernel,
-        far(core, frames_in),
-        [((1024, 128), BF, False), (edge, BF, False), (edge, BF, False), ((FRAMES, ROWS, COLS, 256), BF, False)],
-        [vm((OWN,), F32), vm((8, 128), F32), dma((4,))],
-    )
-    above, below = both_ways(last, first, "rows")
+        far(core),
+        [((1024, 128), BF, False)],
+        [vm((OWN,), F32), vm((8, 128), F32), dma((1,))],
+    )
+    send, one, two = lax.optimization_barrier((send, one, two))
     got = exchange(send)
     own, wide, utp, u, ring, ot, cot, take, give, over = call(
         fetch_kernel,
@@ -453,18 +475,18 @@
             dma((9,)),
         ],
     )
-    low, high = call(
-        sides_kernel,
-        near(inner, above, below),
-        [((SIDE, 256), BF, False)] * 2,
-        [vm((SIDE, 256), F32)] * 2,
-    )
-    left, right = both_ways(high, low, "cols")
+    left, right, one, two = call(
+        rows_kernel,
+        near(inner, one, two),
+        [(side, F32, False), (side, F32, False), (rim, BF, False), (rim, BF, False)],
+        [vm(rim, F32), vm(rim, F32)],
+    )
+    one, two = swap(one, two, "rows")
     (q,) = call(
         rank_kernel,
-        near(own, wide, above.reshape(SIDE, 256), below.reshape(SIDE, 256), left, right),
+        near(own, wide, one, two, left, right),
         [((3, 240, 256), BF, False)],
-        [vm((FRAMES, 8, 8, 256), F32), vm((2, SIDE, 256), F32)],
+        [vm((FRAMES, 8, 8, 256), F32), vm((2, 18, 256), F32), vm((2, 48, 256), F32)],
     )
     send, table, outp = call(
         forward_kernel,

time: 96.7 us -> 91.3 us (0.944)
  blocking collectives: 32.8 us -> 21.4 us
  waiting for transfers between devices: 20 us -> 24.3 us
  starting transfers between devices: 31.6 us -> 32.7 us
    all_to_all x1, blocking collectives: 32.8 us -> 21.4 us  [exchange(): return lax.all_to_all(x, AXES, 0, 0, tiled=True)]
    all_to_all x2, waiting for transfers between devices: 14.9 us -> 22.2 us  [exchange(): return lax.all_to_all(x, AXES, 0, 0, tiled=True)]
    all_to_all x2, starting transfers between devices: 21.8 us -> 25.7 us  [exchange(): return lax.all_to_all(x, AXES, 0, 0, tiled=True)]
    ppermute x4, waiting for transfers between devices: 5.1 us -> 2.15 us  [swap(): lax.ppermute(x, axis, forward + [(b, a) for a, b in forward])]
    ppermute x4, starting transfers between devices: 9.87 us -> 7 us  [swap(): lax.ppermute(x, axis, forward + [(b, a) for a, b in forward])]
    pallas_call x8 -> x9, Pallas kernels: 11.2 us -> 11.9 us  [call(): pl.pallas_call(kernel, out_shape=[jax.ShapeDtypeStruct(shape, dtype) for...]
  transfers between devices with their start and end apart: 6 -> 6, of which waited for: 3 -> 3; matrix products, arithmetic and copies ran while one was open for 0% -> 0% of each run, Pallas kernels for 3% -> 4%
where the time goes in v4:
time: 91.3 us; the launch traced here: 91 us
  starting transfers between devices  32.7 us (36%)
  waiting for transfers between devices  24.3 us (27%)
  blocking collectives  21.4 us (23%)
  Pallas kernels  11.9 us (13%)
    all_to_all x2, starting transfers between devices, exchange(): return lax.all_to_all(x, AXES, 0, 0, tiled=True)  25.7 us
    all_to_all x2, waiting for transfers between devices, exchange(): return lax.all_to_all(x, AXES, 0, 0, tiled=True)  22.2 us
    all_to_all x1, blocking collectives, exchange(): return lax.all_to_all(x, AXES, 0, 0, tiled=True)  21.4 us
    pallas_call x9, Pallas kernels, call(): pl.pallas_call(kernel, out_shape=[jax.ShapeDtypeStruct(shape, dtype) for...  11.9 us
    ppermute x4, starting transfers between devices, swap(): lax.ppermute(x, axis, forward + [(b, a) for a, b in forward])  7 us
    ppermute x4, waiting for transfers between devices, swap(): lax.ppermute(x, axis, forward + [(b, a) for a, b in forward])  2.15 us
  transfers between devices with their start and end apart: 6, of which 3 were waited for; matrix products, arithmetic and copies ran while one was open for 0% of the time, Pallas kernels for 4%

profile of v4, /device:TPU:1, one launch (start us, length us, event | category | flops | bytes accessed | tf_op | source)
XLA Modules:
  0.0 91.0 jit_solution(4096950589952598589)
XLA Ops:
  0.6 0.9 %shard_map.138 = (bf16[3,6,8,256]{3,2,1,0:T(8,128)(2,1)S(1)}, bf16[18,256]{1,0:T(8,128)(2,1)S(1)}, bf16[18,256]{1,0:T(8,128)(2,1)S(1)}) custom-call(bf16[3,6,8,256]{3,2,1,0:T(8,128)(2,1)} %x_ref.1), custom_call_target="tpu_custom_call" | custom-call | flops 10000000 | bytes 100000 | tf_op jit(solution)/shard_map/pallas_call | solution.py:410
  1.6 2.2 %collective-permute-start = (bf16[18,256]{1,0:T(8,128)(2,1)S(1)}, bf16[18,256]{1,0:T(8,128)(2,1)S(1)}, u32[]{:S(2)}, u32[]{:S(2)}) collective-permute-start(bf16[18,256]{1,0:T(8,128)(2,1)S(1)} %get-tuple-element.39), channel_id=1, source_target_pairs={{0,1},{2,3},{4,5},{6,7},{1,0},{3,2},{5,4},{7,6},{8,9},{10,11},{12,... | collective-permute-start | bytes 27656 | tf_op jit(solution)/shard_map/ppermute | solution.py:433
  3.8 0.7 collective-permute-start.1
  4.4 1.5 %shard_map.137 = bf16[1024,128]{1,0:T(8,128)(2,1)} custom-call(f32[432]{0:T(512)} %core_ref.3), custom_call_target="tpu_custom_call" | custom-call | flops 10000000 | bytes 100000 | tf_op jit(solution)/shard_map/pallas_call | solution.py:410
  5.9 0.0 collective-permute-done.one_ref
  6.0 0.0 collective-permute-done.1.two_ref
  6.0 19.6 %all-to-all-start = ((bf16[256,4,128]{2,1,0:T(4,128)(2,1)}), bf16[256,4,128]{2,1,0:T(4,128)(2,1)S(1)}, u32[]{:S(2)}, u32[]{:S(2)}) async-start(bf16[256,4,128]{2,1,0:T(4,128)(2,1)} %bitcast), calls=%async_computation | async-start | bytes 524288 | tf_op jit(solution)/shard_map/all_to_all | solution.py:438
  25.6 2.2 %collective-permute-start.2 = (bf16[48,256]{1,0:T(8,128)(2,1)S(1)}, bf16[48,256]{1,0:T(8,128)(2,1)S(1)}, u32[]{:S(2)}, u32[]{:S(2)}) collective-permute-start(bf16[48,256]{1,0:T(8,128)(2,1)S(1)} %get-tuple-element.47), channel_id=1, source_target_pairs={{0,8},{16,24},{32,40},{48,56},{64,72},{80,88},{96,104},{112,120},{... | collective-permute-start | bytes 73736 | tf_op jit(solution)/shard_map/ppermute | solution.py:433
  27.8 1.9 %collective-permute-start.3 = (bf16[48,256]{1,0:T(8,128)(2,1)S(1)}, bf16[48,256]{1,0:T(8,128)(2,1)S(1)}, u32[]{:S(2)}, u32[]{:S(2)}) collective-permute-start(bf16[48,256]{1,0:T(8,128)(2,1)S(1)} %get-tuple-element.48), channel_id=1, source_target_pairs={{8,16},{24,32},{40,48},{56,64},{72,80},{88,96},{104,112},{120,128}... | collective-permute-start | bytes 73736 | tf_op jit(solution)/shard_map/ppermute | solution.py:433
  29.7 1.4 %shard_map.139 = (f32[144,256]{1,0:T(8,128)S(1)}, bf16[256,256]{1,0:T(8,128)(2,1)S(1)}, bf16[64,256]{1,0:T(8,128)(2,1)S(1)}, bf16[256,64]{1,0:T(8,128)(2,1)S(1)}...) custom-call(bf16[144,256]{1,0:T(8,128)(2,1)S(1)} %bitcast.14, ...), custom_call_target="tpu_custom_call" | custom-call | flops 10000000 | bytes 100000 | tf_op jit(solution)/shard_map/pallas_call | solution.py:410
  31.2 0.0 collective-permute-done.2.one_ref
  31.2 2.1 %collective-permute-done.3.two_ref = bf16[48,256]{1,0:T(8,128)(2,1)S(1)} collective-permute-done((bf16[48,256]{1,0:T(8,128)(2,1)S(1)}, bf16[48,256]{1,0:T(8,128)(2,1)S(1)}, u32[]{:S(2)}, u32[]{:S(2)}) %collective-permute-start.3) | collective-permute-done | bytes 24608 | tf_op jit(solution)/shard_map/ppermute | solution.py:433
  33.3 0.3 shard_map.141.q_ref
  33.7 7.3 %all-to-all-done = bf16[256,4,128]{2,1,0:T(4,128)(2,1)S(1)} async-done(((bf16[256,4,128]{2,1,0:T(4,128)(2,1)}), bf16[256,4,128]{2,1,0:T(4,128)(2,1)S(1)}, u32[]{:S(2)}, u32[]{:S(2)}) %all-to-all-start) | async-done | bytes 262176 | tf_op jit(solution)/shard_map/all_to_all | solution.py:438
  41.0 1.8 %shard_map.142 = (bf16[1024,128]{1,0:T(8,128)(2,1)S(1)}, bf16[864,128]{1,0:T(8,128)(2,1)S(1)}, f32[144,256]{1,0:T(8,128)S(1)}) custom-call(bf16[1024,128]{1,0:T(8,128)(2,1)S(1)} %bitcast.13, bf16[3,240,256]{2,1,0:T(8,128)(2,1)S(1)} %shard_map.141.q_ref, bf16[144,256]{1,0:T(8,128)(2,1)S(1)} %get-tuple-element.51.cot_ref, ...), custom_call_target="tpu_custom_call" | custom-call | flops 10000000 | bytes 100000 | tf_op jit(solution)/shard_map/pallas_call | solution.py:410
  42.8 21.4 %all_to_all.34 = bf16[256,4,128]{2,1,0:T(4,128)(2,1)S(1)} all-to-all(bf16[256,4,128]{2,1,0:T(4,128)(2,1)S(1)} %bitcast.15), channel_id=1, replica_groups=mesh['rows'=32,'cols'=8] {'rows','cols'}, dimensions={0} | all-to-all | bytes 524288 | tf_op jit(solution)/shard_map/all_to_all | solution.py:438
  64.2 0.8 shard_map.143
  65.1 6.1 %all-to-all-start.2 = ((bf16[256,4,128]{2,1,0:T(4,128)(2,1)}), bf16[256,4,128]{2,1,0:T(4,128)(2,1)S(1)}, u32[]{:S(2)}, u32[]{:S(2)}) async-start(bf16[256,4,128]{2,1,0:T(4,128)(2,1)} %bitcast.8), calls=%async_computation.2 | async-start | bytes 524288 | tf_op jit(solution)/shard_map/all_to_all | solution.py:438
  71.2 0.7 shard_map.144
  71.8 14.9 %all-to-all-done.2 = bf16[256,4,128]{2,1,0:T(4,128)(2,1)S(1)} async-done(((bf16[256,4,128]{2,1,0:T(4,128)(2,1)}), bf16[256,4,128]{2,1,0:T(4,128)(2,1)S(1)}, u32[]{:S(2)}, u32[]{:S(2)}) %all-to-all-start.2) | async-done | bytes 262176 | tf_op jit(solution)/shard_map/all_to_all | solution.py:438
  86.7 4.3 %shard_map.145 = (bf16[27,256,256]{2,1,0:T(8,128)(2,1)}, bf16[144,256]{1,0:T(8,128)(2,1)}) custom-call(bf16[1024,128]{1,0:T(8,128)(2,1)S(1)} %bitcast.11, f32[144,256]{1,0:T(8,128)S(1)} %get-tuple-element.64.outp_ref, bf16[864,128]{1,0:T(8,128)(2,1)S(1)} %get-tuple-element.65.old_ref, bf16[64,256]{1,0:T(8,128)(2,1)S(1)} %get-tuple-element.66.utp_ref, ...), custom_call_target="tpu_custom_call" | custom-call | flops 10000000 | bytes 100000 | tf_op jit(solution)/shard_map/pallas_call | solution.py:410
  (1 shorter events, 0.0 us)
Async XLA Ops:
  1.6 4.4 %collective-permute-start = (bf16[18,256]{1,0:T(8,128)(2,1)S(1)}, bf16[18,256]{1,0:T(8,128)(2,1)S(1)}, u32[]{:S(2)}, u32[]{:S(2)}) collective-permute-start(bf16[18,256]{1,0:T(8,128)(2,1)S(1)} %get-tuple-element.39), channel_id=1, source_target_pairs={{0,1},{2,3},{4,5},{6,7},{1,0},{3,2},{5,4},{7,6},{8,9},{10,11},{12,... | collective-permute-start | bytes 27656 | tf_op jit(solution)/shard_map/ppermute | solution.py:433
  3.8 2.2 %collective-permute-start.1 = (bf16[18,256]{1,0:T(8,128)(2,1)S(1)}, bf16[18,256]{1,0:T(8,128)(2,1)S(1)}, u32[]{:S(2)}, u32[]{:S(2)}) collective-permute-start(bf16[18,256]{1,0:T(8,128)(2,1)S(1)} %get-tuple-element.40), channel_id=1, source_target_pairs={{1,2},{3,4},{5,6},{2,1},{4,3},{6,5},{9,10},{11,12},{13,14},{10,9},... | collective-permute-start | bytes 27656 | tf_op jit(solution)/shard_map/ppermute | solution.py:433
  6.0 35.0 %all-to-all-start = ((bf16[256,4,128]{2,1,0:T(4,128)(2,1)}), bf16[256,4,128]{2,1,0:T(4,128)(2,1)S(1)}, u32[]{:S(2)}, u32[]{:S(2)}) async-start(bf16[256,4,128]{2,1,0:T(4,128)(2,1)} %bitcast), calls=%async_computation | async-start | bytes 524288 | tf_op jit(solution)/shard_map/all_to_all | solution.py:438
  25.6 5.6 %collective-permute-start.2 = (bf16[48,256]{1,0:T(8,128)(2,1)S(1)}, bf16[48,256]{1,0:T(8,128)(2,1)S(1)}, u32[]{:S(2)}, u32[]{:S(2)}) collective-permute-start(bf16[48,256]{1,0:T(8,128)(2,1)S(1)} %get-tuple-element.47), channel_id=1, source_target_pairs={{0,8},{16,24},{32,40},{48,56},{64,72},{80,88},{96,104},{112,120},{... | collective-permute-start | bytes 73736 | tf_op jit(solution)/shard_map/ppermute | solution.py:433
  27.8 5.5 %collective-permute-start.3 = (bf16[48,256]{1,0:T(8,128)(2,1)S(1)}, bf16[48,256]{1,0:T(8,128)(2,1)S(1)}, u32[]{:S(2)}, u32[]{:S(2)}) collective-permute-start(bf16[48,256]{1,0:T(8,128)(2,1)S(1)} %get-tuple-element.48), channel_id=1, source_target_pairs={{8,16},{24,32},{40,48},{56,64},{72,80},{88,96},{104,112},{120,128}... | collective-permute-start | bytes 73736 | tf_op jit(solution)/shard_map/ppermute | solution.py:433
  65.1 21.7 %all-to-all-start.2 = ((bf16[256,4,128]{2,1,0:T(4,128)(2,1)}), bf16[256,4,128]{2,1,0:T(4,128)(2,1)S(1)}, u32[]{:S(2)}, u32[]{:S(2)}) async-start(bf16[256,4,128]{2,1,0:T(4,128)(2,1)} %bitcast.8), calls=%async_computation.2 | async-start | bytes 524288 | tf_op jit(solution)/shard_map/all_to_all | solution.py:438

commit v5 on v3

--- a/solution.py
+++ b/solution.py
@@ -114,36 +114,38 @@
     return copies
 
 
-def start_kernel(core_ref, x_ref, send_ref, first_ref, last_ref, inner_ref, own, flat, sems):
-    copies = fetch(
-        (
-            (core_ref, own), (x_ref.at[:, 0], first_ref), (x_ref.at[:, ROWS - 1], last_ref), (x_ref, inner_ref),
-        ),
-        sems,
-    )
+def even_first(axis, first, last):
+    even = jnp.full(first.shape, lax.rem(lax.axis_index(axis), 2), jnp.int32) == 0
+    return jnp.where(even, last, first), jnp.where(even, first, last)
+
+
+def start_kernel(core_ref, x_ref, send_ref, one_ref, two_ref, inner_ref, own, flat, sems):
+    copies = fetch(((x_ref, inner_ref), (core_ref, own)), sems)
     copies[0].wait()
+    for f in range(FRAMES):
+        first, last = inner_ref[f, 0].astype(F32), inner_ref[f, ROWS - 1].astype(F32)
+        one, two = even_first("rows", first, last)
+        one_ref[f] = one.astype(BF)
+        two_ref[f] = two.astype(BF)
+    copies[1].wait()
     v = to_ring(load_flat(own, flat), ring_shift())
     block = jnp.concatenate([v, v, v, v], axis=0).astype(BF)
     for k in range(64):
         send_ref[16 * k : 16 * k + 16, :] = block
-    for k in range(1, 4):
-        copies[k].wait()
-
-
-def sides_kernel(own_ref, above_ref, below_ref, low_ref, high_ref, low, high):
+
+
+def columns_kernel(inner_ref, one_ref, two_ref, above_ref, below_ref, left_ref, right_ref, low, high):
     for f in range(FRAMES):
+        below, above = even_first("rows", two_ref[f].astype(F32), one_ref[f].astype(F32))
+        above_ref[8 * f : 8 * f + 8, :] = above
+        below_ref[8 * f : 8 * f + 8, :] = below
         for y in range(8):
-            if y == 0:
-                tile = above_ref[f]
-            elif y == 7:
-                tile = below_ref[f]
-            else:
-                tile = own_ref[f, y - 1]
-            tile = tile.astype(F32)
+            tile = above if y == 0 else below if y == 7 else inner_ref[f, y - 1].astype(F32)
             low[8 * f + y : 8 * f + y + 1, :] = tile[0:1, :]
             high[8 * f + y : 8 * f + y + 1, :] = tile[7:8, :]
-    low_ref[...] = low[...].astype(BF)
-    high_ref[...] = high[...].astype(BF)
+    one, two = even_first("cols", low[...], high[...])
+    left_ref[...] = one.astype(BF)
+    right_ref[...] = two.astype(BF)
 
 
 def shifted(tile, left, right, bounds, period):
@@ -195,28 +197,28 @@
             out_ref[b, 48 * f + 48 : 48 * f + 96, :] = rows.astype(BF)
 
 
-def rank_kernel(own_ref, wide_ref, above_ref, below_ref, left_ref, right_ref, q_ref, tiles, edge):
+def rank_kernel(own_ref, wide_ref, above_ref, below_ref, one_ref, two_ref, q_ref, tiles, edge, rims):
     wide = wide_ref[...]
 
     def project(v):
-        return dot_nt(v, wide).astype(BF).astype(F32)
-
-    above = project(above_ref[...])
-    below = project(below_ref[...])
-    for f in range(FRAMES):
-        tiles[f, 0] = above[8 * f : 8 * f + 8]
-        tiles[f, 7] = below[8 * f : 8 * f + 8]
-        for y in range(ROWS):
-            at = 48 * f + 8 * y
-            tiles[f, y + 1] = own_ref[at : at + 8, :]
-    edge[0] = project(left_ref[...])
-    edge[1] = project(right_ref[...])
+        return dot_nt(v.astype(BF), wide).astype(BF).astype(F32)
+
+    rims[0] = project(above_ref[...])
+    rims[1] = project(below_ref[...])
+    right, left = even_first("cols", project(two_ref[...]), project(one_ref[...]))
+    edge[0] = left
+    edge[1] = right
     for f in range(FRAMES):
         for y in range(8):
             k = 8 * f + y
+            if y in (0, 7):
+                tile = rims[y // 7, 8 * f : 8 * f + 8, :]
+            else:
+                at = 48 * f + 8 * (y - 1)
+                tile = own_ref[at : at + 8, :]
             left = jnp.broadcast_to(edge[0, k : k + 1, :], (8, 256))
             right = jnp.broadcast_to(edge[1, k : k + 1, :], (8, 256))
-            tiles[f, y] = shifted(tiles[f, y], left, right, (32, 64), 128)
+            tiles[f, y] = shifted(tile, left, right, (32, 64), 128)
     stack_rows(tiles, q_ref)
 
 
@@ -413,11 +415,12 @@
     return [(arg, True) for arg in args]
 
 
-def both_ways(high, low, axis):
+def swap(one, two, axis):
     count = lax.axis_size(axis)
-    forward = [(i, i + 1) for i in range(count - 1)]
-    backward = [(i + 1, i) for i in range(count - 1)]
-    return lax.ppermute(high, axis, forward), lax.ppermute(low, axis, backward)
+    pairs = [[(i, i + 1) for i in range(k, count - 1, 2)] for k in range(2)]
+    return tuple(
+        lax.ppermute(x, axis, forward + [(b, a) for a, b in forward]) for x, forward in zip((one, two), pairs)
+    )
 
 
 def exchange(x):
@@ -428,15 +431,16 @@
     take, give, over = ring_tables()
     take, give, over = jnp.asarray(take, BF), jnp.asarray(give, BF), jnp.asarray(over, F32)
     vm, dma = pltpu.VMEM, pltpu.SemaphoreType.DMA
-    edge = (FRAMES, 8, 256)
-
-    send, first, last, inner = call(
+    rim = (FRAMES * 8, 256)
+    row = (FRAMES, 8, 256)
+
+    send, one, two, inner = call(
         start_kernel,
         far(core, frames_in),
-        [((1024, 128), BF, False), (edge, BF, False), (edge, BF, False), ((FRAMES, ROWS, COLS, 256), BF, False)],
-        [vm((OWN,), F32), vm((8, 128), F32), dma((4,))],
-    )
-    above, below = both_ways(last, first, "rows")
+        [((1024, 128), BF, False), (row, BF, False), (row, BF, False), ((FRAMES, ROWS, COLS, 256), BF, False)],
+        [vm((OWN,), F32), vm((8, 128), F32), dma((2,))],
+    )
+    one, two = swap(one, two, "rows")
     got = exchange(send)
     own, wide, utp, u, ring, ot, cot, take, give, over = call(
         fetch_kernel,
@@ -453,18 +457,19 @@
             dma((9,)),
         ],
     )
-    low, high = call(
-        sides_kernel,
-        near(inner, above, below),
-        [((SIDE, 256), BF, False)] * 2,
-        [vm((SIDE, 256), F32)] * 2,
-    )
-    left, right = both_ways(high, low, "cols")
+    above, below, one, two = call(
+        columns_kernel,
+        near(inner, one, two),
+        [(rim, F32, False), (rim, F32, False), (rim, BF, False), (rim, BF, False)],
+        [vm(rim, F32), vm(rim, F32)],
+        flops=10000000000,
+    )
+    one, two = swap(one, two, "cols")
     (q,) = call(
         rank_kernel,
-        near(own, wide, above.reshape(SIDE, 256), below.reshape(SIDE, 256), left, right),
+        near(own, wide, above, below, one, two),
         [((3, 240, 256), BF, False)],
-        [vm((FRAMES, 8, 8, 256), F32), vm((2, SIDE, 256), F32)],
+        [vm((FRAMES, 8, 8, 256), F32), vm((2, 24, 256), F32), vm((2, 24, 256), F32)],
     )
     send, table, outp = call(
         forward_kernel,

time: 96.7 us -> 88 us (0.910)
  blocking collectives: 32.8 us -> 22.3 us
  waiting for transfers between devices: 20 us -> 26.3 us
  starting transfers between devices: 31.6 us -> 27.2 us
    all_to_all x2, waiting for transfers between devices: 14.9 us -> 26.3 us  [exchange(): return lax.all_to_all(x, AXES, 0, 0, tiled=True)]
    all_to_all x1, blocking collectives: 32.8 us -> 22.3 us  [exchange(): return lax.all_to_all(x, AXES, 0, 0, tiled=True)]
    ppermute x4, waiting for transfers between devices: 5.1 us -> 0.01 us  [swap(): lax.ppermute(x, axis, forward + [(b, a) for a, b in forward])]
    ppermute x4, starting transfers between devices: 9.87 us -> 7.36 us  [swap(): lax.ppermute(x, axis, forward + [(b, a) for a, b in forward])]
    all_to_all x2, starting transfers between devices: 21.8 us -> 19.8 us  [exchange(): return lax.all_to_all(x, AXES, 0, 0, tiled=True)]
  transfers between devices with their start and end apart: 6 -> 6, of which waited for: 3 -> 2; matrix products, arithmetic and copies ran while one was open for 0% -> 0% of each run, Pallas kernels for 3% -> 3%
where the time goes in v5:
time: 88 us; the launch traced here: 87.7 us
  starting transfers between devices  27.2 us (31%)
  waiting for transfers between devices  26.3 us (30%)
  blocking collectives  22.3 us (25%)
  Pallas kernels  11.2 us (13%)
    all_to_all x2, waiting for transfers between devices, exchange(): return lax.all_to_all(x, AXES, 0, 0, tiled=True)  26.3 us
    all_to_all x1, blocking collectives, exchange(): return lax.all_to_all(x, AXES, 0, 0, tiled=True)  22.3 us
    all_to_all x2, starting transfers between devices, exchange(): return lax.all_to_all(x, AXES, 0, 0, tiled=True)  19.8 us
    pallas_call x8, Pallas kernels, call(): pl.pallas_call(kernel, out_shape=[jax.ShapeDtypeStruct(shape, dtype) for...  11.2 us
    ppermute x4, starting transfers between devices, swap(): lax.ppermute(x, axis, forward + [(b, a) for a, b in forward])  7.36 us
  transfers between devices with their start and end apart: 6, of which 2 were waited for; matrix products, arithmetic and copies ran while one was open for 0% of the time, Pallas kernels for 3%

profile of v5, /device:TPU:1, one launch (start us, length us, event | category | flops | bytes accessed | tf_op | source)
XLA Modules:
  0.0 87.7 jit_solution(628930503510388334)
XLA Ops:
  0.6 1.7 %shard_map.137 = (bf16[1024,128]{1,0:T(8,128)(2,1)}, bf16[3,8,256]{2,1,0:T(8,128)(2,1)S(1)}, bf16[3,8,256]{2,1,0:T(8,128)(2,1)S(1)}, bf16[3,6,8,256]{3,2,1,0:T(8,128)(2,1)S(1)}) custom-call(f32[432]{0:T(512)} %core_ref.3, bf16[3,6,8,256]{3,2,1,0:T(8,128)(2,1)} %x_ref.1), custom_call_target="tpu_custom_call" | custom-call | flops 10000000 | bytes 100000 | tf_op jit(solution)/shard_map/pallas_call | solution.py:399
  2.3 3.3 %collective-permute-start = (bf16[3,8,256]{2,1,0:T(8,128)(2,1)S(1)}, bf16[3,8,256]{2,1,0:T(8,128)(2,1)S(1)}, u32[]{:S(2)}, u32[]{:S(2)}) collective-permute-start(bf16[3,8,256]{2,1,0:T(8,128)(2,1)S(1)} %get-tuple-element.41), channel_id=1, source_target_pairs={{0,8},{16,24},{32,40},{48,56},{64,72},{80,88},{96,104},{112,120},{... | collective-permute-start | bytes 36872 | tf_op jit(solution)/shard_map/ppermute | solution.py:422
  5.7 1.9 %collective-permute-start.1 = (bf16[3,8,256]{2,1,0:T(8,128)(2,1)S(1)}, bf16[3,8,256]{2,1,0:T(8,128)(2,1)S(1)}, u32[]{:S(2)}, u32[]{:S(2)}) collective-permute-start(bf16[3,8,256]{2,1,0:T(8,128)(2,1)S(1)} %get-tuple-element.42), channel_id=1, source_target_pairs={{8,16},{24,32},{40,48},{56,64},{72,80},{88,96},{104,112},{120,128}... | collective-permute-start | bytes 36872 | tf_op jit(solution)/shard_map/ppermute | solution.py:422
  7.6 13.7 %all-to-all-start = ((bf16[256,4,128]{2,1,0:T(4,128)(2,1)}), bf16[256,4,128]{2,1,0:T(4,128)(2,1)S(1)}, u32[]{:S(2)}, u32[]{:S(2)}) async-start(bf16[256,4,128]{2,1,0:T(4,128)(2,1)} %bitcast), calls=%async_computation | async-start | bytes 524288 | tf_op jit(solution)/shard_map/all_to_all | solution.py:427
  21.3 0.0 collective-permute-done.one_ref
  21.3 0.0 collective-permute-done.1.two_ref
  21.3 0.1 shard_map.139
  21.4 1.5 %collective-permute-start.2 = (bf16[24,256]{1,0:T(8,128)(2,1)S(1)}, bf16[24,256]{1,0:T(8,128)(2,1)S(1)}, u32[]{:S(2)}, u32[]{:S(2)}) collective-permute-start(bf16[24,256]{1,0:T(8,128)(2,1)S(1)} %get-tuple-element.45), channel_id=1, source_target_pairs={{0,1},{2,3},{4,5},{6,7},{1,0},{3,2},{5,4},{7,6},{8,9},{10,11},{12,... | collective-permute-start | bytes 36872 | tf_op jit(solution)/shard_map/ppermute | solution.py:422
  22.9 0.7 collective-permute-start.3
  23.5 1.4 %shard_map.138 = (f32[144,256]{1,0:T(8,128)S(1)}, bf16[256,256]{1,0:T(8,128)(2,1)S(1)}, bf16[64,256]{1,0:T(8,128)(2,1)S(1)}, bf16[256,64]{1,0:T(8,128)(2,1)S(1)}...) custom-call(bf16[144,256]{1,0:T(8,128)(2,1)S(1)} %bitcast.15, ...), custom_call_target="tpu_custom_call" | custom-call | flops 10000000 | bytes 100000 | tf_op jit(solution)/shard_map/pallas_call | solution.py:399
  25.0 0.0 collective-permute-done.2.one_ref
  25.0 0.0 collective-permute-done.3.two_ref
  25.0 0.3 shard_map.140.q_ref
  25.3 11.4 %all-to-all-done = bf16[256,4,128]{2,1,0:T(4,128)(2,1)S(1)} async-done(((bf16[256,4,128]{2,1,0:T(4,128)(2,1)}), bf16[256,4,128]{2,1,0:T(4,128)(2,1)S(1)}, u32[]{:S(2)}, u32[]{:S(2)}) %all-to-all-start) | async-done | bytes 262176 | tf_op jit(solution)/shard_map/all_to_all | solution.py:427
  36.7 1.8 %shard_map.141 = (bf16[1024,128]{1,0:T(8,128)(2,1)S(1)}, bf16[864,128]{1,0:T(8,128)(2,1)S(1)}, f32[144,256]{1,0:T(8,128)S(1)}) custom-call(bf16[1024,128]{1,0:T(8,128)(2,1)S(1)} %bitcast.13, bf16[3,240,256]{2,1,0:T(8,128)(2,1)S(1)} %shard_map.140.q_ref, bf16[144,256]{1,0:T(8,128)(2,1)S(1)} %get-tuple-element.47.cot_ref, ...), custom_call_target="tpu_custom_call" | custom-call | flops 10000000 | bytes 100000 | tf_op jit(solution)/shard_map/pallas_call | solution.py:399
  38.6 22.3 %all_to_all.34 = bf16[256,4,128]{2,1,0:T(4,128)(2,1)S(1)} all-to-all(bf16[256,4,128]{2,1,0:T(4,128)(2,1)S(1)} %bitcast.14), channel_id=1, replica_groups=mesh['rows'=32,'cols'=8] {'rows','cols'}, dimensions={0} | all-to-all | bytes 524288 | tf_op jit(solution)/shard_map/all_to_all | solution.py:427
  60.9 0.8 shard_map.142
  61.7 6.1 %all-to-all-start.2 = ((bf16[256,4,128]{2,1,0:T(4,128)(2,1)}), bf16[256,4,128]{2,1,0:T(4,128)(2,1)S(1)}, u32[]{:S(2)}, u32[]{:S(2)}) async-start(bf16[256,4,128]{2,1,0:T(4,128)(2,1)} %bitcast.8), calls=%async_computation.2 | async-start | bytes 524288 | tf_op jit(solution)/shard_map/all_to_all | solution.py:427
  67.8 0.7 shard_map.143
  68.5 14.9 %all-to-all-done.2 = bf16[256,4,128]{2,1,0:T(4,128)(2,1)S(1)} async-done(((bf16[256,4,128]{2,1,0:T(4,128)(2,1)}), bf16[256,4,128]{2,1,0:T(4,128)(2,1)S(1)}, u32[]{:S(2)}, u32[]{:S(2)}) %all-to-all-start.2) | async-done | bytes 262176 | tf_op jit(solution)/shard_map/all_to_all | solution.py:427
  83.3 4.3 %shard_map.144 = (bf16[27,256,256]{2,1,0:T(8,128)(2,1)}, bf16[144,256]{1,0:T(8,128)(2,1)}) custom-call(bf16[1024,128]{1,0:T(8,128)(2,1)S(1)} %bitcast.11, f32[144,256]{1,0:T(8,128)S(1)} %get-tuple-element.60.outp_ref, bf16[864,128]{1,0:T(8,128)(2,1)S(1)} %get-tuple-element.61.old_ref, bf16[64,256]{1,0:T(8,128)(2,1)S(1)} %get-tuple-element.62.utp_ref, ...), custom_call_target="tpu_custom_call" | custom-call | flops 10000000 | bytes 100000 | tf_op jit(solution)/shard_map/pallas_call | solution.py:399
Async XLA Ops:
  2.3 19.0 %collective-permute-start = (bf16[3,8,256]{2,1,0:T(8,128)(2,1)S(1)}, bf16[3,8,256]{2,1,0:T(8,128)(2,1)S(1)}, u32[]{:S(2)}, u32[]{:S(2)}) collective-permute-start(bf16[3,8,256]{2,1,0:T(8,128)(2,1)S(1)} %get-tuple-element.41), channel_id=1, source_target_pairs={{0,8},{16,24},{32,40},{48,56},{64,72},{80,88},{96,104},{112,120},{... | collective-permute-start | bytes 36872 | tf_op jit(solution)/shard_map/ppermute | solution.py:422
  5.7 15.7 %collective-permute-start.1 = (bf16[3,8,256]{2,1,0:T(8,128)(2,1)S(1)}, bf16[3,8,256]{2,1,0:T(8,128)(2,1)S(1)}, u32[]{:S(2)}, u32[]{:S(2)}) collective-permute-start(bf16[3,8,256]{2,1,0:T(8,128)(2,1)S(1)} %get-tuple-element.42), channel_id=1, source_target_pairs={{8,16},{24,32},{40,48},{56,64},{72,80},{88,96},{104,112},{120,128}... | collective-permute-start | bytes 36872 | tf_op jit(solution)/shard_map/ppermute | solution.py:422
  7.6 29.1 %all-to-all-start = ((bf16[256,4,128]{2,1,0:T(4,128)(2,1)}), bf16[256,4,128]{2,1,0:T(4,128)(2,1)S(1)}, u32[]{:S(2)}, u32[]{:S(2)}) async-start(bf16[256,4,128]{2,1,0:T(4,128)(2,1)} %bitcast), calls=%async_computation | async-start | bytes 524288 | tf_op jit(solution)/shard_map/all_to_all | solution.py:427
  21.4 3.6 %collective-permute-start.2 = (bf16[24,256]{1,0:T(8,128)(2,1)S(1)}, bf16[24,256]{1,0:T(8,128)(2,1)S(1)}, u32[]{:S(2)}, u32[]{:S(2)}) collective-permute-start(bf16[24,256]{1,0:T(8,128)(2,1)S(1)} %get-tuple-element.45), channel_id=1, source_target_pairs={{0,1},{2,3},{4,5},{6,7},{1,0},{3,2},{5,4},{7,6},{8,9},{10,11},{12,... | collective-permute-start | bytes 36872 | tf_op jit(solution)/shard_map/ppermute | solution.py:422
  22.9 2.1 %collective-permute-start.3 = (bf16[24,256]{1,0:T(8,128)(2,1)S(1)}, bf16[24,256]{1,0:T(8,128)(2,1)S(1)}, u32[]{:S(2)}, u32[]{:S(2)}) collective-permute-start(bf16[24,256]{1,0:T(8,128)(2,1)S(1)} %get-tuple-element.46), channel_id=1, source_target_pairs={{1,2},{3,4},{5,6},{2,1},{4,3},{6,5},{9,10},{11,12},{13,14},{10,9},... | collective-permute-start | bytes 36872 | tf_op jit(solution)/shard_map/ppermute | solution.py:422
  61.7 21.7 %all-to-all-start.2 = ((bf16[256,4,128]{2,1,0:T(4,128)(2,1)}), bf16[256,4,128]{2,1,0:T(4,128)(2,1)S(1)}, u32[]{:S(2)}, u32[]{:S(2)}) async-start(bf16[256,4,128]{2,1,0:T(4,128)(2,1)} %bitcast.8), calls=%async_computation.2 | async-start | bytes 524288 | tf_op jit(solution)/shard_map/all_to_all | solution.py:427

commit v6 on v4

--- a/solution.py
+++ b/solution.py
@@ -119,8 +119,14 @@
     return jnp.where(even, last, first), jnp.where(even, first, last)
 
 
-def columns_kernel(x_ref, inner_ref, one_ref, two_ref, low, high, sems):
-    fetch(((x_ref, inner_ref),), sems)[0].wait()
+def start_kernel(core_ref, x_ref, send_ref, one_ref, two_ref, inner_ref, own, flat, low, high, sems):
+    copies = fetch(((x_ref, inner_ref), (core_ref, own)), sems)
+    copies[1].wait()
+    v = to_ring(load_flat(own, flat), ring_shift())
+    block = jnp.concatenate([v, v, v, v], axis=0).astype(BF)
+    for k in range(64):
+        send_ref[16 * k : 16 * k + 16, :] = block
+    copies[0].wait()
     for f in range(FRAMES):
         for y in range(ROWS):
             tile = inner_ref[f, y].astype(F32)
@@ -130,14 +136,6 @@
     one, two = even_first("cols", low[...], high[...])
     one_ref[...] = one.astype(BF)
     two_ref[...] = two.astype(BF)
-
-
-def start_kernel(core_ref, send_ref, own, flat, sems):
-    fetch(((core_ref, own),), sems)[0].wait()
-    v = to_ring(load_flat(own, flat), ring_shift())
-    block = jnp.concatenate([v, v, v, v], axis=0).astype(BF)
-    for k in range(64):
-        send_ref[16 * k : 16 * k + 16, :] = block
 
 
 def rows_kernel(inner_ref, one_ref, two_ref, left_ref, right_ref, up_ref, down_ref, first, last):
@@ -333,8 +331,17 @@
         store_flat(ref, from_ring(next_ref[k], shift))
 
 
+def turn_kernel(table_ref, back_ref):
+    for k in range(9):
+        for c in range(3):
+            t = 3 * k + c
+            part = table_ref[32 * t : 32 * t + 32, :].astype(F32).T
+            cube = jnp.concatenate([part[0:64], part[64:128]], axis=1)
+            back_ref[k, 64 * (2 - c) : 64 * (2 - c) + 64, :] = cube.astype(BF)
+
+
 def finish_kernel(
-    got_ref, outp_ref, old_ref, utp_ref, u_ref, ot_ref, take_ref, over_ref,
+    got_ref, outp_ref, back_ref, utp_ref, u_ref, ot_ref, take_ref, over_ref,
     out_ref, grad_ref, table, half, result, got, pixels, tiles, qs, sems,
 ):
     gather_table(got_ref, take_ref, over_ref, table)
@@ -392,12 +399,7 @@
     for a in range(3):
         for b in range(3):
             rows = qs[2 - b, 48 * (2 - a) : 48 * (2 - a) + CELLS, :]
-            for c in range(3):
-                t = 9 * a + 3 * b + c
-                part = old_ref[32 * t : 32 * t + 32, :]
-                cube = jnp.concatenate([part[:, 0:64], part[:, 64:128]], axis=0)
-                piece = rows[:, 64 * (2 - c) : 64 * (2 - c) + 64]
-                total = total + dot_nt(piece, cube)
+            total = total + dot(rows[:, 0:192], back_ref[3 * a + b])
     grad_ref[...] = dot(total.astype(BF), utp_ref[...]).astype(BF)
     for a in range(9):
         store(a).wait()
@@ -429,9 +431,10 @@
 def swap(one, two, axis):
     count = lax.axis_size(axis)
     pairs = [[(i, i + 1) for i in range(k, count - 1, 2)] for k in range(2)]
-    return tuple(
-        lax.ppermute(x, axis, forward + [(b, a) for a, b in forward]) for x, forward in zip((one, two), pairs)
-    )
+    two, one = (
+        lax.ppermute(x, axis, forward + [(b, a) for a, b in forward]) for x, forward in ((two, pairs[1]), (one, pairs[0]))
+    )
+    return one, two
 
 
 def exchange(x):
@@ -445,20 +448,13 @@
     side = (FRAMES * ROWS, 256)
     rim = (FRAMES * 16, 256)
 
-    inner, one, two = call(
-        columns_kernel,
-        far(frames_in),
-        [((FRAMES, ROWS, COLS, 256), BF, False), (side, BF, False), (side, BF, False)],
-        [vm(side, F32), vm(side, F32), dma((1,))],
+    send, one, two, inner = call(
+        start_kernel,
+        far(core, frames_in),
+        [((1024, 128), BF, False), (side, BF, False), (side, BF, False), ((FRAMES, ROWS, COLS, 256), BF, False)],
+        [vm((OWN,), F32), vm((8, 128), F32), vm(side, F32), vm(side, F32), dma((2,))],
     )
     one, two = swap(one, two, "cols")
-    (send,) = call(
-        start_kernel,
-        far(core),
-        [((1024, 128), BF, False)],
-        [vm((OWN,), F32), vm((8, 128), F32), dma((1,))],
-    )
-    send, one, two = lax.optimization_barrier((send, one, two))
     got = exchange(send)
     own, wide, utp, u, ring, ot, cot, take, give, over = call(
         fetch_kernel,
@@ -480,6 +476,7 @@
         near(inner, one, two),
         [(side, F32, False), (side, F32, False), (rim, BF, False), (rim, BF, False)],
         [vm(rim, F32), vm(rim, F32)],
+        flops=10**10,
     )
     one, two = swap(one, two, "rows")
     (q,) = call(
@@ -495,6 +492,8 @@
         [vm((TABLE, 128), F32), vm((TABLE, 128), F32), vm((CELLS, 128), F32), vm((96, 128), F32)],
     )
     got = exchange(send)
+    (back,) = call(turn_kernel, near(table), [((9, 192, 64), BF, False)], [])
+    got, back = lax.optimization_barrier((got, back))
     send, latest = call(
         adam_kernel,
         near(got, ring),
@@ -506,7 +505,7 @@
     got, core_next, one_next, two_next = lax.optimization_barrier((got, core_next, one_next, two_next))
     kernel_next, frames_grad = call(
         finish_kernel,
-        near(got, outp, table, utp, u, ot, take, over),
+        near(got, outp, back, utp, u, ot, take, over),
         [((27, 256, 256), BF, True), ((CELLS, 256), BF, False)],
         [
             vm((TABLE, 128), F32), vm((27, 64, 256), BF), vm((27, 256, 256), BF), vm((1024, 128), F32),

time: 91.3 us -> 87.7 us (0.961)
  blocking collectives: 21.4 us -> 0 us
  waiting for transfers between devices: 24.3 us -> 39.4 us
  starting transfers between devices: 32.7 us -> 35.8 us
    all_to_all x1 -> x0, blocking collectives: 21.4 us -> none  [exchange(): return lax.all_to_all(x, AXES, 0, 0, tiled=True)]
    all_to_all x2 -> x3, waiting for transfers between devices: 22.2 us -> 37.2 us  [exchange(): return lax.all_to_all(x, AXES, 0, 0, tiled=True)]
    all_to_all x2 -> x3, starting transfers between devices: 25.7 us -> 28.8 us  [exchange(): return lax.all_to_all(x, AXES, 0, 0, tiled=True)]
  transfers between devices with their start and end apart: 6 -> 7, of which waited for: 3 -> 4; matrix products, arithmetic and copies ran while one was open for 0% -> 0% of each run, Pallas kernels for 4% -> 3%
where the time goes in v6:
time: 87.7 us; the launch traced here: 87.4 us
  waiting for transfers between devices  39.4 us (45%)
  starting transfers between devices  35.8 us (41%)
  Pallas kernels  11.5 us (13%)
    all_to_all x3, waiting for transfers between devices, exchange(): return lax.all_to_all(x, AXES, 0, 0, tiled=True)  37.2 us
    all_to_all x3, starting transfers between devices, exchange(): return lax.all_to_all(x, AXES, 0, 0, tiled=True)  28.8 us
    pallas_call x9, Pallas kernels, call(): pl.pallas_call(kernel, out_shape=[jax.ShapeDtypeStruct(shape, dtype) for...  11.5 us
    ppermute x4, starting transfers between devices, swap(): lax.ppermute(x, axis, forward + [(b, a) for a, b in forward])  7 us
    ppermute x4, waiting for transfers between devices, swap(): lax.ppermute(x, axis, forward + [(b, a) for a, b in forward])  2.14 us
  transfers between devices with their start and end apart: 7, of which 4 were waited for; matrix products, arithmetic and copies ran while one was open for 0% of the time, Pallas kernels for 3%

profile of v6, /device:TPU:1, one launch (start us, length us, event | category | flops | bytes accessed | tf_op | source)
XLA Modules:
  0.0 87.4 jit_solution(6120267436647988744)
XLA Ops:
  0.6 1.6 %shard_map.137 = (bf16[1024,128]{1,0:T(8,128)(2,1)}, bf16[18,256]{1,0:T(8,128)(2,1)S(1)}, bf16[18,256]{1,0:T(8,128)(2,1)S(1)}, bf16[3,6,8,256]{3,2,1,0:T(8,128)(2,1)S(1)}) custom-call(f32[432]{0:T(512)} %core_ref.3, bf16[3,6,8,256]{3,2,1,0:T(8,128)(2,1)} %x_ref.1), custom_call_target="tpu_custom_call" | custom-call | flops 10000000 | bytes 100000 | tf_op jit(solution)/shard_map/pallas_call | solution.py:412
  2.2 2.2 %collective-permute-start = (bf16[18,256]{1,0:T(8,128)(2,1)S(1)}, bf16[18,256]{1,0:T(8,128)(2,1)S(1)}, u32[]{:S(2)}, u32[]{:S(2)}) collective-permute-start(bf16[18,256]{1,0:T(8,128)(2,1)S(1)} %get-tuple-element.43), channel_id=1, source_target_pairs={{0,1},{2,3},{4,5},{6,7},{1,0},{3,2},{5,4},{7,6},{8,9},{10,11},{12,... | collective-permute-start | bytes 27656 | tf_op jit(solution)/shard_map/ppermute | solution.py:435
  4.5 0.7 collective-permute-start.1
  5.1 16.5 %all-to-all-start = ((bf16[256,4,128]{2,1,0:T(4,128)(2,1)}), bf16[256,4,128]{2,1,0:T(4,128)(2,1)S(1)}, u32[]{:S(2)}, u32[]{:S(2)}) async-start(bf16[256,4,128]{2,1,0:T(4,128)(2,1)} %bitcast), calls=%async_computation | async-start | bytes 524288 | tf_op jit(solution)/shard_map/all_to_all | solution.py:441
  21.6 0.0 collective-permute-done.one_ref
  21.6 0.0 collective-permute-done.1.two_ref
  21.7 2.2 %collective-permute-start.2 = (bf16[48,256]{1,0:T(8,128)(2,1)S(1)}, bf16[48,256]{1,0:T(8,128)(2,1)S(1)}, u32[]{:S(2)}, u32[]{:S(2)}) collective-permute-start(bf16[48,256]{1,0:T(8,128)(2,1)S(1)} %get-tuple-element.45), channel_id=1, source_target_pairs={{0,8},{16,24},{32,40},{48,56},{64,72},{80,88},{96,104},{112,120},{... | collective-permute-start | bytes 73736 | tf_op jit(solution)/shard_map/ppermute | solution.py:435
  23.9 1.9 %collective-permute-start.3 = (bf16[48,256]{1,0:T(8,128)(2,1)S(1)}, bf16[48,256]{1,0:T(8,128)(2,1)S(1)}, u32[]{:S(2)}, u32[]{:S(2)}) collective-permute-start(bf16[48,256]{1,0:T(8,128)(2,1)S(1)} %get-tuple-element.46), channel_id=1, source_target_pairs={{8,16},{24,32},{40,48},{56,64},{72,80},{88,96},{104,112},{120,128}... | collective-permute-start | bytes 73736 | tf_op jit(solution)/shard_map/ppermute | solution.py:435
  25.8 1.4 %shard_map.138 = (f32[144,256]{1,0:T(8,128)S(1)}, bf16[256,256]{1,0:T(8,128)(2,1)S(1)}, bf16[64,256]{1,0:T(8,128)(2,1)S(1)}, bf16[256,64]{1,0:T(8,128)(2,1)S(1)}...) custom-call(bf16[144,256]{1,0:T(8,128)(2,1)S(1)} %bitcast.14, ...), custom_call_target="tpu_custom_call" | custom-call | flops 10000000 | bytes 100000 | tf_op jit(solution)/shard_map/pallas_call | solution.py:412
  27.3 0.0 collective-permute-done.2.one_ref
  27.3 2.1 %collective-permute-done.3.two_ref = bf16[48,256]{1,0:T(8,128)(2,1)S(1)} collective-permute-done((bf16[48,256]{1,0:T(8,128)(2,1)S(1)}, bf16[48,256]{1,0:T(8,128)(2,1)S(1)}, u32[]{:S(2)}, u32[]{:S(2)}) %collective-permute-start.3) | collective-permute-done | bytes 24608 | tf_op jit(solution)/shard_map/ppermute | solution.py:435
  29.4 0.3 shard_map.140.q_ref
  29.7 7.3 %all-to-all-done = bf16[256,4,128]{2,1,0:T(4,128)(2,1)S(1)} async-done(((bf16[256,4,128]{2,1,0:T(4,128)(2,1)}), bf16[256,4,128]{2,1,0:T(4,128)(2,1)S(1)}, u32[]{:S(2)}, u32[]{:S(2)}) %all-to-all-start) | async-done | bytes 262176 | tf_op jit(solution)/shard_map/all_to_all | solution.py:441
  37.0 2.5 %shard_map.141 = (bf16[1024,128]{1,0:T(8,128)(2,1)}, bf16[864,128]{1,0:T(8,128)(2,1)S(1)}, f32[144,256]{1,0:T(8,128)S(1)}) custom-call(bf16[1024,128]{1,0:T(8,128)(2,1)S(1)} %bitcast.12, bf16[3,240,256]{2,1,0:T(8,128)(2,1)S(1)} %shard_map.140.q_ref, bf16[144,256]{1,0:T(8,128)(2,1)S(1)} %get-tuple-element.49.cot_ref, ...), custom_call_target="tpu_custom_call" | custom-call | flops 10000000 | bytes 100000 | tf_op jit(solution)/shard_map/pallas_call | solution.py:412
  39.5 6.2 %all-to-all-start.1 = ((bf16[256,4,128]{2,1,0:T(4,128)(2,1)}), bf16[256,4,128]{2,1,0:T(4,128)(2,1)S(1)}, u32[]{:S(2)}, u32[]{:S(2)}) async-start(bf16[256,4,128]{2,1,0:T(4,128)(2,1)} %bitcast.6), calls=%async_computation.1 | async-start | bytes 524288 | tf_op jit(solution)/shard_map/all_to_all | solution.py:441
  45.7 0.4 shard_map.142.back_ref
  46.2 15.1 %all-to-all-done.1 = bf16[256,4,128]{2,1,0:T(4,128)(2,1)S(1)} async-done(((bf16[256,4,128]{2,1,0:T(4,128)(2,1)}), bf16[256,4,128]{2,1,0:T(4,128)(2,1)S(1)}, u32[]{:S(2)}, u32[]{:S(2)}) %all-to-all-start.1) | async-done | bytes 262176 | tf_op jit(solution)/shard_map/all_to_all | solution.py:441
  61.3 0.8 shard_map.143
  62.1 6.2 %all-to-all-start.2 = ((bf16[256,4,128]{2,1,0:T(4,128)(2,1)}), bf16[256,4,128]{2,1,0:T(4,128)(2,1)S(1)}, u32[]{:S(2)}, u32[]{:S(2)}) async-start(bf16[256,4,128]{2,1,0:T(4,128)(2,1)} %bitcast.8), calls=%async_computation.2 | async-start | bytes 524288 | tf_op jit(solution)/shard_map/all_to_all | solution.py:441
  68.3 0.7 shard_map.144
  68.9 14.9 %all-to-all-done.2 = bf16[256,4,128]{2,1,0:T(4,128)(2,1)S(1)} async-done(((bf16[256,4,128]{2,1,0:T(4,128)(2,1)}), bf16[256,4,128]{2,1,0:T(4,128)(2,1)S(1)}, u32[]{:S(2)}, u32[]{:S(2)}) %all-to-all-start.2) | async-done | bytes 262176 | tf_op jit(solution)/shard_map/all_to_all | solution.py:441
  83.8 3.6 %shard_map.145 = (bf16[27,256,256]{2,1,0:T(8,128)(2,1)}, bf16[144,256]{1,0:T(8,128)(2,1)}) custom-call(bf16[1024,128]{1,0:T(8,128)(2,1)S(1)} %bitcast.13, f32[144,256]{1,0:T(8,128)S(1)} %get-tuple-element.64.outp_ref, bf16[9,192,64]{2,1,0:T(8,128)(2,1)S(1)} %shard_map.142.back_ref, bf16[64,256]{1,0:T(8,128)(2,1)S(1)} %get-tuple-element.66.utp_ref, ...), custom_call_target="tpu_custom_call" | custom-call | flops 10000000 | bytes 100000 | tf_op jit(solution)/shard_map/pallas_call | solution.py:412
  (1 shorter events, 0.0 us)
Async XLA Ops:
  2.2 19.4 %collective-permute-start = (bf16[18,256]{1,0:T(8,128)(2,1)S(1)}, bf16[18,256]{1,0:T(8,128)(2,1)S(1)}, u32[]{:S(2)}, u32[]{:S(2)}) collective-permute-start(bf16[18,256]{1,0:T(8,128)(2,1)S(1)} %get-tuple-element.43), channel_id=1, source_target_pairs={{0,1},{2,3},{4,5},{6,7},{1,0},{3,2},{5,4},{7,6},{8,9},{10,11},{12,... | collective-permute-start | bytes 27656 | tf_op jit(solution)/shard_map/ppermute | solution.py:435
  4.5 17.2 %collective-permute-start.1 = (bf16[18,256]{1,0:T(8,128)(2,1)S(1)}, bf16[18,256]{1,0:T(8,128)(2,1)S(1)}, u32[]{:S(2)}, u32[]{:S(2)}) collective-permute-start(bf16[18,256]{1,0:T(8,128)(2,1)S(1)} %get-tuple-element.44), channel_id=1, source_target_pairs={{1,2},{3,4},{5,6},{2,1},{4,3},{6,5},{9,10},{11,12},{13,14},{10,9},... | collective-permute-start | bytes 27656 | tf_op jit(solution)/shard_map/ppermute | solution.py:435
  5.1 31.9 %all-to-all-start = ((bf16[256,4,128]{2,1,0:T(4,128)(2,1)}), bf16[256,4,128]{2,1,0:T(4,128)(2,1)S(1)}, u32[]{:S(2)}, u32[]{:S(2)}) async-start(bf16[256,4,128]{2,1,0:T(4,128)(2,1)} %bitcast), calls=%async_computation | async-start | bytes 524288 | tf_op jit(solution)/shard_map/all_to_all | solution.py:441
  21.7 5.6 %collective-permute-start.2 = (bf16[48,256]{1,0:T(8,128)(2,1)S(1)}, bf16[48,256]{1,0:T(8,128)(2,1)S(1)}, u32[]{:S(2)}, u32[]{:S(2)}) collective-permute-start(bf16[48,256]{1,0:T(8,128)(2,1)S(1)} %get-tuple-element.45), channel_id=1, source_target_pairs={{0,8},{16,24},{32,40},{48,56},{64,72},{80,88},{96,104},{112,120},{... | collective-permute-start | bytes 73736 | tf_op jit(solution)/shard_map/ppermute | solution.py:435
  23.9 5.5 %collective-permute-start.3 = (bf16[48,256]{1,0:T(8,128)(2,1)S(1)}, bf16[48,256]{1,0:T(8,128)(2,1)S(1)}, u32[]{:S(2)}, u32[]{:S(2)}) collective-permute-start(bf16[48,256]{1,0:T(8,128)(2,1)S(1)} %get-tuple-element.46), channel_id=1, source_target_pairs={{8,16},{24,32},{40,48},{56,64},{72,80},{88,96},{104,112},{120,128}... | collective-permute-start | bytes 73736 | tf_op jit(solution)/shard_map/ppermute | solution.py:435
  39.5 21.7 %all-to-all-start.1 = ((bf16[256,4,128]{2,1,0:T(4,128)(2,1)}), bf16[256,4,128]{2,1,0:T(4,128)(2,1)S(1)}, u32[]{:S(2)}, u32[]{:S(2)}) async-start(bf16[256,4,128]{2,1,0:T(4,128)(2,1)} %bitcast.6), calls=%async_computation.1 | async-start | bytes 524288 | tf_op jit(solution)/shard_map/all_to_all | solution.py:441
  62.1 21.7 %all-to-all-start.2 = ((bf16[256,4,128]{2,1,0:T(4,128)(2,1)}), bf16[256,4,128]{2,1,0:T(4,128)(2,1)S(1)}, u32[]{:S(2)}, u32[]{:S(2)}) async-start(bf16[256,4,128]{2,1,0:T(4,128)(2,1)} %bitcast.8), calls=%async_computation.2 | async-start | bytes 524288 | tf_op jit(solution)/shard_map/all_to_all | solution.py:441

commit v7 on v6

--- a/solution.py
+++ b/solution.py
@@ -24,18 +24,21 @@
 TABLE = 864
 
 
-RELAYS = ((7, 0, 0), (4, 0, 0), (3, 3, 64))
-SLOTS = ((0, 24, -8), (24, 24, 8), (48, 18, -1), (66, 18, 1), (84, 3, -9), (87, 3, -7), (90, 3, 7), (93, 3, 9))
+RELAYS = ((7, 0, 0), (4, 0, 0), (3, 3, 64), (0, 3, 64), (2, 0, 16), (5, 0, 32))
+SLOTS = (
+    (0, 24, -1, 0), (24, 24, 1, 0), (48, 18, 0, -1), (66, 18, 0, 1),
+    (84, 3, -1, -1), (87, 3, -1, 1), (90, 3, 1, -1), (93, 3, 1, 1),
+)
 
 
 def ring_tables():
     take = np.zeros((216, 512), np.float32)
-    give = np.zeros((512, 240), np.float32)
-    over = np.zeros((256, 128), np.float32)
+    give = np.zeros((512, 216), np.float32)
+    kind = np.zeros((256, 128), np.float32)
     for r in range(8):
         for c in range(8):
             first = 27 * r + 27 * c // 8
-            col = 32 * r + 4 * c
+            col = 128 * (r % 2) + 32 * (r // 2) + 4 * c
             for j in range(4):
                 take[first + j, col + j] = 1
                 give[col + j, first + j] = 1
@@ -43,12 +46,10 @@
             if wrapped > 0:
                 take[first + 4, 256 + col] = 1
                 give[256 + col, first + 4] = 1
-                over[col, :wrapped] = 1
-        for k, (c, j, at) in enumerate(RELAYS):
-            col = 32 * r + 4 * c + j
-            give[256 + col, 216 + 8 * k + r] = 1
-            over[col, at : at + 64] = 1
-    return take, give, over
+                kind[col, :wrapped] = 1
+        for c, j, at in RELAYS:
+            kind[128 * (r % 2) + 32 * (r // 2) + 4 * c + j, at : at + 64] = 2
+    return take, give, kind
 
 
 def dot(a, b):
@@ -119,14 +120,15 @@
     return jnp.where(even, last, first), jnp.where(even, first, last)
 
 
-def start_kernel(core_ref, x_ref, send_ref, one_ref, two_ref, inner_ref, own, flat, low, high, sems):
-    copies = fetch(((x_ref, inner_ref), (core_ref, own)), sems)
+def start_kernel(core_ref, x_ref, send_ref, one_ref, two_ref, inner_ref, own, flat, block, low, high, sems):
+    copies = fetch(((core_ref, own), (x_ref, inner_ref)), sems)
+    copies[0].wait()
+    v = to_ring(load_flat(own, flat), ring_shift())
+    rows = jnp.concatenate([v, v, v, v], axis=0).astype(BF)
+    for k in range(8):
+        block[16 * k : 16 * k + 16, :] = rows
+    sends = fetch([(block, send_ref.at[pl.ds(128 * k, 128)]) for k in range(4)], sems.at[pl.ds(2, 4)])
     copies[1].wait()
-    v = to_ring(load_flat(own, flat), ring_shift())
-    block = jnp.concatenate([v, v, v, v], axis=0).astype(BF)
-    for k in range(64):
-        send_ref[16 * k : 16 * k + 16, :] = block
-    copies[0].wait()
     for f in range(FRAMES):
         for y in range(ROWS):
             tile = inner_ref[f, y].astype(F32)
@@ -136,6 +138,8 @@
     one, two = even_first("cols", low[...], high[...])
     one_ref[...] = one.astype(BF)
     two_ref[...] = two.astype(BF)
+    for copy in sends:
+        copy.wait()
 
 
 def rows_kernel(inner_ref, one_ref, two_ref, left_ref, right_ref, up_ref, down_ref, first, last):
@@ -164,14 +168,14 @@
 
 
 def fetch_kernel(
-    x_ref, ut_ref, ot_ref, cot_ref, core_ref, one_ref, two_ref, take_ref, give_ref, over_ref,
-    own_ref, wide_ref, utp_ref, u_ref, ring_ref, ot_out, cot_out, take_out, give_out, over_out,
+    x_ref, ut_ref, ot_ref, cot_ref, core_ref, one_ref, two_ref, take_ref, give_ref, kind_ref,
+    own_ref, wide_ref, utp_ref, u_ref, ring_ref, ot_out, cot_out, take_out, give_out, kind_out,
     ut, owns, flat, sems,
 ):
     copies = fetch(
         (
             (ut_ref, ut), (core_ref, owns[0]), (one_ref, owns[1]), (two_ref, owns[2]),
-            (take_ref, take_out), (give_ref, give_out), (over_ref, over_out), (ot_ref, ot_out), (cot_ref, cot_out),
+            (take_ref, take_out), (give_ref, give_out), (kind_ref, kind_out), (ot_ref, ot_out), (cot_ref, cot_out),
         ),
         sems,
     )
@@ -231,23 +235,27 @@
     stack_rows(tiles, q_ref)
 
 
-def gather_table(got_ref, take_ref, over_ref, table_ref):
-    over = over_ref[...] > 0
+def gather_table(got_ref, take_ref, kind_ref, table_ref):
+    kind = kind_ref[...]
     take = take_ref[...]
     for g in range(4):
-        block = got_ref[256 * g : 256 * g + 256, :]
+        block = jnp.concatenate([got_ref[512 * k + 128 * g : 512 * k + 128 * g + 128, :] for k in range(2)], axis=0)
         none = jnp.zeros_like(block)
         both = jnp.concatenate(
-            [jnp.where(over, none, block), jnp.where(over, block, none)], axis=0
+            [jnp.where(kind == 0, block, none), jnp.where(kind == 1, block, none)], axis=0
         )
         table_ref[216 * g : 216 * g + 216, :] = dot(take, both)
 
 
+def inside(lanes, at):
+    return (lanes >= at) & (lanes < at + 64)
+
+
 def forward_kernel(
-    got_ref, q_ref, cot_ref, ot_ref, take_ref, give_ref, over_ref,
-    send_ref, table_out, outp_ref, table, grads, border, pixels,
+    got_ref, q_ref, cot_ref, ot_ref, take_ref, give_ref, kind_ref,
+    send_ref, table_out, outp_ref, table, grads, border, pixels, blocks,
 ):
-    gather_table(got_ref, take_ref, over_ref, table)
+    gather_table(got_ref, take_ref, kind_ref, table)
     table_out[...] = table[...].astype(BF)
     even = jnp.zeros((CELLS, 128), F32)
     odd = jnp.zeros((CELLS, 128), F32)
@@ -281,14 +289,24 @@
             part = dot(out_t, q_ref[b, 48 * a : 48 * a + CELLS, :])
             stack = jnp.concatenate([part[:, 0:128], part[:, 128:256]], axis=0)
             grads[96 * k : 96 * k + 96, :] = stack.T[0:96, :]
-    over = over_ref[...] > 0
+    wrapped = kind_ref[...] == 1
     give = give_ref[...]
     for g in range(4):
-        source = [grads[216 * g : 216 * g + 216, :]]
-        for k in range(3):
-            source.append(pixels[32 * k + 8 * g : 32 * k + 8 * g + 8, :])
-        part = dot(give, jnp.concatenate(source, axis=0).astype(BF))
-        send_ref[256 * g : 256 * g + 256, :] = jnp.where(over, part[256:512], part[0:256]).astype(BF)
+        part = dot(give, grads[216 * g : 216 * g + 216, :].astype(BF))
+        part = jnp.where(wrapped, part[256:512], part[0:256])
+        for k in range(2):
+            blocks[512 * k + 128 * g : 512 * k + 128 * g + 128, :] = part[128 * k : 128 * k + 128]
+    lanes = lane((16, 128))
+    for a, (c, j, at) in enumerate(RELAYS):
+        for k in range(2):
+            first = 32 * (a % 3) + 16 * k
+            pixel = pixels[first : first + 16, :]
+            if at % 64:
+                pixel = pltpu.roll(pixel, at, axis=1)
+            spot = pl.ds(512 * k + 4 * c + j, 16, stride=32)
+            blocks[spot, :] = jnp.where(inside(lanes, at), pixel, blocks[spot, :])
+    for g in range(4):
+        send_ref[256 * g : 256 * g + 256, :] = blocks[256 * g : 256 * g + 256, :].astype(BF)
 
 
 def adam_kernel(got_ref, ring_ref, send_ref, next_ref, passed):
@@ -310,17 +328,24 @@
     own = jnp.where(in_ring(ring_shift()), core, 0.0)
     own = jnp.concatenate([own, own], axis=0)
     row, col = lax.axis_index("rows"), lax.axis_index("cols")
-    slot, mask = row, jnp.zeros((8, 128), jnp.bool_)
-    for k, (c, j, at) in enumerate(RELAYS):
-        slot = slot + jnp.where(col == c, 32 * k, 0)
-        spot = (sublane((8, 128)) % 4 == j) & (lane((8, 128)) // 64 == at // 64)
+    slot = 16 * lax.rem(row, 2) + lax.div(row, 2)
+    parity, mask = 0, jnp.zeros((8, 128), jnp.bool_)
+    for a, (c, j, at) in enumerate(RELAYS):
+        slot = slot + jnp.where(col == c, 32 * (a % 3), 0)
+        parity = parity + jnp.where(col == c, a // 3, 0)
+        spot = (sublane((8, 128)) % 4 == j) & inside(lane((8, 128)), at)
         mask = mask | (spot & (jnp.full((8, 128), col, jnp.int32) == c))
-    move = 0
-    for first, count, offset in SLOTS:
-        move = move + jnp.where((slot >= first) & (slot < first + count), 4 * offset, 0)
-    for k in range(64):
-        upper = passed[pl.ds(40 + 16 * k - move, 8), :]
-        lower = passed[pl.ds(48 + 16 * k - move, 8), :]
+    up, right = 0, 0
+    for first, count, rows, cols in SLOTS:
+        here = (slot >= first) & (slot < first + count)
+        up = up + jnp.where(here, rows, 0)
+        right = right + jnp.where(here, cols, 0)
+    source = lax.rem(parity - up + 2, 2)
+    chips = lax.div(source + up - parity + 2, 2) - 1
+    start = 40 + 512 * source - 4 * (8 * chips + right)
+    for k in range(32):
+        upper = passed[pl.ds(start + 16 * k, 8), :]
+        lower = passed[pl.ds(start + 16 * k + 8, 8), :]
         block = jnp.concatenate([jnp.where(mask, upper, own), jnp.where(mask, lower, own)], axis=0)
         send_ref[16 * k : 16 * k + 16, :] = block.astype(BF)
 
@@ -341,10 +366,10 @@
 
 
 def finish_kernel(
-    got_ref, outp_ref, back_ref, utp_ref, u_ref, ot_ref, take_ref, over_ref,
+    got_ref, outp_ref, back_ref, utp_ref, u_ref, ot_ref, take_ref, kind_ref,
     out_ref, grad_ref, table, half, result, got, pixels, tiles, qs, sems,
 ):
-    gather_table(got_ref, take_ref, over_ref, table)
+    gather_table(got_ref, take_ref, kind_ref, table)
     cube = table[...].astype(BF)
     even = dot(cube[:, 0:64], ot_ref[...]).astype(BF)
     odd = dot(cube[:, 64:128], ot_ref[...]).astype(BF)
@@ -364,15 +389,22 @@
 
     for g in range(4):
         got[256 * g : 256 * g + 256, :] = got_ref[256 * g : 256 * g + 256, :].astype(F32)
-    for k, (c, j, at) in enumerate(RELAYS):
-        rows = got[pl.ds(4 * c + j, 32, stride=32), :]
-        pixels[32 * k : 32 * k + 32, 0:128] = jnp.where(lane((32, 128)) // 64 == at // 64, rows, 0.0)
-    spread = (sublane((128, 256)) % 64 == lane((128, 256)) % 64).astype(BF)
-    pixels[...] = dot(pixels[:, 0:128].astype(BF), spread)
     row, col = lax.axis_index("rows"), lax.axis_index("cols")
+    lanes = lane((16, 128))
+    for q in range(3):
+        for k in range(2):
+            found = []
+            for c, j, at in (RELAYS[q], RELAYS[q + 3]):
+                pixel = got[pl.ds(512 * k + 4 * c + j, 16, stride=32), :]
+                found.append(pltpu.roll(pixel, 128 - at, axis=1) if at else pixel)
+            odd = jnp.full((16, 128), lax.rem(row, 2), jnp.int32) > 0
+            first = 32 * q + 16 * k
+            pixels[first : first + 16, 0:128] = jnp.where(odd, found[1], found[0])
+    spread = (sublane((64, 256)) == lane((64, 256)) % 64).astype(BF)
+    pixels[...] = dot(pixels[:, 0:64].astype(BF), spread)
     zero = jnp.zeros((8, 256), F32)
 
-    def inside(flag, v):
+    def kept(flag, v):
         return jnp.where(jnp.full((8, 256), flag.astype(jnp.int32), jnp.int32) > 0, v, zero)
 
     def spot(k):
@@ -388,11 +420,11 @@
                 at = 48 * f + 8 * (y - 1)
                 tile = outp_ref[at : at + 8, :]
                 left, right = spot(66 + 6 * f + y - 1), spot(48 + 6 * f + y - 1)
-            tile = shifted(tile, inside(col > 0, left), inside(col < 7, right), (64, 128), 256)
+            tile = shifted(tile, kept(col > 0, left), kept(col < 7, right), (64, 128), 256)
             if y == 0:
-                tile = inside(row > 0, tile)
+                tile = kept(row > 0, tile)
             elif y == 7:
-                tile = inside(row < 31, tile)
+                tile = kept(row < 31, tile)
             tiles[f, y] = tile
     stack_rows(tiles, qs)
     total = jnp.zeros((CELLS, 64), F32)
@@ -437,13 +469,29 @@
     return one, two
 
 
+def device(k, chip, col):
+    return 8 * (2 * chip + k) + col
+
+
+ORDER = [[device(k, chip, col) for chip in range(16) for col in range(8)] for k in range(2)]
+
+
 def exchange(x):
-    return lax.all_to_all(x, AXES, 0, 0, tiled=True)
+    return lax.all_to_all(x, AXES, 0, 0, tiled=True, axis_index_groups=[ORDER[0] + ORDER[1]])
+
+
+def exchange_half(x):
+    return lax.all_to_all(x, AXES, 0, 0, tiled=True, axis_index_groups=ORDER)
+
+
+def in_chip(x):
+    chips = [[2 * chip, 2 * chip + 1] for chip in range(16)]
+    return lax.all_gather(x, "rows", axis=0, tiled=True, axis_index_groups=chips)
 
 
 def body(frames_in, cotangent, core, moment_one, moment_two, u_in, u_out):
-    take, give, over = ring_tables()
-    take, give, over = jnp.asarray(take, BF), jnp.asarray(give, BF), jnp.asarray(over, F32)
+    take, give, kind = ring_tables()
+    take, give, kind = jnp.asarray(take, BF), jnp.asarray(give, BF), jnp.asarray(kind, F32)
     vm, dma = pltpu.VMEM, pltpu.SemaphoreType.DMA
     side = (FRAMES * ROWS, 256)
     rim = (FRAMES * 16, 256)
@@ -451,20 +499,20 @@
     send, one, two, inner = call(
         start_kernel,
         far(core, frames_in),
-        [((1024, 128), BF, False), (side, BF, False), (side, BF, False), ((FRAMES, ROWS, COLS, 256), BF, False)],
-        [vm((OWN,), F32), vm((8, 128), F32), vm(side, F32), vm(side, F32), dma((2,))],
+        [((512, 128), BF, True), (side, BF, False), (side, BF, False), ((FRAMES, ROWS, COLS, 256), BF, False)],
+        [vm((OWN,), F32), vm((8, 128), F32), vm((128, 128), BF), vm(side, F32), vm(side, F32), dma((6,))],
     )
     one, two = swap(one, two, "cols")
-    got = exchange(send)
-    own, wide, utp, u, ring, ot, cot, take, give, over = call(
+    got = in_chip(exchange_half(send))
+    own, wide, utp, u, ring, ot, cot, take, give, kind = call(
         fetch_kernel,
         near(inner.reshape(CELLS, 256)) + far(
-            u_in.T, u_out.T, cotangent.reshape(CELLS, 256), core, moment_one, moment_two, take, give, over,
+            u_in.T, u_out.T, cotangent.reshape(CELLS, 256), core, moment_one, moment_two, take, give, kind,
         ),
         [
             ((CELLS, 256), F32, False), ((256, 256), BF, False), ((64, 256), BF, False), ((256, 64), BF, False),
             ((3, 4, 128), F32, False), ((64, 256), BF, False), ((CELLS, 256), BF, False),
-            ((216, 512), BF, False), ((512, 240), BF, False), ((256, 128), F32, False),
+            ((216, 512), BF, False), ((512, 216), BF, False), ((256, 128), F32, False),
         ],
         [
             vm((64, 256), BF), [vm((OWN,), F32) for _ in range(3)], vm((8, 128), F32),
@@ -487,25 +535,25 @@
     )
     send, table, outp = call(
         forward_kernel,
-        near(got, q, cot, ot, take, give, over),
+        near(got, q, cot, ot, take, give, kind),
         [((1024, 128), BF, False), ((TABLE, 128), BF, False), ((CELLS, 256), F32, False)],
-        [vm((TABLE, 128), F32), vm((TABLE, 128), F32), vm((CELLS, 128), F32), vm((96, 128), F32)],
+        [vm((TABLE, 128), F32), vm((TABLE, 128), F32), vm((CELLS, 128), F32), vm((96, 128), F32), vm((1024, 128), F32)],
     )
     got = exchange(send)
-    (back,) = call(turn_kernel, near(table), [((9, 192, 64), BF, False)], [])
-    got, back = lax.optimization_barrier((got, back))
     send, latest = call(
         adam_kernel,
         near(got, ring),
-        [((1024, 128), BF, False), ((3, 4, 128), F32, False)],
+        [((512, 128), BF, False), ((3, 4, 128), F32, False)],
         [vm((1104, 128), F32)],
     )
-    got = exchange(send)
+    got = exchange_half(send)
+    (back,) = call(turn_kernel, near(table), [((9, 192, 64), BF, False)], [])
     core_next, one_next, two_next = call(flat_kernel, near(latest), [((OWN,), F32, False)] * 3, [])
-    got, core_next, one_next, two_next = lax.optimization_barrier((got, core_next, one_next, two_next))
+    got, back, core_next, one_next, two_next = lax.optimization_barrier((got, back, core_next, one_next, two_next))
+    got = in_chip(got)
     kernel_next, frames_grad = call(
         finish_kernel,
-        near(got, outp, back, utp, u, ot, take, over),
+        near(got, outp, back, utp, u, ot, take, kind),
         [((27, 256, 256), BF, True), ((CELLS, 256), BF, False)],
         [
             vm((TABLE, 128), F32), vm((27, 64, 256), BF), vm((27, 256, 256), BF), vm((1024, 128), F32),

time: 87.7 us -> 87.5 us (level)
  blocking collectives: 0 us -> 32.3 us
  waiting for transfers between devices: 39.4 us -> 13.6 us
  starting transfers between devices: 35.8 us -> 29.9 us
  Pallas kernels: 11.5 us -> 10.6 us
    all_to_all x3 -> x2, waiting for transfers between devices: 37.2 us -> 12.3 us  [exchange_half(): return lax.all_to_all(x, AXES, 0, 0, tiled=True, axis_index_groups=ORDER)]
    all_to_all x0 -> x1, blocking collectives: none -> 24.2 us  [exchange(): lax.all_to_all(x, AXES, 0, 0, tiled=True, axis_index_groups=[ORDER[0] + O...]
    all_gather x0 -> x2, blocking collectives: none -> 8.11 us  [in_chip(): lax.all_gather(x, 'rows', axis=0, tiled=True, axis_index_groups=chips)]
    all_to_all x3 -> x2, starting transfers between devices: 28.8 us -> 22.8 us  [exchange_half(): return lax.all_to_all(x, AXES, 0, 0, tiled=True, axis_index_groups=ORDER)]
  transfers between devices with their start and end apart: 7 -> 6, of which waited for: 4 -> 3; matrix products, arithmetic and copies ran while one was open for 0% -> 0% of each run, Pallas kernels for 3% -> 3%
where the time goes in v7:
time: 87.5 us; the launch traced here: 87.1 us
  blocking collectives  32.3 us (37%)
  starting transfers between devices  29.9 us (34%)
  waiting for transfers between devices  13.6 us (16%)
  Pallas kernels  10.6 us (12%)
    all_to_all x1, blocking collectives, exchange(): lax.all_to_all(x, AXES, 0, 0, tiled=True, axis_index_groups=[ORDER[0] + O...  24.2 us
    all_to_all x2, starting transfers between devices, exchange_half(): return lax.all_to_all(x, AXES, 0, 0, tiled=True, axis_index_groups=ORDER)  22.8 us
    all_to_all x2, waiting for transfers between devices, exchange_half(): return lax.all_to_all(x, AXES, 0, 0, tiled=True, axis_index_groups=ORDER)  12.3 us
    pallas_call x9, Pallas kernels, call(): pl.pallas_call(kernel, out_shape=[jax.ShapeDtypeStruct(shape, dtype) for...  10.6 us
    all_gather x2, blocking collectives, in_chip(): lax.all_gather(x, 'rows', axis=0, tiled=True, axis_index_groups=chips)  8.11 us
    ppermute x4, starting transfers between devices, swap(): lax.ppermute(x, axis, forward + [(b, a) for a, b in forward])  7.13 us
  transfers between devices with their start and end apart: 6, of which 3 were waited for; matrix products, arithmetic and copies ran while one was open for 0% of the time, Pallas kernels for 3%

profile of v7, /device:TPU:1, one launch (start us, length us, event | category | flops | bytes accessed | tf_op | source)
XLA Modules:
  0.0 87.1 jit_solution(8395883896484916489)
XLA Ops:
  0.6 1.5 %shard_map.137 = (bf16[512,128]{1,0:T(8,128)(2,1)}, bf16[18,256]{1,0:T(8,128)(2,1)S(1)}, bf16[18,256]{1,0:T(8,128)(2,1)S(1)}, bf16[3,6,8,256]{3,2,1,0:T(8,128)(2,1)S(1)}) custom-call(f32[432]{0:T(512)} %core_ref.3, bf16[3,6,8,256]{3,2,1,0:T(8,128)(2,1)} %x_ref.1), custom_call_target="tpu_custom_call" | custom-call | flops 10000000 | bytes 100000 | tf_op jit(solution)/shard_map/pallas_call | solution.py:444
  2.1 2.2 %collective-permute-start = (bf16[18,256]{1,0:T(8,128)(2,1)S(1)}, bf16[18,256]{1,0:T(8,128)(2,1)S(1)}, u32[]{:S(2)}, u32[]{:S(2)}) collective-permute-start(bf16[18,256]{1,0:T(8,128)(2,1)S(1)} %get-tuple-element.42), channel_id=1, source_target_pairs={{0,1},{2,3},{4,5},{6,7},{1,0},{3,2},{5,4},{7,6},{8,9},{10,11},{12,... | collective-permute-start | bytes 27656 | tf_op jit(solution)/shard_map/ppermute | solution.py:467
  4.3 0.7 collective-permute-start.1
  5.0 16.6 %all-to-all-start = ((bf16[128,4,128]{2,1,0:T(4,128)(2,1)}), bf16[128,4,128]{2,1,0:T(4,128)(2,1)S(1)}, u32[]{:S(2)}, u32[]{:S(2)}) async-start(bf16[128,4,128]{2,1,0:T(4,128)(2,1)} %bitcast), calls=%async_computation | async-start | bytes 262144 | tf_op jit(solution)/shard_map/all_to_all | solution.py:484
  21.6 0.0 collective-permute-done.one_ref
  21.6 0.0 collective-permute-done.1.two_ref
  21.7 1.6 %collective-permute-start.2 = (bf16[48,256]{1,0:T(8,128)(2,1)S(1)}, bf16[48,256]{1,0:T(8,128)(2,1)S(1)}, u32[]{:S(2)}, u32[]{:S(2)}) collective-permute-start(bf16[48,256]{1,0:T(8,128)(2,1)S(1)} %get-tuple-element.44), channel_id=1, source_target_pairs={{0,8},{16,24},{32,40},{48,56},{64,72},{80,88},{96,104},{112,120},{... | collective-permute-start | bytes 73736 | tf_op jit(solution)/shard_map/ppermute | solution.py:467
  23.3 2.7 %collective-permute-start.3 = (bf16[48,256]{1,0:T(8,128)(2,1)S(1)}, bf16[48,256]{1,0:T(8,128)(2,1)S(1)}, u32[]{:S(2)}, u32[]{:S(2)}) collective-permute-start(bf16[48,256]{1,0:T(8,128)(2,1)S(1)} %get-tuple-element.45), channel_id=1, source_target_pairs={{8,16},{24,32},{40,48},{56,64},{72,80},{88,96},{104,112},{120,128}... | collective-permute-start | bytes 73736 | tf_op jit(solution)/shard_map/ppermute | solution.py:467
  25.9 1.4 %shard_map.138 = (f32[144,256]{1,0:T(8,128)S(1)}, bf16[256,256]{1,0:T(8,128)(2,1)S(1)}, bf16[64,256]{1,0:T(8,128)(2,1)S(1)}, bf16[256,64]{1,0:T(8,128)(2,1)S(1)}...) custom-call(bf16[144,256]{1,0:T(8,128)(2,1)S(1)} %bitcast.13, ...), custom_call_target="tpu_custom_call" | custom-call | flops 10000000 | bytes 100000 | tf_op jit(solution)/shard_map/pallas_call | solution.py:444
  27.4 0.0 collective-permute-done.2.one_ref
  27.4 1.3 %collective-permute-done.3.two_ref = bf16[48,256]{1,0:T(8,128)(2,1)S(1)} collective-permute-done((bf16[48,256]{1,0:T(8,128)(2,1)S(1)}, bf16[48,256]{1,0:T(8,128)(2,1)S(1)}, u32[]{:S(2)}, u32[]{:S(2)}) %collective-permute-start.3) | collective-permute-done | bytes 24608 | tf_op jit(solution)/shard_map/ppermute | solution.py:467
  28.7 0.3 shard_map.140.q_ref
  29.0 3.0 %all-to-all-done = bf16[128,4,128]{2,1,0:T(4,128)(2,1)S(1)} async-done(((bf16[128,4,128]{2,1,0:T(4,128)(2,1)}), bf16[128,4,128]{2,1,0:T(4,128)(2,1)S(1)}, u32[]{:S(2)}, u32[]{:S(2)}) %all-to-all-start) | async-done | bytes 131104 | tf_op jit(solution)/shard_map/all_to_all | solution.py:484
  32.0 4.3 %all_gather.6.got_ref = bf16[1024,128]{1,0:T(8,128)(2,1)S(1)} all-gather(bf16[512,128]{1,0:T(8,128)(2,1)S(1)} %bitcast.14), channel_id=1, replica_groups={{0,8},{16,24},{32,40},{48,56},{64,72},{80,88},{96,104},{112,120},{128,1..., dimensions={0}, use_global_device_ids=true | all-gather | bytes 393216 | tf_op jit(solution)/shard_map/all_gather | solution.py:489
  36.3 1.9 %shard_map.141 = (bf16[1024,128]{1,0:T(8,128)(2,1)S(1)}, bf16[864,128]{1,0:T(8,128)(2,1)S(1)}, f32[144,256]{1,0:T(8,128)S(1)}) custom-call(bf16[1024,128]{1,0:T(8,128)(2,1)S(1)} %all_gather.6.got_ref, bf16[3,240,256]{2,1,0:T(8,128)(2,1)S(1)} %shard_map.140.q_ref, bf16[144,256]{1,0:T(8,128)(2,1)S(1)} %get-tuple-element.48.cot_ref, ...), custom_call_target="tpu_custom_call" | custom-call | flops 10000000 | bytes 100000 | tf_op jit(solution)/shard_map/pallas_call | solution.py:444
  38.2 24.2 %all_to_all.35 = bf16[256,4,128]{2,1,0:T(4,128)(2,1)S(1)} all-to-all(bf16[256,4,128]{2,1,0:T(4,128)(2,1)S(1)} %bitcast.12), channel_id=1, replica_groups={{0,1,2,3,4,5,6,7,16,17,18,19,20,21,22,23,32,33,34,35,36,37,38,39,48,49,..., dimensions={0} | all-to-all | bytes 524288 | tf_op jit(solution)/shard_map/all_to_all | solution.py:480
  62.4 0.7 shard_map.142
  63.2 6.2 %all-to-all-start.2 = ((bf16[128,4,128]{2,1,0:T(4,128)(2,1)}), bf16[128,4,128]{2,1,0:T(4,128)(2,1)S(1)}, u32[]{:S(2)}, u32[]{:S(2)}) async-start(bf16[128,4,128]{2,1,0:T(4,128)(2,1)} %bitcast.8), calls=%async_computation.2 | async-start | bytes 262144 | tf_op jit(solution)/shard_map/all_to_all | solution.py:484
  69.3 0.4 shard_map.143.back_ref
  69.8 0.7 shard_map.144
  70.5 9.3 %all-to-all-done.2 = bf16[128,4,128]{2,1,0:T(4,128)(2,1)S(1)} async-done(((bf16[128,4,128]{2,1,0:T(4,128)(2,1)}), bf16[128,4,128]{2,1,0:T(4,128)(2,1)S(1)}, u32[]{:S(2)}, u32[]{:S(2)}) %all-to-all-start.2) | async-done | bytes 131104 | tf_op jit(solution)/shard_map/all_to_all | solution.py:484
  79.8 3.8 %all_gather.7.got_ref = bf16[1024,128]{1,0:T(8,128)(2,1)S(1)} all-gather(bf16[512,128]{1,0:T(8,128)(2,1)S(1)} %bitcast.15), channel_id=1, replica_groups={{0,8},{16,24},{32,40},{48,56},{64,72},{80,88},{96,104},{112,120},{128,1..., dimensions={0}, use_global_device_ids=true | all-gather | bytes 393216 | tf_op jit(solution)/shard_map/all_gather | solution.py:489
  83.5 3.6 %shard_map.145 = (bf16[27,256,256]{2,1,0:T(8,128)(2,1)}, bf16[144,256]{1,0:T(8,128)(2,1)}) custom-call(bf16[1024,128]{1,0:T(8,128)(2,1)S(1)} %all_gather.7.got_ref, f32[144,256]{1,0:T(8,128)S(1)} %get-tuple-element.62.outp_ref, bf16[9,192,64]{2,1,0:T(8,128)(2,1)S(1)} %shard_map.143.back_ref, bf16[64,256]{1,0:T(8,128)(2,1)S(1)} %get-tuple-element.64.utp_ref, ...), custom_call_target="tpu_custom_call" | custom-call | flops 10000000 | bytes 100000 | tf_op jit(solution)/shard_map/pallas_call | solution.py:444
  (1 shorter events, 0.0 us)
Async XLA Ops:
  2.1 19.5 %collective-permute-start = (bf16[18,256]{1,0:T(8,128)(2,1)S(1)}, bf16[18,256]{1,0:T(8,128)(2,1)S(1)}, u32[]{:S(2)}, u32[]{:S(2)}) collective-permute-start(bf16[18,256]{1,0:T(8,128)(2,1)S(1)} %get-tuple-element.42), channel_id=1, source_target_pairs={{0,1},{2,3},{4,5},{6,7},{1,0},{3,2},{5,4},{7,6},{8,9},{10,11},{12,... | collective-permute-start | bytes 27656 | tf_op jit(solution)/shard_map/ppermute | solution.py:467
  4.3 17.3 %collective-permute-start.1 = (bf16[18,256]{1,0:T(8,128)(2,1)S(1)}, bf16[18,256]{1,0:T(8,128)(2,1)S(1)}, u32[]{:S(2)}, u32[]{:S(2)}) collective-permute-start(bf16[18,256]{1,0:T(8,128)(2,1)S(1)} %get-tuple-element.43), channel_id=1, source_target_pairs={{1,2},{3,4},{5,6},{2,1},{4,3},{6,5},{9,10},{11,12},{13,14},{10,9},... | collective-permute-start | bytes 27656 | tf_op jit(solution)/shard_map/ppermute | solution.py:467
  5.0 27.0 %all-to-all-start = ((bf16[128,4,128]{2,1,0:T(4,128)(2,1)}), bf16[128,4,128]{2,1,0:T(4,128)(2,1)S(1)}, u32[]{:S(2)}, u32[]{:S(2)}) async-start(bf16[128,4,128]{2,1,0:T(4,128)(2,1)} %bitcast), calls=%async_computation | async-start | bytes 262144 | tf_op jit(solution)/shard_map/all_to_all | solution.py:484
  21.7 5.7 %collective-permute-start.2 = (bf16[48,256]{1,0:T(8,128)(2,1)S(1)}, bf16[48,256]{1,0:T(8,128)(2,1)S(1)}, u32[]{:S(2)}, u32[]{:S(2)}) collective-permute-start(bf16[48,256]{1,0:T(8,128)(2,1)S(1)} %get-tuple-element.44), channel_id=1, source_target_pairs={{0,8},{16,24},{32,40},{48,56},{64,72},{80,88},{96,104},{112,120},{... | collective-permute-start | bytes 73736 | tf_op jit(solution)/shard_map/ppermute | solution.py:467
  23.3 5.4 %collective-permute-start.3 = (bf16[48,256]{1,0:T(8,128)(2,1)S(1)}, bf16[48,256]{1,0:T(8,128)(2,1)S(1)}, u32[]{:S(2)}, u32[]{:S(2)}) collective-permute-start(bf16[48,256]{1,0:T(8,128)(2,1)S(1)} %get-tuple-element.45), channel_id=1, source_target_pairs={{8,16},{24,32},{40,48},{56,64},{72,80},{88,96},{104,112},{120,128}... | collective-permute-start | bytes 73736 | tf_op jit(solution)/shard_map/ppermute | solution.py:467
  63.2 16.6 %all-to-all-start.2 = ((bf16[128,4,128]{2,1,0:T(4,128)(2,1)}), bf16[128,4,128]{2,1,0:T(4,128)(2,1)S(1)}, u32[]{:S(2)}, u32[]{:S(2)}) async-start(bf16[128,4,128]{2,1,0:T(4,128)(2,1)} %bitcast.8), calls=%async_computation.2 | async-start | bytes 262144 | tf_op jit(solution)/shard_map/all_to_all | solution.py:484

commit v8 on v7

--- a/solution.py
+++ b/solution.py
@@ -168,7 +168,7 @@
 
 
 def fetch_kernel(
-    x_ref, ut_ref, ot_ref, cot_ref, core_ref, one_ref, two_ref, take_ref, give_ref, kind_ref,
+    _, x_ref, ut_ref, ot_ref, cot_ref, core_ref, one_ref, two_ref, take_ref, give_ref, kind_ref,
     own_ref, wide_ref, utp_ref, u_ref, ring_ref, ot_out, cot_out, take_out, give_out, kind_out,
     ut, owns, flat, sems,
 ):
@@ -235,11 +235,17 @@
     stack_rows(tiles, q_ref)
 
 
-def gather_table(got_ref, take_ref, kind_ref, table_ref):
+def core_index(shape):
+    return jnp.full(shape, lax.rem(lax.axis_index("rows"), 2), jnp.int32)
+
+
+def gather_table(mine_ref, other_ref, take_ref, kind_ref, table_ref):
     kind = kind_ref[...]
     take = take_ref[...]
+    first = core_index((128, 128)) == 0
     for g in range(4):
-        block = jnp.concatenate([got_ref[512 * k + 128 * g : 512 * k + 128 * g + 128, :] for k in range(2)], axis=0)
+        mine, other = mine_ref[128 * g : 128 * g + 128, :], other_ref[128 * g : 128 * g + 128, :]
+        block = jnp.concatenate([jnp.where(first, mine, other), jnp.where(first, other, mine)], axis=0)
         none = jnp.zeros_like(block)
         both = jnp.concatenate(
             [jnp.where(kind == 0, block, none), jnp.where(kind == 1, block, none)], axis=0
@@ -252,10 +258,10 @@
 
 
 def forward_kernel(
-    got_ref, q_ref, cot_ref, ot_ref, take_ref, give_ref, kind_ref,
-    send_ref, table_out, outp_ref, table, grads, border, pixels, blocks,
+    mine_ref, other_ref, q_ref, cot_ref, ot_ref, take_ref, give_ref, kind_ref,
+    keep_ref, send_ref, table_out, outp_ref, table, grads, border, pixels, blocks,
 ):
-    gather_table(got_ref, take_ref, kind_ref, table)
+    gather_table(mine_ref, other_ref, take_ref, kind_ref, table)
     table_out[...] = table[...].astype(BF)
     even = jnp.zeros((CELLS, 128), F32)
     odd = jnp.zeros((CELLS, 128), F32)
@@ -300,20 +306,30 @@
     for a, (c, j, at) in enumerate(RELAYS):
         for k in range(2):
             first = 32 * (a % 3) + 16 * k
-            pixel = pixels[first : first + 16, :]
+            slot = sublane((16, 128)) + first
+            odd = core_index((16, 128)) + ((slot < 48) | (slot >= 84)).astype(jnp.int32) == 1
+            pixel = jnp.where(odd if a >= 3 else ~odd, pixels[first : first + 16, :], 0.0)
             if at % 64:
                 pixel = pltpu.roll(pixel, at, axis=1)
             spot = pl.ds(512 * k + 4 * c + j, 16, stride=32)
             blocks[spot, :] = jnp.where(inside(lanes, at), pixel, blocks[spot, :])
+    first = core_index((128, 128)) == 0
     for g in range(4):
-        send_ref[256 * g : 256 * g + 256, :] = blocks[256 * g : 256 * g + 256, :].astype(BF)
+        part = pl.ds(128 * g, 128)
+        low, high = blocks[part, :], blocks[pl.ds(512 + 128 * g, 128), :]
+        keep_ref[part, :] = jnp.where(first, low, high)
+        send_ref[part, :] = jnp.where(first, high, low).astype(BF)
+
+
+def add_kernel(keep_ref, got_ref, send_ref):
+    send_ref[...] = (keep_ref[...] + got_ref[...].astype(F32)).astype(BF)
 
 
 def adam_kernel(got_ref, ring_ref, send_ref, next_ref, passed):
     total = jnp.zeros((8, 128), F32)
     passed[0:40, :] = jnp.zeros((40, 128), F32)
-    passed[1064:1104, :] = jnp.zeros((40, 128), F32)
-    for g in range(8):
+    passed[552:592, :] = jnp.zeros((40, 128), F32)
+    for g in range(4):
         part = got_ref[128 * g : 128 * g + 128, :].astype(F32)
         passed[128 * g + 40 : 128 * g + 168, :] = part
         total = total + part.reshape(16, 8, 128).sum(axis=0)
@@ -342,7 +358,7 @@
         right = right + jnp.where(here, cols, 0)
     source = lax.rem(parity - up + 2, 2)
     chips = lax.div(source + up - parity + 2, 2) - 1
-    start = 40 + 512 * source - 4 * (8 * chips + right)
+    start = 40 - 4 * (8 * chips + right)
     for k in range(32):
         upper = passed[pl.ds(start + 16 * k, 8), :]
         lower = passed[pl.ds(start + 16 * k + 8, 8), :]
@@ -366,10 +382,10 @@
 
 
 def finish_kernel(
-    got_ref, outp_ref, back_ref, utp_ref, u_ref, ot_ref, take_ref, kind_ref,
+    mine_ref, other_ref, outp_ref, back_ref, utp_ref, u_ref, ot_ref, take_ref, kind_ref,
     out_ref, grad_ref, table, half, result, got, pixels, tiles, qs, sems,
 ):
-    gather_table(got_ref, take_ref, kind_ref, table)
+    gather_table(mine_ref, other_ref, take_ref, kind_ref, table)
     cube = table[...].astype(BF)
     even = dot(cube[:, 0:64], ot_ref[...]).astype(BF)
     odd = dot(cube[:, 64:128], ot_ref[...]).astype(BF)
@@ -387,8 +403,12 @@
             result[t] = dot(u, half[t]).astype(BF)
         store(a).start()
 
+    first = core_index((128, 128)) == 0
     for g in range(4):
-        got[256 * g : 256 * g + 256, :] = got_ref[256 * g : 256 * g + 256, :].astype(F32)
+        part = pl.ds(128 * g, 128)
+        mine, other = mine_ref[part, :], other_ref[part, :]
+        got[part, :] = jnp.where(first, mine, other).astype(F32)
+        got[pl.ds(512 + 128 * g, 128), :] = jnp.where(first, other, mine).astype(F32)
     row, col = lax.axis_index("rows"), lax.axis_index("cols")
     lanes = lane((16, 128))
     for q in range(3):
@@ -477,16 +497,11 @@
 
 
 def exchange(x):
-    return lax.all_to_all(x, AXES, 0, 0, tiled=True, axis_index_groups=[ORDER[0] + ORDER[1]])
-
-
-def exchange_half(x):
     return lax.all_to_all(x, AXES, 0, 0, tiled=True, axis_index_groups=ORDER)
 
 
 def in_chip(x):
-    chips = [[2 * chip, 2 * chip + 1] for chip in range(16)]
-    return lax.all_gather(x, "rows", axis=0, tiled=True, axis_index_groups=chips)
+    return lax.ppermute(x, "rows", [(r, r ^ 1) for r in range(32)])
 
 
 def body(frames_in, cotangent, core, moment_one, moment_two, u_in, u_out):
@@ -503,10 +518,17 @@
         [vm((OWN,), F32), vm((8, 128), F32), vm((128, 128), BF), vm(side, F32), vm(side, F32), dma((6,))],
     )
     one, two = swap(one, two, "cols")
-    got = in_chip(exchange_half(send))
+    mine = exchange(send)
+    left, right, one, two = call(
+        rows_kernel,
+        near(inner, one, two),
+        [(side, F32, False), (side, F32, False), (rim, BF, False), (rim, BF, False)],
+        [vm(rim, F32), vm(rim, F32)],
+        flops=10**10,
+    )
     own, wide, utp, u, ring, ot, cot, take, give, kind = call(
         fetch_kernel,
-        near(inner.reshape(CELLS, 256)) + far(
+        near(left, inner.reshape(CELLS, 256)) + far(
             u_in.T, u_out.T, cotangent.reshape(CELLS, 256), core, moment_one, moment_two, take, give, kind,
         ),
         [
@@ -518,42 +540,42 @@
             vm((64, 256), BF), [vm((OWN,), F32) for _ in range(3)], vm((8, 128), F32),
             dma((9,)),
         ],
-    )
-    left, right, one, two = call(
-        rows_kernel,
-        near(inner, one, two),
-        [(side, F32, False), (side, F32, False), (rim, BF, False), (rim, BF, False)],
-        [vm(rim, F32), vm(rim, F32)],
-        flops=10**10,
-    )
+        flops=10000000000,
+    )
+    mine, _ = lax.optimization_barrier((mine, ring))
+    other = in_chip(mine)
     one, two = swap(one, two, "rows")
     (q,) = call(
         rank_kernel,
         near(own, wide, one, two, left, right),
         [((3, 240, 256), BF, False)],
         [vm((FRAMES, 8, 8, 256), F32), vm((2, 18, 256), F32), vm((2, 48, 256), F32)],
-    )
-    send, table, outp = call(
+        flops=10000000000,
+    )
+    keep, send, table, outp = call(
         forward_kernel,
-        near(got, q, cot, ot, take, give, kind),
-        [((1024, 128), BF, False), ((TABLE, 128), BF, False), ((CELLS, 256), F32, False)],
+        near(mine, other, q, cot, ot, take, give, kind),
+        [
+            ((512, 128), F32, False), ((512, 128), BF, False), ((TABLE, 128), BF, False), ((CELLS, 256), F32, False),
+        ],
         [vm((TABLE, 128), F32), vm((TABLE, 128), F32), vm((CELLS, 128), F32), vm((96, 128), F32), vm((1024, 128), F32)],
     )
+    (send,) = call(add_kernel, near(keep, in_chip(send)), [((512, 128), BF, False)], [])
     got = exchange(send)
     send, latest = call(
         adam_kernel,
         near(got, ring),
         [((512, 128), BF, False), ((3, 4, 128), F32, False)],
-        [vm((1104, 128), F32)],
-    )
-    got = exchange_half(send)
+        [vm((592, 128), F32)],
+    )
+    mine = exchange(send)
     (back,) = call(turn_kernel, near(table), [((9, 192, 64), BF, False)], [])
     core_next, one_next, two_next = call(flat_kernel, near(latest), [((OWN,), F32, False)] * 3, [])
-    got, back, core_next, one_next, two_next = lax.optimization_barrier((got, back, core_next, one_next, two_next))
-    got = in_chip(got)
+    mine, back, core_next, one_next, two_next = lax.optimization_barrier((mine, back, core_next, one_next, two_next))
+    other = in_chip(mine)
     kernel_next, frames_grad = call(
         finish_kernel,
-        near(got, outp, back, utp, u, ot, take, kind),
+        near(mine, other, outp, back, utp, u, ot, take, kind),
         [((27, 256, 256), BF, True), ((CELLS, 256), BF, False)],
         [
             vm((TABLE, 128), F32), vm((27, 64, 256), BF), vm((27, 256, 256), BF), vm((1024, 128), F32),

time: 87.5 us -> 83.3 us (0.952)
  blocking collectives: 32.3 us -> 18.8 us
  starting transfers between devices: 29.9 us -> 36.3 us
  waiting for transfers between devices: 13.6 us -> 16.5 us
    all_gather x2 -> x0, blocking collectives: 8.11 us -> none  [in_chip(): lax.all_gather(x, 'rows', axis=0, tiled=True, axis_index_groups=chips)]
    ppermute x0 -> x3, starting transfers between devices: none -> 6.08 us  [in_chip(): return lax.ppermute(x, 'rows', [(r, r ^ 1) for r in range(32)])]
    all_to_all x1, blocking collectives: 24.2 us -> 18.8 us  [exchange(): return lax.all_to_all(x, AXES, 0, 0, tiled=True, axis_index_groups=ORDER)]
    ppermute x0 -> x3, waiting for transfers between devices: none -> 2.63 us  [in_chip(): return lax.ppermute(x, 'rows', [(r, r ^ 1) for r in range(32)])]
    all_to_all x2, waiting for transfers between devices: 12.3 us -> 13.9 us  [exchange(): return lax.all_to_all(x, AXES, 0, 0, tiled=True, axis_index_groups=ORDER)]
    ppermute x4, waiting for transfers between devices: 1.31 us -> 0.01 us  [swap(): lax.ppermute(x, axis, forward + [(b, a) for a, b in forward])]
    pallas_call x9 -> x10, Pallas kernels: 10.6 us -> 10.7 us  [call(): pl.pallas_call(kernel, out_shape=[jax.ShapeDtypeStruct(shape, dtype) for...]
  transfers between devices with their start and end apart: 6 -> 9, of which waited for: 3 -> 5; matrix products, arithmetic and copies ran while one was open for 0% -> 0% of each run, Pallas kernels for 3% -> 4%
where the time goes in v8:
time: 83.3 us; the launch traced here: 82.9 us
  starting transfers between devices  36.3 us (44%)
  blocking collectives  18.8 us (23%)
  waiting for transfers between devices  16.5 us (20%)
  Pallas kernels  10.7 us (13%)
    all_to_all x2, starting transfers between devices, exchange(): return lax.all_to_all(x, AXES, 0, 0, tiled=True, axis_index_groups=ORDER)  23.1 us
    all_to_all x1, blocking collectives, exchange(): return lax.all_to_all(x, AXES, 0, 0, tiled=True, axis_index_groups=ORDER)  18.8 us
    all_to_all x2, waiting for transfers between devices, exchange(): return lax.all_to_all(x, AXES, 0, 0, tiled=True, axis_index_groups=ORDER)  13.9 us
    pallas_call x10, Pallas kernels, call(): pl.pallas_call(kernel, out_shape=[jax.ShapeDtypeStruct(shape, dtype) for...  10.7 us
    ppermute x4, starting transfers between devices, swap(): lax.ppermute(x, axis, forward + [(b, a) for a, b in forward])  7.13 us
    ppermute x3, starting transfers between devices, in_chip(): return lax.ppermute(x, 'rows', [(r, r ^ 1) for r in range(32)])  6.08 us
    ppermute x3, waiting for transfers between devices, in_chip(): return lax.ppermute(x, 'rows', [(r, r ^ 1) for r in range(32)])  2.63 us
  transfers between devices with their start and end apart: 9, of which 5 were waited for; matrix products, arithmetic and copies ran while one was open for 0% of the time, Pallas kernels for 4%

profile of v8, /device:TPU:1, one launch (start us, length us, event | category | flops | bytes accessed | tf_op | source)
XLA Modules:
  0.0 82.9 jit_solution(4586632078345752197)
XLA Ops:
  0.6 1.5 %shard_map.137 = (bf16[512,128]{1,0:T(8,128)(2,1)}, bf16[18,256]{1,0:T(8,128)(2,1)S(1)}, bf16[18,256]{1,0:T(8,128)(2,1)S(1)}, bf16[3,6,8,256]{3,2,1,0:T(8,128)(2,1)S(1)}) custom-call(f32[432]{0:T(512)} %core_ref.3, bf16[3,6,8,256]{3,2,1,0:T(8,128)(2,1)} %x_ref.1), custom_call_target="tpu_custom_call" | custom-call | flops 10000000 | bytes 100000 | tf_op jit(solution)/shard_map/pallas_call | solution.py:464
  2.1 2.2 %collective-permute-start = (bf16[18,256]{1,0:T(8,128)(2,1)S(1)}, bf16[18,256]{1,0:T(8,128)(2,1)S(1)}, u32[]{:S(2)}, u32[]{:S(2)}) collective-permute-start(bf16[18,256]{1,0:T(8,128)(2,1)S(1)} %get-tuple-element.42), channel_id=1, source_target_pairs={{0,1},{2,3},{4,5},{6,7},{1,0},{3,2},{5,4},{7,6},{8,9},{10,11},{12,... | collective-permute-start | bytes 27656 | tf_op jit(solution)/shard_map/ppermute | solution.py:487
  4.3 0.7 collective-permute-start.1
  5.0 16.6 %all-to-all-start = ((bf16[128,4,128]{2,1,0:T(4,128)(2,1)}), bf16[128,4,128]{2,1,0:T(4,128)(2,1)S(1)}, u32[]{:S(2)}, u32[]{:S(2)}) async-start(bf16[128,4,128]{2,1,0:T(4,128)(2,1)} %bitcast), calls=%async_computation | async-start | bytes 262144 | tf_op jit(solution)/shard_map/all_to_all | solution.py:500
  21.6 0.0 collective-permute-done.one_ref
  21.6 0.0 collective-permute-done.1.two_ref
  21.7 1.6 %collective-permute-start.3 = (bf16[48,256]{1,0:T(8,128)(2,1)S(1)}, bf16[48,256]{1,0:T(8,128)(2,1)S(1)}, u32[]{:S(2)}, u32[]{:S(2)}) collective-permute-start(bf16[48,256]{1,0:T(8,128)(2,1)S(1)} %get-tuple-element.49), channel_id=1, source_target_pairs={{0,8},{16,24},{32,40},{48,56},{64,72},{80,88},{96,104},{112,120},{... | collective-permute-start | bytes 73736 | tf_op jit(solution)/shard_map/ppermute | solution.py:487
  23.3 2.7 %collective-permute-start.4 = (bf16[48,256]{1,0:T(8,128)(2,1)S(1)}, bf16[48,256]{1,0:T(8,128)(2,1)S(1)}, u32[]{:S(2)}, u32[]{:S(2)}) collective-permute-start(bf16[48,256]{1,0:T(8,128)(2,1)S(1)} %get-tuple-element.50), channel_id=1, source_target_pairs={{8,16},{24,32},{40,48},{56,64},{72,80},{88,96},{104,112},{120,128}... | collective-permute-start | bytes 73736 | tf_op jit(solution)/shard_map/ppermute | solution.py:487
  25.9 1.4 %shard_map.139 = (f32[144,256]{1,0:T(8,128)S(1)}, bf16[256,256]{1,0:T(8,128)(2,1)S(1)}, bf16[64,256]{1,0:T(8,128)(2,1)S(1)}, bf16[256,64]{1,0:T(8,128)(2,1)S(1)}...) custom-call(f32[18,256]{1,0:T(8,128)S(1)} %get-tuple-element.44._.le, ...), custom_call_target="tpu_custom_call" | custom-call | flops 10000000000 | bytes 100000 | tf_op jit(solution)/shard_map/pallas_call | solution.py:464
  27.4 4.6 %all-to-all-done = bf16[128,4,128]{2,1,0:T(4,128)(2,1)S(1)} async-done(((bf16[128,4,128]{2,1,0:T(4,128)(2,1)}), bf16[128,4,128]{2,1,0:T(4,128)(2,1)S(1)}, u32[]{:S(2)}, u32[]{:S(2)}) %all-to-all-start) | async-done | bytes 131104 | tf_op jit(solution)/shard_map/all_to_all | solution.py:500
  32.0 2.7 %collective-permute-start.2 = (bf16[512,128]{1,0:T(8,128)(2,1)S(1)}, bf16[512,128]{1,0:T(8,128)(2,1)S(1)}, u32[]{:S(2)}, u32[]{:S(2)}) collective-permute-start(bf16[512,128]{1,0:T(8,128)(2,1)S(1)} %bitcast.13), channel_id=1, source_target_pairs={{0,8},{8,0},{16,24},{24,16},{32,40},{40,32},{48,56},{56,48},{64,72... | collective-permute-start | bytes 393224 | tf_op jit(solution)/shard_map/ppermute | solution.py:504
  34.7 0.0 collective-permute-done.3.one_ref
  34.7 0.0 collective-permute-done.4.two_ref
  34.7 0.3 shard_map.140.q_ref
  35.0 0.7 collective-permute-done.2.other_ref
  35.7 1.9 %shard_map.141 = (f32[512,128]{1,0:T(8,128)S(1)}, bf16[512,128]{1,0:T(8,128)(2,1)S(1)}, bf16[864,128]{1,0:T(8,128)(2,1)S(1)}, f32[144,256]{1,0:T(8,128)S(1)}) custom-call(bf16[512,128]{1,0:T(8,128)(2,1)S(1)} %bitcast.14, bf16[512,128]{1,0:T(8,128)(2,1)S(1)} %collective-permute-done.2.other_ref, bf16[3,240,256]{2,1,0:T(8,128)(2,1)S(1)} %shard_map.140.q_ref, ...), custom_call_target="tpu_custom_call" | custom-call | flops 10000000 | bytes 100000 | tf_op jit(solution)/shard_map/pallas_call | solution.py:464
  37.6 0.4 collective-permute-start.5
  38.1 1.0 %collective-permute-done.5.got_ref = bf16[512,128]{1,0:T(8,128)(2,1)S(1)} collective-permute-done((bf16[512,128]{1,0:T(8,128)(2,1)S(1)}, bf16[512,128]{1,0:T(8,128)(2,1)S(1)}, u32[]{:S(2)}, u32[]{:S(2)}) %collective-permute-start.5) | collective-permute-done | bytes 131104 | tf_op jit(solution)/shard_map/ppermute | solution.py:504
  39.1 18.8 %all_to_all.35 = bf16[128,4,128]{2,1,0:T(4,128)(2,1)S(1)} all-to-all(bf16[128,4,128]{2,1,0:T(4,128)(2,1)S(1)} %bitcast.12), channel_id=1, replica_groups={{0,1,2,3,4,5,6,7,16,17,18,19,20,21,22,23,32,33,34,35,36,37,38,39,48,49,..., dimensions={0} | all-to-all | bytes 262144 | tf_op jit(solution)/shard_map/all_to_all | solution.py:500
  57.8 0.7 shard_map.143
  58.6 6.5 %all-to-all-start.2 = ((bf16[128,4,128]{2,1,0:T(4,128)(2,1)}), bf16[128,4,128]{2,1,0:T(4,128)(2,1)S(1)}, u32[]{:S(2)}, u32[]{:S(2)}) async-start(bf16[128,4,128]{2,1,0:T(4,128)(2,1)} %bitcast.8), calls=%async_computation.2 | async-start | bytes 262144 | tf_op jit(solution)/shard_map/all_to_all | solution.py:500
  65.0 0.4 shard_map.144.back_ref
  65.5 0.7 shard_map.145
  66.2 9.3 %all-to-all-done.2 = bf16[128,4,128]{2,1,0:T(4,128)(2,1)S(1)} async-done(((bf16[128,4,128]{2,1,0:T(4,128)(2,1)}), bf16[128,4,128]{2,1,0:T(4,128)(2,1)S(1)}, u32[]{:S(2)}, u32[]{:S(2)}) %all-to-all-start.2) | async-done | bytes 131104 | tf_op jit(solution)/shard_map/all_to_all | solution.py:500
  75.4 2.9 %collective-permute-start.6 = (bf16[512,128]{1,0:T(8,128)(2,1)S(1)}, bf16[512,128]{1,0:T(8,128)(2,1)S(1)}, u32[]{:S(2)}, u32[]{:S(2)}) collective-permute-start(bf16[512,128]{1,0:T(8,128)(2,1)S(1)} %bitcast.15), channel_id=1, source_target_pairs={{0,8},{8,0},{16,24},{24,16},{32,40},{40,32},{48,56},{56,48},{64,72... | collective-permute-start | bytes 393224 | tf_op jit(solution)/shard_map/ppermute | solution.py:504
  78.3 1.0 %collective-permute-done.6.other_ref = bf16[512,128]{1,0:T(8,128)(2,1)S(1)} collective-permute-done((bf16[512,128]{1,0:T(8,128)(2,1)S(1)}, bf16[512,128]{1,0:T(8,128)(2,1)S(1)}, u32[]{:S(2)}, u32[]{:S(2)}) %collective-permute-start.6) | collective-permute-done | bytes 131104 | tf_op jit(solution)/shard_map/ppermute | solution.py:504
  79.3 3.6 %shard_map.146 = (bf16[27,256,256]{2,1,0:T(8,128)(2,1)}, bf16[144,256]{1,0:T(8,128)(2,1)}) custom-call(bf16[512,128]{1,0:T(8,128)(2,1)S(1)} %bitcast.16, bf16[512,128]{1,0:T(8,128)(2,1)S(1)} %collective-permute-done.6.other_ref, f32[144,256]{1,0:T(8,128)S(1)} %get-tuple-element.66.outp_ref, bf16[9,192,64]{2,1,0:T(8,128)(2,1)S(1)} %shard_map.144.back_ref, ...), custom_call_target="tpu_custom_call" | custom-call | flops 10000000 | bytes 100000 | tf_op jit(solution)/shard_map/pallas_call | solution.py:464
  (2 shorter events, 0.1 us)
Async XLA Ops:
  2.1 19.5 %collective-permute-start = (bf16[18,256]{1,0:T(8,128)(2,1)S(1)}, bf16[18,256]{1,0:T(8,128)(2,1)S(1)}, u32[]{:S(2)}, u32[]{:S(2)}) collective-permute-start(bf16[18,256]{1,0:T(8,128)(2,1)S(1)} %get-tuple-element.42), channel_id=1, source_target_pairs={{0,1},{2,3},{4,5},{6,7},{1,0},{3,2},{5,4},{7,6},{8,9},{10,11},{12,... | collective-permute-start | bytes 27656 | tf_op jit(solution)/shard_map/ppermute | solution.py:487
  4.3 17.3 %collective-permute-start.1 = (bf16[18,256]{1,0:T(8,128)(2,1)S(1)}, bf16[18,256]{1,0:T(8,128)(2,1)S(1)}, u32[]{:S(2)}, u32[]{:S(2)}) collective-permute-start(bf16[18,256]{1,0:T(8,128)(2,1)S(1)} %get-tuple-element.43), channel_id=1, source_target_pairs={{1,2},{3,4},{5,6},{2,1},{4,3},{6,5},{9,10},{11,12},{13,14},{10,9},... | collective-permute-start | bytes 27656 | tf_op jit(solution)/shard_map/ppermute | solution.py:487
  5.0 27.0 %all-to-all-start = ((bf16[128,4,128]{2,1,0:T(4,128)(2,1)}), bf16[128,4,128]{2,1,0:T(4,128)(2,1)S(1)}, u32[]{:S(2)}, u32[]{:S(2)}) async-start(bf16[128,4,128]{2,1,0:T(4,128)(2,1)} %bitcast), calls=%async_computation | async-start | bytes 262144 | tf_op jit(solution)/shard_map/all_to_all | solution.py:500
  21.7 13.0 %collective-permute-start.3 = (bf16[48,256]{1,0:T(8,128)(2,1)S(1)}, bf16[48,256]{1,0:T(8,128)(2,1)S(1)}, u32[]{:S(2)}, u32[]{:S(2)}) collective-permute-start(bf16[48,256]{1,0:T(8,128)(2,1)S(1)} %get-tuple-element.49), channel_id=1, source_target_pairs={{0,8},{16,24},{32,40},{48,56},{64,72},{80,88},{96,104},{112,120},{... | collective-permute-start | bytes 73736 | tf_op jit(solution)/shard_map/ppermute | solution.py:487
  23.3 11.4 %collective-permute-start.4 = (bf16[48,256]{1,0:T(8,128)(2,1)S(1)}, bf16[48,256]{1,0:T(8,128)(2,1)S(1)}, u32[]{:S(2)}, u32[]{:S(2)}) collective-permute-start(bf16[48,256]{1,0:T(8,128)(2,1)S(1)} %get-tuple-element.50), channel_id=1, source_target_pairs={{8,16},{24,32},{40,48},{56,64},{72,80},{88,96},{104,112},{120,128}... | collective-permute-start | bytes 73736 | tf_op jit(solution)/shard_map/ppermute | solution.py:487
  32.0 3.7 %collective-permute-start.2 = (bf16[512,128]{1,0:T(8,128)(2,1)S(1)}, bf16[512,128]{1,0:T(8,128)(2,1)S(1)}, u32[]{:S(2)}, u32[]{:S(2)}) collective-permute-start(bf16[512,128]{1,0:T(8,128)(2,1)S(1)} %bitcast.13), channel_id=1, source_target_pairs={{0,8},{8,0},{16,24},{24,16},{32,40},{40,32},{48,56},{56,48},{64,72... | collective-permute-start | bytes 393224 | tf_op jit(solution)/shard_map/ppermute | solution.py:504
  37.6 1.4 %collective-permute-start.5 = (bf16[512,128]{1,0:T(8,128)(2,1)S(1)}, bf16[512,128]{1,0:T(8,128)(2,1)S(1)}, u32[]{:S(2)}, u32[]{:S(2)}) collective-permute-start(bf16[512,128]{1,0:T(8,128)(2,1)S(1)} %get-tuple-element.58), channel_id=1, source_target_pairs={{0,8},{8,0},{16,24},{24,16},{32,40},{40,32},{48,56},{56,48},{64,72... | collective-permute-start | bytes 393224 | tf_op jit(solution)/shard_map/ppermute | solution.py:504
  58.6 16.9 %all-to-all-start.2 = ((bf16[128,4,128]{2,1,0:T(4,128)(2,1)}), bf16[128,4,128]{2,1,0:T(4,128)(2,1)S(1)}, u32[]{:S(2)}, u32[]{:S(2)}) async-start(bf16[128,4,128]{2,1,0:T(4,128)(2,1)} %bitcast.8), calls=%async_computation.2 | async-start | bytes 262144 | tf_op jit(solution)/shard_map/all_to_all | solution.py:500
  75.4 3.9 %collective-permute-start.6 = (bf16[512,128]{1,0:T(8,128)(2,1)S(1)}, bf16[512,128]{1,0:T(8,128)(2,1)S(1)}, u32[]{:S(2)}, u32[]{:S(2)}) collective-permute-start(bf16[512,128]{1,0:T(8,128)(2,1)S(1)} %bitcast.15), channel_id=1, source_target_pairs={{0,8},{8,0},{16,24},{24,16},{32,40},{40,32},{48,56},{56,48},{64,72... | collective-permute-start | bytes 393224 | tf_op jit(solution)/shard_map/ppermute | solution.py:504

commit v9 on v8

--- a/solution.py
+++ b/solution.py
@@ -33,7 +33,7 @@
 
 def ring_tables():
     take = np.zeros((216, 512), np.float32)
-    give = np.zeros((512, 216), np.float32)
+    give = np.zeros((2, 256, 216), np.float32)
     kind = np.zeros((256, 128), np.float32)
     for r in range(8):
         for c in range(8):
@@ -41,11 +41,11 @@
             col = 128 * (r % 2) + 32 * (r // 2) + 4 * c
             for j in range(4):
                 take[first + j, col + j] = 1
-                give[col + j, first + j] = 1
+                give[r % 2, col % 128 + j, first + j] = 1
             wrapped = 48 * c % 128 + OWN - 512
             if wrapped > 0:
                 take[first + 4, 256 + col] = 1
-                give[256 + col, first + 4] = 1
+                give[r % 2, 128 + col % 128, first + 4] = 1
                 kind[col, :wrapped] = 1
         for c, j, at in RELAYS:
             kind[128 * (r % 2) + 32 * (r // 2) + 4 * c + j, at : at + 64] = 2
@@ -257,9 +257,28 @@
     return (lanes >= at) & (lanes < at + 64)
 
 
+def gradient_blocks(half, grads, pixels, give_ref, kind_ref, blocks):
+    wrapped = kind_ref[0:128, :] == 1
+    for g in range(4):
+        source = grads[216 * g : 216 * g + 216, :].astype(BF)
+        part = dot(give_ref[half], source)
+        blocks[128 * g : 128 * g + 128, :] = jnp.where(wrapped, part[128:256], part[0:128])
+    lanes = lane((16, 128))
+    row = lax.axis_index("rows")
+    for a, (c, j, at) in enumerate(RELAYS):
+        slot = sublane((16, 128)) + 16 * a
+        across = ((slot < 48) | (slot >= 84)).astype(jnp.int32)
+        goes = lax.rem(jnp.full((16, 128), row + half, jnp.int32) + across, 2) == 0
+        pixel = jnp.where(goes, pixels[16 * a : 16 * a + 16, :], 0.0)
+        if at % 64:
+            pixel = pltpu.roll(pixel, at, axis=1)
+        spot = pl.ds(4 * c + j, 16, stride=32)
+        blocks[spot, :] = jnp.where(inside(lanes, at), pixel, blocks[spot, :])
+
+
 def forward_kernel(
     mine_ref, other_ref, q_ref, cot_ref, ot_ref, take_ref, give_ref, kind_ref,
-    keep_ref, send_ref, table_out, outp_ref, table, grads, border, pixels, blocks,
+    send_ref, grads, pixels, table_out, outp_ref, table, border, blocks,
 ):
     gather_table(mine_ref, other_ref, take_ref, kind_ref, table)
     table_out[...] = table[...].astype(BF)
@@ -295,30 +314,12 @@
             part = dot(out_t, q_ref[b, 48 * a : 48 * a + CELLS, :])
             stack = jnp.concatenate([part[:, 0:128], part[:, 128:256]], axis=0)
             grads[96 * k : 96 * k + 96, :] = stack.T[0:96, :]
-    wrapped = kind_ref[...] == 1
-    give = give_ref[...]
-    for g in range(4):
-        part = dot(give, grads[216 * g : 216 * g + 216, :].astype(BF))
-        part = jnp.where(wrapped, part[256:512], part[0:256])
-        for k in range(2):
-            blocks[512 * k + 128 * g : 512 * k + 128 * g + 128, :] = part[128 * k : 128 * k + 128]
-    lanes = lane((16, 128))
-    for a, (c, j, at) in enumerate(RELAYS):
-        for k in range(2):
-            first = 32 * (a % 3) + 16 * k
-            slot = sublane((16, 128)) + first
-            odd = core_index((16, 128)) + ((slot < 48) | (slot >= 84)).astype(jnp.int32) == 1
-            pixel = jnp.where(odd if a >= 3 else ~odd, pixels[first : first + 16, :], 0.0)
-            if at % 64:
-                pixel = pltpu.roll(pixel, at, axis=1)
-            spot = pl.ds(512 * k + 4 * c + j, 16, stride=32)
-            blocks[spot, :] = jnp.where(inside(lanes, at), pixel, blocks[spot, :])
-    first = core_index((128, 128)) == 0
-    for g in range(4):
-        part = pl.ds(128 * g, 128)
-        low, high = blocks[part, :], blocks[pl.ds(512 + 128 * g, 128), :]
-        keep_ref[part, :] = jnp.where(first, low, high)
-        send_ref[part, :] = jnp.where(first, high, low).astype(BF)
+    gradient_blocks(1 - lax.rem(lax.axis_index("rows"), 2), grads, pixels, give_ref, kind_ref, blocks)
+    send_ref[...] = blocks[...].astype(BF)
+
+
+def keep_kernel(grads, pixels, give_ref, kind_ref, keep_ref):
+    gradient_blocks(lax.rem(lax.axis_index("rows"), 2), grads, pixels, give_ref, kind_ref, keep_ref)
 
 
 def add_kernel(keep_ref, got_ref, send_ref):
@@ -344,11 +345,9 @@
     own = jnp.where(in_ring(ring_shift()), core, 0.0)
     own = jnp.concatenate([own, own], axis=0)
     row, col = lax.axis_index("rows"), lax.axis_index("cols")
-    slot = 16 * lax.rem(row, 2) + lax.div(row, 2)
-    parity, mask = 0, jnp.zeros((8, 128), jnp.bool_)
+    slot, parity, mask = lax.div(row, 2), lax.rem(row, 2), jnp.zeros((8, 128), jnp.bool_)
     for a, (c, j, at) in enumerate(RELAYS):
-        slot = slot + jnp.where(col == c, 32 * (a % 3), 0)
-        parity = parity + jnp.where(col == c, a // 3, 0)
+        slot = slot + jnp.where(col == c, 16 * a, 0)
         spot = (sublane((8, 128)) % 4 == j) & inside(lane((8, 128)), at)
         mask = mask | (spot & (jnp.full((8, 128), col, jnp.int32) == c))
     up, right = 0, 0
@@ -381,45 +380,12 @@
             back_ref[k, 64 * (2 - c) : 64 * (2 - c) + 64, :] = cube.astype(BF)
 
 
-def finish_kernel(
-    mine_ref, other_ref, outp_ref, back_ref, utp_ref, u_ref, ot_ref, take_ref, kind_ref,
-    out_ref, grad_ref, table, half, result, got, pixels, tiles, qs, sems,
-):
-    gather_table(mine_ref, other_ref, take_ref, kind_ref, table)
-    cube = table[...].astype(BF)
-    even = dot(cube[:, 0:64], ot_ref[...]).astype(BF)
-    odd = dot(cube[:, 64:128], ot_ref[...]).astype(BF)
-    for t in range(27):
-        half[t, 0:32, :] = even[32 * t : 32 * t + 32]
-        half[t, 32:64, :] = odd[32 * t : 32 * t + 32]
-    u = u_ref[...]
-
-    def store(a):
-        part = pl.ds(3 * a, 3)
-        return pltpu.make_async_copy(result.at[part], out_ref.at[part], sems.at[a])
-
-    for a in range(9):
-        for t in range(3 * a, 3 * a + 3):
-            result[t] = dot(u, half[t]).astype(BF)
-        store(a).start()
-
-    first = core_index((128, 128)) == 0
-    for g in range(4):
-        part = pl.ds(128 * g, 128)
-        mine, other = mine_ref[part, :], other_ref[part, :]
-        got[part, :] = jnp.where(first, mine, other).astype(F32)
-        got[pl.ds(512 + 128 * g, 128), :] = jnp.where(first, other, mine).astype(F32)
+def backward_kernel(mine_ref, outp_ref, back_ref, utp_ref, grad_ref, got, pixels, tiles, qs):
     row, col = lax.axis_index("rows"), lax.axis_index("cols")
-    lanes = lane((16, 128))
-    for q in range(3):
-        for k in range(2):
-            found = []
-            for c, j, at in (RELAYS[q], RELAYS[q + 3]):
-                pixel = got[pl.ds(512 * k + 4 * c + j, 16, stride=32), :]
-                found.append(pltpu.roll(pixel, 128 - at, axis=1) if at else pixel)
-            odd = jnp.full((16, 128), lax.rem(row, 2), jnp.int32) > 0
-            first = 32 * q + 16 * k
-            pixels[first : first + 16, 0:128] = jnp.where(odd, found[1], found[0])
+    got[...] = mine_ref[...].astype(F32)
+    for a, (c, j, at) in enumerate(RELAYS):
+        pixel = got[pl.ds(4 * c + j, 16, stride=32), :]
+        pixels[16 * a : 16 * a + 16, 0:128] = pltpu.roll(pixel, 128 - at, axis=1) if at else pixel
     spread = (sublane((64, 256)) == lane((64, 256)) % 64).astype(BF)
     pixels[...] = dot(pixels[:, 0:64].astype(BF), spread)
     zero = jnp.zeros((8, 256), F32)
@@ -453,6 +419,25 @@
             rows = qs[2 - b, 48 * (2 - a) : 48 * (2 - a) + CELLS, :]
             total = total + dot(rows[:, 0:192], back_ref[3 * a + b])
     grad_ref[...] = dot(total.astype(BF), utp_ref[...]).astype(BF)
+
+def build_kernel(mine_ref, other_ref, u_ref, ot_ref, take_ref, kind_ref, out_ref, table, half, result, sems):
+    gather_table(mine_ref, other_ref, take_ref, kind_ref, table)
+    cube = table[...].astype(BF)
+    even = dot(cube[:, 0:64], ot_ref[...]).astype(BF)
+    odd = dot(cube[:, 64:128], ot_ref[...]).astype(BF)
+    for t in range(27):
+        half[t, 0:32, :] = even[32 * t : 32 * t + 32]
+        half[t, 32:64, :] = odd[32 * t : 32 * t + 32]
+    u = u_ref[...]
+
+    def store(a):
+        part = pl.ds(3 * a, 3)
+        return pltpu.make_async_copy(result.at[part], out_ref.at[part], sems.at[a])
+
+    for a in range(9):
+        for t in range(3 * a, 3 * a + 3):
+            result[t] = dot(u, half[t]).astype(BF)
+        store(a).start()
     for a in range(9):
         store(a).wait()
 
@@ -534,7 +519,7 @@
         [
             ((CELLS, 256), F32, False), ((256, 256), BF, False), ((64, 256), BF, False), ((256, 64), BF, False),
             ((3, 4, 128), F32, False), ((64, 256), BF, False), ((CELLS, 256), BF, False),
-            ((216, 512), BF, False), ((512, 216), BF, False), ((256, 128), F32, False),
+            ((216, 512), BF, False), ((2, 256, 216), BF, False), ((256, 128), F32, False),
         ],
         [
             vm((64, 256), BF), [vm((OWN,), F32) for _ in range(3)], vm((8, 128), F32),
@@ -552,15 +537,18 @@
         [vm((FRAMES, 8, 8, 256), F32), vm((2, 18, 256), F32), vm((2, 48, 256), F32)],
         flops=10000000000,
     )
-    keep, send, table, outp = call(
+    send, grads, pixels, table, outp = call(
         forward_kernel,
         near(mine, other, q, cot, ot, take, give, kind),
         [
-            ((512, 128), F32, False), ((512, 128), BF, False), ((TABLE, 128), BF, False), ((CELLS, 256), F32, False),
+            ((512, 128), BF, False), ((TABLE, 128), F32, False), ((96, 128), F32, False), ((TABLE, 128), BF, False),
+            ((CELLS, 256), F32, False),
         ],
-        [vm((TABLE, 128), F32), vm((TABLE, 128), F32), vm((CELLS, 128), F32), vm((96, 128), F32), vm((1024, 128), F32)],
-    )
-    (send,) = call(add_kernel, near(keep, in_chip(send)), [((512, 128), BF, False)], [])
+        [vm((TABLE, 128), F32), vm((CELLS, 128), F32), vm((512, 128), F32)],
+    )
+    got = in_chip(send)
+    (keep,) = call(keep_kernel, near(grads, pixels, give, kind), [((512, 128), F32, False)], [], flops=10**9)
+    (send,) = call(add_kernel, near(keep, got), [((512, 128), BF, False)], [])
     got = exchange(send)
     send, latest = call(
         adam_kernel,
@@ -573,14 +561,19 @@
     core_next, one_next, two_next = call(flat_kernel, near(latest), [((OWN,), F32, False)] * 3, [])
     mine, back, core_next, one_next, two_next = lax.optimization_barrier((mine, back, core_next, one_next, two_next))
     other = in_chip(mine)
-    kernel_next, frames_grad = call(
-        finish_kernel,
-        near(mine, other, outp, back, utp, u, ot, take, kind),
-        [((27, 256, 256), BF, True), ((CELLS, 256), BF, False)],
-        [
-            vm((TABLE, 128), F32), vm((27, 64, 256), BF), vm((27, 256, 256), BF), vm((1024, 128), F32),
-            vm((96, 256), F32), vm((FRAMES, 8, 8, 256), F32), vm((3, 240, 256), BF), dma((9,)),
-        ],
+    (frames_grad,) = call(
+        backward_kernel,
+        near(mine, outp, back, utp),
+        [((CELLS, 256), BF, False)],
+        [vm((512, 128), F32), vm((96, 256), F32), vm((FRAMES, 8, 8, 256), F32), vm((3, 240, 256), BF)],
+        flops=10**9,
+    )
+    other, frames_grad = lax.optimization_barrier((other, frames_grad))
+    (kernel_next,) = call(
+        build_kernel,
+        near(mine, other, u, ot, take, kind),
+        [((27, 256, 256), BF, True)],
+        [vm((TABLE, 128), F32), vm((27, 64, 256), BF), vm((27, 256, 256), BF), dma((9,))],
     )
     frames_grad = frames_grad.reshape(FRAMES, ROWS, COLS, 256)
     return frames_grad, core_next, one_next, two_next, kernel_next

time: 83.3 us -> 82.4 us (0.989)
  waiting for transfers between devices: 16.5 us -> 15.2 us
    ppermute x3, waiting for transfers between devices: 2.63 us -> 1.32 us  [in_chip(): return lax.ppermute(x, 'rows', [(r, r ^ 1) for r in range(32)])]
    pallas_call x10 -> x12, Pallas kernels: 10.7 us -> 11.1 us  [call(): pl.pallas_call(kernel, out_shape=[jax.ShapeDtypeStruct(shape, dtype) for...]
  transfers between devices with their start and end apart: 9 -> 9, of which waited for: 5 -> 4; matrix products, arithmetic and copies ran while one was open for 0% -> 0% of each run, Pallas kernels for 4% -> 6%
where the time goes in v9:
time: 82.4 us; the launch traced here: 82 us
  starting transfers between devices  36.3 us (44%)
  blocking collectives  18.7 us (23%)
  waiting for transfers between devices  15.2 us (18%)
  Pallas kernels  11.1 us (13%)
    all_to_all x2, starting transfers between devices, exchange(): return lax.all_to_all(x, AXES, 0, 0, tiled=True, axis_index_groups=ORDER)  23.1 us
    all_to_all x1, blocking collectives, exchange(): return lax.all_to_all(x, AXES, 0, 0, tiled=True, axis_index_groups=ORDER)  18.7 us
    all_to_all x2, waiting for transfers between devices, exchange(): return lax.all_to_all(x, AXES, 0, 0, tiled=True, axis_index_groups=ORDER)  13.9 us
    pallas_call x12, Pallas kernels, call(): pl.pallas_call(kernel, out_shape=[jax.ShapeDtypeStruct(shape, dtype) for...  11.1 us
    ppermute x4, starting transfers between devices, swap(): lax.ppermute(x, axis, forward + [(b, a) for a, b in forward])  7.13 us
    ppermute x3, starting transfers between devices, in_chip(): return lax.ppermute(x, 'rows', [(r, r ^ 1) for r in range(32)])  6.08 us
  transfers between devices with their start and end apart: 9, of which 4 were waited for; matrix products, arithmetic and copies ran while one was open for 0% of the time, Pallas kernels for 6%

profile of v9, /device:TPU:1, one launch (start us, length us, event | category | flops | bytes accessed | tf_op | source)
XLA Modules:
  0.0 82.0 jit_solution(13197706488196129156)
XLA Ops:
  0.6 1.5 %shard_map.137 = (bf16[512,128]{1,0:T(8,128)(2,1)}, bf16[18,256]{1,0:T(8,128)(2,1)S(1)}, bf16[18,256]{1,0:T(8,128)(2,1)S(1)}, bf16[3,6,8,256]{3,2,1,0:T(8,128)(2,1)S(1)}) custom-call(f32[432]{0:T(512)} %core_ref.3, bf16[3,6,8,256]{3,2,1,0:T(8,128)(2,1)} %x_ref.1), custom_call_target="tpu_custom_call" | custom-call | flops 10000000 | bytes 100000 | tf_op jit(solution)/shard_map/pallas_call | solution.py:449
  2.1 2.2 %collective-permute-start = (bf16[18,256]{1,0:T(8,128)(2,1)S(1)}, bf16[18,256]{1,0:T(8,128)(2,1)S(1)}, u32[]{:S(2)}, u32[]{:S(2)}) collective-permute-start(bf16[18,256]{1,0:T(8,128)(2,1)S(1)} %get-tuple-element.43), channel_id=1, source_target_pairs={{0,1},{2,3},{4,5},{6,7},{1,0},{3,2},{5,4},{7,6},{8,9},{10,11},{12,... | collective-permute-start | bytes 27656 | tf_op jit(solution)/shard_map/ppermute | solution.py:472
  4.3 0.7 collective-permute-start.1
  5.0 16.6 %all-to-all-start = ((bf16[128,4,128]{2,1,0:T(4,128)(2,1)}), bf16[128,4,128]{2,1,0:T(4,128)(2,1)S(1)}, u32[]{:S(2)}, u32[]{:S(2)}) async-start(bf16[128,4,128]{2,1,0:T(4,128)(2,1)} %bitcast), calls=%async_computation | async-start | bytes 262144 | tf_op jit(solution)/shard_map/all_to_all | solution.py:485
  21.6 0.0 collective-permute-done.one_ref
  21.6 0.0 collective-permute-done.1.two_ref
  21.7 1.6 %collective-permute-start.3 = (bf16[48,256]{1,0:T(8,128)(2,1)S(1)}, bf16[48,256]{1,0:T(8,128)(2,1)S(1)}, u32[]{:S(2)}, u32[]{:S(2)}) collective-permute-start(bf16[48,256]{1,0:T(8,128)(2,1)S(1)} %get-tuple-element.50), channel_id=1, source_target_pairs={{0,8},{16,24},{32,40},{48,56},{64,72},{80,88},{96,104},{112,120},{... | collective-permute-start | bytes 73736 | tf_op jit(solution)/shard_map/ppermute | solution.py:472
  23.3 2.7 %collective-permute-start.4 = (bf16[48,256]{1,0:T(8,128)(2,1)S(1)}, bf16[48,256]{1,0:T(8,128)(2,1)S(1)}, u32[]{:S(2)}, u32[]{:S(2)}) collective-permute-start(bf16[48,256]{1,0:T(8,128)(2,1)S(1)} %get-tuple-element.51), channel_id=1, source_target_pairs={{8,16},{24,32},{40,48},{56,64},{72,80},{88,96},{104,112},{120,128}... | collective-permute-start | bytes 73736 | tf_op jit(solution)/shard_map/ppermute | solution.py:472
  25.9 1.4 %shard_map.139 = (f32[144,256]{1,0:T(8,128)S(1)}, bf16[256,256]{1,0:T(8,128)(2,1)S(1)}, bf16[64,256]{1,0:T(8,128)(2,1)S(1)}, bf16[256,64]{1,0:T(8,128)(2,1)S(1)}...) custom-call(f32[18,256]{1,0:T(8,128)S(1)} %get-tuple-element.45._.le, ...), custom_call_target="tpu_custom_call" | custom-call | flops 10000000000 | bytes 100000 | tf_op jit(solution)/shard_map/pallas_call | solution.py:449
  27.4 4.6 %all-to-all-done = bf16[128,4,128]{2,1,0:T(4,128)(2,1)S(1)} async-done(((bf16[128,4,128]{2,1,0:T(4,128)(2,1)}), bf16[128,4,128]{2,1,0:T(4,128)(2,1)S(1)}, u32[]{:S(2)}, u32[]{:S(2)}) %all-to-all-start) | async-done | bytes 131104 | tf_op jit(solution)/shard_map/all_to_all | solution.py:485
  32.0 2.7 %collective-permute-start.2 = (bf16[512,128]{1,0:T(8,128)(2,1)S(1)}, bf16[512,128]{1,0:T(8,128)(2,1)S(1)}, u32[]{:S(2)}, u32[]{:S(2)}) collective-permute-start(bf16[512,128]{1,0:T(8,128)(2,1)S(1)} %bitcast.16), channel_id=1, source_target_pairs={{0,8},{8,0},{16,24},{24,16},{32,40},{40,32},{48,56},{56,48},{64,72... | collective-permute-start | bytes 393224 | tf_op jit(solution)/shard_map/ppermute | solution.py:489
  34.7 0.0 collective-permute-done.3.one_ref
  34.7 0.0 collective-permute-done.4.two_ref
  34.7 0.3 shard_map.140.q_ref
  35.0 0.7 collective-permute-done.2.other_ref
  35.7 1.7 %shard_map.141 = (bf16[512,128]{1,0:T(8,128)(2,1)S(1)}, f32[864,128]{1,0:T(8,128)S(1)}, f32[96,128]{1,0:T(8,128)S(1)}, bf16[864,128]{1,0:T(8,128)(2,1)S(1)}, f32[144,256]{1,0:T(8,128)S(1)}) custom-call(bf16[512,128]{1,0:T(8,128)(2,1)S(1)} %bitcast.17, bf16[512,128]{1,0:T(8,128)(2,1)S(1)} %collective-permute-done.2.other_ref, ...), custom_call_target="tpu_custom_call" | custom-call | flops 10000000 | bytes 100000 | tf_op jit(solution)/shard_map/pallas_call | solution.py:449
  37.4 0.4 collective-permute-start.5
  37.9 0.3 shard_map.142.keep_ref
  38.2 0.7 collective-permute-done.5.got_ref
  38.9 18.7 %all_to_all.35 = bf16[128,4,128]{2,1,0:T(4,128)(2,1)S(1)} all-to-all(bf16[128,4,128]{2,1,0:T(4,128)(2,1)S(1)} %bitcast.15), channel_id=1, replica_groups={{0,1,2,3,4,5,6,7,16,17,18,19,20,21,22,23,32,33,34,35,36,37,38,39,48,49,..., dimensions={0} | all-to-all | bytes 262144 | tf_op jit(solution)/shard_map/all_to_all | solution.py:485
  57.6 0.7 shard_map.144
  58.4 6.5 %all-to-all-start.2 = ((bf16[128,4,128]{2,1,0:T(4,128)(2,1)}), bf16[128,4,128]{2,1,0:T(4,128)(2,1)S(1)}, u32[]{:S(2)}, u32[]{:S(2)}) async-start(bf16[128,4,128]{2,1,0:T(4,128)(2,1)} %bitcast.8), calls=%async_computation.2 | async-start | bytes 262144 | tf_op jit(solution)/shard_map/all_to_all | solution.py:485
  64.8 0.4 shard_map.145.back_ref
  65.3 0.7 shard_map.146
  66.0 9.3 %all-to-all-done.2 = bf16[128,4,128]{2,1,0:T(4,128)(2,1)S(1)} async-done(((bf16[128,4,128]{2,1,0:T(4,128)(2,1)}), bf16[128,4,128]{2,1,0:T(4,128)(2,1)S(1)}, u32[]{:S(2)}, u32[]{:S(2)}) %all-to-all-start.2) | async-done | bytes 131104 | tf_op jit(solution)/shard_map/all_to_all | solution.py:485
  75.2 2.9 %collective-permute-start.6 = (bf16[512,128]{1,0:T(8,128)(2,1)S(1)}, bf16[512,128]{1,0:T(8,128)(2,1)S(1)}, u32[]{:S(2)}, u32[]{:S(2)}) collective-permute-start(bf16[512,128]{1,0:T(8,128)(2,1)S(1)} %bitcast.11), channel_id=1, source_target_pairs={{0,8},{8,0},{16,24},{24,16},{32,40},{40,32},{48,56},{56,48},{64,72... | collective-permute-start | bytes 393224 | tf_op jit(solution)/shard_map/ppermute | solution.py:489
  78.1 1.3 %shard_map.147 = bf16[144,256]{1,0:T(8,128)(2,1)} custom-call(bf16[512,128]{1,0:T(8,128)(2,1)S(1)} %bitcast.12, f32[144,256]{1,0:T(8,128)S(1)} %get-tuple-element.68.outp_ref, bf16[9,192,64]{2,1,0:T(8,128)(2,1)S(1)} %shard_map.145.back_ref, bf16[64,256]{1,0:T(8,128)(2,1)S(1)} %get-tuple-element.70.utp_ref), custom_call_target="tpu_custom_call" | custom-call | flops 1000000000 | bytes 100000 | tf_op jit(solution)/shard_map/pallas_call | solution.py:449
  79.4 0.0 collective-permute-done.6.other_ref
  79.4 2.6 %shard_map.148 = bf16[27,256,256]{2,1,0:T(8,128)(2,1)} custom-call(bf16[512,128]{1,0:T(8,128)(2,1)S(1)} %bitcast.13, bf16[512,128]{1,0:T(8,128)(2,1)S(1)} %collective-permute-done.6.other_ref, bf16[256,64]{1,0:T(8,128)(2,1)S(1)} %get-tuple-element.76.u_ref, bf16[64,256]{1,0:T(8,128)(2,1)S(1)} %get-tuple-element.54.ot_ref, ...), custom_call_target="tpu_custom_call" | custom-call | flops 10000000 | bytes 100000 | tf_op jit(solution)/shard_map/pallas_call | solution.py:449
  (2 shorter events, 0.1 us)
Async XLA Ops:
  2.1 19.5 %collective-permute-start = (bf16[18,256]{1,0:T(8,128)(2,1)S(1)}, bf16[18,256]{1,0:T(8,128)(2,1)S(1)}, u32[]{:S(2)}, u32[]{:S(2)}) collective-permute-start(bf16[18,256]{1,0:T(8,128)(2,1)S(1)} %get-tuple-element.43), channel_id=1, source_target_pairs={{0,1},{2,3},{4,5},{6,7},{1,0},{3,2},{5,4},{7,6},{8,9},{10,11},{12,... | collective-permute-start | bytes 27656 | tf_op jit(solution)/shard_map/ppermute | solution.py:472
  4.3 17.3 %collective-permute-start.1 = (bf16[18,256]{1,0:T(8,128)(2,1)S(1)}, bf16[18,256]{1,0:T(8,128)(2,1)S(1)}, u32[]{:S(2)}, u32[]{:S(2)}) collective-permute-start(bf16[18,256]{1,0:T(8,128)(2,1)S(1)} %get-tuple-element.44), channel_id=1, source_target_pairs={{1,2},{3,4},{5,6},{2,1},{4,3},{6,5},{9,10},{11,12},{13,14},{10,9},... | collective-permute-start | bytes 27656 | tf_op jit(solution)/shard_map/ppermute | solution.py:472
  5.0 27.0 %all-to-all-start = ((bf16[128,4,128]{2,1,0:T(4,128)(2,1)}), bf16[128,4,128]{2,1,0:T(4,128)(2,1)S(1)}, u32[]{:S(2)}, u32[]{:S(2)}) async-start(bf16[128,4,128]{2,1,0:T(4,128)(2,1)} %bitcast), calls=%async_computation | async-start | bytes 262144 | tf_op jit(solution)/shard_map/all_to_all | solution.py:485
  21.7 13.0 %collective-permute-start.3 = (bf16[48,256]{1,0:T(8,128)(2,1)S(1)}, bf16[48,256]{1,0:T(8,128)(2,1)S(1)}, u32[]{:S(2)}, u32[]{:S(2)}) collective-permute-start(bf16[48,256]{1,0:T(8,128)(2,1)S(1)} %get-tuple-element.50), channel_id=1, source_target_pairs={{0,8},{16,24},{32,40},{48,56},{64,72},{80,88},{96,104},{112,120},{... | collective-permute-start | bytes 73736 | tf_op jit(solution)/shard_map/ppermute | solution.py:472
  23.3 11.4 %collective-permute-start.4 = (bf16[48,256]{1,0:T(8,128)(2,1)S(1)}, bf16[48,256]{1,0:T(8,128)(2,1)S(1)}, u32[]{:S(2)}, u32[]{:S(2)}) collective-permute-start(bf16[48,256]{1,0:T(8,128)(2,1)S(1)} %get-tuple-element.51), channel_id=1, source_target_pairs={{8,16},{24,32},{40,48},{56,64},{72,80},{88,96},{104,112},{120,128}... | collective-permute-start | bytes 73736 | tf_op jit(solution)/shard_map/ppermute | solution.py:472
  32.0 3.7 %collective-permute-start.2 = (bf16[512,128]{1,0:T(8,128)(2,1)S(1)}, bf16[512,128]{1,0:T(8,128)(2,1)S(1)}, u32[]{:S(2)}, u32[]{:S(2)}) collective-permute-start(bf16[512,128]{1,0:T(8,128)(2,1)S(1)} %bitcast.16), channel_id=1, source_target_pairs={{0,8},{8,0},{16,24},{24,16},{32,40},{40,32},{48,56},{56,48},{64,72... | collective-permute-start | bytes 393224 | tf_op jit(solution)/shard_map/ppermute | solution.py:489
  37.4 1.4 %collective-permute-start.5 = (bf16[512,128]{1,0:T(8,128)(2,1)S(1)}, bf16[512,128]{1,0:T(8,128)(2,1)S(1)}, u32[]{:S(2)}, u32[]{:S(2)}) collective-permute-start(bf16[512,128]{1,0:T(8,128)(2,1)S(1)} %get-tuple-element.60), channel_id=1, source_target_pairs={{0,8},{8,0},{16,24},{24,16},{32,40},{40,32},{48,56},{56,48},{64,72... | collective-permute-start | bytes 393224 | tf_op jit(solution)/shard_map/ppermute | solution.py:489
  58.4 16.9 %all-to-all-start.2 = ((bf16[128,4,128]{2,1,0:T(4,128)(2,1)}), bf16[128,4,128]{2,1,0:T(4,128)(2,1)S(1)}, u32[]{:S(2)}, u32[]{:S(2)}) async-start(bf16[128,4,128]{2,1,0:T(4,128)(2,1)} %bitcast.8), calls=%async_computation.2 | async-start | bytes 262144 | tf_op jit(solution)/shard_map/all_to_all | solution.py:485
  75.2 4.2 %collective-permute-start.6 = (bf16[512,128]{1,0:T(8,128)(2,1)S(1)}, bf16[512,128]{1,0:T(8,128)(2,1)S(1)}, u32[]{:S(2)}, u32[]{:S(2)}) collective-permute-start(bf16[512,128]{1,0:T(8,128)(2,1)S(1)} %bitcast.11), channel_id=1, source_target_pairs={{0,8},{8,0},{16,24},{24,16},{32,40},{40,32},{48,56},{56,48},{64,72... | collective-permute-start | bytes 393224 | tf_op jit(solution)/shard_map/ppermute | solution.py:489

commit v10 on v9

--- a/solution.py
+++ b/solution.py
@@ -142,7 +142,7 @@
         copy.wait()
 
 
-def rows_kernel(inner_ref, one_ref, two_ref, left_ref, right_ref, up_ref, down_ref, first, last):
+def rows_kernel(inner_ref, two_ref, one_ref, left_ref, right_ref, up_ref, down_ref, first, last):
     right, left = even_first("cols", two_ref[...].astype(F32), one_ref[...].astype(F32))
     left_ref[...] = left
     right_ref[...] = right
@@ -208,7 +208,7 @@
             out_ref[b, 48 * f + 48 : 48 * f + 96, :] = rows.astype(BF)
 
 
-def rank_kernel(own_ref, wide_ref, one_ref, two_ref, left_ref, right_ref, q_ref, tiles, edge, rims):
+def rank_kernel(own_ref, wide_ref, two_ref, one_ref, left_ref, right_ref, q_ref, tiles, edge, rims):
     wide = wide_ref[...]
 
     def project(v):
@@ -506,7 +506,7 @@
     mine = exchange(send)
     left, right, one, two = call(
         rows_kernel,
-        near(inner, one, two),
+        near(inner, two, one),
         [(side, F32, False), (side, F32, False), (rim, BF, False), (rim, BF, False)],
         [vm(rim, F32), vm(rim, F32)],
         flops=10**10,
@@ -532,7 +532,7 @@
     one, two = swap(one, two, "rows")
     (q,) = call(
         rank_kernel,
-        near(own, wide, one, two, left, right),
+        near(own, wide, two, one, left, right),
         [((3, 240, 256), BF, False)],
         [vm((FRAMES, 8, 8, 256), F32), vm((2, 18, 256), F32), vm((2, 48, 256), F32)],
         flops=10000000000,

time: 82.4 us -> 83 us (level)
    ppermute x4, starting transfers between devices: 7.13 us -> 9.68 us  [swap(): lax.ppermute(x, axis, forward + [(b, a) for a, b in forward])]
    all_to_all x2, starting transfers between devices: 23.1 us -> 21.2 us  [exchange(): return lax.all_to_all(x, AXES, 0, 0, tiled=True, axis_index_groups=ORDER)]
  transfers between devices with their start and end apart: 9 -> 9, of which waited for: 4 -> 4; matrix products, arithmetic and copies ran while one was open for 0% -> 0% of each run, Pallas kernels for 6% -> 5%
where the time goes in v10:
time: 83 us; the launch traced here: 82.7 us
  starting transfers between devices  37 us (45%)
  blocking collectives  18.7 us (23%)
  waiting for transfers between devices  15.2 us (18%)
  Pallas kernels  11.1 us (13%)
    all_to_all x2, starting transfers between devices, exchange(): return lax.all_to_all(x, AXES, 0, 0, tiled=True, axis_index_groups=ORDER)  21.2 us
    all_to_all x1, blocking collectives, exchange(): return lax.all_to_all(x, AXES, 0, 0, tiled=True, axis_index_groups=ORDER)  18.7 us
    all_to_all x2, waiting for transfers between devices, exchange(): return lax.all_to_all(x, AXES, 0, 0, tiled=True, axis_index_groups=ORDER)  13.9 us
    pallas_call x12, Pallas kernels, call(): pl.pallas_call(kernel, out_shape=[jax.ShapeDtypeStruct(shape, dtype) for...  11.1 us
    ppermute x4, starting transfers between devices, swap(): lax.ppermute(x, axis, forward + [(b, a) for a, b in forward])  9.68 us
    ppermute x3, starting transfers between devices, in_chip(): return lax.ppermute(x, 'rows', [(r, r ^ 1) for r in range(32)])  6.08 us
  transfers between devices with their start and end apart: 9, of which 4 were waited for; matrix products, arithmetic and copies ran while one was open for 0% of the time, Pallas kernels for 5%

profile of v10, /device:TPU:1, one launch (start us, length us, event | category | flops | bytes accessed | tf_op | source)
XLA Modules:
  0.0 82.7 jit_solution(12110180766079133483)
XLA Ops:
  0.6 1.5 %shard_map.137 = (bf16[512,128]{1,0:T(8,128)(2,1)}, bf16[18,256]{1,0:T(8,128)(2,1)S(1)}, bf16[18,256]{1,0:T(8,128)(2,1)S(1)}, bf16[3,6,8,256]{3,2,1,0:T(8,128)(2,1)S(1)}) custom-call(f32[432]{0:T(512)} %core_ref.3, bf16[3,6,8,256]{3,2,1,0:T(8,128)(2,1)} %x_ref.1), custom_call_target="tpu_custom_call" | custom-call | flops 10000000 | bytes 100000 | tf_op jit(solution)/shard_map/pallas_call | solution.py:449
  2.1 0.7 collective-permute-start
  2.8 4.8 %collective-permute-start.1 = (bf16[18,256]{1,0:T(8,128)(2,1)S(1)}, bf16[18,256]{1,0:T(8,128)(2,1)S(1)}, u32[]{:S(2)}, u32[]{:S(2)}) collective-permute-start(bf16[18,256]{1,0:T(8,128)(2,1)S(1)} %get-tuple-element.44), channel_id=1, source_target_pairs={{0,1},{2,3},{4,5},{6,7},{1,0},{3,2},{5,4},{7,6},{8,9},{10,11},{12,... | collective-permute-start | bytes 27656 | tf_op jit(solution)/shard_map/ppermute | solution.py:472
  7.5 14.8 %all-to-all-start = ((bf16[128,4,128]{2,1,0:T(4,128)(2,1)}), bf16[128,4,128]{2,1,0:T(4,128)(2,1)S(1)}, u32[]{:S(2)}, u32[]{:S(2)}) async-start(bf16[128,4,128]{2,1,0:T(4,128)(2,1)} %bitcast), calls=%async_computation | async-start | bytes 262144 | tf_op jit(solution)/shard_map/all_to_all | solution.py:485
  22.3 0.0 collective-permute-done.two_ref
  22.3 0.0 collective-permute-done.1.one_ref
  22.4 4.2 %collective-permute-start.3 = (bf16[48,256]{1,0:T(8,128)(2,1)S(1)}, bf16[48,256]{1,0:T(8,128)(2,1)S(1)}, u32[]{:S(2)}, u32[]{:S(2)}) collective-permute-start(bf16[48,256]{1,0:T(8,128)(2,1)S(1)} %get-tuple-element.50), channel_id=1, source_target_pairs={{8,16},{24,32},{40,48},{56,64},{72,80},{88,96},{104,112},{120,128}... | collective-permute-start | bytes 73736 | tf_op jit(solution)/shard_map/ppermute | solution.py:472
  26.5 0.1 collective-permute-start.4
  26.6 1.4 %shard_map.139 = (f32[144,256]{1,0:T(8,128)S(1)}, bf16[256,256]{1,0:T(8,128)(2,1)S(1)}, bf16[64,256]{1,0:T(8,128)(2,1)S(1)}, bf16[256,64]{1,0:T(8,128)(2,1)S(1)}...) custom-call(f32[18,256]{1,0:T(8,128)S(1)} %get-tuple-element.45._.le, ...), custom_call_target="tpu_custom_call" | custom-call | flops 10000000000 | bytes 100000 | tf_op jit(solution)/shard_map/pallas_call | solution.py:449
  28.1 4.6 %all-to-all-done = bf16[128,4,128]{2,1,0:T(4,128)(2,1)S(1)} async-done(((bf16[128,4,128]{2,1,0:T(4,128)(2,1)}), bf16[128,4,128]{2,1,0:T(4,128)(2,1)S(1)}, u32[]{:S(2)}, u32[]{:S(2)}) %all-to-all-start) | async-done | bytes 131104 | tf_op jit(solution)/shard_map/all_to_all | solution.py:485
  32.7 2.7 %collective-permute-start.2 = (bf16[512,128]{1,0:T(8,128)(2,1)S(1)}, bf16[512,128]{1,0:T(8,128)(2,1)S(1)}, u32[]{:S(2)}, u32[]{:S(2)}) collective-permute-start(bf16[512,128]{1,0:T(8,128)(2,1)S(1)} %bitcast.16), channel_id=1, source_target_pairs={{0,8},{8,0},{16,24},{24,16},{32,40},{40,32},{48,56},{56,48},{64,72... | collective-permute-start | bytes 393224 | tf_op jit(solution)/shard_map/ppermute | solution.py:489
  35.4 0.0 collective-permute-done.3.two_ref
  35.4 0.0 collective-permute-done.4.one_ref
  35.4 0.3 shard_map.140.q_ref
  35.7 0.7 collective-permute-done.2.other_ref
  36.4 1.7 %shard_map.141 = (bf16[512,128]{1,0:T(8,128)(2,1)S(1)}, f32[864,128]{1,0:T(8,128)S(1)}, f32[96,128]{1,0:T(8,128)S(1)}, bf16[864,128]{1,0:T(8,128)(2,1)S(1)}, f32[144,256]{1,0:T(8,128)S(1)}) custom-call(bf16[512,128]{1,0:T(8,128)(2,1)S(1)} %bitcast.17, bf16[512,128]{1,0:T(8,128)(2,1)S(1)} %collective-permute-done.2.other_ref, ...), custom_call_target="tpu_custom_call" | custom-call | flops 10000000 | bytes 100000 | tf_op jit(solution)/shard_map/pallas_call | solution.py:449
  38.1 0.4 collective-permute-start.5
  38.6 0.3 shard_map.142.keep_ref
  38.9 0.7 collective-permute-done.5.got_ref
  39.6 18.7 %all_to_all.35 = bf16[128,4,128]{2,1,0:T(4,128)(2,1)S(1)} all-to-all(bf16[128,4,128]{2,1,0:T(4,128)(2,1)S(1)} %bitcast.15), channel_id=1, replica_groups={{0,1,2,3,4,5,6,7,16,17,18,19,20,21,22,23,32,33,34,35,36,37,38,39,48,49,..., dimensions={0} | all-to-all | bytes 262144 | tf_op jit(solution)/shard_map/all_to_all | solution.py:485
  58.3 0.7 shard_map.144
  59.0 6.5 %all-to-all-start.2 = ((bf16[128,4,128]{2,1,0:T(4,128)(2,1)}), bf16[128,4,128]{2,1,0:T(4,128)(2,1)S(1)}, u32[]{:S(2)}, u32[]{:S(2)}) async-start(bf16[128,4,128]{2,1,0:T(4,128)(2,1)} %bitcast.8), calls=%async_computation.2 | async-start | bytes 262144 | tf_op jit(solution)/shard_map/all_to_all | solution.py:485
  65.5 0.4 shard_map.145.back_ref
  65.9 0.7 shard_map.146
  66.6 9.3 %all-to-all-done.2 = bf16[128,4,128]{2,1,0:T(4,128)(2,1)S(1)} async-done(((bf16[128,4,128]{2,1,0:T(4,128)(2,1)}), bf16[128,4,128]{2,1,0:T(4,128)(2,1)S(1)}, u32[]{:S(2)}, u32[]{:S(2)}) %all-to-all-start.2) | async-done | bytes 131104 | tf_op jit(solution)/shard_map/all_to_all | solution.py:485
  75.8 2.9 %collective-permute-start.6 = (bf16[512,128]{1,0:T(8,128)(2,1)S(1)}, bf16[512,128]{1,0:T(8,128)(2,1)S(1)}, u32[]{:S(2)}, u32[]{:S(2)}) collective-permute-start(bf16[512,128]{1,0:T(8,128)(2,1)S(1)} %bitcast.11), channel_id=1, source_target_pairs={{0,8},{8,0},{16,24},{24,16},{32,40},{40,32},{48,56},{56,48},{64,72... | collective-permute-start | bytes 393224 | tf_op jit(solution)/shard_map/ppermute | solution.py:489
  78.8 1.3 %shard_map.147 = bf16[144,256]{1,0:T(8,128)(2,1)} custom-call(bf16[512,128]{1,0:T(8,128)(2,1)S(1)} %bitcast.12, f32[144,256]{1,0:T(8,128)S(1)} %get-tuple-element.68.outp_ref, bf16[9,192,64]{2,1,0:T(8,128)(2,1)S(1)} %shard_map.145.back_ref, bf16[64,256]{1,0:T(8,128)(2,1)S(1)} %get-tuple-element.70.utp_ref), custom_call_target="tpu_custom_call" | custom-call | flops 1000000000 | bytes 100000 | tf_op jit(solution)/shard_map/pallas_call | solution.py:449
  80.1 0.0 collective-permute-done.6.other_ref
  80.1 2.6 %shard_map.148 = bf16[27,256,256]{2,1,0:T(8,128)(2,1)} custom-call(bf16[512,128]{1,0:T(8,128)(2,1)S(1)} %bitcast.13, bf16[512,128]{1,0:T(8,128)(2,1)S(1)} %collective-permute-done.6.other_ref, bf16[256,64]{1,0:T(8,128)(2,1)S(1)} %get-tuple-element.76.u_ref, bf16[64,256]{1,0:T(8,128)(2,1)S(1)} %get-tuple-element.54.ot_ref, ...), custom_call_target="tpu_custom_call" | custom-call | flops 10000000 | bytes 100000 | tf_op jit(solution)/shard_map/pallas_call | solution.py:449
  (2 shorter events, 0.1 us)
Async XLA Ops:
  2.1 20.2 %collective-permute-start = (bf16[18,256]{1,0:T(8,128)(2,1)S(1)}, bf16[18,256]{1,0:T(8,128)(2,1)S(1)}, u32[]{:S(2)}, u32[]{:S(2)}) collective-permute-start(bf16[18,256]{1,0:T(8,128)(2,1)S(1)} %get-tuple-element.43), channel_id=1, source_target_pairs={{1,2},{3,4},{5,6},{2,1},{4,3},{6,5},{9,10},{11,12},{13,14},{10,9},... | collective-permute-start | bytes 27656 | tf_op jit(solution)/shard_map/ppermute | solution.py:472
  2.8 19.6 %collective-permute-start.1 = (bf16[18,256]{1,0:T(8,128)(2,1)S(1)}, bf16[18,256]{1,0:T(8,128)(2,1)S(1)}, u32[]{:S(2)}, u32[]{:S(2)}) collective-permute-start(bf16[18,256]{1,0:T(8,128)(2,1)S(1)} %get-tuple-element.44), channel_id=1, source_target_pairs={{0,1},{2,3},{4,5},{6,7},{1,0},{3,2},{5,4},{7,6},{8,9},{10,11},{12,... | collective-permute-start | bytes 27656 | tf_op jit(solution)/shard_map/ppermute | solution.py:472
  7.5 25.2 %all-to-all-start = ((bf16[128,4,128]{2,1,0:T(4,128)(2,1)}), bf16[128,4,128]{2,1,0:T(4,128)(2,1)S(1)}, u32[]{:S(2)}, u32[]{:S(2)}) async-start(bf16[128,4,128]{2,1,0:T(4,128)(2,1)} %bitcast), calls=%async_computation | async-start | bytes 262144 | tf_op jit(solution)/shard_map/all_to_all | solution.py:485
  22.4 13.0 %collective-permute-start.3 = (bf16[48,256]{1,0:T(8,128)(2,1)S(1)}, bf16[48,256]{1,0:T(8,128)(2,1)S(1)}, u32[]{:S(2)}, u32[]{:S(2)}) collective-permute-start(bf16[48,256]{1,0:T(8,128)(2,1)S(1)} %get-tuple-element.50), channel_id=1, source_target_pairs={{8,16},{24,32},{40,48},{56,64},{72,80},{88,96},{104,112},{120,128}... | collective-permute-start | bytes 73736 | tf_op jit(solution)/shard_map/ppermute | solution.py:472
  26.5 8.9 %collective-permute-start.4 = (bf16[48,256]{1,0:T(8,128)(2,1)S(1)}, bf16[48,256]{1,0:T(8,128)(2,1)S(1)}, u32[]{:S(2)}, u32[]{:S(2)}) collective-permute-start(bf16[48,256]{1,0:T(8,128)(2,1)S(1)} %get-tuple-element.51), channel_id=1, source_target_pairs={{0,8},{16,24},{32,40},{48,56},{64,72},{80,88},{96,104},{112,120},{... | collective-permute-start | bytes 73736 | tf_op jit(solution)/shard_map/ppermute | solution.py:472
  32.7 3.7 %collective-permute-start.2 = (bf16[512,128]{1,0:T(8,128)(2,1)S(1)}, bf16[512,128]{1,0:T(8,128)(2,1)S(1)}, u32[]{:S(2)}, u32[]{:S(2)}) collective-permute-start(bf16[512,128]{1,0:T(8,128)(2,1)S(1)} %bitcast.16), channel_id=1, source_target_pairs={{0,8},{8,0},{16,24},{24,16},{32,40},{40,32},{48,56},{56,48},{64,72... | collective-permute-start | bytes 393224 | tf_op jit(solution)/shard_map/ppermute | solution.py:489
  38.1 1.4 %collective-permute-start.5 = (bf16[512,128]{1,0:T(8,128)(2,1)S(1)}, bf16[512,128]{1,0:T(8,128)(2,1)S(1)}, u32[]{:S(2)}, u32[]{:S(2)}) collective-permute-start(bf16[512,128]{1,0:T(8,128)(2,1)S(1)} %get-tuple-element.60), channel_id=1, source_target_pairs={{0,8},{8,0},{16,24},{24,16},{32,40},{40,32},{48,56},{56,48},{64,72... | collective-permute-start | bytes 393224 | tf_op jit(solution)/shard_map/ppermute | solution.py:489
  59.0 16.9 %all-to-all-start.2 = ((bf16[128,4,128]{2,1,0:T(4,128)(2,1)}), bf16[128,4,128]{2,1,0:T(4,128)(2,1)S(1)}, u32[]{:S(2)}, u32[]{:S(2)}) async-start(bf16[128,4,128]{2,1,0:T(4,128)(2,1)} %bitcast.8), calls=%async_computation.2 | async-start | bytes 262144 | tf_op jit(solution)/shard_map/all_to_all | solution.py:485
  75.8 4.2 %collective-permute-start.6 = (bf16[512,128]{1,0:T(8,128)(2,1)S(1)}, bf16[512,128]{1,0:T(8,128)(2,1)S(1)}, u32[]{:S(2)}, u32[]{:S(2)}) collective-permute-start(bf16[512,128]{1,0:T(8,128)(2,1)S(1)} %bitcast.11), channel_id=1, source_target_pairs={{0,8},{8,0},{16,24},{24,16},{32,40},{40,32},{48,56},{56,48},{64,72... | collective-permute-start | bytes 393224 | tf_op jit(solution)/shard_map/ppermute | solution.py:489

commit v11 on v10

--- a/solution.py
+++ b/solution.py
@@ -120,14 +120,25 @@
     return jnp.where(even, last, first), jnp.where(even, first, last)
 
 
-def start_kernel(core_ref, x_ref, send_ref, one_ref, two_ref, inner_ref, own, flat, block, low, high, sems):
-    copies = fetch(((core_ref, own), (x_ref, inner_ref)), sems)
+def start_kernel(
+    core_ref, x_ref, one_ref, two_ref, ut_ref, ot_ref, cot_ref, take_ref, give_ref, kind_ref,
+    send_ref, near_ref, far_ref, inner_ref, ring_ref, one_out, two_out, ut_out, ot_out, cot_out, take_out, give_out, kind_out,
+    own, flat, block, low, high, sems,
+):
+    copies = fetch(
+        (
+            (core_ref, own), (x_ref, inner_ref), (one_ref, one_out), (two_ref, two_out), (ut_ref, ut_out),
+            (ot_ref, ot_out), (take_ref, take_out), (kind_ref, kind_out), (give_ref, give_out), (cot_ref, cot_out),
+        ),
+        sems,
+    )
     copies[0].wait()
     v = to_ring(load_flat(own, flat), ring_shift())
+    ring_ref[...] = v
     rows = jnp.concatenate([v, v, v, v], axis=0).astype(BF)
     for k in range(8):
         block[16 * k : 16 * k + 16, :] = rows
-    sends = fetch([(block, send_ref.at[pl.ds(128 * k, 128)]) for k in range(4)], sems.at[pl.ds(2, 4)])
+    sends = fetch([(block, send_ref.at[pl.ds(128 * k, 128)]) for k in range(4)], sems.at[pl.ds(10, 4)])
     copies[1].wait()
     for f in range(FRAMES):
         for y in range(ROWS):
@@ -136,9 +147,9 @@
             low[k : k + 1, :] = tile[0:1, :]
             high[k : k + 1, :] = tile[7:8, :]
     one, two = even_first("cols", low[...], high[...])
-    one_ref[...] = one.astype(BF)
-    two_ref[...] = two.astype(BF)
-    for copy in sends:
+    near_ref[...] = one.astype(BF)
+    far_ref[...] = two.astype(BF)
+    for copy in copies[2:] + sends:
         copy.wait()
 
 
@@ -167,36 +178,21 @@
     return jnp.where(at < bounds[0], back, jnp.where(at < bounds[1], tile, ahead))
 
 
-def fetch_kernel(
-    _, x_ref, ut_ref, ot_ref, cot_ref, core_ref, one_ref, two_ref, take_ref, give_ref, kind_ref,
-    own_ref, wide_ref, utp_ref, u_ref, ring_ref, ot_out, cot_out, take_out, give_out, kind_out,
-    ut, owns, flat, sems,
-):
-    copies = fetch(
-        (
-            (ut_ref, ut), (core_ref, owns[0]), (one_ref, owns[1]), (two_ref, owns[2]),
-            (take_ref, take_out), (give_ref, give_out), (kind_ref, kind_out), (ot_ref, ot_out), (cot_ref, cot_out),
-        ),
-        sems,
-    )
+def prepare_kernel(_, x_ref, ut_ref, one_ref, two_ref, own_ref, wide_ref, utp_ref, u_ref, ring_ref, flat):
     row = sublane((256, 64))
     at = row % 128
     pick = (lane((256, 64)) == (at % 32) * 2 + row // 128) & (at < 96)
     half_row = sublane((64, 64))
     half_pick = lane((64, 64)) == (half_row % 32) * 2 + half_row // 32
-    copies[0].wait()
-    wide = dot(pick.astype(BF), ut[...]).astype(BF)
+    wide = dot(pick.astype(BF), ut_ref[...]).astype(BF)
     wide_ref[...] = wide
-    utp = dot(half_pick.astype(BF), ut[...])
+    utp = dot(half_pick.astype(BF), ut_ref[...])
     utp_ref[...] = utp.astype(BF)
     u_ref[...] = utp.T.astype(BF)
     own_ref[...] = dot_nt(x_ref[...], wide).astype(BF).astype(F32)
     shift = ring_shift()
-    for k in range(3):
-        copies[1 + k].wait()
-        ring_ref[k] = to_ring(load_flat(owns[k], flat), shift)
-    for k in range(4, 9):
-        copies[k].wait()
+    ring_ref[0] = to_ring(load_flat(one_ref, flat), shift)
+    ring_ref[1] = to_ring(load_flat(two_ref, flat), shift)
 
 
 def stack_rows(tiles, out_ref):
@@ -208,7 +204,7 @@
             out_ref[b, 48 * f + 48 : 48 * f + 96, :] = rows.astype(BF)
 
 
-def rank_kernel(own_ref, wide_ref, two_ref, one_ref, left_ref, right_ref, q_ref, tiles, edge, rims):
+def rank_kernel(_, own_ref, wide_ref, two_ref, one_ref, left_ref, right_ref, q_ref, tiles, edge, rims):
     wide = wide_ref[...]
 
     def project(v):
@@ -276,18 +272,20 @@
         blocks[spot, :] = jnp.where(inside(lanes, at), pixel, blocks[spot, :])
 
 
-def forward_kernel(
-    mine_ref, other_ref, q_ref, cot_ref, ot_ref, take_ref, give_ref, kind_ref,
-    send_ref, grads, pixels, table_out, outp_ref, table, border, blocks,
-):
+def table_kernel(mine_ref, other_ref, take_ref, kind_ref, table_out, table):
     gather_table(mine_ref, other_ref, take_ref, kind_ref, table)
     table_out[...] = table[...].astype(BF)
+
+
+def forward_kernel(
+    table_ref, q_ref, cot_ref, ot_ref, give_ref, kind_ref, send_ref, grads, pixels, outp_ref, border, blocks
+):
     even = jnp.zeros((CELLS, 128), F32)
     odd = jnp.zeros((CELLS, 128), F32)
     for a in range(3):
         for b in range(3):
             k = 3 * a + b
-            weights = table_out[96 * k : 96 * k + 96, :]
+            weights = table_ref[96 * k : 96 * k + 96, :]
             rows = q_ref[b, 48 * a : 48 * a + CELLS, :]
             even = even + dot(rows[:, 0:96], weights)
             odd = odd + dot(rows[:, 128:224], weights)
@@ -326,7 +324,7 @@
     send_ref[...] = (keep_ref[...] + got_ref[...].astype(F32)).astype(BF)
 
 
-def adam_kernel(got_ref, ring_ref, send_ref, next_ref, passed):
+def adam_kernel(got_ref, core_ref, ring_ref, send_ref, next_ref, passed):
     total = jnp.zeros((8, 128), F32)
     passed[0:40, :] = jnp.zeros((40, 128), F32)
     passed[552:592, :] = jnp.zeros((40, 128), F32)
@@ -335,7 +333,7 @@
         passed[128 * g + 40 : 128 * g + 168, :] = part
         total = total + part.reshape(16, 8, 128).sum(axis=0)
     grad = (total[0:4] + total[4:8]) * (1.0 / 192.0)
-    core, one, two = ring_ref[0], ring_ref[1], ring_ref[2]
+    core, one, two = core_ref[...], ring_ref[0], ring_ref[1]
     one = beta_one * one + (1.0 - beta_one) * grad
     two = beta_two * two + (1.0 - beta_two) * grad * grad
     core = core - learn_rate * (one / fix_one) / (jnp.sqrt(two / fix_two) + epsilon)
@@ -496,11 +494,18 @@
     side = (FRAMES * ROWS, 256)
     rim = (FRAMES * 16, 256)
 
-    send, one, two, inner = call(
+    send, one, two, inner, core_ring, m_one, m_two, ut, ot, cot, take, give, kind = call(
         start_kernel,
-        far(core, frames_in),
-        [((512, 128), BF, True), (side, BF, False), (side, BF, False), ((FRAMES, ROWS, COLS, 256), BF, False)],
-        [vm((OWN,), F32), vm((8, 128), F32), vm((128, 128), BF), vm(side, F32), vm(side, F32), dma((6,))],
+        far(
+            core, frames_in, moment_one, moment_two, u_in.T, u_out.T, cotangent.reshape(CELLS, 256), take, give, kind,
+        ),
+        [
+            ((512, 128), BF, True), (side, BF, False), (side, BF, False), ((FRAMES, ROWS, COLS, 256), BF, False),
+            ((4, 128), F32, False), ((OWN,), F32, False), ((OWN,), F32, False), ((64, 256), BF, False),
+            ((64, 256), BF, False), ((CELLS, 256), BF, False), ((216, 512), BF, False), ((2, 256, 216), BF, False),
+            ((256, 128), F32, False),
+        ],
+        [vm((OWN,), F32), vm((8, 128), F32), vm((128, 128), BF), vm(side, F32), vm(side, F32), dma((14,))],
     )
     one, two = swap(one, two, "cols")
     mine = exchange(send)
@@ -511,40 +516,38 @@
         [vm(rim, F32), vm(rim, F32)],
         flops=10**10,
     )
-    own, wide, utp, u, ring, ot, cot, take, give, kind = call(
-        fetch_kernel,
-        near(left, inner.reshape(CELLS, 256)) + far(
-            u_in.T, u_out.T, cotangent.reshape(CELLS, 256), core, moment_one, moment_two, take, give, kind,
-        ),
+    own, wide, utp, u, ring = call(
+        prepare_kernel,
+        near(left, inner.reshape(CELLS, 256), ut, m_one, m_two),
         [
             ((CELLS, 256), F32, False), ((256, 256), BF, False), ((64, 256), BF, False), ((256, 64), BF, False),
-            ((3, 4, 128), F32, False), ((64, 256), BF, False), ((CELLS, 256), BF, False),
-            ((216, 512), BF, False), ((2, 256, 216), BF, False), ((256, 128), F32, False),
+            ((2, 4, 128), F32, False),
         ],
-        [
-            vm((64, 256), BF), [vm((OWN,), F32) for _ in range(3)], vm((8, 128), F32),
-            dma((9,)),
-        ],
+        [vm((8, 128), F32)],
+        flops=10**10,
+    )
+    mine, _ = lax.optimization_barrier((mine, left))
+    other = in_chip(mine)
+    (table,) = call(
+        table_kernel,
+        near(mine, other, take, kind),
+        [((TABLE, 128), BF, False)],
+        [vm((TABLE, 128), F32)],
         flops=10000000000,
     )
-    mine, _ = lax.optimization_barrier((mine, ring))
-    other = in_chip(mine)
     one, two = swap(one, two, "rows")
     (q,) = call(
         rank_kernel,
-        near(own, wide, two, one, left, right),
+        near(table, own, wide, two, one, left, right),
         [((3, 240, 256), BF, False)],
         [vm((FRAMES, 8, 8, 256), F32), vm((2, 18, 256), F32), vm((2, 48, 256), F32)],
-        flops=10000000000,
-    )
-    send, grads, pixels, table, outp = call(
+        flops=10000000,
+    )
+    send, grads, pixels, outp = call(
         forward_kernel,
-        near(mine, other, q, cot, ot, take, give, kind),
-        [
-            ((512, 128), BF, False), ((TABLE, 128), F32, False), ((96, 128), F32, False), ((TABLE, 128), BF, False),
-            ((CELLS, 256), F32, False),
-        ],
-        [vm((TABLE, 128), F32), vm((CELLS, 128), F32), vm((512, 128), F32)],
+        near(table, q, cot, ot, give, kind),
+        [((512, 128), BF, False), ((TABLE, 128), F32, False), ((96, 128), F32, False), ((CELLS, 256), F32, False)],
+        [vm((CELLS, 128), F32), vm((512, 128), F32)],
     )
     got = in_chip(send)
     (keep,) = call(keep_kernel, near(grads, pixels, give, kind), [((512, 128), F32, False)], [], flops=10**9)
@@ -552,7 +555,7 @@
     got = exchange(send)
     send, latest = call(
         adam_kernel,
-        near(got, ring),
+        near(got, core_ring, ring),
         [((512, 128), BF, False), ((3, 4, 128), F32, False)],
         [vm((592, 128), F32)],
     )

time: 83 us -> 82.8 us (level)
  waiting for transfers between devices: 15.2 us -> 16.6 us
  Pallas kernels: 11.1 us -> 10.2 us
    all_to_all x2, waiting for transfers between devices: 13.9 us -> 15.3 us  [exchange(): return lax.all_to_all(x, AXES, 0, 0, tiled=True, axis_index_groups=ORDER)]
    pallas_call x12 -> x13, Pallas kernels: 11.1 us -> 10.2 us  [call(): pl.pallas_call(kernel, out_shape=[jax.ShapeDtypeStruct(shape, dtype) for...]
  transfers between devices with their start and end apart: 9 -> 9, of which waited for: 4 -> 4; matrix products, arithmetic and copies ran while one was open for 0% -> 0% of each run, Pallas kernels for 5% -> 4%
where the time goes in v11:
time: 82.8 us; the launch traced here: 82.5 us
  starting transfers between devices  37 us (45%)
  blocking collectives  17.9 us (22%)
  waiting for transfers between devices  16.6 us (20%)
  Pallas kernels  10.2 us (12%)
    all_to_all x2, starting transfers between devices, exchange(): return lax.all_to_all(x, AXES, 0, 0, tiled=True, axis_index_groups=ORDER)  21.2 us
    all_to_all x1, blocking collectives, exchange(): return lax.all_to_all(x, AXES, 0, 0, tiled=True, axis_index_groups=ORDER)  17.9 us
    all_to_all x2, waiting for transfers between devices, exchange(): return lax.all_to_all(x, AXES, 0, 0, tiled=True, axis_index_groups=ORDER)  15.3 us
    pallas_call x13, Pallas kernels, call(): pl.pallas_call(kernel, out_shape=[jax.ShapeDtypeStruct(shape, dtype) for...  10.2 us
    ppermute x4, starting transfers between devices, swap(): lax.ppermute(x, axis, forward + [(b, a) for a, b in forward])  9.68 us
    ppermute x3, starting transfers between devices, in_chip(): return lax.ppermute(x, 'rows', [(r, r ^ 1) for r in range(32)])  6.08 us
  transfers between devices with their start and end apart: 9, of which 4 were waited for; matrix products, arithmetic and copies ran while one was open for 0% of the time, Pallas kernels for 4%

profile of v11, /device:TPU:1, one launch (start us, length us, event | category | flops | bytes accessed | tf_op | source)
XLA Modules:
  0.0 82.5 jit_solution(17596398848922826406)
XLA Ops:
  0.6 1.5 %shard_map.137 = (bf16[512,128]{1,0:T(8,128)(2,1)}, bf16[18,256]{1,0:T(8,128)(2,1)S(1)}, bf16[18,256]{1,0:T(8,128)(2,1)S(1)}, bf16[3,6,8,256]{3,2,1,0:T(8,128)(2...) custom-call(f32[432]{0:T(512)} %core_ref.1, ...), custom_call_target="tpu_custom_call" | custom-call | flops 10000000 | bytes 100000 | tf_op jit(solution)/shard_map/pallas_call | solution.py:447
  2.2 0.7 collective-permute-start
  2.9 4.8 %collective-permute-start.1 = (bf16[18,256]{1,0:T(8,128)(2,1)S(1)}, bf16[18,256]{1,0:T(8,128)(2,1)S(1)}, u32[]{:S(2)}, u32[]{:S(2)}) collective-permute-start(bf16[18,256]{1,0:T(8,128)(2,1)S(1)} %get-tuple-element.47), channel_id=1, source_target_pairs={{0,1},{2,3},{4,5},{6,7},{1,0},{3,2},{5,4},{7,6},{8,9},{10,11},{12,... | collective-permute-start | bytes 27656 | tf_op jit(solution)/shard_map/ppermute | solution.py:470
  7.6 14.8 %all-to-all-start = ((bf16[128,4,128]{2,1,0:T(4,128)(2,1)}), bf16[128,4,128]{2,1,0:T(4,128)(2,1)S(1)}, u32[]{:S(2)}, u32[]{:S(2)}) async-start(bf16[128,4,128]{2,1,0:T(4,128)(2,1)} %bitcast.3), calls=%async_computation | async-start | bytes 262144 | tf_op jit(solution)/shard_map/all_to_all | solution.py:483
  22.4 0.0 collective-permute-done.two_ref
  22.4 0.0 collective-permute-done.1.one_ref
  22.5 4.2 %collective-permute-start.3 = (bf16[48,256]{1,0:T(8,128)(2,1)S(1)}, bf16[48,256]{1,0:T(8,128)(2,1)S(1)}, u32[]{:S(2)}, u32[]{:S(2)}) collective-permute-start(bf16[48,256]{1,0:T(8,128)(2,1)S(1)} %get-tuple-element.57), channel_id=1, source_target_pairs={{8,16},{24,32},{40,48},{56,64},{72,80},{88,96},{104,112},{120,128}... | collective-permute-start | bytes 73736 | tf_op jit(solution)/shard_map/ppermute | solution.py:470
  26.6 0.1 collective-permute-start.4
  26.7 6.0 %all-to-all-done = bf16[128,4,128]{2,1,0:T(4,128)(2,1)S(1)} async-done(((bf16[128,4,128]{2,1,0:T(4,128)(2,1)}), bf16[128,4,128]{2,1,0:T(4,128)(2,1)S(1)}, u32[]{:S(2)}, u32[]{:S(2)}) %all-to-all-start) | async-done | bytes 131104 | tf_op jit(solution)/shard_map/all_to_all | solution.py:483
  32.8 2.7 %collective-permute-start.2 = (bf16[512,128]{1,0:T(8,128)(2,1)S(1)}, bf16[512,128]{1,0:T(8,128)(2,1)S(1)}, u32[]{:S(2)}, u32[]{:S(2)}) collective-permute-start(bf16[512,128]{1,0:T(8,128)(2,1)S(1)} %bitcast.16), channel_id=1, source_target_pairs={{0,8},{8,0},{16,24},{24,16},{32,40},{40,32},{48,56},{56,48},{64,72... | collective-permute-start | bytes 393224 | tf_op jit(solution)/shard_map/ppermute | solution.py:487
  35.5 0.3 shard_map.140
  35.8 0.6 collective-permute-done.2.other_ref
  36.5 0.4 shard_map.139._.table_ref
  36.9 0.0 collective-permute-done.3.two_ref
  36.9 0.0 collective-permute-done.4.one_ref
  36.9 0.3 shard_map.141.q_ref
  37.2 1.5 %shard_map.142 = (bf16[512,128]{1,0:T(8,128)(2,1)S(1)}, f32[864,128]{1,0:T(8,128)S(1)}, f32[96,128]{1,0:T(8,128)S(1)}, f32[144,256]{1,0:T(8,128)S(1)}) custom-call(bf16[864,128]{1,0:T(8,128)(2,1)S(1)} %shard_map.139._.table_ref, bf16[3,240,256]{2,1,0:T(8,128)(2,1)S(1)} %shard_map.141.q_ref, bf16[144,256]{1,0:T(8,128)(2,1)S(1)} %get-tuple-element.60.cot_ref, ...), custom_call_target="tpu_custom_call" | custom-call | flops 10000000 | bytes 100000 | tf_op jit(solution)/shard_map/pallas_call | solution.py:447
  38.7 0.4 collective-permute-start.5
  39.1 0.3 shard_map.143.keep_ref
  39.5 0.7 collective-permute-done.5.got_ref
  40.2 17.9 %all_to_all.35 = bf16[128,4,128]{2,1,0:T(4,128)(2,1)S(1)} all-to-all(bf16[128,4,128]{2,1,0:T(4,128)(2,1)S(1)} %bitcast.15), channel_id=1, replica_groups={{0,1,2,3,4,5,6,7,16,17,18,19,20,21,22,23,32,33,34,35,36,37,38,39,48,49,..., dimensions={0} | all-to-all | bytes 262144 | tf_op jit(solution)/shard_map/all_to_all | solution.py:483
  58.1 0.7 shard_map.145
  58.8 6.5 %all-to-all-start.2 = ((bf16[128,4,128]{2,1,0:T(4,128)(2,1)}), bf16[128,4,128]{2,1,0:T(4,128)(2,1)S(1)}, u32[]{:S(2)}, u32[]{:S(2)}) async-start(bf16[128,4,128]{2,1,0:T(4,128)(2,1)} %bitcast.8), calls=%async_computation.2 | async-start | bytes 262144 | tf_op jit(solution)/shard_map/all_to_all | solution.py:483
  65.3 0.4 shard_map.146.back_ref
  65.7 0.7 shard_map.147
  66.4 9.3 %all-to-all-done.2 = bf16[128,4,128]{2,1,0:T(4,128)(2,1)S(1)} async-done(((bf16[128,4,128]{2,1,0:T(4,128)(2,1)}), bf16[128,4,128]{2,1,0:T(4,128)(2,1)S(1)}, u32[]{:S(2)}, u32[]{:S(2)}) %all-to-all-start.2) | async-done | bytes 131104 | tf_op jit(solution)/shard_map/all_to_all | solution.py:483
  75.6 2.9 %collective-permute-start.6 = (bf16[512,128]{1,0:T(8,128)(2,1)S(1)}, bf16[512,128]{1,0:T(8,128)(2,1)S(1)}, u32[]{:S(2)}, u32[]{:S(2)}) collective-permute-start(bf16[512,128]{1,0:T(8,128)(2,1)S(1)} %bitcast.11), channel_id=1, source_target_pairs={{0,8},{8,0},{16,24},{24,16},{32,40},{40,32},{48,56},{56,48},{64,72... | collective-permute-start | bytes 393224 | tf_op jit(solution)/shard_map/ppermute | solution.py:487
  78.6 1.3 %shard_map.148 = bf16[144,256]{1,0:T(8,128)(2,1)} custom-call(bf16[512,128]{1,0:T(8,128)(2,1)S(1)} %bitcast.12, f32[144,256]{1,0:T(8,128)S(1)} %get-tuple-element.74.outp_ref, bf16[9,192,64]{2,1,0:T(8,128)(2,1)S(1)} %shard_map.146.back_ref, bf16[64,256]{1,0:T(8,128)(2,1)S(1)} %get-tuple-element.76.utp_ref), custom_call_target="tpu_custom_call" | custom-call | flops 1000000000 | bytes 100000 | tf_op jit(solution)/shard_map/pallas_call | solution.py:447
  79.9 0.0 collective-permute-done.6.other_ref
  79.9 2.6 %shard_map.149 = bf16[27,256,256]{2,1,0:T(8,128)(2,1)} custom-call(bf16[512,128]{1,0:T(8,128)(2,1)S(1)} %bitcast.13, bf16[512,128]{1,0:T(8,128)(2,1)S(1)} %collective-permute-done.6.other_ref, bf16[256,64]{1,0:T(8,128)(2,1)S(1)} %get-tuple-element.82.u_ref, bf16[64,256]{1,0:T(8,128)(2,1)S(1)} %get-tuple-element.61.ot_ref, ...), custom_call_target="tpu_custom_call" | custom-call | flops 10000000 | bytes 100000 | tf_op jit(solution)/shard_map/pallas_call | solution.py:447
  (2 shorter events, 0.1 us)
Async XLA Ops:
  2.2 20.2 %collective-permute-start = (bf16[18,256]{1,0:T(8,128)(2,1)S(1)}, bf16[18,256]{1,0:T(8,128)(2,1)S(1)}, u32[]{:S(2)}, u32[]{:S(2)}) collective-permute-start(bf16[18,256]{1,0:T(8,128)(2,1)S(1)} %get-tuple-element.46), channel_id=1, source_target_pairs={{1,2},{3,4},{5,6},{2,1},{4,3},{6,5},{9,10},{11,12},{13,14},{10,9},... | collective-permute-start | bytes 27656 | tf_op jit(solution)/shard_map/ppermute | solution.py:470
  2.9 19.6 %collective-permute-start.1 = (bf16[18,256]{1,0:T(8,128)(2,1)S(1)}, bf16[18,256]{1,0:T(8,128)(2,1)S(1)}, u32[]{:S(2)}, u32[]{:S(2)}) collective-permute-start(bf16[18,256]{1,0:T(8,128)(2,1)S(1)} %get-tuple-element.47), channel_id=1, source_target_pairs={{0,1},{2,3},{4,5},{6,7},{1,0},{3,2},{5,4},{7,6},{8,9},{10,11},{12,... | collective-permute-start | bytes 27656 | tf_op jit(solution)/shard_map/ppermute | solution.py:470
  7.6 25.2 %all-to-all-start = ((bf16[128,4,128]{2,1,0:T(4,128)(2,1)}), bf16[128,4,128]{2,1,0:T(4,128)(2,1)S(1)}, u32[]{:S(2)}, u32[]{:S(2)}) async-start(bf16[128,4,128]{2,1,0:T(4,128)(2,1)} %bitcast.3), calls=%async_computation | async-start | bytes 262144 | tf_op jit(solution)/shard_map/all_to_all | solution.py:483
  22.5 14.4 %collective-permute-start.3 = (bf16[48,256]{1,0:T(8,128)(2,1)S(1)}, bf16[48,256]{1,0:T(8,128)(2,1)S(1)}, u32[]{:S(2)}, u32[]{:S(2)}) collective-permute-start(bf16[48,256]{1,0:T(8,128)(2,1)S(1)} %get-tuple-element.57), channel_id=1, source_target_pairs={{8,16},{24,32},{40,48},{56,64},{72,80},{88,96},{104,112},{120,128}... | collective-permute-start | bytes 73736 | tf_op jit(solution)/shard_map/ppermute | solution.py:470
  26.6 10.3 %collective-permute-start.4 = (bf16[48,256]{1,0:T(8,128)(2,1)S(1)}, bf16[48,256]{1,0:T(8,128)(2,1)S(1)}, u32[]{:S(2)}, u32[]{:S(2)}) collective-permute-start(bf16[48,256]{1,0:T(8,128)(2,1)S(1)} %get-tuple-element.58), channel_id=1, source_target_pairs={{0,8},{16,24},{32,40},{48,56},{64,72},{80,88},{96,104},{112,120},{... | collective-permute-start | bytes 73736 | tf_op jit(solution)/shard_map/ppermute | solution.py:470
  32.8 3.7 %collective-permute-start.2 = (bf16[512,128]{1,0:T(8,128)(2,1)S(1)}, bf16[512,128]{1,0:T(8,128)(2,1)S(1)}, u32[]{:S(2)}, u32[]{:S(2)}) collective-permute-start(bf16[512,128]{1,0:T(8,128)(2,1)S(1)} %bitcast.16), channel_id=1, source_target_pairs={{0,8},{8,0},{16,24},{24,16},{32,40},{40,32},{48,56},{56,48},{64,72... | collective-permute-start | bytes 393224 | tf_op jit(solution)/shard_map/ppermute | solution.py:487
  38.7 1.4 %collective-permute-start.5 = (bf16[512,128]{1,0:T(8,128)(2,1)S(1)}, bf16[512,128]{1,0:T(8,128)(2,1)S(1)}, u32[]{:S(2)}, u32[]{:S(2)}) collective-permute-start(bf16[512,128]{1,0:T(8,128)(2,1)S(1)} %get-tuple-element.65), channel_id=1, source_target_pairs={{0,8},{8,0},{16,24},{24,16},{32,40},{40,32},{48,56},{56,48},{64,72... | collective-permute-start | bytes 393224 | tf_op jit(solution)/shard_map/ppermute | solution.py:487
  58.8 16.9 %all-to-all-start.2 = ((bf16[128,4,128]{2,1,0:T(4,128)(2,1)}), bf16[128,4,128]{2,1,0:T(4,128)(2,1)S(1)}, u32[]{:S(2)}, u32[]{:S(2)}) async-start(bf16[128,4,128]{2,1,0:T(4,128)(2,1)} %bitcast.8), calls=%async_computation.2 | async-start | bytes 262144 | tf_op jit(solution)/shard_map/all_to_all | solution.py:483
  75.6 4.2 %collective-permute-start.6 = (bf16[512,128]{1,0:T(8,128)(2,1)S(1)}, bf16[512,128]{1,0:T(8,128)(2,1)S(1)}, u32[]{:S(2)}, u32[]{:S(2)}) collective-permute-start(bf16[512,128]{1,0:T(8,128)(2,1)S(1)} %bitcast.11), channel_id=1, source_target_pairs={{0,8},{8,0},{16,24},{24,16},{32,40},{40,32},{48,56},{56,48},{64,72... | collective-permute-start | bytes 393224 | tf_op jit(solution)/shard_map/ppermute | solution.py:487

commit v12 on v11

--- a/solution.py
+++ b/solution.py
@@ -235,18 +235,14 @@
     return jnp.full(shape, lax.rem(lax.axis_index("rows"), 2), jnp.int32)
 
 
-def gather_table(mine_ref, other_ref, take_ref, kind_ref, table_ref):
+def gather_rows(g, mine_ref, other_ref, take_ref, kind_ref, table_ref):
     kind = kind_ref[...]
-    take = take_ref[...]
     first = core_index((128, 128)) == 0
-    for g in range(4):
-        mine, other = mine_ref[128 * g : 128 * g + 128, :], other_ref[128 * g : 128 * g + 128, :]
-        block = jnp.concatenate([jnp.where(first, mine, other), jnp.where(first, other, mine)], axis=0)
-        none = jnp.zeros_like(block)
-        both = jnp.concatenate(
-            [jnp.where(kind == 0, block, none), jnp.where(kind == 1, block, none)], axis=0
-        )
-        table_ref[216 * g : 216 * g + 216, :] = dot(take, both)
+    mine, other = mine_ref[128 * g : 128 * g + 128, :], other_ref[128 * g : 128 * g + 128, :]
+    block = jnp.concatenate([jnp.where(first, mine, other), jnp.where(first, other, mine)], axis=0)
+    none = jnp.zeros_like(block)
+    both = jnp.concatenate([jnp.where(kind == 0, block, none), jnp.where(kind == 1, block, none)], axis=0)
+    table_ref[216 * g : 216 * g + 216, :] = dot(take_ref[...], both)
 
 
 def inside(lanes, at):
@@ -273,7 +269,8 @@
 
 
 def table_kernel(mine_ref, other_ref, take_ref, kind_ref, table_out, table):
-    gather_table(mine_ref, other_ref, take_ref, kind_ref, table)
+    for g in range(4):
+        gather_rows(g, mine_ref, other_ref, take_ref, kind_ref, table)
     table_out[...] = table[...].astype(BF)
 
 
@@ -324,7 +321,7 @@
     send_ref[...] = (keep_ref[...] + got_ref[...].astype(F32)).astype(BF)
 
 
-def adam_kernel(got_ref, core_ref, ring_ref, send_ref, next_ref, passed):
+def adam_kernel(got_ref, core_ref, ring_ref, send_ref, next_ref, passed, blocks, sems):
     total = jnp.zeros((8, 128), F32)
     passed[0:40, :] = jnp.zeros((40, 128), F32)
     passed[552:592, :] = jnp.zeros((40, 128), F32)
@@ -355,12 +352,17 @@
         right = right + jnp.where(here, cols, 0)
     source = lax.rem(parity - up + 2, 2)
     chips = lax.div(source + up - parity + 2, 2) - 1
-    start = 40 - 4 * (8 * chips + right)
+    start, copies = 40 - 4 * (8 * chips + right), []
     for k in range(32):
         upper = passed[pl.ds(start + 16 * k, 8), :]
         lower = passed[pl.ds(start + 16 * k + 8, 8), :]
         block = jnp.concatenate([jnp.where(mask, upper, own), jnp.where(mask, lower, own)], axis=0)
-        send_ref[16 * k : 16 * k + 16, :] = block.astype(BF)
+        blocks[16 * k : 16 * k + 16, :] = block.astype(BF)
+        if k % 8 == 7:
+            part = pl.ds(16 * k - 112, 128)
+            copies += fetch(((blocks.at[part], send_ref.at[part]),), sems.at[pl.ds(k // 8, 1)])
+    for copy in copies:
+        copy.wait()
 
 
 def flat_kernel(next_ref, core_ref, one_ref, two_ref):
@@ -419,25 +421,22 @@
     grad_ref[...] = dot(total.astype(BF), utp_ref[...]).astype(BF)
 
 def build_kernel(mine_ref, other_ref, u_ref, ot_ref, take_ref, kind_ref, out_ref, table, half, result, sems):
-    gather_table(mine_ref, other_ref, take_ref, kind_ref, table)
-    cube = table[...].astype(BF)
-    even = dot(cube[:, 0:64], ot_ref[...]).astype(BF)
-    odd = dot(cube[:, 64:128], ot_ref[...]).astype(BF)
-    for t in range(27):
-        half[t, 0:32, :] = even[32 * t : 32 * t + 32]
-        half[t, 32:64, :] = odd[32 * t : 32 * t + 32]
-    u = u_ref[...]
-
-    def store(a):
-        part = pl.ds(3 * a, 3)
-        return pltpu.make_async_copy(result.at[part], out_ref.at[part], sems.at[a])
-
-    for a in range(9):
-        for t in range(3 * a, 3 * a + 3):
+    u, ot = u_ref[...], ot_ref[...]
+    copies = []
+    for g, (start, end) in enumerate(((0, 6), (6, 13), (13, 20), (20, 27))):
+        gather_rows(g, mine_ref, other_ref, take_ref, kind_ref, table)
+        cube = table[32 * start : 32 * end, :].astype(BF)
+        even = dot(cube[:, 0:64], ot).astype(BF)
+        odd = dot(cube[:, 64:128], ot).astype(BF)
+        for t in range(start, end):
+            at = 32 * (t - start)
+            half[t, 0:32, :] = even[at : at + 32]
+            half[t, 32:64, :] = odd[at : at + 32]
             result[t] = dot(u, half[t]).astype(BF)
-        store(a).start()
-    for a in range(9):
-        store(a).wait()
+            copies.append(pltpu.make_async_copy(result.at[t], out_ref.at[t], sems.at[t]))
+            copies[-1].start()
+    for copy in copies:
+        copy.wait()
 
 
 def call(kernel, args, outs, scratch, flops=10**7):
@@ -556,8 +555,8 @@
     send, latest = call(
         adam_kernel,
         near(got, core_ring, ring),
-        [((512, 128), BF, False), ((3, 4, 128), F32, False)],
-        [vm((592, 128), F32)],
+        [((512, 128), BF, True), ((3, 4, 128), F32, False)],
+        [vm((592, 128), F32), vm((512, 128), BF), dma((4,))],
     )
     mine = exchange(send)
     (back,) = call(turn_kernel, near(table), [((9, 192, 64), BF, False)], [])
@@ -576,7 +575,7 @@
         build_kernel,
         near(mine, other, u, ot, take, kind),
         [((27, 256, 256), BF, True)],
-        [vm((TABLE, 128), F32), vm((27, 64, 256), BF), vm((27, 256, 256), BF), dma((9,))],
+        [vm((TABLE, 128), F32), vm((27, 64, 256), BF), vm((27, 256, 256), BF), dma((27,))],
     )
     frames_grad = frames_grad.reshape(FRAMES, ROWS, COLS, 256)
     return frames_grad, core_next, one_next, two_next, kernel_next

time: 82.8 us -> 83.7 us (1.011)
  Pallas kernels: 10.2 us -> 11.1 us
    pallas_call x13, Pallas kernels: 10.2 us -> 11.1 us  [call(): pl.pallas_call(kernel, out_shape=[jax.ShapeDtypeStruct(shape, dtype) for...]
where the time goes in v12:
time: 83.7 us; the launch traced here: 83.4 us
  starting transfers between devices  37 us (44%)
  blocking collectives  17.9 us (21%)
  waiting for transfers between devices  16.6 us (20%)
  Pallas kernels  11.1 us (13%)
    all_to_all x2, starting transfers between devices, exchange(): return lax.all_to_all(x, AXES, 0, 0, tiled=True, axis_index_groups=ORDER)  21.2 us
    all_to_all x1, blocking collectives, exchange(): return lax.all_to_all(x, AXES, 0, 0, tiled=True, axis_index_groups=ORDER)  17.9 us
    all_to_all x2, waiting for transfers between devices, exchange(): return lax.all_to_all(x, AXES, 0, 0, tiled=True, axis_index_groups=ORDER)  15.3 us
    pallas_call x13, Pallas kernels, call(): pl.pallas_call(kernel, out_shape=[jax.ShapeDtypeStruct(shape, dtype) for...  11.1 us
    ppermute x4, starting transfers between devices, swap(): lax.ppermute(x, axis, forward + [(b, a) for a, b in forward])  9.68 us
    ppermute x3, starting transfers between devices, in_chip(): return lax.ppermute(x, 'rows', [(r, r ^ 1) for r in range(32)])  6.08 us
  transfers between devices with their start and end apart: 9, of which 4 were waited for; matrix products, arithmetic and copies ran while one was open for 0% of the time, Pallas kernels for 4%

profile of v12, /device:TPU:1, one launch (start us, length us, event | category | flops | bytes accessed | tf_op | source)
XLA Modules:
  0.0 83.4 jit_solution(16951622021488026963)
XLA Ops:
  0.6 1.5 %shard_map.137 = (bf16[512,128]{1,0:T(8,128)(2,1)}, bf16[18,256]{1,0:T(8,128)(2,1)S(1)}, bf16[18,256]{1,0:T(8,128)(2,1)S(1)}, bf16[3,6,8,256]{3,2,1,0:T(8,128)(2...) custom-call(f32[432]{0:T(512)} %core_ref.1, ...), custom_call_target="tpu_custom_call" | custom-call | flops 10000000 | bytes 100000 | tf_op jit(solution)/shard_map/pallas_call | solution.py:446
  2.2 0.7 collective-permute-start
  2.9 4.8 %collective-permute-start.1 = (bf16[18,256]{1,0:T(8,128)(2,1)S(1)}, bf16[18,256]{1,0:T(8,128)(2,1)S(1)}, u32[]{:S(2)}, u32[]{:S(2)}) collective-permute-start(bf16[18,256]{1,0:T(8,128)(2,1)S(1)} %get-tuple-element.47), channel_id=1, source_target_pairs={{0,1},{2,3},{4,5},{6,7},{1,0},{3,2},{5,4},{7,6},{8,9},{10,11},{12,... | collective-permute-start | bytes 27656 | tf_op jit(solution)/shard_map/ppermute | solution.py:469
  7.6 14.8 %all-to-all-start = ((bf16[128,4,128]{2,1,0:T(4,128)(2,1)}), bf16[128,4,128]{2,1,0:T(4,128)(2,1)S(1)}, u32[]{:S(2)}, u32[]{:S(2)}) async-start(bf16[128,4,128]{2,1,0:T(4,128)(2,1)} %bitcast.3), calls=%async_computation | async-start | bytes 262144 | tf_op jit(solution)/shard_map/all_to_all | solution.py:482
  22.4 0.0 collective-permute-done.two_ref
  22.4 0.0 collective-permute-done.1.one_ref
  22.5 4.2 %collective-permute-start.3 = (bf16[48,256]{1,0:T(8,128)(2,1)S(1)}, bf16[48,256]{1,0:T(8,128)(2,1)S(1)}, u32[]{:S(2)}, u32[]{:S(2)}) collective-permute-start(bf16[48,256]{1,0:T(8,128)(2,1)S(1)} %get-tuple-element.57), channel_id=1, source_target_pairs={{8,16},{24,32},{40,48},{56,64},{72,80},{88,96},{104,112},{120,128}... | collective-permute-start | bytes 73736 | tf_op jit(solution)/shard_map/ppermute | solution.py:469
  26.6 0.1 collective-permute-start.4
  26.7 6.0 %all-to-all-done = bf16[128,4,128]{2,1,0:T(4,128)(2,1)S(1)} async-done(((bf16[128,4,128]{2,1,0:T(4,128)(2,1)}), bf16[128,4,128]{2,1,0:T(4,128)(2,1)S(1)}, u32[]{:S(2)}, u32[]{:S(2)}) %all-to-all-start) | async-done | bytes 131104 | tf_op jit(solution)/shard_map/all_to_all | solution.py:482
  32.8 2.7 %collective-permute-start.2 = (bf16[512,128]{1,0:T(8,128)(2,1)S(1)}, bf16[512,128]{1,0:T(8,128)(2,1)S(1)}, u32[]{:S(2)}, u32[]{:S(2)}) collective-permute-start(bf16[512,128]{1,0:T(8,128)(2,1)S(1)} %bitcast.16), channel_id=1, source_target_pairs={{0,8},{8,0},{16,24},{24,16},{32,40},{40,32},{48,56},{56,48},{64,72... | collective-permute-start | bytes 393224 | tf_op jit(solution)/shard_map/ppermute | solution.py:486
  35.5 0.3 shard_map.140
  35.8 0.6 collective-permute-done.2.other_ref
  36.5 0.4 shard_map.139._.table_ref
  36.9 0.0 collective-permute-done.3.two_ref
  36.9 0.0 collective-permute-done.4.one_ref
  36.9 0.3 shard_map.141.q_ref
  37.2 1.5 %shard_map.142 = (bf16[512,128]{1,0:T(8,128)(2,1)S(1)}, f32[864,128]{1,0:T(8,128)S(1)}, f32[96,128]{1,0:T(8,128)S(1)}, f32[144,256]{1,0:T(8,128)S(1)}) custom-call(bf16[864,128]{1,0:T(8,128)(2,1)S(1)} %shard_map.139._.table_ref, bf16[3,240,256]{2,1,0:T(8,128)(2,1)S(1)} %shard_map.141.q_ref, bf16[144,256]{1,0:T(8,128)(2,1)S(1)} %get-tuple-element.60.cot_ref, ...), custom_call_target="tpu_custom_call" | custom-call | flops 10000000 | bytes 100000 | tf_op jit(solution)/shard_map/pallas_call | solution.py:446
  38.7 0.4 collective-permute-start.5
  39.2 0.3 shard_map.143.keep_ref
  39.5 0.7 collective-permute-done.5.got_ref
  40.2 17.9 %all_to_all.35 = bf16[128,4,128]{2,1,0:T(4,128)(2,1)S(1)} all-to-all(bf16[128,4,128]{2,1,0:T(4,128)(2,1)S(1)} %bitcast.15), channel_id=1, replica_groups={{0,1,2,3,4,5,6,7,16,17,18,19,20,21,22,23,32,33,34,35,36,37,38,39,48,49,..., dimensions={0} | all-to-all | bytes 262144 | tf_op jit(solution)/shard_map/all_to_all | solution.py:482
  58.1 0.7 shard_map.145
  58.8 6.5 %all-to-all-start.2 = ((bf16[128,4,128]{2,1,0:T(4,128)(2,1)}), bf16[128,4,128]{2,1,0:T(4,128)(2,1)S(1)}, u32[]{:S(2)}, u32[]{:S(2)}) async-start(bf16[128,4,128]{2,1,0:T(4,128)(2,1)} %bitcast.8), calls=%async_computation.2 | async-start | bytes 262144 | tf_op jit(solution)/shard_map/all_to_all | solution.py:482
  65.3 0.4 shard_map.146.back_ref
  65.7 0.7 shard_map.147
  66.4 9.3 %all-to-all-done.2 = bf16[128,4,128]{2,1,0:T(4,128)(2,1)S(1)} async-done(((bf16[128,4,128]{2,1,0:T(4,128)(2,1)}), bf16[128,4,128]{2,1,0:T(4,128)(2,1)S(1)}, u32[]{:S(2)}, u32[]{:S(2)}) %all-to-all-start.2) | async-done | bytes 131104 | tf_op jit(solution)/shard_map/all_to_all | solution.py:482
  75.7 2.9 %collective-permute-start.6 = (bf16[512,128]{1,0:T(8,128)(2,1)S(1)}, bf16[512,128]{1,0:T(8,128)(2,1)S(1)}, u32[]{:S(2)}, u32[]{:S(2)}) collective-permute-start(bf16[512,128]{1,0:T(8,128)(2,1)S(1)} %bitcast.11), channel_id=1, source_target_pairs={{0,8},{8,0},{16,24},{24,16},{32,40},{40,32},{48,56},{56,48},{64,72... | collective-permute-start | bytes 393224 | tf_op jit(solution)/shard_map/ppermute | solution.py:486
  78.6 1.3 %shard_map.148 = bf16[144,256]{1,0:T(8,128)(2,1)} custom-call(bf16[512,128]{1,0:T(8,128)(2,1)S(1)} %bitcast.12, f32[144,256]{1,0:T(8,128)S(1)} %get-tuple-element.74.outp_ref, bf16[9,192,64]{2,1,0:T(8,128)(2,1)S(1)} %shard_map.146.back_ref, bf16[64,256]{1,0:T(8,128)(2,1)S(1)} %get-tuple-element.76.utp_ref), custom_call_target="tpu_custom_call" | custom-call | flops 1000000000 | bytes 100000 | tf_op jit(solution)/shard_map/pallas_call | solution.py:446
  79.9 0.0 collective-permute-done.6.other_ref
  79.9 3.5 %shard_map.149 = bf16[27,256,256]{2,1,0:T(8,128)(2,1)} custom-call(bf16[512,128]{1,0:T(8,128)(2,1)S(1)} %bitcast.13, bf16[512,128]{1,0:T(8,128)(2,1)S(1)} %collective-permute-done.6.other_ref, bf16[256,64]{1,0:T(8,128)(2,1)S(1)} %get-tuple-element.82.u_ref, bf16[64,256]{1,0:T(8,128)(2,1)S(1)} %get-tuple-element.61.ot_ref, ...), custom_call_target="tpu_custom_call" | custom-call | flops 10000000 | bytes 100000 | tf_op jit(solution)/shard_map/pallas_call | solution.py:446
  (2 shorter events, 0.1 us)
Async XLA Ops:
  2.2 20.2 %collective-permute-start = (bf16[18,256]{1,0:T(8,128)(2,1)S(1)}, bf16[18,256]{1,0:T(8,128)(2,1)S(1)}, u32[]{:S(2)}, u32[]{:S(2)}) collective-permute-start(bf16[18,256]{1,0:T(8,128)(2,1)S(1)} %get-tuple-element.46), channel_id=1, source_target_pairs={{1,2},{3,4},{5,6},{2,1},{4,3},{6,5},{9,10},{11,12},{13,14},{10,9},... | collective-permute-start | bytes 27656 | tf_op jit(solution)/shard_map/ppermute | solution.py:469
  2.9 19.6 %collective-permute-start.1 = (bf16[18,256]{1,0:T(8,128)(2,1)S(1)}, bf16[18,256]{1,0:T(8,128)(2,1)S(1)}, u32[]{:S(2)}, u32[]{:S(2)}) collective-permute-start(bf16[18,256]{1,0:T(8,128)(2,1)S(1)} %get-tuple-element.47), channel_id=1, source_target_pairs={{0,1},{2,3},{4,5},{6,7},{1,0},{3,2},{5,4},{7,6},{8,9},{10,11},{12,... | collective-permute-start | bytes 27656 | tf_op jit(solution)/shard_map/ppermute | solution.py:469
  7.6 25.2 %all-to-all-start = ((bf16[128,4,128]{2,1,0:T(4,128)(2,1)}), bf16[128,4,128]{2,1,0:T(4,128)(2,1)S(1)}, u32[]{:S(2)}, u32[]{:S(2)}) async-start(bf16[128,4,128]{2,1,0:T(4,128)(2,1)} %bitcast.3), calls=%async_computation | async-start | bytes 262144 | tf_op jit(solution)/shard_map/all_to_all | solution.py:482
  22.5 14.4 %collective-permute-start.3 = (bf16[48,256]{1,0:T(8,128)(2,1)S(1)}, bf16[48,256]{1,0:T(8,128)(2,1)S(1)}, u32[]{:S(2)}, u32[]{:S(2)}) collective-permute-start(bf16[48,256]{1,0:T(8,128)(2,1)S(1)} %get-tuple-element.57), channel_id=1, source_target_pairs={{8,16},{24,32},{40,48},{56,64},{72,80},{88,96},{104,112},{120,128}... | collective-permute-start | bytes 73736 | tf_op jit(solution)/shard_map/ppermute | solution.py:469
  26.6 10.3 %collective-permute-start.4 = (bf16[48,256]{1,0:T(8,128)(2,1)S(1)}, bf16[48,256]{1,0:T(8,128)(2,1)S(1)}, u32[]{:S(2)}, u32[]{:S(2)}) collective-permute-start(bf16[48,256]{1,0:T(8,128)(2,1)S(1)} %get-tuple-element.58), channel_id=1, source_target_pairs={{0,8},{16,24},{32,40},{48,56},{64,72},{80,88},{96,104},{112,120},{... | collective-permute-start | bytes 73736 | tf_op jit(solution)/shard_map/ppermute | solution.py:469
  32.8 3.7 %collective-permute-start.2 = (bf16[512,128]{1,0:T(8,128)(2,1)S(1)}, bf16[512,128]{1,0:T(8,128)(2,1)S(1)}, u32[]{:S(2)}, u32[]{:S(2)}) collective-permute-start(bf16[512,128]{1,0:T(8,128)(2,1)S(1)} %bitcast.16), channel_id=1, source_target_pairs={{0,8},{8,0},{16,24},{24,16},{32,40},{40,32},{48,56},{56,48},{64,72... | collective-permute-start | bytes 393224 | tf_op jit(solution)/shard_map/ppermute | solution.py:486
  38.7 1.4 %collective-permute-start.5 = (bf16[512,128]{1,0:T(8,128)(2,1)S(1)}, bf16[512,128]{1,0:T(8,128)(2,1)S(1)}, u32[]{:S(2)}, u32[]{:S(2)}) collective-permute-start(bf16[512,128]{1,0:T(8,128)(2,1)S(1)} %get-tuple-element.65), channel_id=1, source_target_pairs={{0,8},{8,0},{16,24},{24,16},{32,40},{40,32},{48,56},{56,48},{64,72... | collective-permute-start | bytes 393224 | tf_op jit(solution)/shard_map/ppermute | solution.py:486
  58.8 16.9 %all-to-all-start.2 = ((bf16[128,4,128]{2,1,0:T(4,128)(2,1)}), bf16[128,4,128]{2,1,0:T(4,128)(2,1)S(1)}, u32[]{:S(2)}, u32[]{:S(2)}) async-start(bf16[128,4,128]{2,1,0:T(4,128)(2,1)} %bitcast.8), calls=%async_computation.2 | async-start | bytes 262144 | tf_op jit(solution)/shard_map/all_to_all | solution.py:482
  75.7 4.2 %collective-permute-start.6 = (bf16[512,128]{1,0:T(8,128)(2,1)S(1)}, bf16[512,128]{1,0:T(8,128)(2,1)S(1)}, u32[]{:S(2)}, u32[]{:S(2)}) collective-permute-start(bf16[512,128]{1,0:T(8,128)(2,1)S(1)} %bitcast.11), channel_id=1, source_target_pairs={{0,8},{8,0},{16,24},{24,16},{32,40},{40,32},{48,56},{56,48},{64,72... | collective-permute-start | bytes 393224 | tf_op jit(solution)/shard_map/ppermute | solution.py:486

commit v13 on v11

--- a/solution.py
+++ b/solution.py
@@ -123,7 +123,7 @@
 def start_kernel(
     core_ref, x_ref, one_ref, two_ref, ut_ref, ot_ref, cot_ref, take_ref, give_ref, kind_ref,
     send_ref, near_ref, far_ref, inner_ref, ring_ref, one_out, two_out, ut_out, ot_out, cot_out, take_out, give_out, kind_out,
-    own, flat, block, low, high, sems,
+    own, flat, block, sems,
 ):
     copies = fetch(
         (
@@ -141,33 +141,26 @@
     sends = fetch([(block, send_ref.at[pl.ds(128 * k, 128)]) for k in range(4)], sems.at[pl.ds(10, 4)])
     copies[1].wait()
     for f in range(FRAMES):
-        for y in range(ROWS):
-            tile = inner_ref[f, y].astype(F32)
-            k = ROWS * f + y
-            low[k : k + 1, :] = tile[0:1, :]
-            high[k : k + 1, :] = tile[7:8, :]
-    one, two = even_first("cols", low[...], high[...])
-    near_ref[...] = one.astype(BF)
-    far_ref[...] = two.astype(BF)
+        first, last = inner_ref[f, 0].astype(F32), inner_ref[f, ROWS - 1].astype(F32)
+        one, two = even_first("rows", first, last)
+        near_ref[f] = one.astype(BF)
+        far_ref[f] = two.astype(BF)
     for copy in copies[2:] + sends:
         copy.wait()
 
 
-def rows_kernel(inner_ref, two_ref, one_ref, left_ref, right_ref, up_ref, down_ref, first, last):
-    right, left = even_first("cols", two_ref[...].astype(F32), one_ref[...].astype(F32))
-    left_ref[...] = left
-    right_ref[...] = right
-    first[...] = jnp.zeros_like(first)
-    last[...] = jnp.zeros_like(last)
+def columns_kernel(inner_ref, two_ref, one_ref, above_ref, below_ref, left_ref, right_ref, low, high):
     for f in range(FRAMES):
-        for y, rows in ((0, first), (ROWS - 1, last)):
-            k = ROWS * f + y
-            rows[16 * f : 16 * f + 8, :] = inner_ref[f, y].astype(F32)
-            rows[16 * f + 8 : 16 * f + 9, :] = left_ref[k : k + 1, :]
-            rows[16 * f + 9 : 16 * f + 10, :] = right_ref[k : k + 1, :]
-    one, two = even_first("rows", first[...], last[...])
-    up_ref[...] = one.astype(BF)
-    down_ref[...] = two.astype(BF)
+        below, above = even_first("rows", two_ref[f].astype(F32), one_ref[f].astype(F32))
+        above_ref[8 * f : 8 * f + 8, :] = above
+        below_ref[8 * f : 8 * f + 8, :] = below
+        for y in range(8):
+            tile = above if y == 0 else below if y == 7 else inner_ref[f, y - 1].astype(F32)
+            low[8 * f + y : 8 * f + y + 1, :] = tile[0:1, :]
+            high[8 * f + y : 8 * f + y + 1, :] = tile[7:8, :]
+    one, two = even_first("cols", low[...], high[...])
+    left_ref[...] = one.astype(BF)
+    right_ref[...] = two.astype(BF)
 
 
 def shifted(tile, left, right, bounds, period):
@@ -204,29 +197,27 @@
             out_ref[b, 48 * f + 48 : 48 * f + 96, :] = rows.astype(BF)
 
 
-def rank_kernel(_, own_ref, wide_ref, two_ref, one_ref, left_ref, right_ref, q_ref, tiles, edge, rims):
+def rank_kernel(_, own_ref, wide_ref, above_ref, below_ref, two_ref, one_ref, q_ref, tiles, edge, rims):
     wide = wide_ref[...]
 
     def project(v):
         return dot_nt(v.astype(BF), wide).astype(BF).astype(F32)
 
-    below, above = even_first("rows", project(two_ref[...]), project(one_ref[...]))
-    rims[0] = above
-    rims[1] = below
-    edge[0] = project(left_ref[...])
-    edge[1] = project(right_ref[...])
+    rims[0] = project(above_ref[...])
+    rims[1] = project(below_ref[...])
+    right, left = even_first("cols", project(two_ref[...]), project(one_ref[...]))
+    edge[0] = left
+    edge[1] = right
     for f in range(FRAMES):
         for y in range(8):
+            k = 8 * f + y
             if y in (0, 7):
-                rim = rims.at[y // 7]
-                at = 16 * f
-                tile, left, right = rim[at : at + 8, :], rim[at + 8 : at + 9, :], rim[at + 9 : at + 10, :]
+                tile = rims[y // 7, 8 * f : 8 * f + 8, :]
             else:
-                k = ROWS * f + y - 1
-                tile = own_ref[8 * k : 8 * k + 8, :]
-                left, right = edge[0, k : k + 1, :], edge[1, k : k + 1, :]
-            left = jnp.broadcast_to(left, (8, 256))
-            right = jnp.broadcast_to(right, (8, 256))
+                at = 48 * f + 8 * (y - 1)
+                tile = own_ref[at : at + 8, :]
+            left = jnp.broadcast_to(edge[0, k : k + 1, :], (8, 256))
+            right = jnp.broadcast_to(edge[1, k : k + 1, :], (8, 256))
             tiles[f, y] = shifted(tile, left, right, (32, 64), 128)
     stack_rows(tiles, q_ref)
 
@@ -491,8 +482,8 @@
     take, give, kind = ring_tables()
     take, give, kind = jnp.asarray(take, BF), jnp.asarray(give, BF), jnp.asarray(kind, F32)
     vm, dma = pltpu.VMEM, pltpu.SemaphoreType.DMA
-    side = (FRAMES * ROWS, 256)
-    rim = (FRAMES * 16, 256)
+    rim = (FRAMES * 8, 256)
+    row = (FRAMES, 8, 256)
 
     send, one, two, inner, core_ring, m_one, m_two, ut, ot, cot, take, give, kind = call(
         start_kernel,
@@ -500,25 +491,25 @@
             core, frames_in, moment_one, moment_two, u_in.T, u_out.T, cotangent.reshape(CELLS, 256), take, give, kind,
         ),
         [
-            ((512, 128), BF, True), (side, BF, False), (side, BF, False), ((FRAMES, ROWS, COLS, 256), BF, False),
+            ((512, 128), BF, True), (row, BF, False), (row, BF, False), ((FRAMES, ROWS, COLS, 256), BF, False),
             ((4, 128), F32, False), ((OWN,), F32, False), ((OWN,), F32, False), ((64, 256), BF, False),
             ((64, 256), BF, False), ((CELLS, 256), BF, False), ((216, 512), BF, False), ((2, 256, 216), BF, False),
             ((256, 128), F32, False),
         ],
-        [vm((OWN,), F32), vm((8, 128), F32), vm((128, 128), BF), vm(side, F32), vm(side, F32), dma((14,))],
-    )
-    one, two = swap(one, two, "cols")
+        [vm((OWN,), F32), vm((8, 128), F32), vm((128, 128), BF), dma((14,))],
+    )
+    one, two = swap(one, two, "rows")
     mine = exchange(send)
-    left, right, one, two = call(
-        rows_kernel,
+    above, below, one, two = call(
+        columns_kernel,
         near(inner, two, one),
-        [(side, F32, False), (side, F32, False), (rim, BF, False), (rim, BF, False)],
+        [(rim, F32, False), (rim, F32, False), (rim, BF, False), (rim, BF, False)],
         [vm(rim, F32), vm(rim, F32)],
         flops=10**10,
     )
     own, wide, utp, u, ring = call(
         prepare_kernel,
-        near(left, inner.reshape(CELLS, 256), ut, m_one, m_two),
+        near(above, inner.reshape(CELLS, 256), ut, m_one, m_two),
         [
             ((CELLS, 256), F32, False), ((256, 256), BF, False), ((64, 256), BF, False), ((256, 64), BF, False),
             ((2, 4, 128), F32, False),
@@ -526,7 +517,7 @@
         [vm((8, 128), F32)],
         flops=10**10,
     )
-    mine, _ = lax.optimization_barrier((mine, left))
+    mine, _ = lax.optimization_barrier((mine, above))
     other = in_chip(mine)
     (table,) = call(
         table_kernel,
@@ -535,12 +526,12 @@
         [vm((TABLE, 128), F32)],
         flops=10000000000,
     )
-    one, two = swap(one, two, "rows")
+    one, two = swap(one, two, "cols")
     (q,) = call(
         rank_kernel,
-        near(table, own, wide, two, one, left, right),
+        near(table, own, wide, above, below, two, one),
         [((3, 240, 256), BF, False)],
-        [vm((FRAMES, 8, 8, 256), F32), vm((2, 18, 256), F32), vm((2, 48, 256), F32)],
+        [vm((FRAMES, 8, 8, 256), F32), vm((2, 24, 256), F32), vm((2, 24, 256), F32)],
         flops=10000000,
     )
     send, grads, pixels, outp = call(

time: 82.8 us -> 81.9 us (0.989)
  starting transfers between devices: 37 us -> 35.5 us
    ppermute x4, starting transfers between devices: 9.68 us -> 8.35 us  [swap(): lax.ppermute(x, axis, forward + [(b, a) for a, b in forward])]
where the time goes in v13:
time: 81.9 us; the launch traced here: 81.6 us
  starting transfers between devices  35.5 us (43%)
  blocking collectives  18 us (22%)
  waiting for transfers between devices  17.1 us (21%)
  Pallas kernels  10.2 us (12%)
    all_to_all x2, starting transfers between devices, exchange(): return lax.all_to_all(x, AXES, 0, 0, tiled=True, axis_index_groups=ORDER)  21.7 us
    all_to_all x1, blocking collectives, exchange(): return lax.all_to_all(x, AXES, 0, 0, tiled=True, axis_index_groups=ORDER)  18 us
    all_to_all x2, waiting for transfers between devices, exchange(): return lax.all_to_all(x, AXES, 0, 0, tiled=True, axis_index_groups=ORDER)  15.8 us
    pallas_call x13, Pallas kernels, call(): pl.pallas_call(kernel, out_shape=[jax.ShapeDtypeStruct(shape, dtype) for...  10.2 us
    ppermute x4, starting transfers between devices, swap(): lax.ppermute(x, axis, forward + [(b, a) for a, b in forward])  8.35 us
    ppermute x3, starting transfers between devices, in_chip(): return lax.ppermute(x, 'rows', [(r, r ^ 1) for r in range(32)])  5.46 us
  transfers between devices with their start and end apart: 9, of which 4 were waited for; matrix products, arithmetic and copies ran while one was open for 0% of the time, Pallas kernels for 4%

profile of v13, /device:TPU:1, one launch (start us, length us, event | category | flops | bytes accessed | tf_op | source)
XLA Modules:
  0.0 81.6 jit_solution(15270205434145194665)
XLA Ops:
  0.6 1.5 %shard_map.137 = (bf16[512,128]{1,0:T(8,128)(2,1)}, bf16[3,8,256]{2,1,0:T(8,128)(2,1)S(1)}, bf16[3,8,256]{2,1,0:T(8,128)(2,1)S(1)}, bf16[3,6,8,256]{3,2,1,0:T(8,...) custom-call(f32[432]{0:T(512)} %core_ref.1, ...), custom_call_target="tpu_custom_call" | custom-call | flops 10000000 | bytes 100000 | tf_op jit(solution)/shard_map/pallas_call | solution.py:438
  2.2 4.5 %collective-permute-start = (bf16[3,8,256]{2,1,0:T(8,128)(2,1)S(1)}, bf16[3,8,256]{2,1,0:T(8,128)(2,1)S(1)}, u32[]{:S(2)}, u32[]{:S(2)}) collective-permute-start(bf16[3,8,256]{2,1,0:T(8,128)(2,1)S(1)} %get-tuple-element.46), channel_id=1, source_target_pairs={{8,16},{24,32},{40,48},{56,64},{72,80},{88,96},{104,112},{120,128}... | collective-permute-start | bytes 36872 | tf_op jit(solution)/shard_map/ppermute | solution.py:461
  6.7 0.1 collective-permute-start.1
  6.8 15.2 %all-to-all-start = ((bf16[128,4,128]{2,1,0:T(4,128)(2,1)}), bf16[128,4,128]{2,1,0:T(4,128)(2,1)S(1)}, u32[]{:S(2)}, u32[]{:S(2)}) async-start(bf16[128,4,128]{2,1,0:T(4,128)(2,1)} %bitcast.3), calls=%async_computation | async-start | bytes 262144 | tf_op jit(solution)/shard_map/all_to_all | solution.py:474
  22.0 0.0 collective-permute-done.two_ref
  22.0 0.0 collective-permute-done.1.one_ref
  22.1 0.1 shard_map.138
  22.1 0.7 collective-permute-start.3
  22.8 3.1 %collective-permute-start.4 = (bf16[24,256]{1,0:T(8,128)(2,1)S(1)}, bf16[24,256]{1,0:T(8,128)(2,1)S(1)}, u32[]{:S(2)}, u32[]{:S(2)}) collective-permute-start(bf16[24,256]{1,0:T(8,128)(2,1)S(1)} %get-tuple-element.59), channel_id=1, source_target_pairs={{0,1},{2,3},{4,5},{6,7},{1,0},{3,2},{5,4},{7,6},{8,9},{10,11},{12,... | collective-permute-start | bytes 36872 | tf_op jit(solution)/shard_map/ppermute | solution.py:461
  25.9 6.5 %all-to-all-done = bf16[128,4,128]{2,1,0:T(4,128)(2,1)S(1)} async-done(((bf16[128,4,128]{2,1,0:T(4,128)(2,1)}), bf16[128,4,128]{2,1,0:T(4,128)(2,1)S(1)}, u32[]{:S(2)}, u32[]{:S(2)}) %all-to-all-start) | async-done | bytes 131104 | tf_op jit(solution)/shard_map/all_to_all | solution.py:474
  32.4 2.1 %collective-permute-start.2 = (bf16[512,128]{1,0:T(8,128)(2,1)S(1)}, bf16[512,128]{1,0:T(8,128)(2,1)S(1)}, u32[]{:S(2)}, u32[]{:S(2)}) collective-permute-start(bf16[512,128]{1,0:T(8,128)(2,1)S(1)} %bitcast.16), channel_id=1, source_target_pairs={{0,8},{8,0},{16,24},{24,16},{32,40},{40,32},{48,56},{56,48},{64,72... | collective-permute-start | bytes 393224 | tf_op jit(solution)/shard_map/ppermute | solution.py:478
  34.5 0.3 shard_map.140
  34.9 0.6 collective-permute-done.2.other_ref
  35.5 0.4 shard_map.139._.table_ref
  35.9 0.0 collective-permute-done.3.two_ref
  35.9 0.0 collective-permute-done.4.one_ref
  35.9 0.3 shard_map.141.q_ref
  36.3 1.5 %shard_map.142 = (bf16[512,128]{1,0:T(8,128)(2,1)S(1)}, f32[864,128]{1,0:T(8,128)S(1)}, f32[96,128]{1,0:T(8,128)S(1)}, f32[144,256]{1,0:T(8,128)S(1)}) custom-call(bf16[864,128]{1,0:T(8,128)(2,1)S(1)} %shard_map.139._.table_ref, bf16[3,240,256]{2,1,0:T(8,128)(2,1)S(1)} %shard_map.141.q_ref, bf16[144,256]{1,0:T(8,128)(2,1)S(1)} %get-tuple-element.60.cot_ref, ...), custom_call_target="tpu_custom_call" | custom-call | flops 10000000 | bytes 100000 | tf_op jit(solution)/shard_map/pallas_call | solution.py:438
  37.7 0.4 collective-permute-start.5
  38.2 0.3 shard_map.143.keep_ref
  38.5 0.7 collective-permute-done.5.got_ref
  39.2 18.0 %all_to_all.35 = bf16[128,4,128]{2,1,0:T(4,128)(2,1)S(1)} all-to-all(bf16[128,4,128]{2,1,0:T(4,128)(2,1)S(1)} %bitcast.15), channel_id=1, replica_groups={{0,1,2,3,4,5,6,7,16,17,18,19,20,21,22,23,32,33,34,35,36,37,38,39,48,49,..., dimensions={0} | all-to-all | bytes 262144 | tf_op jit(solution)/shard_map/all_to_all | solution.py:474
  57.1 0.7 shard_map.145
  57.9 6.5 %all-to-all-start.2 = ((bf16[128,4,128]{2,1,0:T(4,128)(2,1)}), bf16[128,4,128]{2,1,0:T(4,128)(2,1)S(1)}, u32[]{:S(2)}, u32[]{:S(2)}) async-start(bf16[128,4,128]{2,1,0:T(4,128)(2,1)} %bitcast.8), calls=%async_computation.2 | async-start | bytes 262144 | tf_op jit(solution)/shard_map/all_to_all | solution.py:474
  64.3 0.4 shard_map.146.back_ref
  64.8 0.7 shard_map.147
  65.5 9.3 %all-to-all-done.2 = bf16[128,4,128]{2,1,0:T(4,128)(2,1)S(1)} async-done(((bf16[128,4,128]{2,1,0:T(4,128)(2,1)}), bf16[128,4,128]{2,1,0:T(4,128)(2,1)S(1)}, u32[]{:S(2)}, u32[]{:S(2)}) %all-to-all-start.2) | async-done | bytes 131104 | tf_op jit(solution)/shard_map/all_to_all | solution.py:474
  74.7 2.9 %collective-permute-start.6 = (bf16[512,128]{1,0:T(8,128)(2,1)S(1)}, bf16[512,128]{1,0:T(8,128)(2,1)S(1)}, u32[]{:S(2)}, u32[]{:S(2)}) collective-permute-start(bf16[512,128]{1,0:T(8,128)(2,1)S(1)} %bitcast.11), channel_id=1, source_target_pairs={{0,8},{8,0},{16,24},{24,16},{32,40},{40,32},{48,56},{56,48},{64,72... | collective-permute-start | bytes 393224 | tf_op jit(solution)/shard_map/ppermute | solution.py:478
  77.6 1.3 %shard_map.148 = bf16[144,256]{1,0:T(8,128)(2,1)} custom-call(bf16[512,128]{1,0:T(8,128)(2,1)S(1)} %bitcast.12, f32[144,256]{1,0:T(8,128)S(1)} %get-tuple-element.74.outp_ref, bf16[9,192,64]{2,1,0:T(8,128)(2,1)S(1)} %shard_map.146.back_ref, bf16[64,256]{1,0:T(8,128)(2,1)S(1)} %get-tuple-element.76.utp_ref), custom_call_target="tpu_custom_call" | custom-call | flops 1000000000 | bytes 100000 | tf_op jit(solution)/shard_map/pallas_call | solution.py:438
  78.9 0.0 collective-permute-done.6.other_ref
  78.9 2.6 %shard_map.149 = bf16[27,256,256]{2,1,0:T(8,128)(2,1)} custom-call(bf16[512,128]{1,0:T(8,128)(2,1)S(1)} %bitcast.13, bf16[512,128]{1,0:T(8,128)(2,1)S(1)} %collective-permute-done.6.other_ref, bf16[256,64]{1,0:T(8,128)(2,1)S(1)} %get-tuple-element.82.u_ref, bf16[64,256]{1,0:T(8,128)(2,1)S(1)} %get-tuple-element.61.ot_ref, ...), custom_call_target="tpu_custom_call" | custom-call | flops 10000000 | bytes 100000 | tf_op jit(solution)/shard_map/pallas_call | solution.py:438
  (1 shorter events, 0.0 us)
Async XLA Ops:
  2.2 19.9 %collective-permute-start = (bf16[3,8,256]{2,1,0:T(8,128)(2,1)S(1)}, bf16[3,8,256]{2,1,0:T(8,128)(2,1)S(1)}, u32[]{:S(2)}, u32[]{:S(2)}) collective-permute-start(bf16[3,8,256]{2,1,0:T(8,128)(2,1)S(1)} %get-tuple-element.46), channel_id=1, source_target_pairs={{8,16},{24,32},{40,48},{56,64},{72,80},{88,96},{104,112},{120,128}... | collective-permute-start | bytes 36872 | tf_op jit(solution)/shard_map/ppermute | solution.py:461
  6.7 15.3 %collective-permute-start.1 = (bf16[3,8,256]{2,1,0:T(8,128)(2,1)S(1)}, bf16[3,8,256]{2,1,0:T(8,128)(2,1)S(1)}, u32[]{:S(2)}, u32[]{:S(2)}) collective-permute-start(bf16[3,8,256]{2,1,0:T(8,128)(2,1)S(1)} %get-tuple-element.47), channel_id=1, source_target_pairs={{0,8},{16,24},{32,40},{48,56},{64,72},{80,88},{96,104},{112,120},{... | collective-permute-start | bytes 36872 | tf_op jit(solution)/shard_map/ppermute | solution.py:461
  6.8 25.6 %all-to-all-start = ((bf16[128,4,128]{2,1,0:T(4,128)(2,1)}), bf16[128,4,128]{2,1,0:T(4,128)(2,1)S(1)}, u32[]{:S(2)}, u32[]{:S(2)}) async-start(bf16[128,4,128]{2,1,0:T(4,128)(2,1)} %bitcast.3), calls=%async_computation | async-start | bytes 262144 | tf_op jit(solution)/shard_map/all_to_all | solution.py:474
  22.1 13.8 %collective-permute-start.3 = (bf16[24,256]{1,0:T(8,128)(2,1)S(1)}, bf16[24,256]{1,0:T(8,128)(2,1)S(1)}, u32[]{:S(2)}, u32[]{:S(2)}) collective-permute-start(bf16[24,256]{1,0:T(8,128)(2,1)S(1)} %get-tuple-element.58), channel_id=1, source_target_pairs={{1,2},{3,4},{5,6},{2,1},{4,3},{6,5},{9,10},{11,12},{13,14},{10,9},... | collective-permute-start | bytes 36872 | tf_op jit(solution)/shard_map/ppermute | solution.py:461
  22.8 13.2 %collective-permute-start.4 = (bf16[24,256]{1,0:T(8,128)(2,1)S(1)}, bf16[24,256]{1,0:T(8,128)(2,1)S(1)}, u32[]{:S(2)}, u32[]{:S(2)}) collective-permute-start(bf16[24,256]{1,0:T(8,128)(2,1)S(1)} %get-tuple-element.59), channel_id=1, source_target_pairs={{0,1},{2,3},{4,5},{6,7},{1,0},{3,2},{5,4},{7,6},{8,9},{10,11},{12,... | collective-permute-start | bytes 36872 | tf_op jit(solution)/shard_map/ppermute | solution.py:461
  32.4 3.1 %collective-permute-start.2 = (bf16[512,128]{1,0:T(8,128)(2,1)S(1)}, bf16[512,128]{1,0:T(8,128)(2,1)S(1)}, u32[]{:S(2)}, u32[]{:S(2)}) collective-permute-start(bf16[512,128]{1,0:T(8,128)(2,1)S(1)} %bitcast.16), channel_id=1, source_target_pairs={{0,8},{8,0},{16,24},{24,16},{32,40},{40,32},{48,56},{56,48},{64,72... | collective-permute-start | bytes 393224 | tf_op jit(solution)/shard_map/ppermute | solution.py:478
  37.7 1.4 %collective-permute-start.5 = (bf16[512,128]{1,0:T(8,128)(2,1)S(1)}, bf16[512,128]{1,0:T(8,128)(2,1)S(1)}, u32[]{:S(2)}, u32[]{:S(2)}) collective-permute-start(bf16[512,128]{1,0:T(8,128)(2,1)S(1)} %get-tuple-element.65), channel_id=1, source_target_pairs={{0,8},{8,0},{16,24},{24,16},{32,40},{40,32},{48,56},{56,48},{64,72... | collective-permute-start | bytes 393224 | tf_op jit(solution)/shard_map/ppermute | solution.py:478
  57.9 16.9 %all-to-all-start.2 = ((bf16[128,4,128]{2,1,0:T(4,128)(2,1)}), bf16[128,4,128]{2,1,0:T(4,128)(2,1)S(1)}, u32[]{:S(2)}, u32[]{:S(2)}) async-start(bf16[128,4,128]{2,1,0:T(4,128)(2,1)} %bitcast.8), calls=%async_computation.2 | async-start | bytes 262144 | tf_op jit(solution)/shard_map/all_to_all | solution.py:474
  74.7 4.2 %collective-permute-start.6 = (bf16[512,128]{1,0:T(8,128)(2,1)S(1)}, bf16[512,128]{1,0:T(8,128)(2,1)S(1)}, u32[]{:S(2)}, u32[]{:S(2)}) collective-permute-start(bf16[512,128]{1,0:T(8,128)(2,1)S(1)} %bitcast.11), channel_id=1, source_target_pairs={{0,8},{8,0},{16,24},{24,16},{32,40},{40,32},{48,56},{56,48},{64,72... | collective-permute-start | bytes 393224 | tf_op jit(solution)/shard_map/ppermute | solution.py:478

commit v14 on v13

--- a/solution.py
+++ b/solution.py
@@ -263,24 +263,26 @@
         blocks[spot, :] = jnp.where(inside(lanes, at), pixel, blocks[spot, :])
 
 
-def table_kernel(mine_ref, other_ref, take_ref, kind_ref, table_out, table):
+def table_kernel(mine_ref, other_ref, take_ref, kind_ref, table_out, weights_ref, table):
     gather_table(mine_ref, other_ref, take_ref, kind_ref, table)
     table_out[...] = table[...].astype(BF)
+    none = jnp.zeros((32, 64), BF)
+    for k in range(9):
+        part = table[96 * k : 96 * k + 96, :]
+        weights_ref[k, 0:96, :] = part[:, 0:64].astype(BF)
+        weights_ref[k, 96:128, :] = none
+        weights_ref[k, 128:224, :] = part[:, 64:128].astype(BF)
+        weights_ref[k, 224:256, :] = none
 
 
 def forward_kernel(
-    table_ref, q_ref, cot_ref, ot_ref, give_ref, kind_ref, send_ref, grads, pixels, outp_ref, border, blocks
+    weights_ref, q_ref, cot_ref, ot_ref, give_ref, kind_ref, send_ref, grads, pixels, outp_ref, border, blocks
 ):
-    even = jnp.zeros((CELLS, 128), F32)
-    odd = jnp.zeros((CELLS, 128), F32)
+    total = jnp.zeros((CELLS, 64), F32)
     for a in range(3):
         for b in range(3):
-            k = 3 * a + b
-            weights = table_ref[96 * k : 96 * k + 96, :]
-            rows = q_ref[b, 48 * a : 48 * a + CELLS, :]
-            even = even + dot(rows[:, 0:96], weights)
-            odd = odd + dot(rows[:, 128:224], weights)
-    mid = (even[:, 0:64] + odd[:, 64:128]).astype(BF)
+            total = total + dot(q_ref[b, 48 * a : 48 * a + CELLS, :], weights_ref[3 * a + b])
+    mid = total.astype(BF)
     pre = dot(mid, ot_ref[...])
     sig = jax.nn.sigmoid(pre)
     slope = (cot_ref[...].astype(F32) * sig * (1.0 + pre * (1.0 - sig))).astype(BF)
@@ -519,10 +521,10 @@
     )
     mine, _ = lax.optimization_barrier((mine, above))
     other = in_chip(mine)
-    (table,) = call(
+    table, weights = call(
         table_kernel,
         near(mine, other, take, kind),
-        [((TABLE, 128), BF, False)],
+        [((TABLE, 128), BF, False), ((9, 256, 64), BF, False)],
         [vm((TABLE, 128), F32)],
         flops=10000000000,
     )
@@ -536,7 +538,7 @@
     )
     send, grads, pixels, outp = call(
         forward_kernel,
-        near(table, q, cot, ot, give, kind),
+        near(weights, q, cot, ot, give, kind),
         [((512, 128), BF, False), ((TABLE, 128), F32, False), ((96, 128), F32, False), ((CELLS, 256), F32, False)],
         [vm((CELLS, 128), F32), vm((512, 128), F32)],
     )

time: 81.9 us -> 81.6 us (level)
  no operation moved by 1% of the time
where the time goes in v14:
time: 81.6 us; the launch traced here: 81.3 us
  starting transfers between devices  35.5 us (44%)
  blocking collectives  17.9 us (22%)
  waiting for transfers between devices  17.1 us (21%)
  Pallas kernels  10.1 us (12%)
    all_to_all x2, starting transfers between devices, exchange(): return lax.all_to_all(x, AXES, 0, 0, tiled=True, axis_index_groups=ORDER)  21.7 us
    all_to_all x1, blocking collectives, exchange(): return lax.all_to_all(x, AXES, 0, 0, tiled=True, axis_index_groups=ORDER)  17.9 us
    all_to_all x2, waiting for transfers between devices, exchange(): return lax.all_to_all(x, AXES, 0, 0, tiled=True, axis_index_groups=ORDER)  15.8 us
    pallas_call x13, Pallas kernels, call(): pl.pallas_call(kernel, out_shape=[jax.ShapeDtypeStruct(shape, dtype) for...  10.1 us
    ppermute x4, starting transfers between devices, swap(): lax.ppermute(x, axis, forward + [(b, a) for a, b in forward])  8.35 us
    ppermute x3, starting transfers between devices, in_chip(): return lax.ppermute(x, 'rows', [(r, r ^ 1) for r in range(32)])  5.46 us
  transfers between devices with their start and end apart: 9, of which 4 were waited for; matrix products, arithmetic and copies ran while one was open for 0% of the time, Pallas kernels for 4%

profile of v14, /device:TPU:1, one launch (start us, length us, event | category | flops | bytes accessed | tf_op | source)
XLA Modules:
  0.0 81.3 jit_solution(3163486798974536249)
XLA Ops:
  0.6 1.5 %shard_map.137 = (bf16[512,128]{1,0:T(8,128)(2,1)}, bf16[3,8,256]{2,1,0:T(8,128)(2,1)S(1)}, bf16[3,8,256]{2,1,0:T(8,128)(2,1)S(1)}, bf16[3,6,8,256]{3,2,1,0:T(8,...) custom-call(f32[432]{0:T(512)} %core_ref.1, ...), custom_call_target="tpu_custom_call" | custom-call | flops 10000000 | bytes 100000 | tf_op jit(solution)/shard_map/pallas_call | solution.py:440
  2.2 4.5 %collective-permute-start = (bf16[3,8,256]{2,1,0:T(8,128)(2,1)S(1)}, bf16[3,8,256]{2,1,0:T(8,128)(2,1)S(1)}, u32[]{:S(2)}, u32[]{:S(2)}) collective-permute-start(bf16[3,8,256]{2,1,0:T(8,128)(2,1)S(1)} %get-tuple-element.48), channel_id=1, source_target_pairs={{8,16},{24,32},{40,48},{56,64},{72,80},{88,96},{104,112},{120,128}... | collective-permute-start | bytes 36872 | tf_op jit(solution)/shard_map/ppermute | solution.py:463
  6.7 0.1 collective-permute-start.1
  6.8 15.2 %all-to-all-start = ((bf16[128,4,128]{2,1,0:T(4,128)(2,1)}), bf16[128,4,128]{2,1,0:T(4,128)(2,1)S(1)}, u32[]{:S(2)}, u32[]{:S(2)}) async-start(bf16[128,4,128]{2,1,0:T(4,128)(2,1)} %bitcast.3), calls=%async_computation | async-start | bytes 262144 | tf_op jit(solution)/shard_map/all_to_all | solution.py:476
  22.0 0.0 collective-permute-done.two_ref
  22.0 0.0 collective-permute-done.1.one_ref
  22.1 0.1 shard_map.138
  22.1 0.7 collective-permute-start.3
  22.8 3.1 %collective-permute-start.4 = (bf16[24,256]{1,0:T(8,128)(2,1)S(1)}, bf16[24,256]{1,0:T(8,128)(2,1)S(1)}, u32[]{:S(2)}, u32[]{:S(2)}) collective-permute-start(bf16[24,256]{1,0:T(8,128)(2,1)S(1)} %get-tuple-element.63), channel_id=1, source_target_pairs={{0,1},{2,3},{4,5},{6,7},{1,0},{3,2},{5,4},{7,6},{8,9},{10,11},{12,... | collective-permute-start | bytes 36872 | tf_op jit(solution)/shard_map/ppermute | solution.py:463
  25.9 6.5 %all-to-all-done = bf16[128,4,128]{2,1,0:T(4,128)(2,1)S(1)} async-done(((bf16[128,4,128]{2,1,0:T(4,128)(2,1)}), bf16[128,4,128]{2,1,0:T(4,128)(2,1)S(1)}, u32[]{:S(2)}, u32[]{:S(2)}) %all-to-all-start) | async-done | bytes 131104 | tf_op jit(solution)/shard_map/all_to_all | solution.py:476
  32.4 2.1 %collective-permute-start.2 = (bf16[512,128]{1,0:T(8,128)(2,1)S(1)}, bf16[512,128]{1,0:T(8,128)(2,1)S(1)}, u32[]{:S(2)}, u32[]{:S(2)}) collective-permute-start(bf16[512,128]{1,0:T(8,128)(2,1)S(1)} %bitcast.16), channel_id=1, source_target_pairs={{0,8},{8,0},{16,24},{24,16},{32,40},{40,32},{48,56},{56,48},{64,72... | collective-permute-start | bytes 393224 | tf_op jit(solution)/shard_map/ppermute | solution.py:480
  34.5 0.3 shard_map.140
  34.9 0.6 collective-permute-done.2.other_ref
  35.5 0.5 shard_map.139
  36.0 0.0 collective-permute-done.3.two_ref
  36.0 0.0 collective-permute-done.4.one_ref
  36.0 0.3 shard_map.141.q_ref
  36.3 1.2 %shard_map.142 = (bf16[512,128]{1,0:T(8,128)(2,1)S(1)}, f32[864,128]{1,0:T(8,128)S(1)}, f32[96,128]{1,0:T(8,128)S(1)}, f32[144,256]{1,0:T(8,128)S(1)}) custom-call(bf16[9,256,64]{2,1,0:T(8,128)(2,1)S(1)} %get-tuple-element.54.weights_ref, bf16[3,240,256]{2,1,0:T(8,128)(2,1)S(1)} %shard_map.141.q_ref, bf16[144,256]{1,0:T(8,128)(2,1)S(1)} %get-tuple-element.64.cot_ref, ...), custom_call_target="tpu_custom_call" | custom-call | flops 10000000 | bytes 100000 | tf_op jit(solution)/shard_map/pallas_call | solution.py:440
  37.5 0.4 collective-permute-start.5
  38.0 0.3 shard_map.143.keep_ref
  38.3 0.7 collective-permute-done.5.got_ref
  39.0 17.9 %all_to_all.35 = bf16[128,4,128]{2,1,0:T(4,128)(2,1)S(1)} all-to-all(bf16[128,4,128]{2,1,0:T(4,128)(2,1)S(1)} %bitcast.15), channel_id=1, replica_groups={{0,1,2,3,4,5,6,7,16,17,18,19,20,21,22,23,32,33,34,35,36,37,38,39,48,49,..., dimensions={0} | all-to-all | bytes 262144 | tf_op jit(solution)/shard_map/all_to_all | solution.py:476
  56.9 0.7 shard_map.145
  57.6 6.5 %all-to-all-start.2 = ((bf16[128,4,128]{2,1,0:T(4,128)(2,1)}), bf16[128,4,128]{2,1,0:T(4,128)(2,1)S(1)}, u32[]{:S(2)}, u32[]{:S(2)}) async-start(bf16[128,4,128]{2,1,0:T(4,128)(2,1)} %bitcast.8), calls=%async_computation.2 | async-start | bytes 262144 | tf_op jit(solution)/shard_map/all_to_all | solution.py:476
  64.1 0.4 shard_map.146.back_ref
  64.6 0.7 shard_map.147
  65.2 9.3 %all-to-all-done.2 = bf16[128,4,128]{2,1,0:T(4,128)(2,1)S(1)} async-done(((bf16[128,4,128]{2,1,0:T(4,128)(2,1)}), bf16[128,4,128]{2,1,0:T(4,128)(2,1)S(1)}, u32[]{:S(2)}, u32[]{:S(2)}) %all-to-all-start.2) | async-done | bytes 131104 | tf_op jit(solution)/shard_map/all_to_all | solution.py:476
  74.5 2.9 %collective-permute-start.6 = (bf16[512,128]{1,0:T(8,128)(2,1)S(1)}, bf16[512,128]{1,0:T(8,128)(2,1)S(1)}, u32[]{:S(2)}, u32[]{:S(2)}) collective-permute-start(bf16[512,128]{1,0:T(8,128)(2,1)S(1)} %bitcast.11), channel_id=1, source_target_pairs={{0,8},{8,0},{16,24},{24,16},{32,40},{40,32},{48,56},{56,48},{64,72... | collective-permute-start | bytes 393224 | tf_op jit(solution)/shard_map/ppermute | solution.py:480
  77.4 1.3 %shard_map.148 = bf16[144,256]{1,0:T(8,128)(2,1)} custom-call(bf16[512,128]{1,0:T(8,128)(2,1)S(1)} %bitcast.12, f32[144,256]{1,0:T(8,128)S(1)} %get-tuple-element.78.outp_ref, bf16[9,192,64]{2,1,0:T(8,128)(2,1)S(1)} %shard_map.146.back_ref, bf16[64,256]{1,0:T(8,128)(2,1)S(1)} %get-tuple-element.80.utp_ref), custom_call_target="tpu_custom_call" | custom-call | flops 1000000000 | bytes 100000 | tf_op jit(solution)/shard_map/pallas_call | solution.py:440
  78.7 0.0 collective-permute-done.6.other_ref
  78.7 2.6 %shard_map.149 = bf16[27,256,256]{2,1,0:T(8,128)(2,1)} custom-call(bf16[512,128]{1,0:T(8,128)(2,1)S(1)} %bitcast.13, bf16[512,128]{1,0:T(8,128)(2,1)S(1)} %collective-permute-done.6.other_ref, bf16[256,64]{1,0:T(8,128)(2,1)S(1)} %get-tuple-element.86.u_ref, bf16[64,256]{1,0:T(8,128)(2,1)S(1)} %get-tuple-element.65.ot_ref, ...), custom_call_target="tpu_custom_call" | custom-call | flops 10000000 | bytes 100000 | tf_op jit(solution)/shard_map/pallas_call | solution.py:440
  (1 shorter events, 0.0 us)
Async XLA Ops:
  2.2 19.9 %collective-permute-start = (bf16[3,8,256]{2,1,0:T(8,128)(2,1)S(1)}, bf16[3,8,256]{2,1,0:T(8,128)(2,1)S(1)}, u32[]{:S(2)}, u32[]{:S(2)}) collective-permute-start(bf16[3,8,256]{2,1,0:T(8,128)(2,1)S(1)} %get-tuple-element.48), channel_id=1, source_target_pairs={{8,16},{24,32},{40,48},{56,64},{72,80},{88,96},{104,112},{120,128}... | collective-permute-start | bytes 36872 | tf_op jit(solution)/shard_map/ppermute | solution.py:463
  6.7 15.3 %collective-permute-start.1 = (bf16[3,8,256]{2,1,0:T(8,128)(2,1)S(1)}, bf16[3,8,256]{2,1,0:T(8,128)(2,1)S(1)}, u32[]{:S(2)}, u32[]{:S(2)}) collective-permute-start(bf16[3,8,256]{2,1,0:T(8,128)(2,1)S(1)} %get-tuple-element.49), channel_id=1, source_target_pairs={{0,8},{16,24},{32,40},{48,56},{64,72},{80,88},{96,104},{112,120},{... | collective-permute-start | bytes 36872 | tf_op jit(solution)/shard_map/ppermute | solution.py:463
  6.8 25.6 %all-to-all-start = ((bf16[128,4,128]{2,1,0:T(4,128)(2,1)}), bf16[128,4,128]{2,1,0:T(4,128)(2,1)S(1)}, u32[]{:S(2)}, u32[]{:S(2)}) async-start(bf16[128,4,128]{2,1,0:T(4,128)(2,1)} %bitcast.3), calls=%async_computation | async-start | bytes 262144 | tf_op jit(solution)/shard_map/all_to_all | solution.py:476
  22.1 13.9 %collective-permute-start.3 = (bf16[24,256]{1,0:T(8,128)(2,1)S(1)}, bf16[24,256]{1,0:T(8,128)(2,1)S(1)}, u32[]{:S(2)}, u32[]{:S(2)}) collective-permute-start(bf16[24,256]{1,0:T(8,128)(2,1)S(1)} %get-tuple-element.62), channel_id=1, source_target_pairs={{1,2},{3,4},{5,6},{2,1},{4,3},{6,5},{9,10},{11,12},{13,14},{10,9},... | collective-permute-start | bytes 36872 | tf_op jit(solution)/shard_map/ppermute | solution.py:463
  22.8 13.2 %collective-permute-start.4 = (bf16[24,256]{1,0:T(8,128)(2,1)S(1)}, bf16[24,256]{1,0:T(8,128)(2,1)S(1)}, u32[]{:S(2)}, u32[]{:S(2)}) collective-permute-start(bf16[24,256]{1,0:T(8,128)(2,1)S(1)} %get-tuple-element.63), channel_id=1, source_target_pairs={{0,1},{2,3},{4,5},{6,7},{1,0},{3,2},{5,4},{7,6},{8,9},{10,11},{12,... | collective-permute-start | bytes 36872 | tf_op jit(solution)/shard_map/ppermute | solution.py:463
  32.4 3.1 %collective-permute-start.2 = (bf16[512,128]{1,0:T(8,128)(2,1)S(1)}, bf16[512,128]{1,0:T(8,128)(2,1)S(1)}, u32[]{:S(2)}, u32[]{:S(2)}) collective-permute-start(bf16[512,128]{1,0:T(8,128)(2,1)S(1)} %bitcast.16), channel_id=1, source_target_pairs={{0,8},{8,0},{16,24},{24,16},{32,40},{40,32},{48,56},{56,48},{64,72... | collective-permute-start | bytes 393224 | tf_op jit(solution)/shard_map/ppermute | solution.py:480
  37.5 1.4 %collective-permute-start.5 = (bf16[512,128]{1,0:T(8,128)(2,1)S(1)}, bf16[512,128]{1,0:T(8,128)(2,1)S(1)}, u32[]{:S(2)}, u32[]{:S(2)}) collective-permute-start(bf16[512,128]{1,0:T(8,128)(2,1)S(1)} %get-tuple-element.69), channel_id=1, source_target_pairs={{0,8},{8,0},{16,24},{24,16},{32,40},{40,32},{48,56},{56,48},{64,72... | collective-permute-start | bytes 393224 | tf_op jit(solution)/shard_map/ppermute | solution.py:480
  57.6 16.9 %all-to-all-start.2 = ((bf16[128,4,128]{2,1,0:T(4,128)(2,1)}), bf16[128,4,128]{2,1,0:T(4,128)(2,1)S(1)}, u32[]{:S(2)}, u32[]{:S(2)}) async-start(bf16[128,4,128]{2,1,0:T(4,128)(2,1)} %bitcast.8), calls=%async_computation.2 | async-start | bytes 262144 | tf_op jit(solution)/shard_map/all_to_all | solution.py:476
  74.5 4.2 %collective-permute-start.6 = (bf16[512,128]{1,0:T(8,128)(2,1)S(1)}, bf16[512,128]{1,0:T(8,128)(2,1)S(1)}, u32[]{:S(2)}, u32[]{:S(2)}) collective-permute-start(bf16[512,128]{1,0:T(8,128)(2,1)S(1)} %bitcast.11), channel_id=1, source_target_pairs={{0,8},{8,0},{16,24},{24,16},{32,40},{40,32},{48,56},{56,48},{64,72... | collective-permute-start | bytes 393224 | tf_op jit(solution)/shard_map/ppermute | solution.py:480

commit v15 on v14

--- a/solution.py
+++ b/solution.py
@@ -197,7 +197,7 @@
             out_ref[b, 48 * f + 48 : 48 * f + 96, :] = rows.astype(BF)
 
 
-def rank_kernel(_, own_ref, wide_ref, above_ref, below_ref, two_ref, one_ref, q_ref, tiles, edge, rims):
+def stack_inputs(own_ref, wide_ref, above_ref, below_ref, two_ref, one_ref, q_ref, tiles, edge, rims):
     wide = wide_ref[...]
 
     def project(v):
@@ -276,8 +276,10 @@
 
 
 def forward_kernel(
-    weights_ref, q_ref, cot_ref, ot_ref, give_ref, kind_ref, send_ref, grads, pixels, outp_ref, border, blocks
+    own_ref, wide_ref, above_ref, below_ref, two_ref, one_ref, weights_ref, cot_ref, ot_ref, give_ref, kind_ref,
+    send_ref, grads, pixels, outp_ref, border, blocks, q_ref, tiles, edge, rims,
 ):
+    stack_inputs(own_ref, wide_ref, above_ref, below_ref, two_ref, one_ref, q_ref, tiles, edge, rims)
     total = jnp.zeros((CELLS, 64), F32)
     for a in range(3):
         for b in range(3):
@@ -529,18 +531,15 @@
         flops=10000000000,
     )
     one, two = swap(one, two, "cols")
-    (q,) = call(
-        rank_kernel,
-        near(table, own, wide, above, below, two, one),
-        [((3, 240, 256), BF, False)],
-        [vm((FRAMES, 8, 8, 256), F32), vm((2, 24, 256), F32), vm((2, 24, 256), F32)],
-        flops=10000000,
-    )
     send, grads, pixels, outp = call(
         forward_kernel,
-        near(weights, q, cot, ot, give, kind),
+        near(own, wide, above, below, two, one, weights, cot, ot, give, kind),
         [((512, 128), BF, False), ((TABLE, 128), F32, False), ((96, 128), F32, False), ((CELLS, 256), F32, False)],
-        [vm((CELLS, 128), F32), vm((512, 128), F32)],
+        [
+            vm((CELLS, 128), F32), vm((512, 128), F32), vm((3, 240, 256), BF), vm((FRAMES, 8, 8, 256), F32),
+            vm((2, SIDE, 256), F32), vm((2, SIDE, 256), F32),
+        ],
+        flops=10**7,
     )
     got = in_chip(send)
     (keep,) = call(keep_kernel, near(grads, pixels, give, kind), [((512, 128), F32, False)], [], flops=10**9)

time: 81.6 us -> 81.5 us (level)
    pallas_call x13 -> x12, Pallas kernels: 10.1 us -> 9.98 us  [call(): pl.pallas_call(kernel, out_shape=[jax.ShapeDtypeStruct(shape, dtype) for...]
where the time goes in v15:
time: 81.5 us; the launch traced here: 81.2 us
  starting transfers between devices  35.5 us (44%)
  blocking collectives  17.9 us (22%)
  waiting for transfers between devices  17.1 us (21%)
  Pallas kernels  9.98 us (12%)
    all_to_all x2, starting transfers between devices, exchange(): return lax.all_to_all(x, AXES, 0, 0, tiled=True, axis_index_groups=ORDER)  21.7 us
    all_to_all x1, blocking collectives, exchange(): return lax.all_to_all(x, AXES, 0, 0, tiled=True, axis_index_groups=ORDER)  17.9 us
    all_to_all x2, waiting for transfers between devices, exchange(): return lax.all_to_all(x, AXES, 0, 0, tiled=True, axis_index_groups=ORDER)  15.8 us
    pallas_call x12, Pallas kernels, call(): pl.pallas_call(kernel, out_shape=[jax.ShapeDtypeStruct(shape, dtype) for...  9.98 us
    ppermute x4, starting transfers between devices, swap(): lax.ppermute(x, axis, forward + [(b, a) for a, b in forward])  8.35 us
    ppermute x3, starting transfers between devices, in_chip(): return lax.ppermute(x, 'rows', [(r, r ^ 1) for r in range(32)])  5.46 us
  transfers between devices with their start and end apart: 9, of which 4 were waited for; matrix products, arithmetic and copies ran while one was open for 0% of the time, Pallas kernels for 4%

profile of v15, /device:TPU:1, one launch (start us, length us, event | category | flops | bytes accessed | tf_op | source)
XLA Modules:
  0.0 81.2 jit_solution(7033255504543241270)
XLA Ops:
  0.6 1.5 %shard_map.137 = (bf16[512,128]{1,0:T(8,128)(2,1)}, bf16[3,8,256]{2,1,0:T(8,128)(2,1)S(1)}, bf16[3,8,256]{2,1,0:T(8,128)(2,1)S(1)}, bf16[3,6,8,256]{3,2,1,0:T(8,...) custom-call(f32[432]{0:T(512)} %core_ref.1, ...), custom_call_target="tpu_custom_call" | custom-call | flops 10000000 | bytes 100000 | tf_op jit(solution)/shard_map/pallas_call | solution.py:442
  2.2 4.5 %collective-permute-start = (bf16[3,8,256]{2,1,0:T(8,128)(2,1)S(1)}, bf16[3,8,256]{2,1,0:T(8,128)(2,1)S(1)}, u32[]{:S(2)}, u32[]{:S(2)}) collective-permute-start(bf16[3,8,256]{2,1,0:T(8,128)(2,1)S(1)} %get-tuple-element.47), channel_id=1, source_target_pairs={{8,16},{24,32},{40,48},{56,64},{72,80},{88,96},{104,112},{120,128}... | collective-permute-start | bytes 36872 | tf_op jit(solution)/shard_map/ppermute | solution.py:465
  6.7 0.1 collective-permute-start.1
  6.8 15.2 %all-to-all-start = ((bf16[128,4,128]{2,1,0:T(4,128)(2,1)}), bf16[128,4,128]{2,1,0:T(4,128)(2,1)S(1)}, u32[]{:S(2)}, u32[]{:S(2)}) async-start(bf16[128,4,128]{2,1,0:T(4,128)(2,1)} %bitcast.4), calls=%async_computation | async-start | bytes 262144 | tf_op jit(solution)/shard_map/all_to_all | solution.py:478
  22.0 0.0 collective-permute-done.two_ref
  22.0 0.0 collective-permute-done.1.one_ref
  22.1 0.1 shard_map.138
  22.1 0.7 collective-permute-start.2
  22.8 3.1 %collective-permute-start.3 = (bf16[24,256]{1,0:T(8,128)(2,1)S(1)}, bf16[24,256]{1,0:T(8,128)(2,1)S(1)}, u32[]{:S(2)}, u32[]{:S(2)}) collective-permute-start(bf16[24,256]{1,0:T(8,128)(2,1)S(1)} %get-tuple-element.57), channel_id=1, source_target_pairs={{0,1},{2,3},{4,5},{6,7},{1,0},{3,2},{5,4},{7,6},{8,9},{10,11},{12,... | collective-permute-start | bytes 36872 | tf_op jit(solution)/shard_map/ppermute | solution.py:465
  25.9 6.5 %all-to-all-done = bf16[128,4,128]{2,1,0:T(4,128)(2,1)S(1)} async-done(((bf16[128,4,128]{2,1,0:T(4,128)(2,1)}), bf16[128,4,128]{2,1,0:T(4,128)(2,1)S(1)}, u32[]{:S(2)}, u32[]{:S(2)}) %all-to-all-start) | async-done | bytes 131104 | tf_op jit(solution)/shard_map/all_to_all | solution.py:478
  32.4 2.1 %collective-permute-start.4 = (bf16[512,128]{1,0:T(8,128)(2,1)S(1)}, bf16[512,128]{1,0:T(8,128)(2,1)S(1)}, u32[]{:S(2)}, u32[]{:S(2)}) collective-permute-start(bf16[512,128]{1,0:T(8,128)(2,1)S(1)} %bitcast.16), channel_id=1, source_target_pairs={{0,8},{8,0},{16,24},{24,16},{32,40},{40,32},{48,56},{56,48},{64,72... | collective-permute-start | bytes 393224 | tf_op jit(solution)/shard_map/ppermute | solution.py:482
  34.5 0.3 shard_map.139
  34.9 0.6 collective-permute-done.4.other_ref
  35.5 0.5 shard_map.140
  36.0 0.0 collective-permute-done.2.two_ref
  36.0 0.0 collective-permute-done.3.one_ref
  36.0 1.5 %shard_map.141 = (bf16[512,128]{1,0:T(8,128)(2,1)S(1)}, f32[864,128]{1,0:T(8,128)S(1)}, f32[96,128]{1,0:T(8,128)S(1)}, f32[144,256]{1,0:T(8,128)S(1)}) custom-call(f32[144,256]{1,0:T(8,128)S(1)} %get-tuple-element.53.own_ref, bf16[256,256]{1,0:T(8,128)(2,1)S(1)} %get-tuple-element.54.wide_ref, f32[24,256]{1,0:T(8,128)S(1)} %get-tuple-element.49._.above_ref, ...), custom_call_target="tpu_custom_call" | custom-call | flops 10000000 | bytes 100000 | tf_op jit(solution)/shard_map/pallas_call | solution.py:442
  37.5 0.4 collective-permute-start.5
  37.9 0.3 shard_map.142.keep_ref
  38.2 0.7 collective-permute-done.5.got_ref
  38.9 17.9 %all_to_all.35 = bf16[128,4,128]{2,1,0:T(4,128)(2,1)S(1)} all-to-all(bf16[128,4,128]{2,1,0:T(4,128)(2,1)S(1)} %bitcast.15), channel_id=1, replica_groups={{0,1,2,3,4,5,6,7,16,17,18,19,20,21,22,23,32,33,34,35,36,37,38,39,48,49,..., dimensions={0} | all-to-all | bytes 262144 | tf_op jit(solution)/shard_map/all_to_all | solution.py:478
  56.8 0.7 shard_map.144
  57.6 6.5 %all-to-all-start.2 = ((bf16[128,4,128]{2,1,0:T(4,128)(2,1)}), bf16[128,4,128]{2,1,0:T(4,128)(2,1)S(1)}, u32[]{:S(2)}, u32[]{:S(2)}) async-start(bf16[128,4,128]{2,1,0:T(4,128)(2,1)} %bitcast.8), calls=%async_computation.2 | async-start | bytes 262144 | tf_op jit(solution)/shard_map/all_to_all | solution.py:478
  64.0 0.4 shard_map.145.back_ref
  64.5 0.7 shard_map.146
  65.1 9.3 %all-to-all-done.2 = bf16[128,4,128]{2,1,0:T(4,128)(2,1)S(1)} async-done(((bf16[128,4,128]{2,1,0:T(4,128)(2,1)}), bf16[128,4,128]{2,1,0:T(4,128)(2,1)S(1)}, u32[]{:S(2)}, u32[]{:S(2)}) %all-to-all-start.2) | async-done | bytes 131104 | tf_op jit(solution)/shard_map/all_to_all | solution.py:478
  74.4 2.9 %collective-permute-start.6 = (bf16[512,128]{1,0:T(8,128)(2,1)S(1)}, bf16[512,128]{1,0:T(8,128)(2,1)S(1)}, u32[]{:S(2)}, u32[]{:S(2)}) collective-permute-start(bf16[512,128]{1,0:T(8,128)(2,1)S(1)} %bitcast.11), channel_id=1, source_target_pairs={{0,8},{8,0},{16,24},{24,16},{32,40},{40,32},{48,56},{56,48},{64,72... | collective-permute-start | bytes 393224 | tf_op jit(solution)/shard_map/ppermute | solution.py:482
  77.3 1.3 %shard_map.147 = bf16[144,256]{1,0:T(8,128)(2,1)} custom-call(bf16[512,128]{1,0:T(8,128)(2,1)S(1)} %bitcast.12, f32[144,256]{1,0:T(8,128)S(1)} %get-tuple-element.78.outp_ref, bf16[9,192,64]{2,1,0:T(8,128)(2,1)S(1)} %shard_map.145.back_ref, bf16[64,256]{1,0:T(8,128)(2,1)S(1)} %get-tuple-element.80.utp_ref), custom_call_target="tpu_custom_call" | custom-call | flops 1000000000 | bytes 100000 | tf_op jit(solution)/shard_map/pallas_call | solution.py:442
  78.6 0.0 collective-permute-done.6.other_ref
  78.6 2.6 %shard_map.148 = bf16[27,256,256]{2,1,0:T(8,128)(2,1)} custom-call(bf16[512,128]{1,0:T(8,128)(2,1)S(1)} %bitcast.13, bf16[512,128]{1,0:T(8,128)(2,1)S(1)} %collective-permute-done.6.other_ref, bf16[256,64]{1,0:T(8,128)(2,1)S(1)} %get-tuple-element.86.u_ref, bf16[64,256]{1,0:T(8,128)(2,1)S(1)} %get-tuple-element.64.ot_ref, ...), custom_call_target="tpu_custom_call" | custom-call | flops 10000000 | bytes 100000 | tf_op jit(solution)/shard_map/pallas_call | solution.py:442
  (1 shorter events, 0.0 us)
Async XLA Ops:
  2.2 19.9 %collective-permute-start = (bf16[3,8,256]{2,1,0:T(8,128)(2,1)S(1)}, bf16[3,8,256]{2,1,0:T(8,128)(2,1)S(1)}, u32[]{:S(2)}, u32[]{:S(2)}) collective-permute-start(bf16[3,8,256]{2,1,0:T(8,128)(2,1)S(1)} %get-tuple-element.47), channel_id=1, source_target_pairs={{8,16},{24,32},{40,48},{56,64},{72,80},{88,96},{104,112},{120,128}... | collective-permute-start | bytes 36872 | tf_op jit(solution)/shard_map/ppermute | solution.py:465
  6.7 15.3 %collective-permute-start.1 = (bf16[3,8,256]{2,1,0:T(8,128)(2,1)S(1)}, bf16[3,8,256]{2,1,0:T(8,128)(2,1)S(1)}, u32[]{:S(2)}, u32[]{:S(2)}) collective-permute-start(bf16[3,8,256]{2,1,0:T(8,128)(2,1)S(1)} %get-tuple-element.48), channel_id=1, source_target_pairs={{0,8},{16,24},{32,40},{48,56},{64,72},{80,88},{96,104},{112,120},{... | collective-permute-start | bytes 36872 | tf_op jit(solution)/shard_map/ppermute | solution.py:465
  6.8 25.6 %all-to-all-start = ((bf16[128,4,128]{2,1,0:T(4,128)(2,1)}), bf16[128,4,128]{2,1,0:T(4,128)(2,1)S(1)}, u32[]{:S(2)}, u32[]{:S(2)}) async-start(bf16[128,4,128]{2,1,0:T(4,128)(2,1)} %bitcast.4), calls=%async_computation | async-start | bytes 262144 | tf_op jit(solution)/shard_map/all_to_all | solution.py:478
  22.1 13.9 %collective-permute-start.2 = (bf16[24,256]{1,0:T(8,128)(2,1)S(1)}, bf16[24,256]{1,0:T(8,128)(2,1)S(1)}, u32[]{:S(2)}, u32[]{:S(2)}) collective-permute-start(bf16[24,256]{1,0:T(8,128)(2,1)S(1)} %get-tuple-element.56), channel_id=1, source_target_pairs={{1,2},{3,4},{5,6},{2,1},{4,3},{6,5},{9,10},{11,12},{13,14},{10,9},... | collective-permute-start | bytes 36872 | tf_op jit(solution)/shard_map/ppermute | solution.py:465
  22.8 13.2 %collective-permute-start.3 = (bf16[24,256]{1,0:T(8,128)(2,1)S(1)}, bf16[24,256]{1,0:T(8,128)(2,1)S(1)}, u32[]{:S(2)}, u32[]{:S(2)}) collective-permute-start(bf16[24,256]{1,0:T(8,128)(2,1)S(1)} %get-tuple-element.57), channel_id=1, source_target_pairs={{0,1},{2,3},{4,5},{6,7},{1,0},{3,2},{5,4},{7,6},{8,9},{10,11},{12,... | collective-permute-start | bytes 36872 | tf_op jit(solution)/shard_map/ppermute | solution.py:465
  32.4 3.1 %collective-permute-start.4 = (bf16[512,128]{1,0:T(8,128)(2,1)S(1)}, bf16[512,128]{1,0:T(8,128)(2,1)S(1)}, u32[]{:S(2)}, u32[]{:S(2)}) collective-permute-start(bf16[512,128]{1,0:T(8,128)(2,1)S(1)} %bitcast.16), channel_id=1, source_target_pairs={{0,8},{8,0},{16,24},{24,16},{32,40},{40,32},{48,56},{56,48},{64,72... | collective-permute-start | bytes 393224 | tf_op jit(solution)/shard_map/ppermute | solution.py:482
  37.5 1.4 %collective-permute-start.5 = (bf16[512,128]{1,0:T(8,128)(2,1)S(1)}, bf16[512,128]{1,0:T(8,128)(2,1)S(1)}, u32[]{:S(2)}, u32[]{:S(2)}) collective-permute-start(bf16[512,128]{1,0:T(8,128)(2,1)S(1)} %get-tuple-element.68), channel_id=1, source_target_pairs={{0,8},{8,0},{16,24},{24,16},{32,40},{40,32},{48,56},{56,48},{64,72... | collective-permute-start | bytes 393224 | tf_op jit(solution)/shard_map/ppermute | solution.py:482
  57.6 16.9 %all-to-all-start.2 = ((bf16[128,4,128]{2,1,0:T(4,128)(2,1)}), bf16[128,4,128]{2,1,0:T(4,128)(2,1)S(1)}, u32[]{:S(2)}, u32[]{:S(2)}) async-start(bf16[128,4,128]{2,1,0:T(4,128)(2,1)} %bitcast.8), calls=%async_computation.2 | async-start | bytes 262144 | tf_op jit(solution)/shard_map/all_to_all | solution.py:478
  74.4 4.2 %collective-permute-start.6 = (bf16[512,128]{1,0:T(8,128)(2,1)S(1)}, bf16[512,128]{1,0:T(8,128)(2,1)S(1)}, u32[]{:S(2)}, u32[]{:S(2)}) collective-permute-start(bf16[512,128]{1,0:T(8,128)(2,1)S(1)} %bitcast.11), channel_id=1, source_target_pairs={{0,8},{8,0},{16,24},{24,16},{32,40},{40,32},{48,56},{56,48},{64,72... | collective-permute-start | bytes 393224 | tf_op jit(solution)/shard_map/ppermute | solution.py:482

commit v16 on v15

--- a/solution.py
+++ b/solution.py
@@ -475,7 +475,7 @@
 
 
 def exchange(x):
-    return lax.all_to_all(x, AXES, 0, 0, tiled=True, axis_index_groups=ORDER)
+    return lax.all_to_all(x, AXES, 0, 0, tiled=True, axis_index_groups=ORDER[::-1])
 
 
 def in_chip(x):

time: 81.5 us -> 81.5 us (level)
  no operation moved by 1% of the time
where the time goes in v16:
time: 81.5 us; the launch traced here: 81.2 us
  starting transfers between devices  35.5 us (44%)
  blocking collectives  17.9 us (22%)
  waiting for transfers between devices  17.1 us (21%)
  Pallas kernels  9.98 us (12%)
    all_to_all x2, starting transfers between devices, exchange(): lax.all_to_all(x, AXES, 0, 0, tiled=True, axis_index_groups=ORDER[::-1])  21.7 us
    all_to_all x1, blocking collectives, exchange(): lax.all_to_all(x, AXES, 0, 0, tiled=True, axis_index_groups=ORDER[::-1])  17.9 us
    all_to_all x2, waiting for transfers between devices, exchange(): lax.all_to_all(x, AXES, 0, 0, tiled=True, axis_index_groups=ORDER[::-1])  15.8 us
    pallas_call x12, Pallas kernels, call(): pl.pallas_call(kernel, out_shape=[jax.ShapeDtypeStruct(shape, dtype) for...  9.98 us
    ppermute x4, starting transfers between devices, swap(): lax.ppermute(x, axis, forward + [(b, a) for a, b in forward])  8.35 us
    ppermute x3, starting transfers between devices, in_chip(): return lax.ppermute(x, 'rows', [(r, r ^ 1) for r in range(32)])  5.46 us
  transfers between devices with their start and end apart: 9, of which 4 were waited for; matrix products, arithmetic and copies ran while one was open for 0% of the time, Pallas kernels for 4%

profile of v16, /device:TPU:1, one launch (start us, length us, event | category | flops | bytes accessed | tf_op | source)
XLA Modules:
  0.0 81.2 jit_solution(4131104202923709535)
XLA Ops:
  0.6 1.5 %shard_map.137 = (bf16[512,128]{1,0:T(8,128)(2,1)}, bf16[3,8,256]{2,1,0:T(8,128)(2,1)S(1)}, bf16[3,8,256]{2,1,0:T(8,128)(2,1)S(1)}, bf16[3,6,8,256]{3,2,1,0:T(8,...) custom-call(f32[432]{0:T(512)} %core_ref.1, ...), custom_call_target="tpu_custom_call" | custom-call | flops 10000000 | bytes 100000 | tf_op jit(solution)/shard_map/pallas_call | solution.py:442
  2.2 4.5 %collective-permute-start = (bf16[3,8,256]{2,1,0:T(8,128)(2,1)S(1)}, bf16[3,8,256]{2,1,0:T(8,128)(2,1)S(1)}, u32[]{:S(2)}, u32[]{:S(2)}) collective-permute-start(bf16[3,8,256]{2,1,0:T(8,128)(2,1)S(1)} %get-tuple-element.47), channel_id=1, source_target_pairs={{8,16},{24,32},{40,48},{56,64},{72,80},{88,96},{104,112},{120,128}... | collective-permute-start | bytes 36872 | tf_op jit(solution)/shard_map/ppermute | solution.py:465
  6.7 0.1 collective-permute-start.1
  6.8 15.2 %all-to-all-start = ((bf16[128,4,128]{2,1,0:T(4,128)(2,1)}), bf16[128,4,128]{2,1,0:T(4,128)(2,1)S(1)}, u32[]{:S(2)}, u32[]{:S(2)}) async-start(bf16[128,4,128]{2,1,0:T(4,128)(2,1)} %bitcast.4), calls=%async_computation | async-start | bytes 262144 | tf_op jit(solution)/shard_map/all_to_all | solution.py:478
  22.0 0.0 collective-permute-done.two_ref
  22.0 0.0 collective-permute-done.1.one_ref
  22.1 0.1 shard_map.138
  22.1 0.7 collective-permute-start.2
  22.8 3.1 %collective-permute-start.3 = (bf16[24,256]{1,0:T(8,128)(2,1)S(1)}, bf16[24,256]{1,0:T(8,128)(2,1)S(1)}, u32[]{:S(2)}, u32[]{:S(2)}) collective-permute-start(bf16[24,256]{1,0:T(8,128)(2,1)S(1)} %get-tuple-element.57), channel_id=1, source_target_pairs={{0,1},{2,3},{4,5},{6,7},{1,0},{3,2},{5,4},{7,6},{8,9},{10,11},{12,... | collective-permute-start | bytes 36872 | tf_op jit(solution)/shard_map/ppermute | solution.py:465
  25.9 6.5 %all-to-all-done = bf16[128,4,128]{2,1,0:T(4,128)(2,1)S(1)} async-done(((bf16[128,4,128]{2,1,0:T(4,128)(2,1)}), bf16[128,4,128]{2,1,0:T(4,128)(2,1)S(1)}, u32[]{:S(2)}, u32[]{:S(2)}) %all-to-all-start) | async-done | bytes 131104 | tf_op jit(solution)/shard_map/all_to_all | solution.py:478
  32.4 2.1 %collective-permute-start.4 = (bf16[512,128]{1,0:T(8,128)(2,1)S(1)}, bf16[512,128]{1,0:T(8,128)(2,1)S(1)}, u32[]{:S(2)}, u32[]{:S(2)}) collective-permute-start(bf16[512,128]{1,0:T(8,128)(2,1)S(1)} %bitcast.16), channel_id=1, source_target_pairs={{0,8},{8,0},{16,24},{24,16},{32,40},{40,32},{48,56},{56,48},{64,72... | collective-permute-start | bytes 393224 | tf_op jit(solution)/shard_map/ppermute | solution.py:482
  34.5 0.3 shard_map.139
  34.9 0.6 collective-permute-done.4.other_ref
  35.5 0.5 shard_map.140
  36.0 0.0 collective-permute-done.2.two_ref
  36.0 0.0 collective-permute-done.3.one_ref
  36.0 1.5 %shard_map.141 = (bf16[512,128]{1,0:T(8,128)(2,1)S(1)}, f32[864,128]{1,0:T(8,128)S(1)}, f32[96,128]{1,0:T(8,128)S(1)}, f32[144,256]{1,0:T(8,128)S(1)}) custom-call(f32[144,256]{1,0:T(8,128)S(1)} %get-tuple-element.53.own_ref, bf16[256,256]{1,0:T(8,128)(2,1)S(1)} %get-tuple-element.54.wide_ref, f32[24,256]{1,0:T(8,128)S(1)} %get-tuple-element.49._.above_ref, ...), custom_call_target="tpu_custom_call" | custom-call | flops 10000000 | bytes 100000 | tf_op jit(solution)/shard_map/pallas_call | solution.py:442
  37.5 0.4 collective-permute-start.5
  37.9 0.3 shard_map.142.keep_ref
  38.2 0.7 collective-permute-done.5.got_ref
  38.9 17.9 %all_to_all.35 = bf16[128,4,128]{2,1,0:T(4,128)(2,1)S(1)} all-to-all(bf16[128,4,128]{2,1,0:T(4,128)(2,1)S(1)} %bitcast.15), channel_id=1, replica_groups={{8,9,10,11,12,13,14,15,24,25,26,27,28,29,30,31,40,41,42,43,44,45,46,47,..., dimensions={0} | all-to-all | bytes 262144 | tf_op jit(solution)/shard_map/all_to_all | solution.py:478
  56.8 0.7 shard_map.144
  57.6 6.5 %all-to-all-start.2 = ((bf16[128,4,128]{2,1,0:T(4,128)(2,1)}), bf16[128,4,128]{2,1,0:T(4,128)(2,1)S(1)}, u32[]{:S(2)}, u32[]{:S(2)}) async-start(bf16[128,4,128]{2,1,0:T(4,128)(2,1)} %bitcast.8), calls=%async_computation.2 | async-start | bytes 262144 | tf_op jit(solution)/shard_map/all_to_all | solution.py:478
  64.0 0.4 shard_map.145.back_ref
  64.5 0.7 shard_map.146
  65.1 9.3 %all-to-all-done.2 = bf16[128,4,128]{2,1,0:T(4,128)(2,1)S(1)} async-done(((bf16[128,4,128]{2,1,0:T(4,128)(2,1)}), bf16[128,4,128]{2,1,0:T(4,128)(2,1)S(1)}, u32[]{:S(2)}, u32[]{:S(2)}) %all-to-all-start.2) | async-done | bytes 131104 | tf_op jit(solution)/shard_map/all_to_all | solution.py:478
  74.4 2.9 %collective-permute-start.6 = (bf16[512,128]{1,0:T(8,128)(2,1)S(1)}, bf16[512,128]{1,0:T(8,128)(2,1)S(1)}, u32[]{:S(2)}, u32[]{:S(2)}) collective-permute-start(bf16[512,128]{1,0:T(8,128)(2,1)S(1)} %bitcast.11), channel_id=1, source_target_pairs={{0,8},{8,0},{16,24},{24,16},{32,40},{40,32},{48,56},{56,48},{64,72... | collective-permute-start | bytes 393224 | tf_op jit(solution)/shard_map/ppermute | solution.py:482
  77.3 1.3 %shard_map.147 = bf16[144,256]{1,0:T(8,128)(2,1)} custom-call(bf16[512,128]{1,0:T(8,128)(2,1)S(1)} %bitcast.12, f32[144,256]{1,0:T(8,128)S(1)} %get-tuple-element.78.outp_ref, bf16[9,192,64]{2,1,0:T(8,128)(2,1)S(1)} %shard_map.145.back_ref, bf16[64,256]{1,0:T(8,128)(2,1)S(1)} %get-tuple-element.80.utp_ref), custom_call_target="tpu_custom_call" | custom-call | flops 1000000000 | bytes 100000 | tf_op jit(solution)/shard_map/pallas_call | solution.py:442
  78.6 0.0 collective-permute-done.6.other_ref
  78.6 2.6 %shard_map.148 = bf16[27,256,256]{2,1,0:T(8,128)(2,1)} custom-call(bf16[512,128]{1,0:T(8,128)(2,1)S(1)} %bitcast.13, bf16[512,128]{1,0:T(8,128)(2,1)S(1)} %collective-permute-done.6.other_ref, bf16[256,64]{1,0:T(8,128)(2,1)S(1)} %get-tuple-element.86.u_ref, bf16[64,256]{1,0:T(8,128)(2,1)S(1)} %get-tuple-element.64.ot_ref, ...), custom_call_target="tpu_custom_call" | custom-call | flops 10000000 | bytes 100000 | tf_op jit(solution)/shard_map/pallas_call | solution.py:442
  (1 shorter events, 0.0 us)
Async XLA Ops:
  2.2 19.9 %collective-permute-start = (bf16[3,8,256]{2,1,0:T(8,128)(2,1)S(1)}, bf16[3,8,256]{2,1,0:T(8,128)(2,1)S(1)}, u32[]{:S(2)}, u32[]{:S(2)}) collective-permute-start(bf16[3,8,256]{2,1,0:T(8,128)(2,1)S(1)} %get-tuple-element.47), channel_id=1, source_target_pairs={{8,16},{24,32},{40,48},{56,64},{72,80},{88,96},{104,112},{120,128}... | collective-permute-start | bytes 36872 | tf_op jit(solution)/shard_map/ppermute | solution.py:465
  6.7 15.3 %collective-permute-start.1 = (bf16[3,8,256]{2,1,0:T(8,128)(2,1)S(1)}, bf16[3,8,256]{2,1,0:T(8,128)(2,1)S(1)}, u32[]{:S(2)}, u32[]{:S(2)}) collective-permute-start(bf16[3,8,256]{2,1,0:T(8,128)(2,1)S(1)} %get-tuple-element.48), channel_id=1, source_target_pairs={{0,8},{16,24},{32,40},{48,56},{64,72},{80,88},{96,104},{112,120},{... | collective-permute-start | bytes 36872 | tf_op jit(solution)/shard_map/ppermute | solution.py:465
  6.8 25.6 %all-to-all-start = ((bf16[128,4,128]{2,1,0:T(4,128)(2,1)}), bf16[128,4,128]{2,1,0:T(4,128)(2,1)S(1)}, u32[]{:S(2)}, u32[]{:S(2)}) async-start(bf16[128,4,128]{2,1,0:T(4,128)(2,1)} %bitcast.4), calls=%async_computation | async-start | bytes 262144 | tf_op jit(solution)/shard_map/all_to_all | solution.py:478
  22.1 13.9 %collective-permute-start.2 = (bf16[24,256]{1,0:T(8,128)(2,1)S(1)}, bf16[24,256]{1,0:T(8,128)(2,1)S(1)}, u32[]{:S(2)}, u32[]{:S(2)}) collective-permute-start(bf16[24,256]{1,0:T(8,128)(2,1)S(1)} %get-tuple-element.56), channel_id=1, source_target_pairs={{1,2},{3,4},{5,6},{2,1},{4,3},{6,5},{9,10},{11,12},{13,14},{10,9},... | collective-permute-start | bytes 36872 | tf_op jit(solution)/shard_map/ppermute | solution.py:465
  22.8 13.2 %collective-permute-start.3 = (bf16[24,256]{1,0:T(8,128)(2,1)S(1)}, bf16[24,256]{1,0:T(8,128)(2,1)S(1)}, u32[]{:S(2)}, u32[]{:S(2)}) collective-permute-start(bf16[24,256]{1,0:T(8,128)(2,1)S(1)} %get-tuple-element.57), channel_id=1, source_target_pairs={{0,1},{2,3},{4,5},{6,7},{1,0},{3,2},{5,4},{7,6},{8,9},{10,11},{12,... | collective-permute-start | bytes 36872 | tf_op jit(solution)/shard_map/ppermute | solution.py:465
  32.4 3.1 %collective-permute-start.4 = (bf16[512,128]{1,0:T(8,128)(2,1)S(1)}, bf16[512,128]{1,0:T(8,128)(2,1)S(1)}, u32[]{:S(2)}, u32[]{:S(2)}) collective-permute-start(bf16[512,128]{1,0:T(8,128)(2,1)S(1)} %bitcast.16), channel_id=1, source_target_pairs={{0,8},{8,0},{16,24},{24,16},{32,40},{40,32},{48,56},{56,48},{64,72... | collective-permute-start | bytes 393224 | tf_op jit(solution)/shard_map/ppermute | solution.py:482
  37.5 1.4 %collective-permute-start.5 = (bf16[512,128]{1,0:T(8,128)(2,1)S(1)}, bf16[512,128]{1,0:T(8,128)(2,1)S(1)}, u32[]{:S(2)}, u32[]{:S(2)}) collective-permute-start(bf16[512,128]{1,0:T(8,128)(2,1)S(1)} %get-tuple-element.68), channel_id=1, source_target_pairs={{0,8},{8,0},{16,24},{24,16},{32,40},{40,32},{48,56},{56,48},{64,72... | collective-permute-start | bytes 393224 | tf_op jit(solution)/shard_map/ppermute | solution.py:482
  57.6 16.9 %all-to-all-start.2 = ((bf16[128,4,128]{2,1,0:T(4,128)(2,1)}), bf16[128,4,128]{2,1,0:T(4,128)(2,1)S(1)}, u32[]{:S(2)}, u32[]{:S(2)}) async-start(bf16[128,4,128]{2,1,0:T(4,128)(2,1)} %bitcast.8), calls=%async_computation.2 | async-start | bytes 262144 | tf_op jit(solution)/shard_map/all_to_all | solution.py:478
  74.4 4.2 %collective-permute-start.6 = (bf16[512,128]{1,0:T(8,128)(2,1)S(1)}, bf16[512,128]{1,0:T(8,128)(2,1)S(1)}, u32[]{:S(2)}, u32[]{:S(2)}) collective-permute-start(bf16[512,128]{1,0:T(8,128)(2,1)S(1)} %bitcast.11), channel_id=1, source_target_pairs={{0,8},{8,0},{16,24},{24,16},{32,40},{40,32},{48,56},{56,48},{64,72... | collective-permute-start | bytes 393224 | tf_op jit(solution)/shard_map/ppermute | solution.py:482
